TPU v7x, 256 devices: a whole 4x4x8 slice. The times are simulated.
256 devices in a mesh: row: 32 (over x_lo, z, core), feat: 8 (over x_hi, y).
Axes of the slice: x: 4 (x_hi: 2, x_lo: 2; x = x_hi * 2 + x_lo), y: 4, z: 8, core: 2. Of those that a mesh axis runs over, the one named last changes fastest.
Arguments:
- features: bfloat16 [8192, 1024], P('row', 'feat'), may hold values from -6 to 6
- weight: bfloat16 [1024, 1024], P('feat'), may hold values from -0.1875 to 0.1875
- bias_vector: bfloat16 [1024], P('feat'), may hold values from -3 to 3
- adj_tiles: bfloat16 [2048, 128, 128], P('row'), may hold values from -0.09375 to 0.09375
- col_blocks: int32 [2048], P('row'), may hold values from 0 to 63, as said below
- dest_blocks: int32 [2048], P('row'), may hold values from 0 to 1
- out_grad: bfloat16 [8192, 1024], P('row', 'feat'), may hold values from -6 to 6
Outputs:
- hidden: float32 [8192, 1024], P('row', 'feat')
- input_grad: float32 [8192, 1024], P('row', 'feat')
- weight_grad: float32 [1024, 1024], P('feat')
- bias_grad: float32 [1024], P('feat')
Inputs may be any that keep to these rules, and one draw needn't show every extreme that they name: Within the 64 entries of one index r of row, col_blocks // 2 never falls from one entry to the next and is never r; at most 4 of them lie in any one index's range of 2 blocks, and exactly 4 lie in the range of index (r + 1) mod 32.
All inputs are finite; a program needn't handle non-finite values.
Results may differ from a plain program's by a relative error of at most 0.0055.
Values may be sent and summed in bfloat16 or wider, within the bound.
No kernel may reach another device: no remote copies, remote signals or barrier semaphores. Data moves between devices by JAX's collectives and lax.ppermute only.
A program may use at most 64 MiB of HBM per device.

v0:
```python
import functools

import jax
import jax.numpy as jnp
from jax import lax
from jax.experimental import pallas as pl
from jax.experimental.pallas import tpu as pltpu
from jax.sharding import PartitionSpec as P

bf16 = jnp.bfloat16
f32 = jnp.float32
B = 128
NZ = 8
VM = pl.BlockSpec(memory_space=pltpu.VMEM)
SM = pl.BlockSpec(memory_space=pltpu.SMEM)
HB = pl.BlockSpec(memory_space=pltpu.HBM)
ANY = pl.BlockSpec(memory_space=pl.ANY)


def row_send(v, dx=0, dz=0, dc=0):
    perm = []
    for i in range(32):
        x, z, c = i >> 4, (i >> 1) & 7, i & 1
        perm.append((i, ((x ^ dx) << 4) | (((z + dz) % NZ) << 1) | (c ^ dc)))
    return lax.ppermute(v, "row", perm)


def feat_send(v, dx=0, dy=0):
    return lax.ppermute(v, "feat", [(i, (((i >> 2) ^ dx) << 2) | ((i + dy) & 3)) for i in range(8)])


def params(mib=20):
    return pltpu.CompilerParams(vmem_limit_bytes=mib << 20)


def spin_send(v, k, way=1):
    perm = []
    for i in range(32):
        x, z, c = i >> 4, (i >> 1) & 7, i & 1
        perm.append((i, (x << 4) | (((z + way * (k if c == 0 else -k)) % NZ) << 1) | c))
    return lax.ppermute(v, "row", perm)


def tie(a, b):
    return lax.optimization_barrier((a, b))


def cost(flops, nbytes):
    return pl.CostEstimate(flops=flops, bytes_accessed=nbytes, transcendentals=0)


def pack_body(ids, w, og, bias, out):
    core = ids[0] & 1
    for m in range(4):
        at = pl.multiple_of(core * 512 + m * B, B)
        out[m * B : (m + 1) * B, :] = w[:, pl.ds(at, B)]
    out[512:768, :] = og[...]
    out[768:784, :] = jnp.broadcast_to(bias[...], (16, B))


def pack_up(ids, w, og, bias):
    return pl.pallas_call(
        pack_body,
        out_shape=jax.ShapeDtypeStruct((784, B), bf16),
        in_specs=[SM, VM, VM, VM],
        out_specs=VM,
        compiler_params=params(8),
        cost_estimate=cost(0, 1 << 19),
        name="pack_up",
    )(ids, w, og, bias)


def plan_body(ids, c0, d0, c1, d1, out):
    me = ids[0]
    mx, mz, mc = me >> 4, (me >> 1) & 7, me & 1
    for side, (cols, dest) in enumerate(((c0, d0), (c1, d1))):
        base = 8 + 72 * side

        def step(i, n, cols=cols, dest=dest, base=base, side=side):
            b = cols[i]
            o = b >> 1
            dx, dz, dc = (o >> 4) ^ mx, ((o >> 1) - mz) & 7, (o & 1) ^ mc
            k = jnp.where(mc == 0, dz, NZ - dz)
            edge = (dz & 3) == 0
            held = jnp.where(edge, 1 - dc, jnp.where(k <= 3, 1, 0))
            j = jnp.where(edge, jnp.where(dz == 0, 7, 6), (3 - k) * 2 + dc)
            slot = dx * 16 + j * 2 + (b & 1)
            out[base + n] = i | (slot << 8) | ((dest[i] + 2 * side) << 16)
            return n + held

        n = lax.fori_loop(0, 64, step, 0)
        for u in range(4):
            out[base + n + u] = (32 << 8) | (4 << 16)
        out[side] = (n + 3) >> 2


def plan_tiles(ids, c0, d0, c1, d1):
    return pl.pallas_call(
        plan_body,
        out_shape=jax.ShapeDtypeStruct((160,), jnp.int32),
        in_specs=[SM] * 5,
        out_specs=SM,
        compiler_params=params(4),
        cost_estimate=cost(10000, 4096),
        name="plan_tiles",
    )(ids, c0, d0, c1, d1)


def each_tile(plan, tiles, more, use):
    for side, ref in enumerate((tiles, more)):
        def step(g, carry, side=side, ref=ref):
            for u in range(4):
                e = plan[8 + 72 * side + g * 4 + u]
                use(ref[e & 255], (e >> 8) & 255, e >> 16)
            return carry

        lax.fori_loop(0, plan[side], step, 0)


def agg_body(plan, tiles, more, *refs):
    pieces, mine, theirs, src, acc, sem = refs[0:10], refs[10], refs[11], refs[12], refs[13], refs[14]
    both, x0, o4, o1, o2, o3, p4, p1, p2, p3 = pieces
    copies = []

    def put(dx, j, v):
        n = v.shape[0]
        at = dx * 16 + j * 2
        copies.append(pltpu.make_async_copy(v, src.at[at : at + n], sem.at[len(copies)]))
        copies[-1].start()

    for dx, (v3, v2, v1, v4, v0) in enumerate(((o3, o2, o1, o4, both.at[0:2]), (p3, p2, p1, p4, x0))):
        for j, v in ((0, v3), (2, v2), (4, v1), (6, v4), (7, v0)):
            put(dx, j, v)
    acc[...] = jnp.zeros_like(acc)
    src[32] = jnp.zeros((B, B), bf16)
    for c in copies:
        c.wait()

    def use(tile, slot, dest):
        acc[dest] += jnp.dot(tile, src[slot], preferred_element_type=f32)

    each_tile(plan, tiles, more, use)
    mine[...] = acc[0:2]
    theirs[...] = acc[2:4]


def aggregate(plan, tiles, more, pieces):
    parts = [v.reshape(-1, B, B) for v in pieces]
    return pl.pallas_call(
        agg_body,
        out_shape=(jax.ShapeDtypeStruct((2, B, B), f32), jax.ShapeDtypeStruct((2, B, B), f32)),
        in_specs=[SM, VM, VM] + [HB] * 10,
        out_specs=(VM, VM),
        scratch_shapes=[
            pltpu.VMEM((33, B, B), bf16),
            pltpu.VMEM((5, B, B), f32),
            pltpu.SemaphoreType.DMA((10,)),
        ],
        compiler_params=params(12),
        cost_estimate=cost(2 * 64 * B**3, 4 << 20),
        name="aggregate",
    )(plan, tiles, more, *parts)


def lay_body(ids, *refs):
    own = refs[0:5]
    w_out, og_out, bias_out, rows, sem = refs[5:10]
    yy, xx = ids[1] & 3, ids[1] >> 2
    copies, cols = [], []

    def put(src, dst):
        copies.append(pltpu.make_async_copy(src, dst, sem.at[len(copies)]))
        copies[-1].start()

    for j, off in enumerate((0, -1, 1, 2)):
        for i in range(2):
            k = j * 2 + i
            n, base = (j, i * 784) if j < 3 else (3 + i, 0)
            col = pl.multiple_of((((xx ^ i) << 2) | ((yy + off) & 3)) * B, B)
            cols.append(col)
            for m in range(4):
                put(own[n].at[pl.ds(base + m * B, B), :], w_out.at[pl.ds(k * B, B), pl.ds(m * B, B)])
            put(own[n].at[pl.ds(base + 512, 256), :], og_out.at[:, pl.ds(col, B)])
            put(own[n].at[pl.ds(base + 768, 16), :], rows.at[k])
    for c in copies:
        c.wait()
    for k in range(8):
        bias_out[:, pl.ds(cols[k], B)] = rows[k].astype(f32)[0:8]


def lay_out(ids, own):
    return pl.pallas_call(
        lay_body,
        out_shape=(
            jax.ShapeDtypeStruct((1024, 512), bf16),
            jax.ShapeDtypeStruct((256, 1024), bf16),
            jax.ShapeDtypeStruct((8, 1024), f32),
        ),
        in_specs=[SM] + [HB] * 5,
        out_specs=(VM, VM, VM),
        scratch_shapes=[pltpu.VMEM((8, 16, B), bf16), pltpu.SemaphoreType.DMA((48,))],
        compiler_params=params(8),
        cost_estimate=cost(0, 3 << 20),
        name="lay_out",
    )(ids, *own)


def mid_body(ids, p0, p1, p2, p3, w0, w1, og, bias, w_own, hidden, prop, keep, give, agg, pre, gp, wp):
    x, core = ids[0] >> 4, ids[0] & 1
    for j, p in enumerate((p0, p1, p2, p3)):
        for i in range(2):
            agg[:, (j * 2 + i) * B : (j * 2 + i + 1) * B] = p[i * 256 : (i + 1) * 256, :]
    for w, c in ((w0, core), (w1, 1 - core)):
        for m in range(2):
            cols = pl.ds(pl.multiple_of(c * 512 + m * 256, 256), 256)
            v = jnp.dot(agg[...], w[:, m * 256 : (m + 1) * 256], preferred_element_type=f32)
            v = v + bias[0:1, cols]
            pre[:, cols] = v
            s = jax.nn.sigmoid(v)
            gp[:, cols] = (og[:, cols].astype(f32) * s * (1.0 + v * (1.0 - s))).astype(bf16)
    mine = pl.ds(pl.multiple_of(ids[1] * B, B), B)
    v = pre[:, mine]
    hidden[...] = v * jax.nn.sigmoid(v)
    prop[...] = lax.dot_general(
        gp[...], w_own[...], (((1,), (1,)), ((), ())), preferred_element_type=f32
    ).astype(bf16)
    wp[:, 0:1024] = lax.dot_general(
        agg[:, 0:B], gp[...], (((0,), (0,)), ((), ())), preferred_element_type=f32
    )
    total = jnp.sum(gp[:, mine].astype(f32), axis=0, keepdims=True)
    wp[:, 1024:1152] = jnp.broadcast_to(total, (B, B))
    for ref, c in ((keep, core), (give, 1 - core)):
        for i in range(2):
            ref[i * 32 : (i + 1) * 32, :] = wp[pl.ds(pl.multiple_of(c * 64 + (x ^ i) * 32, 32), 32), :]


def middle(ids, pieces, w0, w1, og, bias, w_own):
    return pl.pallas_call(
        mid_body,
        out_shape=(
            jax.ShapeDtypeStruct((256, B), f32),
            jax.ShapeDtypeStruct((256, B), bf16),
            jax.ShapeDtypeStruct((64, 1152), f32),
            jax.ShapeDtypeStruct((64, 1152), f32),
        ),
        in_specs=[SM] + [VM] * 9,
        out_specs=(VM, VM, VM, VM),
        scratch_shapes=[
            pltpu.VMEM((256, 1024), bf16),
            pltpu.VMEM((256, 1024), f32),
            pltpu.VMEM((256, 1024), bf16),
            pltpu.VMEM((B, 1152), f32),
        ],
        compiler_params=params(),
        cost_estimate=cost(2 * 256 * 1024 * 1280, 5 << 20),
        name="middle",
    )(ids, *pieces, w0, w1, og, bias, w_own)


def spread_body(plan, tiles, more, prop, peer, keep, got, near, first, rest, acc, both):
    acc[...] = jnp.zeros_like(acc)
    both[0:2] = prop[...]
    both[2:4] = peer[...]
    both[4] = jnp.zeros((B, B), bf16)

    def use(tile, slot, dest):
        acc[slot] += lax.dot_general(
            tile, both[dest], (((0,), (0,)), ((), ())), preferred_element_type=f32
        )

    each_tile(plan, tiles, more, use)
    near[...] = acc[0:16]
    for n in range(2):
        first[n * B : (n + 1) * B, :] = acc[28 + n].astype(bf16)
    for n in range(9):
        cols = slice(n * B, (n + 1) * B)
        first[256 + 32 * n : 288 + 32 * n, :] = (keep[32:64, cols] + got[32:64, cols]).astype(bf16)
    rest[0:12] = acc[16:28].astype(bf16)
    rest[12:14] = acc[30:32].astype(bf16)


def spread(plan, tiles, more, prop, peer, keep, got):
    return pl.pallas_call(
        spread_body,
        out_shape=(
            jax.ShapeDtypeStruct((16, B, B), f32),
            jax.ShapeDtypeStruct((544, B), bf16),
            jax.ShapeDtypeStruct((14, B, B), bf16),
        ),
        in_specs=[SM] + [VM] * 6,
        out_specs=(VM, VM, VM),
        scratch_shapes=[pltpu.VMEM((33, B, B), f32), pltpu.VMEM((5, B, B), bf16)],
        compiler_params=params(12),
        cost_estimate=cost(2 * 64 * B**3, 6 << 20),
        name="spread",
    )(plan, tiles, more, prop, peer, keep, got)


def meet_body(keep, got, came, near, quarter, far):
    for n in range(9):
        cols = slice(n * B, (n + 1) * B)
        v = came[256 + 32 * n : 288 + 32 * n, :].astype(f32)
        quarter[:, cols] = (keep[0:32, cols] + got[0:32, cols] + v).astype(bf16)
    for n in range(2):
        far[n] = (near[12 + n] + came[n * B : (n + 1) * B, :].astype(f32)).astype(bf16)


def meet(keep, got, came, near):
    return pl.pallas_call(
        meet_body,
        out_shape=(jax.ShapeDtypeStruct((32, 1152), bf16), jax.ShapeDtypeStruct((2, B, B), bf16)),
        in_specs=[VM] * 4,
        out_specs=(VM, VM),
        compiler_params=params(8),
        cost_estimate=cost(0, 1 << 20),
        name="meet",
    )(keep, got, came, near)


def rows_body(d1, d2, d3, t, out):
    for n, d in enumerate((d1, d2, d3)):
        out[32 * n : 32 * n + 32, :] = d[32:64, :]


def peer_rows(d1, d2, d3, t):
    return pl.pallas_call(
        rows_body,
        out_shape=jax.ShapeDtypeStruct((96, 1152), bf16),
        in_specs=[VM] * 3 + [ANY],
        out_specs=VM,
        compiler_params=params(4),
        cost_estimate=cost(0, 1 << 18),
        name="peer_rows",
    )(d1, d2, d3, t)


def sum_body(scale, ids, own, d1, d2, d3, d4, e, t, out, buf):
    core, z = ids[0] & 1, (ids[0] >> 1) & 7
    buf[0] = own[...]
    buf[4] = d4[...]
    for k, d in ((1, d1), (2, d2), (3, d3)):
        mine = jnp.where(core == 0, k, NZ - k)
        buf[mine] = d[0:32, :]
        buf[NZ - mine] = e[(k - 1) * 32 : k * 32, :]
    acc = buf[(NZ - z) & 7].astype(f32)
    for n in range(1, NZ):
        acc = acc + buf[(n - z) & 7].astype(f32)
    out[...] = (acc * scale).astype(bf16)


def sum_z(scale, ids, *parts):
    return pl.pallas_call(
        functools.partial(sum_body, scale),
        out_shape=jax.ShapeDtypeStruct((32, 1152), bf16),
        in_specs=[SM] + [VM] * 6 + [ANY],
        out_specs=VM,
        scratch_shapes=[pltpu.VMEM((NZ, 32, 1152), bf16)],
        compiler_params=params(8),
        cost_estimate=cost(32 * 1152 * 8, 1 << 20),
        name="sum_z",
    )(ids, *parts)


def wout_body(ids, mine, theirs, w_out, b_out, buf):
    x, core = ids[0] >> 4, ids[0] & 1
    for ref, c in ((mine, core), (theirs, 1 - core)):
        for i in range(2):
            at = pl.multiple_of(c * 64 + (x ^ i) * 32, 32)
            buf[pl.ds(at, 32), :] = ref[i * 32 : (i + 1) * 32, :].astype(f32)
    w_out[...] = buf[:, 0:1024]
    b_out[...] = buf[0:8, 1024:1152]


def weight_out(ids, mine, theirs):
    return pl.pallas_call(
        wout_body,
        out_shape=(jax.ShapeDtypeStruct((B, 1024), f32), jax.ShapeDtypeStruct((8, B), f32)),
        in_specs=[SM, VM, VM],
        out_specs=(VM, VM),
        scratch_shapes=[pltpu.VMEM((B, 1152), f32)],
        compiler_params=params(8),
        cost_estimate=cost(0, 1 << 20),
        name="weight_out",
    )(ids, mine, theirs)


def body(features, weight, bias_vector, adj_tiles, col_blocks, dest_blocks, out_grad):
    ids = jnp.stack([lax.axis_index("row"), lax.axis_index("feat")]).astype(jnp.int32)

    both = jnp.concatenate([features, row_send(features, dc=1)], axis=0)
    x0 = row_send(features, dx=1)
    lists = row_send(jnp.stack([col_blocks, dest_blocks]), dc=1)
    swap, both_a = tie(adj_tiles, both)
    more = row_send(swap, dc=1)

    pack, both_b = tie(pack_up(ids, weight, out_grad, bias_vector[None, :]), both_a)
    pair = jnp.concatenate([pack, feat_send(pack, dx=1)], axis=0)

    o3 = spin_send(both, 3, -1)
    o2 = spin_send(both, 2, -1)
    o1 = spin_send(both, 1, -1)
    o4 = spin_send(o3[:256], 1, -1)
    p3, p2 = row_send(o3, dx=1), row_send(o2, dx=1)
    p1, p4 = row_send(o1, dx=1), row_send(o4, dx=1)
    pair, o1 = tie(pair, o1)
    pair, o2 = tie(pair, o2)
    wu, wd = feat_send(pair, dy=1), feat_send(pair, dy=-1)
    wa, wb = feat_send(wu[:784], dy=1), feat_send(wd[784:], dy=-1)
    plan = plan_tiles(ids, col_blocks, dest_blocks, lists[0], lists[1])

    mine, theirs = aggregate(plan, adj_tiles, more, (both_b, x0, o4, o1, o2, o3, p4, p1, p2, p3))
    aggregated = (mine + row_send(theirs, dc=1)).astype(bf16).reshape(256, B)

    q = jnp.concatenate([aggregated, feat_send(aggregated, dx=1)], axis=0)
    w0, og, bias = lay_out(ids, (pair, wu, wd, wa, wb))
    pieces = (q, feat_send(q, dy=1), feat_send(q, dy=-1), feat_send(q, dy=2))
    hidden, prop, keep, give = middle(ids, pieces, w0, row_send(w0, dc=1), og, bias, weight)
    prop = prop.reshape(2, B, B)

    peer = row_send(prop, dc=1)
    got = row_send(give, dc=1)
    near, first, rest = spread(plan, adj_tiles, more, prop, peer, keep, got)
    came, came_rest = row_send(first, dx=1), row_send(rest, dx=1)
    quarter, t4 = meet(keep, got, came, near)

    r4 = spin_send(t4, 1)
    halves = jnp.concatenate([quarter, row_send(quarter, dc=1)], axis=0)
    d3, d2, d1 = (spin_send(halves, k, -1) for k in (3, 2, 1))
    d4 = spin_send(d3[:32], 1, -1)

    t = near[:12] + came_rest[:12].astype(f32)
    t0 = near[14:] + came_rest[12:].astype(f32)
    low = t[4:12].astype(bf16)
    r2, r1 = spin_send(low[:4], 2), spin_send(low[4:], 1)
    t3 = jnp.concatenate([t[:2] + r4.astype(f32), t[2:4]], axis=0).astype(bf16)
    r3 = spin_send(t3, 3)

    e = row_send(peer_rows(d1, d2, d3, low), dc=1)
    scale = float(256 * lax.axis_size("row")) ** (-0.5)
    total = sum_z(scale, ids, quarter, d1, d2, d3, d4, e, t3)
    two = jnp.concatenate([total, row_send(total, dx=1)], axis=0)
    weight_grad, bias_grad = weight_out(ids, two, row_send(two, dc=1))

    r = r1.astype(f32) + r2.astype(f32) + r3.astype(f32)
    out = t0 + r[:2] + row_send(r[2:], dc=1)
    return hidden, out.reshape(256, B), weight_grad, bias_grad[0]


def solution(mesh):
    in_specs = (
        P("row", "feat"),
        P("feat", None),
        P("feat"),
        P("row", None, None),
        P("row"),
        P("row"),
        P("row", "feat"),
    )
    out_specs = (P("row", "feat"), P("row", "feat"), P("feat", None), P("feat"))
    return jax.shard_map(body, mesh=mesh, in_specs=in_specs, out_specs=out_specs, check_vma=False)
```

profile of v0, /device:TPU:1, one launch (start us, length us, event | category | flops | bytes accessed | tf_op | source)
XLA Modules:
  0.0 141.4 jit_solution(6791737008884040070)
XLA Ops:
  0.6 3.3 %collective-permute-start.1 = (bf16[256,128]{1,0:T(8,128)(2,1)}, bf16[256,128]{1,0:T(8,128)(2,1)S(1)}, u32[]{:S(2)}, u32[]{:S(2)}) collective-permute-start(bf16[256,128]{1,0:T(8,128)(2,1)} %param.7), channel_id=1, source_target_pairs={{0,8},{8,0},{16,24},{24,16},{32,40},{40,32},{48,56},{56,48},{64,72... | collective-permute-start | bytes 196616 | tf_op jit(solution)/shard_map/ppermute | solution.py:25
  5.6 0.9 copy-done.1
  8.7 1.1 collective-permute-start.6
  9.7 1.6 %collective-permute-start.7 = (bf16[512,128]{1,0:T(8,128)(2,1)S(1)}, bf16[512,128]{1,0:T(8,128)(2,1)S(1)}, u32[]{:S(2)}, u32[]{:S(2)}) collective-permute-start(bf16[512,128]{1,0:T(8,128)(2,1)S(1)} %constant_dynamic-update-slice_fusion), channel_id=1, source_target_pairs={{0,112},{8,24},{16,0},{24,40},{32,16},{40,56},{48,32},{56,72},{64,... | collective-permute-start | bytes 393224 | tf_op jit(solution)/shard_map/ppermute | solution.py:41
  11.4 3.0 %collective-permute-start.8 = (bf16[512,128]{1,0:T(8,128)(2,1)S(1)}, bf16[512,128]{1,0:T(8,128)(2,1)S(1)}, u32[]{:S(2)}, u32[]{:S(2)}) collective-permute-start(bf16[512,128]{1,0:T(8,128)(2,1)S(1)} %constant_dynamic-update-slice_fusion), channel_id=1, source_target_pairs={{0,96},{8,40},{16,112},{24,56},{32,0},{40,72},{48,16},{56,88},{64,... | collective-permute-start | bytes 393224 | tf_op jit(solution)/shard_map/ppermute | solution.py:41
  14.4 2.3 %collective-permute-done.6 = bf16[784,128]{1,0:T(8,128)(2,1)S(1)} collective-permute-done((bf16[784,128]{1,0:T(8,128)(2,1)S(1)}, bf16[784,128]{1,0:T(8,128)(2,1)S(1)}, u32[]{:S(2)}, u32[]{:S(2)}) %collective-permute-start.6) | collective-permute-done | bytes 200736 | tf_op jit(solution)/shard_map/ppermute | solution.py:29
  16.7 1.0 collective-permute-done.7
  17.7 3.1 %collective-permute-done.8 = bf16[512,128]{1,0:T(8,128)(2,1)S(1)} collective-permute-done((bf16[512,128]{1,0:T(8,128)(2,1)S(1)}, bf16[512,128]{1,0:T(8,128)(2,1)S(1)}, u32[]{:S(2)}, u32[]{:S(2)}) %collective-permute-start.8) | collective-permute-done | bytes 131104 | tf_op jit(solution)/shard_map/ppermute | solution.py:41
  20.8 1.3 collective-permute-start.18
  22.1 1.4 %collective-permute-start.19 = (bf16[1568,128]{1,0:T(8,128)(2,1)S(1)}, bf16[1568,128]{1,0:T(8,128)(2,1)S(1)}, u32[]{:S(2)}, u32[]{:S(2)}) collective-permute-start(bf16[1568,128]{1,0:T(8,128)(2,1)S(1)} %pad_maximum_fusion.refs_0_), channel_id=1, source_target_pairs={{0,3},{1,0},{2,1},{3,2},{4,7},{5,4},{6,5},{7,6},{8,11},{9,8},{10,9... | collective-permute-start | bytes 1204232 | tf_op jit(solution)/shard_map/ppermute | solution.py:29
  23.5 8.2 %collective-permute-done.18.refs_1_ = bf16[1568,128]{1,0:T(8,128)(2,1)S(1)} collective-permute-done((bf16[1568,128]{1,0:T(8,128)(2,1)S(1)}, bf16[1568,128]{1,0:T(8,128)(2,1)S(1)}, u32[]{:S(2)}, u32[]{:S(2)}) %collective-permute-start.18) | collective-permute-done | bytes 401440 | tf_op jit(solution)/shard_map/ppermute | solution.py:29
  31.9 2.7 %collective-permute-start.21 = (bf16[784,128]{1,0:T(8,128)(2,1)S(1)}, bf16[784,128]{1,0:T(8,128)(2,1)S(1)}, u32[]{:S(2)}, u32[]{:S(2)}) collective-permute-start(bf16[784,128]{1,0:T(8,128)(2,1)S(1)} %slice.78), channel_id=1, source_target_pairs={{0,3},{1,0},{2,1},{3,2},{4,7},{5,4},{6,5},{7,6},{8,11},{9,8},{10,9... | collective-permute-start | bytes 602120 | tf_op jit(solution)/shard_map/ppermute | solution.py:29
  34.9 8.0 %collective-permute-done.4 = bf16[512,128]{1,0:T(8,128)(2,1)S(1)} collective-permute-done((bf16[512,128]{1,0:T(8,128)(2,1)S(1)}, bf16[512,128]{1,0:T(8,128)(2,1)S(1)}, u32[]{:S(2)}, u32[]{:S(2)}) %collective-permute-start.4) | collective-permute-done | bytes 131104 | tf_op jit(solution)/shard_map/ppermute | solution.py:41
  42.9 1.5 %collective-permute-start.5 = (bf16[256,128]{1,0:T(8,128)(2,1)S(1)}, bf16[256,128]{1,0:T(8,128)(2,1)S(1)}, u32[]{:S(2)}, u32[]{:S(2)}) collective-permute-start(bf16[256,128]{1,0:T(8,128)(2,1)S(1)} %slice.76), channel_id=1, source_target_pairs={{0,112},{8,24},{16,0},{24,40},{32,16},{40,56},{48,32},{56,72},{64,... | collective-permute-start | bytes 196616 | tf_op jit(solution)/shard_map/ppermute | solution.py:41
  44.5 1.4 %lay_out.1 = (bf16[1024,512]{1,0:T(8,128)(2,1)S(1)}, bf16[256,1024]{1,0:T(8,128)(2,1)S(1)}, f32[8,1024]{1,0:T(8,128)S(1)}) custom-call(s32[2]{0:T(128)S(1)} %pad_add_fusion.1.ids, bf16[1568,128]{1,0:T(8,128)(2,1)S(1)} %pad_maximum_fusion.refs_0_, bf16[1568,128]{1,0:T(8,128)(2,1)S(1)} %collective-permute-done.18.refs_1_, ...), custom_call_target="tpu_custom_call" | custom-call | bytes 3145728 | tf_op jit(solution)/shard_map/lay_out/pallas_call | solution.py:192
  45.9 4.0 %collective-permute-start.22 = (bf16[1024,512]{1,0:T(8,128)(2,1)S(1)}, bf16[1024,512]{1,0:T(8,128)(2,1)S(1)}, u32[]{:S(2)}, u32[]{:S(2)}) collective-permute-start(bf16[1024,512]{1,0:T(8,128)(2,1)S(1)} %get-tuple-element.38.w0), channel_id=1, source_target_pairs={{0,8},{8,0},{16,24},{24,16},{32,40},{40,32},{48,56},{56,48},{64,72... | collective-permute-start | bytes 3145736 | tf_op jit(solution)/shard_map/ppermute | solution.py:25
  50.3 1.1 collective-permute-start.9
  53.5 0.9 collective-permute-start.11
  55.3 3.5 %plan_tiles.1.plan = s32[160]{0:T(256)S(1)} custom-call(s32[2]{0:T(128)S(1)} %pad_add_fusion.1.ids, s32[64]{0:T(128)S(1)} %copy-done.4, s32[64]{0:T(128)S(1)} %copy-done.5, s32[64]{0:T(128)S(1)} %get-tuple-element.57.c1, s32[64]{0:T(128)S(1)} %get-tuple-element.56.d1), custom_call_target="tpu_custom_call" | custom-call | flops 10000 | bytes 4096 | tf_op jit(solution)/shard_map/plan_tiles/pallas_call | solution.py:98
  58.8 1.7 %collective-permute-done.11 = bf16[512,128]{1,0:T(8,128)(2,1)S(1)} collective-permute-done((bf16[512,128]{1,0:T(8,128)(2,1)S(1)}, bf16[512,128]{1,0:T(8,128)(2,1)S(1)}, u32[]{:S(2)}, u32[]{:S(2)}) %collective-permute-start.11) | collective-permute-done | bytes 131104 | tf_op jit(solution)/shard_map/ppermute | solution.py:25
  60.5 2.8 %collective-permute-done.12 = bf16[512,128]{1,0:T(8,128)(2,1)S(1)} collective-permute-done((bf16[512,128]{1,0:T(8,128)(2,1)S(1)}, bf16[512,128]{1,0:T(8,128)(2,1)S(1)}, u32[]{:S(2)}, u32[]{:S(2)}) %collective-permute-start.12) | collective-permute-done | bytes 131104 | tf_op jit(solution)/shard_map/ppermute | solution.py:25
  63.3 6.3 %aggregate.1 = (f32[2,128,128]{2,1,0:T(8,128)S(1)}, f32[2,128,128]{2,1,0:T(8,128)S(1)}) custom-call(s32[160]{0:T(256)S(1)} %plan_tiles.1.plan, bf16[64,128,128]{2,1,0:T(8,128)(2,1)S(1)} %copy-done, bf16[64,128,128]{2,1,0:T(8,128)(2,1)} %collective-permute-done.2.more, bf16[4,128,128]{2,1,0:T(8,128)(2,1)S(1)} %bitcast.25, bf16[2,128,128]{2,1,0:T(8,128)(2,1)S(1)} %bitcast.32, ...), custom_call_target="tpu_custom_call" | custom-call | flops 268435456 | bytes 4194304 | tf_op jit(solution)/shard_map/aggregate/pallas_call | solution.py:149
  69.6 1.2 collective-permute-start.13
  70.9 1.0 collective-permute-done.13
  71.9 0.9 collective-permute-start.14
  72.8 3.8 %collective-permute-done.14 = bf16[256,128]{1,0:T(8,128)(2,1)S(1)} collective-permute-done((bf16[256,128]{1,0:T(8,128)(2,1)S(1)}, bf16[256,128]{1,0:T(8,128)(2,1)S(1)}, u32[]{:S(2)}, u32[]{:S(2)}) %collective-permute-start.14) | collective-permute-done | bytes 65568 | tf_op jit(solution)/shard_map/ppermute | solution.py:29
  76.7 2.7 %collective-permute-start.16 = (bf16[512,128]{1,0:T(8,128)(2,1)S(1)}, bf16[512,128]{1,0:T(8,128)(2,1)S(1)}, u32[]{:S(2)}, u32[]{:S(2)}) collective-permute-start(bf16[512,128]{1,0:T(8,128)(2,1)S(1)} %pad_maximum_fusion.2.p0), channel_id=1, source_target_pairs={{0,3},{1,0},{2,1},{3,2},{4,7},{5,4},{6,5},{7,6},{8,11},{9,8},{10,9... | collective-permute-start | bytes 393224 | tf_op jit(solution)/shard_map/ppermute | solution.py:29
  79.4 2.3 %collective-permute-done.15.p1 = bf16[512,128]{1,0:T(8,128)(2,1)S(1)} collective-permute-done((bf16[512,128]{1,0:T(8,128)(2,1)S(1)}, bf16[512,128]{1,0:T(8,128)(2,1)S(1)}, u32[]{:S(2)}, u32[]{:S(2)}) %collective-permute-start.15) | collective-permute-done | bytes 131104 | tf_op jit(solution)/shard_map/ppermute | solution.py:29
  82.5 2.2 %collective-permute-done.17.p3 = bf16[512,128]{1,0:T(8,128)(2,1)S(1)} collective-permute-done((bf16[512,128]{1,0:T(8,128)(2,1)S(1)}, bf16[512,128]{1,0:T(8,128)(2,1)S(1)}, u32[]{:S(2)}, u32[]{:S(2)}) %collective-permute-start.17) | collective-permute-done | bytes 131104 | tf_op jit(solution)/shard_map/ppermute | solution.py:29
  84.8 2.2 %middle.1 = (f32[256,128]{1,0:T(8,128)}, bf16[256,128]{1,0:T(8,128)(2,1)S(1)}, f32[64,1152]{1,0:T(8,128)S(1)}, f32[64,1152]{1,0:T(8,128)S(1)}) custom-call(s32[2]{0:T(128)S(1)} %pad_add_fusion.1.ids, bf16[512,128]{1,0:T(8,128)(2,1)S(1)} %pad_maximum_fusion.2.p0, bf16[512,128]{1,0:T(8,128)(2,1)S(1)} %collective-permute-done.15.p1, ...), custom_call_target="tpu_custom_call" | custom-call | flops 671088640 | bytes 5242880 | tf_op jit(solution)/shard_map/middle/pallas_call | solution.py:238
  87.0 3.1 %collective-permute-start.24 = (f32[64,1152]{1,0:T(8,128)S(1)}, f32[64,1152]{1,0:T(8,128)S(1)}, u32[]{:S(2)}, u32[]{:S(2)}) collective-permute-start(f32[64,1152]{1,0:T(8,128)S(1)} %get-tuple-element.44), channel_id=1, source_target_pairs={{0,8},{8,0},{16,24},{24,16},{32,40},{40,32},{48,56},{56,48},{64,72... | collective-permute-start | bytes 884744 | tf_op jit(solution)/shard_map/ppermute | solution.py:25
  90.1 1.3 collective-permute-done.23.peer
  91.4 5.7 %spread.1 = (f32[16,128,128]{2,1,0:T(8,128)S(1)}, bf16[544,128]{1,0:T(8,128)(2,1)S(1)}, bf16[14,128,128]{2,1,0:T(8,128)(2,1)S(1)}) custom-call(s32[160]{0:T(256)S(1)} %plan_tiles.1.plan, bf16[64,128,128]{2,1,0:T(8,128)(2,1)S(1)} %copy-done, bf16[64,128,128]{2,1,0:T(8,128)(2,1)} %collective-permute-done.2.more, bf16[2,128,128]{2,1,0:T(8,128)(2,1)S(1)} %bitcast.35, ...), custom_call_target="tpu_custom_call" | custom-call | flops 268435456 | bytes 6291456 | tf_op jit(solution)/shard_map/spread/pallas_call | solution.py:283
  97.5 1.1 collective-permute-start.25
  98.6 3.4 %collective-permute-done.28.came = bf16[544,128]{1,0:T(8,128)(2,1)S(1)} collective-permute-done((bf16[544,128]{1,0:T(8,128)(2,1)S(1)}, bf16[544,128]{1,0:T(8,128)(2,1)S(1)}, u32[]{:S(2)}, u32[]{:S(2)}) %collective-permute-start.28) | collective-permute-done | bytes 139296 | tf_op jit(solution)/shard_map/ppermute | solution.py:25
  102.1 2.1 %collective-permute-start.32 = (bf16[32,1152]{1,0:T(8,128)(2,1)S(1)}, bf16[32,1152]{1,0:T(8,128)(2,1)S(1)}, u32[]{:S(2)}, u32[]{:S(2)}) collective-permute-start(bf16[32,1152]{1,0:T(8,128)(2,1)S(1)} %get-tuple-element.49.own), channel_id=1, source_target_pairs={{0,8},{8,0},{16,24},{24,16},{32,40},{40,32},{48,56},{56,48},{64,72... | collective-permute-start | bytes 221192 | tf_op jit(solution)/shard_map/ppermute | solution.py:25
  104.2 2.2 %collective-permute-start.29 = (bf16[2,128,128]{2,1,0:T(8,128)(2,1)S(1)}, bf16[2,128,128]{2,1,0:T(8,128)(2,1)S(1)}, u32[]{:S(2)}, u32[]{:S(2)}) collective-permute-start(bf16[2,128,128]{2,1,0:T(8,128)(2,1)S(1)} %get-tuple-element.48), channel_id=1, source_target_pairs={{0,16},{8,120},{16,32},{24,8},{32,48},{40,24},{48,64},{56,40},{64,... | collective-permute-start | bytes 196616 | tf_op jit(solution)/shard_map/ppermute | solution.py:41
  107.6 2.1 %collective-permute-start.35 = (bf16[64,1152]{1,0:T(8,128)(2,1)S(1)}, bf16[64,1152]{1,0:T(8,128)(2,1)S(1)}, u32[]{:S(2)}, u32[]{:S(2)}) collective-permute-start(bf16[64,1152]{1,0:T(8,128)(2,1)S(1)} %constant_dynamic-update-slice_fusion.2), channel_id=1, source_target_pairs={{0,80},{8,56},{16,96},{24,72},{32,112},{40,88},{48,0},{56,104},{64... | collective-permute-start | bytes 442376 | tf_op jit(solution)/shard_map/ppermute | solution.py:41
  109.7 2.2 %collective-permute-done.25 = bf16[14,128,128]{2,1,0:T(8,128)(2,1)S(1)} collective-permute-done((bf16[14,128,128]{2,1,0:T(8,128)(2,1)S(1)}, bf16[14,128,128]{2,1,0:T(8,128)(2,1)S(1)}, u32[]{:S(2)}, u32[]{:S(2)}) %collective-permute-start.25) | collective-permute-done | bytes 458784 | tf_op jit(solution)/shard_map/ppermute | solution.py:25
  112.1 1.3 collective-permute-done.33.d1
  113.4 6.3 %collective-permute-done.35.d3 = bf16[64,1152]{1,0:T(8,128)(2,1)S(1)} collective-permute-done((bf16[64,1152]{1,0:T(8,128)(2,1)S(1)}, bf16[64,1152]{1,0:T(8,128)(2,1)S(1)}, u32[]{:S(2)}, u32[]{:S(2)}) %collective-permute-start.35) | collective-permute-done | bytes 147488 | tf_op jit(solution)/shard_map/ppermute | solution.py:41
  119.9 1.9 %collective-permute-start.30 = (bf16[4,128,128]{2,1,0:T(8,128)(2,1)S(1)}, bf16[4,128,128]{2,1,0:T(8,128)(2,1)S(1)}, u32[]{:S(2)}, u32[]{:S(2)}) collective-permute-start(bf16[4,128,128]{2,1,0:T(8,128)(2,1)S(1)} %pad_maximum_fusion.3.t), channel_id=1, source_target_pairs={{0,48},{8,88},{16,64},{24,104},{32,80},{40,120},{48,96},{56,8},{64... | collective-permute-start | bytes 393224 | tf_op jit(solution)/shard_map/ppermute | solution.py:41
  121.9 4.0 %collective-permute-start.27 = (bf16[4,128,128]{2,1,0:T(8,128)(2,1)S(1)}, bf16[4,128,128]{2,1,0:T(8,128)(2,1)S(1)}, u32[]{:S(2)}, u32[]{:S(2)}) collective-permute-start(bf16[4,128,128]{2,1,0:T(8,128)(2,1)S(1)} %get-tuple-element.55), channel_id=1, source_target_pairs={{0,32},{8,104},{16,48},{24,120},{32,64},{40,8},{48,80},{56,24},{64... | collective-permute-start | bytes 393224 | tf_op jit(solution)/shard_map/ppermute | solution.py:41
  125.8 1.5 %collective-permute-start.36 = (bf16[32,1152]{1,0:T(8,128)(2,1)S(1)}, bf16[32,1152]{1,0:T(8,128)(2,1)S(1)}, u32[]{:S(2)}, u32[]{:S(2)}) collective-permute-start(bf16[32,1152]{1,0:T(8,128)(2,1)S(1)} %slice.87), channel_id=1, source_target_pairs={{0,112},{8,24},{16,0},{24,40},{32,16},{40,56},{48,32},{56,72},{64,... | collective-permute-start | bytes 221192 | tf_op jit(solution)/shard_map/ppermute | solution.py:41
  127.3 5.5 %collective-permute-done.36.d4 = bf16[32,1152]{1,0:T(8,128)(2,1)S(1)} collective-permute-done((bf16[32,1152]{1,0:T(8,128)(2,1)S(1)}, bf16[32,1152]{1,0:T(8,128)(2,1)S(1)}, u32[]{:S(2)}, u32[]{:S(2)}) %collective-permute-start.36) | collective-permute-done | bytes 73760 | tf_op jit(solution)/shard_map/ppermute | solution.py:41
  133.5 1.8 %collective-permute-start.38 = (bf16[32,1152]{1,0:T(8,128)(2,1)S(1)}, bf16[32,1152]{1,0:T(8,128)(2,1)S(1)}, u32[]{:S(2)}, u32[]{:S(2)}) collective-permute-start(bf16[32,1152]{1,0:T(8,128)(2,1)S(1)} %sum_z.1), channel_id=1, source_target_pairs={{0,128},{8,136},{16,144},{24,152},{32,160},{40,168},{48,176},{56,1... | collective-permute-start | bytes 221192 | tf_op jit(solution)/shard_map/ppermute | solution.py:25
  136.1 1.9 %collective-permute-done.38 = bf16[32,1152]{1,0:T(8,128)(2,1)S(1)} collective-permute-done((bf16[32,1152]{1,0:T(8,128)(2,1)S(1)}, bf16[32,1152]{1,0:T(8,128)(2,1)S(1)}, u32[]{:S(2)}, u32[]{:S(2)}) %collective-permute-start.38) | collective-permute-done | bytes 73760 | tf_op jit(solution)/shard_map/ppermute | solution.py:25
  139.5 1.4 weight_out.1
  (83 shorter events, 14.2 us)
Async XLA Ops:
  0.6 62.7 %copy-start = (bf16[64,128,128]{2,1,0:T(8,128)(2,1)S(1)}, bf16[64,128,128]{2,1,0:T(8,128)(2,1)}, u32[]{:S(2)}) copy-start(bf16[64,128,128]{2,1,0:T(8,128)(2,1)} %tiles.3) | copy-start | bytes 6291460
  0.6 4.4 %collective-permute-start.1 = (bf16[256,128]{1,0:T(8,128)(2,1)}, bf16[256,128]{1,0:T(8,128)(2,1)S(1)}, u32[]{:S(2)}, u32[]{:S(2)}) collective-permute-start(bf16[256,128]{1,0:T(8,128)(2,1)} %param.7), channel_id=1, source_target_pairs={{0,8},{8,0},{16,24},{24,16},{32,40},{40,32},{48,56},{56,48},{64,72... | collective-permute-start | bytes 196616 | tf_op jit(solution)/shard_map/ppermute | solution.py:25
  5.1 58.2 %collective-permute-start.2 = (bf16[64,128,128]{2,1,0:T(8,128)(2,1)}, bf16[64,128,128]{2,1,0:T(8,128)(2,1)}, u32[]{:S(2)}, u32[]{:S(2)}) collective-permute-start(bf16[64,128,128]{2,1,0:T(8,128)(2,1)} %tiles.3), channel_id=1, source_target_pairs={{0,8},{8,0},{16,24},{24,16},{32,40},{40,32},{48,56},{56,48},{64,72... | collective-permute-start | bytes 6291464 | tf_op jit(solution)/shard_map/ppermute | solution.py:25
  5.6 0.9 copy-start.1
  6.6 0.8 copy-start.3
  7.4 0.7 copy-start.6
  8.1 41.8 %copy-start.7 = (bf16[256,128]{1,0:T(8,128)(2,1)S(1)}, bf16[256,128]{1,0:T(8,128)(2,1)}, u32[]{:S(2)}) copy-start(bf16[256,128]{1,0:T(8,128)(2,1)} %param.7) | copy-start | bytes 196612
  8.1 43.3 %copy-start.4 = (s32[64]{0:T(128)S(1)}, s32[64]{0:T(128)}, u32[]{:S(2)}) copy-start(s32[64]{0:T(128)} %c0.1) | copy-start | bytes 772
  8.1 43.3 %copy-start.5 = (s32[64]{0:T(128)S(1)}, s32[64]{0:T(128)}, u32[]{:S(2)}) copy-start(s32[64]{0:T(128)} %d0.1) | copy-start | bytes 772
  8.7 8.0 %collective-permute-start.6 = (bf16[784,128]{1,0:T(8,128)(2,1)S(1)}, bf16[784,128]{1,0:T(8,128)(2,1)S(1)}, u32[]{:S(2)}, u32[]{:S(2)}) collective-permute-start(bf16[784,128]{1,0:T(8,128)(2,1)S(1)} %pack_up.1), channel_id=1, source_target_pairs={{0,4},{1,5},{2,6},{3,7},{4,0},{5,1},{6,2},{7,3},{8,12},{9,13},{10,... | collective-permute-start | bytes 602120 | tf_op jit(solution)/shard_map/ppermute | solution.py:29
  9.7 7.9 %collective-permute-start.7 = (bf16[512,128]{1,0:T(8,128)(2,1)S(1)}, bf16[512,128]{1,0:T(8,128)(2,1)S(1)}, u32[]{:S(2)}, u32[]{:S(2)}) collective-permute-start(bf16[512,128]{1,0:T(8,128)(2,1)S(1)} %constant_dynamic-update-slice_fusion), channel_id=1, source_target_pairs={{0,112},{8,24},{16,0},{24,40},{32,16},{40,56},{48,32},{56,72},{64,... | collective-permute-start | bytes 393224 | tf_op jit(solution)/shard_map/ppermute | solution.py:41
  11.4 9.4 %collective-permute-start.8 = (bf16[512,128]{1,0:T(8,128)(2,1)S(1)}, bf16[512,128]{1,0:T(8,128)(2,1)S(1)}, u32[]{:S(2)}, u32[]{:S(2)}) collective-permute-start(bf16[512,128]{1,0:T(8,128)(2,1)S(1)} %constant_dynamic-update-slice_fusion), channel_id=1, source_target_pairs={{0,96},{8,40},{16,112},{24,56},{32,0},{40,72},{48,16},{56,88},{64,... | collective-permute-start | bytes 393224 | tf_op jit(solution)/shard_map/ppermute | solution.py:41
  20.8 10.9 %collective-permute-start.18 = (bf16[1568,128]{1,0:T(8,128)(2,1)S(1)}, bf16[1568,128]{1,0:T(8,128)(2,1)S(1)}, u32[]{:S(2)}, u32[]{:S(2)}) collective-permute-start(bf16[1568,128]{1,0:T(8,128)(2,1)S(1)} %pad_maximum_fusion.refs_0_), channel_id=1, source_target_pairs={{0,1},{1,2},{2,3},{3,0},{4,5},{5,6},{6,7},{7,4},{8,9},{9,10},{10,1... | collective-permute-start | bytes 1204232 | tf_op jit(solution)/shard_map/ppermute | solution.py:29
  22.1 9.7 %collective-permute-start.19 = (bf16[1568,128]{1,0:T(8,128)(2,1)S(1)}, bf16[1568,128]{1,0:T(8,128)(2,1)S(1)}, u32[]{:S(2)}, u32[]{:S(2)}) collective-permute-start(bf16[1568,128]{1,0:T(8,128)(2,1)S(1)} %pad_maximum_fusion.refs_0_), channel_id=1, source_target_pairs={{0,3},{1,0},{2,1},{3,2},{4,7},{5,4},{6,5},{7,6},{8,11},{9,8},{10,9... | collective-permute-start | bytes 1204232 | tf_op jit(solution)/shard_map/ppermute | solution.py:29
  31.7 12.7 %collective-permute-start.20 = (bf16[784,128]{1,0:T(8,128)(2,1)S(1)}, bf16[784,128]{1,0:T(8,128)(2,1)S(1)}, u32[]{:S(2)}, u32[]{:S(2)}) collective-permute-start(bf16[784,128]{1,0:T(8,128)(2,1)S(1)} %slice.77), channel_id=1, source_target_pairs={{0,1},{1,2},{2,3},{3,0},{4,5},{5,6},{6,7},{7,4},{8,9},{9,10},{10,1... | collective-permute-start | bytes 602120 | tf_op jit(solution)/shard_map/ppermute | solution.py:29
  31.9 12.6 %collective-permute-start.21 = (bf16[784,128]{1,0:T(8,128)(2,1)S(1)}, bf16[784,128]{1,0:T(8,128)(2,1)S(1)}, u32[]{:S(2)}, u32[]{:S(2)}) collective-permute-start(bf16[784,128]{1,0:T(8,128)(2,1)S(1)} %slice.78), channel_id=1, source_target_pairs={{0,3},{1,0},{2,1},{3,2},{4,7},{5,4},{6,5},{7,6},{8,11},{9,8},{10,9... | collective-permute-start | bytes 602120 | tf_op jit(solution)/shard_map/ppermute | solution.py:29
  34.6 8.3 %collective-permute-start.4 = (bf16[512,128]{1,0:T(8,128)(2,1)S(1)}, bf16[512,128]{1,0:T(8,128)(2,1)S(1)}, u32[]{:S(2)}, u32[]{:S(2)}) collective-permute-start(bf16[512,128]{1,0:T(8,128)(2,1)S(1)} %constant_dynamic-update-slice_fusion), channel_id=1, source_target_pairs={{0,80},{8,56},{16,96},{24,72},{32,112},{40,88},{48,0},{56,104},{64... | collective-permute-start | bytes 393224 | tf_op jit(solution)/shard_map/ppermute | solution.py:41
  42.9 7.3 %collective-permute-start.5 = (bf16[256,128]{1,0:T(8,128)(2,1)S(1)}, bf16[256,128]{1,0:T(8,128)(2,1)S(1)}, u32[]{:S(2)}, u32[]{:S(2)}) collective-permute-start(bf16[256,128]{1,0:T(8,128)(2,1)S(1)} %slice.76), channel_id=1, source_target_pairs={{0,112},{8,24},{16,0},{24,40},{32,16},{40,56},{48,32},{56,72},{64,... | collective-permute-start | bytes 196616 | tf_op jit(solution)/shard_map/ppermute | solution.py:41
  45.9 33.4 %collective-permute-start.22 = (bf16[1024,512]{1,0:T(8,128)(2,1)S(1)}, bf16[1024,512]{1,0:T(8,128)(2,1)S(1)}, u32[]{:S(2)}, u32[]{:S(2)}) collective-permute-start(bf16[1024,512]{1,0:T(8,128)(2,1)S(1)} %get-tuple-element.38.w0), channel_id=1, source_target_pairs={{0,8},{8,0},{16,24},{24,16},{32,40},{40,32},{48,56},{56,48},{64,72... | collective-permute-start | bytes 3145736 | tf_op jit(solution)/shard_map/ppermute | solution.py:25
  49.9 3.7 %collective-permute-start.3 = (bf16[256,128]{1,0:T(8,128)(2,1)S(1)}, bf16[256,128]{1,0:T(8,128)(2,1)S(1)}, u32[]{:S(2)}, u32[]{:S(2)}) collective-permute-start(bf16[256,128]{1,0:T(8,128)(2,1)S(1)} %copy-done.7), channel_id=1, source_target_pairs={{0,128},{8,136},{16,144},{24,152},{32,160},{40,168},{48,176},{56,1... | collective-permute-start | bytes 196616 | tf_op jit(solution)/shard_map/ppermute | solution.py:25
  50.3 4.7 %collective-permute-start.9 = (bf16[256,128]{1,0:T(8,128)(2,1)S(1)}, bf16[256,128]{1,0:T(8,128)(2,1)S(1)}, u32[]{:S(2)}, u32[]{:S(2)}) collective-permute-start(bf16[256,128]{1,0:T(8,128)(2,1)S(1)} %collective-permute-done.5), channel_id=1, source_target_pairs={{0,128},{8,136},{16,144},{24,152},{32,160},{40,168},{48,176},{56,1... | collective-permute-start | bytes 196616 | tf_op jit(solution)/shard_map/ppermute | solution.py:25
  51.4 1.5 %collective-permute-start = (s32[2,64]{1,0:T(2,128)S(1)}, s32[2,64]{1,0:T(2,128)S(1)}, u32[]{:S(2)}, u32[]{:S(2)}) collective-permute-start(s32[2,64]{1,0:T(2,128)S(1)} %pad_add_fusion), channel_id=1, source_target_pairs={{0,8},{8,0},{16,24},{24,16},{32,40},{40,32},{48,56},{56,48},{64,72... | collective-permute-start | bytes 1544 | tf_op jit(solution)/shard_map/ppermute | solution.py:25
  52.9 5.8 %collective-permute-start.10 = (bf16[512,128]{1,0:T(8,128)(2,1)S(1)}, bf16[512,128]{1,0:T(8,128)(2,1)S(1)}, u32[]{:S(2)}, u32[]{:S(2)}) collective-permute-start(bf16[512,128]{1,0:T(8,128)(2,1)S(1)} %collective-permute-done.7), channel_id=1, source_target_pairs={{0,128},{8,136},{16,144},{24,152},{32,160},{40,168},{48,176},{56,1... | collective-permute-start | bytes 393224 | tf_op jit(solution)/shard_map/ppermute | solution.py:25
  53.5 7.0 %collective-permute-start.11 = (bf16[512,128]{1,0:T(8,128)(2,1)S(1)}, bf16[512,128]{1,0:T(8,128)(2,1)S(1)}, u32[]{:S(2)}, u32[]{:S(2)}) collective-permute-start(bf16[512,128]{1,0:T(8,128)(2,1)S(1)} %collective-permute-done.8), channel_id=1, source_target_pairs={{0,128},{8,136},{16,144},{24,152},{32,160},{40,168},{48,176},{56,1... | collective-permute-start | bytes 393224 | tf_op jit(solution)/shard_map/ppermute | solution.py:25
  54.9 8.4 %collective-permute-start.12 = (bf16[512,128]{1,0:T(8,128)(2,1)S(1)}, bf16[512,128]{1,0:T(8,128)(2,1)S(1)}, u32[]{:S(2)}, u32[]{:S(2)}) collective-permute-start(bf16[512,128]{1,0:T(8,128)(2,1)S(1)} %collective-permute-done.4), channel_id=1, source_target_pairs={{0,128},{8,136},{16,144},{24,152},{32,160},{40,168},{48,176},{56,1... | collective-permute-start | bytes 393224 | tf_op jit(solution)/shard_map/ppermute | solution.py:25
  63.3 21.4 %copy-start.2 = (bf16[128,1024]{1,0:T(8,128)(2,1)S(1)}, bf16[128,1024]{1,0:T(8,128)(2,1)}, u32[]{:S(2)}) copy-start(bf16[128,1024]{1,0:T(8,128)(2,1)} %w_own.1) | copy-start | bytes 786436
  69.6 2.2 %collective-permute-start.13 = (f32[2,128,128]{2,1,0:T(8,128)S(1)}, f32[2,128,128]{2,1,0:T(8,128)S(1)}, u32[]{:S(2)}, u32[]{:S(2)}) collective-permute-start(f32[2,128,128]{2,1,0:T(8,128)S(1)} %get-tuple-element.36), channel_id=1, source_target_pairs={{0,8},{8,0},{16,24},{24,16},{32,40},{40,32},{48,56},{56,48},{64,72... | collective-permute-start | bytes 393224 | tf_op jit(solution)/shard_map/ppermute | solution.py:25
  71.9 4.7 %collective-permute-start.14 = (bf16[256,128]{1,0:T(8,128)(2,1)S(1)}, bf16[256,128]{1,0:T(8,128)(2,1)S(1)}, u32[]{:S(2)}, u32[]{:S(2)}) collective-permute-start(bf16[256,128]{1,0:T(8,128)(2,1)S(1)} %bitcast.39), channel_id=1, source_target_pairs={{0,4},{1,5},{2,6},{3,7},{4,0},{5,1},{6,2},{7,3},{8,12},{9,13},{10,... | collective-permute-start | bytes 196616 | tf_op jit(solution)/shard_map/ppermute | solution.py:29
  76.6 5.1 %collective-permute-start.15 = (bf16[512,128]{1,0:T(8,128)(2,1)S(1)}, bf16[512,128]{1,0:T(8,128)(2,1)S(1)}, u32[]{:S(2)}, u32[]{:S(2)}) collective-permute-start(bf16[512,128]{1,0:T(8,128)(2,1)S(1)} %pad_maximum_fusion.2.p0), channel_id=1, source_target_pairs={{0,1},{1,2},{2,3},{3,0},{4,5},{5,6},{6,7},{7,4},{8,9},{9,10},{10,1... | collective-permute-start | bytes 393224 | tf_op jit(solution)/shard_map/ppermute | solution.py:29
  76.7 5.8 %collective-permute-start.16 = (bf16[512,128]{1,0:T(8,128)(2,1)S(1)}, bf16[512,128]{1,0:T(8,128)(2,1)S(1)}, u32[]{:S(2)}, u32[]{:S(2)}) collective-permute-start(bf16[512,128]{1,0:T(8,128)(2,1)S(1)} %pad_maximum_fusion.2.p0), channel_id=1, source_target_pairs={{0,3},{1,0},{2,1},{3,2},{4,7},{5,4},{6,5},{7,6},{8,11},{9,8},{10,9... | collective-permute-start | bytes 393224 | tf_op jit(solution)/shard_map/ppermute | solution.py:29
  79.3 5.4 %collective-permute-start.17 = (bf16[512,128]{1,0:T(8,128)(2,1)S(1)}, bf16[512,128]{1,0:T(8,128)(2,1)S(1)}, u32[]{:S(2)}, u32[]{:S(2)}) collective-permute-start(bf16[512,128]{1,0:T(8,128)(2,1)S(1)} %pad_maximum_fusion.2.p0), channel_id=1, source_target_pairs={{0,2},{1,3},{2,0},{3,1},{4,6},{5,7},{6,4},{7,5},{8,10},{9,11},{10,... | collective-permute-start | bytes 393224 | tf_op jit(solution)/shard_map/ppermute | solution.py:29
  87.0 4.4 %collective-permute-start.24 = (f32[64,1152]{1,0:T(8,128)S(1)}, f32[64,1152]{1,0:T(8,128)S(1)}, u32[]{:S(2)}, u32[]{:S(2)}) collective-permute-start(f32[64,1152]{1,0:T(8,128)S(1)} %get-tuple-element.44), channel_id=1, source_target_pairs={{0,8},{8,0},{16,24},{24,16},{32,40},{40,32},{48,56},{56,48},{64,72... | collective-permute-start | bytes 884744 | tf_op jit(solution)/shard_map/ppermute | solution.py:25
  90.1 1.3 collective-permute-start.23
  97.1 5.0 %collective-permute-start.28 = (bf16[544,128]{1,0:T(8,128)(2,1)S(1)}, bf16[544,128]{1,0:T(8,128)(2,1)S(1)}, u32[]{:S(2)}, u32[]{:S(2)}) collective-permute-start(bf16[544,128]{1,0:T(8,128)(2,1)S(1)} %get-tuple-element.47), channel_id=1, source_target_pairs={{0,128},{8,136},{16,144},{24,152},{32,160},{40,168},{48,176},{56,1... | collective-permute-start | bytes 417800 | tf_op jit(solution)/shard_map/ppermute | solution.py:25
  97.5 14.4 %collective-permute-start.25 = (bf16[14,128,128]{2,1,0:T(8,128)(2,1)S(1)}, bf16[14,128,128]{2,1,0:T(8,128)(2,1)S(1)}, u32[]{:S(2)}, u32[]{:S(2)}) collective-permute-start(bf16[14,128,128]{2,1,0:T(8,128)(2,1)S(1)} %get-tuple-element.46), channel_id=1, source_target_pairs={{0,128},{8,136},{16,144},{24,152},{32,160},{40,168},{48,176},{56,1... | collective-permute-start | bytes 1376264 | tf_op jit(solution)/shard_map/ppermute | solution.py:25
  102.1 4.3 %collective-permute-start.32 = (bf16[32,1152]{1,0:T(8,128)(2,1)S(1)}, bf16[32,1152]{1,0:T(8,128)(2,1)S(1)}, u32[]{:S(2)}, u32[]{:S(2)}) collective-permute-start(bf16[32,1152]{1,0:T(8,128)(2,1)S(1)} %get-tuple-element.49.own), channel_id=1, source_target_pairs={{0,8},{8,0},{16,24},{24,16},{32,40},{40,32},{48,56},{56,48},{64,72... | collective-permute-start | bytes 221192 | tf_op jit(solution)/shard_map/ppermute | solution.py:25
  104.2 15.7 %collective-permute-start.29 = (bf16[2,128,128]{2,1,0:T(8,128)(2,1)S(1)}, bf16[2,128,128]{2,1,0:T(8,128)(2,1)S(1)}, u32[]{:S(2)}, u32[]{:S(2)}) collective-permute-start(bf16[2,128,128]{2,1,0:T(8,128)(2,1)S(1)} %get-tuple-element.48), channel_id=1, source_target_pairs={{0,16},{8,120},{16,32},{24,8},{32,48},{40,24},{48,64},{56,40},{64,... | collective-permute-start | bytes 196616 | tf_op jit(solution)/shard_map/ppermute | solution.py:41
  106.4 7.0 %collective-permute-start.33 = (bf16[64,1152]{1,0:T(8,128)(2,1)S(1)}, bf16[64,1152]{1,0:T(8,128)(2,1)S(1)}, u32[]{:S(2)}, u32[]{:S(2)}) collective-permute-start(bf16[64,1152]{1,0:T(8,128)(2,1)S(1)} %constant_dynamic-update-slice_fusion.2), channel_id=1, source_target_pairs={{0,112},{8,24},{16,0},{24,40},{32,16},{40,56},{48,32},{56,72},{64,... | collective-permute-start | bytes 442376 | tf_op jit(solution)/shard_map/ppermute | solution.py:41
  107.0 6.4 %collective-permute-start.34 = (bf16[64,1152]{1,0:T(8,128)(2,1)S(1)}, bf16[64,1152]{1,0:T(8,128)(2,1)S(1)}, u32[]{:S(2)}, u32[]{:S(2)}) collective-permute-start(bf16[64,1152]{1,0:T(8,128)(2,1)S(1)} %constant_dynamic-update-slice_fusion.2), channel_id=1, source_target_pairs={{0,96},{8,40},{16,112},{24,56},{32,0},{40,72},{48,16},{56,88},{64,... | collective-permute-start | bytes 442376 | tf_op jit(solution)/shard_map/ppermute | solution.py:41
  107.6 12.2 %collective-permute-start.35 = (bf16[64,1152]{1,0:T(8,128)(2,1)S(1)}, bf16[64,1152]{1,0:T(8,128)(2,1)S(1)}, u32[]{:S(2)}, u32[]{:S(2)}) collective-permute-start(bf16[64,1152]{1,0:T(8,128)(2,1)S(1)} %constant_dynamic-update-slice_fusion.2), channel_id=1, source_target_pairs={{0,80},{8,56},{16,96},{24,72},{32,112},{40,88},{48,0},{56,104},{64... | collective-permute-start | bytes 442376 | tf_op jit(solution)/shard_map/ppermute | solution.py:41
  119.8 13.0 %collective-permute-start.37 = (bf16[96,1152]{1,0:T(8,128)(2,1)S(1)}, bf16[96,1152]{1,0:T(8,128)(2,1)S(1)}, u32[]{:S(2)}, u32[]{:S(2)}) collective-permute-start(bf16[96,1152]{1,0:T(8,128)(2,1)S(1)} %peer_rows.1), channel_id=1, source_target_pairs={{0,8},{8,0},{16,24},{24,16},{32,40},{40,32},{48,56},{56,48},{64,72... | collective-permute-start | bytes 663560 | tf_op jit(solution)/shard_map/ppermute | solution.py:25
  119.9 15.3 %collective-permute-start.30 = (bf16[4,128,128]{2,1,0:T(8,128)(2,1)S(1)}, bf16[4,128,128]{2,1,0:T(8,128)(2,1)S(1)}, u32[]{:S(2)}, u32[]{:S(2)}) collective-permute-start(bf16[4,128,128]{2,1,0:T(8,128)(2,1)S(1)} %pad_maximum_fusion.3.t), channel_id=1, source_target_pairs={{0,48},{8,88},{16,64},{24,104},{32,80},{40,120},{48,96},{56,8},{64... | collective-permute-start | bytes 393224 | tf_op jit(solution)/shard_map/ppermute | solution.py:41
  121.9 13.3 %collective-permute-start.27 = (bf16[4,128,128]{2,1,0:T(8,128)(2,1)S(1)}, bf16[4,128,128]{2,1,0:T(8,128)(2,1)S(1)}, u32[]{:S(2)}, u32[]{:S(2)}) collective-permute-start(bf16[4,128,128]{2,1,0:T(8,128)(2,1)S(1)} %get-tuple-element.55), channel_id=1, source_target_pairs={{0,32},{8,104},{16,48},{24,120},{32,64},{40,8},{48,80},{56,24},{64... | collective-permute-start | bytes 393224 | tf_op jit(solution)/shard_map/ppermute | solution.py:41
  125.8 9.4 %collective-permute-start.26 = (bf16[4,128,128]{2,1,0:T(8,128)(2,1)S(1)}, bf16[4,128,128]{2,1,0:T(8,128)(2,1)S(1)}, u32[]{:S(2)}, u32[]{:S(2)}) collective-permute-start(bf16[4,128,128]{2,1,0:T(8,128)(2,1)S(1)} %get-tuple-element.54), channel_id=1, source_target_pairs={{0,16},{8,120},{16,32},{24,8},{32,48},{40,24},{48,64},{56,40},{64,... | collective-permute-start | bytes 393224 | tf_op jit(solution)/shard_map/ppermute | solution.py:41
  125.8 6.9 %collective-permute-start.36 = (bf16[32,1152]{1,0:T(8,128)(2,1)S(1)}, bf16[32,1152]{1,0:T(8,128)(2,1)S(1)}, u32[]{:S(2)}, u32[]{:S(2)}) collective-permute-start(bf16[32,1152]{1,0:T(8,128)(2,1)S(1)} %slice.87), channel_id=1, source_target_pairs={{0,112},{8,24},{16,0},{24,40},{32,16},{40,56},{48,32},{56,72},{64,... | collective-permute-start | bytes 221192 | tf_op jit(solution)/shard_map/ppermute | solution.py:41
  133.5 4.5 %collective-permute-start.38 = (bf16[32,1152]{1,0:T(8,128)(2,1)S(1)}, bf16[32,1152]{1,0:T(8,128)(2,1)S(1)}, u32[]{:S(2)}, u32[]{:S(2)}) collective-permute-start(bf16[32,1152]{1,0:T(8,128)(2,1)S(1)} %sum_z.1), channel_id=1, source_target_pairs={{0,128},{8,136},{16,144},{24,152},{32,160},{40,168},{48,176},{56,1... | collective-permute-start | bytes 221192 | tf_op jit(solution)/shard_map/ppermute | solution.py:25
  135.3 3.2 %collective-permute-start.31 = (f32[2,128,128]{2,1,0:T(8,128)S(1)}, f32[2,128,128]{2,1,0:T(8,128)S(1)}, u32[]{:S(2)}, u32[]{:S(2)}) collective-permute-start(f32[2,128,128]{2,1,0:T(8,128)S(1)} %slice.86), channel_id=1, source_target_pairs={{0,8},{8,0},{16,24},{24,16},{32,40},{40,32},{48,56},{56,48},{64,72... | collective-permute-start | bytes 393224 | tf_op jit(solution)/shard_map/ppermute | solution.py:25
  138.0 1.5 %collective-permute-start.39 = (bf16[64,1152]{1,0:T(8,128)(2,1)S(1)}, bf16[64,1152]{1,0:T(8,128)(2,1)S(1)}, u32[]{:S(2)}, u32[]{:S(2)}) collective-permute-start(bf16[64,1152]{1,0:T(8,128)(2,1)S(1)} %pad_maximum_fusion.1.mine), channel_id=1, source_target_pairs={{0,8},{8,0},{16,24},{24,16},{32,40},{40,32},{48,56},{56,48},{64,72... | collective-permute-start | bytes 442376 | tf_op jit(solution)/shard_map/ppermute | solution.py:25
where the time goes:
time: 142 us; the launch traced here: 141 us
  waiting for transfers between devices  61.4 us (43%)
  starting transfers between devices  52.3 us (37%)
  Pallas kernels  21.8 us (15%)
  local copies, waits for them, and re-layouts  3.95 us (3%)
    ppermute x12, waiting for transfers between devices, spin_send(): return lax.ppermute(v, 'row', perm)  25.2 us
    ppermute x19, starting transfers between devices, row_send(): return lax.ppermute(v, 'row', perm)  22.6 us
    ppermute x9, waiting for transfers between devices, feat_send(): lax.ppermute(v, 'feat', [(i, (i >> 2 ^ dx) << 2 | i + dy & 3) for i in ra...  19.7 us
    ppermute x12, starting transfers between devices, spin_send(): return lax.ppermute(v, 'row', perm)  19.3 us
    ppermute x19, waiting for transfers between devices, row_send(): return lax.ppermute(v, 'row', perm)  16.5 us
    ppermute x9, starting transfers between devices, feat_send(): lax.ppermute(v, 'feat', [(i, (i >> 2 ^ dx) << 2 | i + dy & 3) for i in ra...  10.3 us
    pallas_call x1, Pallas kernels, aggregate(): pl.pallas_call(agg_body, out_shape=(jax.ShapeDtypeStruct((2, B, B), f32),...  6.28 us
    pallas_call x1, Pallas kernels, spread(): pl.pallas_call(spread_body, out_shape=(jax.ShapeDtypeStruct((16, B, B), f...  5.69 us
  transfers between devices with their start and end apart: 40, of which 24 were waited for; matrix products, arithmetic and copies ran while one was open for 1% of the time, Pallas kernels for 9%

commit v1 on v0

--- a/solution.py
+++ b/solution.py
@@ -49,25 +49,52 @@
     return pl.CostEstimate(flops=flops, bytes_accessed=nbytes, transcendentals=0)
 
 
-def pack_body(ids, w, og, bias, out):
+def pack_body(ids, w, og, bias, *refs):
+    out, sem = refs[-2:]
     core = ids[0] & 1
+    copies = []
     for m in range(4):
         at = pl.multiple_of(core * 512 + m * B, B)
-        out[m * B : (m + 1) * B, :] = w[:, pl.ds(at, B)]
-    out[512:768, :] = og[...]
+        copies.append(
+            pltpu.make_async_copy(w.at[:, pl.ds(at, B)], out.at[m * B : (m + 1) * B, :], sem.at[m])
+        )
+    copies.append(pltpu.make_async_copy(og, out.at[512:768, :], sem.at[4]))
+    for c in copies:
+        c.start()
     out[768:784, :] = jnp.broadcast_to(bias[...], (16, B))
-
-
-def pack_up(ids, w, og, bias):
+    for c in copies:
+        c.wait()
+
+
+def pack_up(ids, w, og, bias, *ready):
     return pl.pallas_call(
         pack_body,
         out_shape=jax.ShapeDtypeStruct((784, B), bf16),
-        in_specs=[SM, VM, VM, VM],
+        in_specs=[SM, HB, HB, VM] + [ANY] * len(ready),
         out_specs=VM,
-        compiler_params=params(8),
+        scratch_shapes=[pltpu.SemaphoreType.DMA((5,))],
+        compiler_params=params(4),
         cost_estimate=cost(0, 1 << 19),
         name="pack_up",
-    )(ids, w, og, bias)
+    )(ids, w, og, bias, *ready)
+
+
+def pair_body(a, b, *refs):
+    out = refs[-1]
+    out[0:784, :] = a[...]
+    out[784:1568, :] = b[...]
+
+
+def pair_up(a, b, *ready):
+    return pl.pallas_call(
+        pair_body,
+        out_shape=jax.ShapeDtypeStruct((1568, B), bf16),
+        in_specs=[VM, VM] + [ANY] * len(ready),
+        out_specs=VM,
+        compiler_params=params(4),
+        cost_estimate=cost(0, 1 << 19),
+        name="pair_up",
+    )(a, b, *ready)
 
 
 def plan_body(ids, c0, d0, c1, d1, out):
@@ -257,7 +284,7 @@
     )(ids, *pieces, w0, w1, og, bias, w_own)
 
 
-def spread_body(plan, tiles, more, prop, peer, keep, got, near, first, rest, acc, both):
+def spread_body(plan, tiles, more, prop, peer, send, near, first, rest, acc, both):
     acc[...] = jnp.zeros_like(acc)
     both[0:2] = prop[...]
     both[2:4] = peer[...]
@@ -270,51 +297,26 @@
 
     each_tile(plan, tiles, more, use)
     near[...] = acc[0:16]
-    for n in range(2):
-        first[n * B : (n + 1) * B, :] = acc[28 + n].astype(bf16)
-    for n in range(9):
-        cols = slice(n * B, (n + 1) * B)
-        first[256 + 32 * n : 288 + 32 * n, :] = (keep[32:64, cols] + got[32:64, cols]).astype(bf16)
+    first[...] = acc[28:30].astype(bf16)
     rest[0:12] = acc[16:28].astype(bf16)
     rest[12:14] = acc[30:32].astype(bf16)
 
 
-def spread(plan, tiles, more, prop, peer, keep, got):
+def spread(plan, tiles, more, prop, peer, send):
     return pl.pallas_call(
         spread_body,
         out_shape=(
             jax.ShapeDtypeStruct((16, B, B), f32),
-            jax.ShapeDtypeStruct((544, B), bf16),
+            jax.ShapeDtypeStruct((2, B, B), bf16),
             jax.ShapeDtypeStruct((14, B, B), bf16),
         ),
-        in_specs=[SM] + [VM] * 6,
+        in_specs=[SM] + [VM] * 4 + [ANY],
         out_specs=(VM, VM, VM),
         scratch_shapes=[pltpu.VMEM((33, B, B), f32), pltpu.VMEM((5, B, B), bf16)],
         compiler_params=params(12),
         cost_estimate=cost(2 * 64 * B**3, 6 << 20),
         name="spread",
-    )(plan, tiles, more, prop, peer, keep, got)
-
-
-def meet_body(keep, got, came, near, quarter, far):
-    for n in range(9):
-        cols = slice(n * B, (n + 1) * B)
-        v = came[256 + 32 * n : 288 + 32 * n, :].astype(f32)
-        quarter[:, cols] = (keep[0:32, cols] + got[0:32, cols] + v).astype(bf16)
-    for n in range(2):
-        far[n] = (near[12 + n] + came[n * B : (n + 1) * B, :].astype(f32)).astype(bf16)
-
-
-def meet(keep, got, came, near):
-    return pl.pallas_call(
-        meet_body,
-        out_shape=(jax.ShapeDtypeStruct((32, 1152), bf16), jax.ShapeDtypeStruct((2, B, B), bf16)),
-        in_specs=[VM] * 4,
-        out_specs=(VM, VM),
-        compiler_params=params(8),
-        cost_estimate=cost(0, 1 << 20),
-        name="meet",
-    )(keep, got, came, near)
+    )(plan, tiles, more, prop, peer, send)
 
 
 def rows_body(d1, d2, d3, t, out):
@@ -392,23 +394,20 @@
     lists = row_send(jnp.stack([col_blocks, dest_blocks]), dc=1)
     swap, both_a = tie(adj_tiles, both)
     more = row_send(swap, dc=1)
-
-    pack, both_b = tie(pack_up(ids, weight, out_grad, bias_vector[None, :]), both_a)
-    pair = jnp.concatenate([pack, feat_send(pack, dx=1)], axis=0)
-
     o3 = spin_send(both, 3, -1)
     o2 = spin_send(both, 2, -1)
     o1 = spin_send(both, 1, -1)
     o4 = spin_send(o3[:256], 1, -1)
     p3, p2 = row_send(o3, dx=1), row_send(o2, dx=1)
     p1, p4 = row_send(o1, dx=1), row_send(o4, dx=1)
-    pair, o1 = tie(pair, o1)
-    pair, o2 = tie(pair, o2)
+    plan = plan_tiles(ids, col_blocks, dest_blocks, lists[0], lists[1])
+
+    pack = pack_up(ids, weight, out_grad, bias_vector[None, :], o1, o2, o3)
+    pair = pair_up(pack, feat_send(pack, dx=1), p1, p2, p3, p4, plan)
     wu, wd = feat_send(pair, dy=1), feat_send(pair, dy=-1)
     wa, wb = feat_send(wu[:784], dy=1), feat_send(wd[784:], dy=-1)
-    plan = plan_tiles(ids, col_blocks, dest_blocks, lists[0], lists[1])
-
-    mine, theirs = aggregate(plan, adj_tiles, more, (both_b, x0, o4, o1, o2, o3, p4, p1, p2, p3))
+
+    mine, theirs = aggregate(plan, adj_tiles, more, (both_a, x0, o4, o1, o2, o3, p4, p1, p2, p3))
     aggregated = (mine + row_send(theirs, dc=1)).astype(bf16).reshape(256, B)
 
     q = jnp.concatenate([aggregated, feat_send(aggregated, dx=1)], axis=0)
@@ -419,11 +418,13 @@
 
     peer = row_send(prop, dc=1)
     got = row_send(give, dc=1)
-    near, first, rest = spread(plan, adj_tiles, more, prop, peer, keep, got)
+    send = (keep[32:] + got[32:]).astype(bf16)
+    got_x = row_send(send, dx=1)
+    near, first, rest = spread(plan, adj_tiles, more, prop, peer, send)
     came, came_rest = row_send(first, dx=1), row_send(rest, dx=1)
-    quarter, t4 = meet(keep, got, came, near)
-
-    r4 = spin_send(t4, 1)
+    quarter = (keep[:32] + got[:32] + got_x.astype(f32)).astype(bf16)
+
+    r4 = spin_send((near[12:14] + came.astype(f32)).astype(bf16), 1)
     halves = jnp.concatenate([quarter, row_send(quarter, dc=1)], axis=0)
     d3, d2, d1 = (spin_send(halves, k, -1) for k in (3, 2, 1))
     d4 = spin_send(d3[:32], 1, -1)

time: 142 us -> 150 us (1.056)
  starting transfers between devices: 52.3 us -> 67.2 us
  waiting for transfers between devices: 61.4 us -> 56.1 us
  Pallas kernels: 21.8 us -> 19.1 us
    ppermute x12, starting transfers between devices: 19.3 us -> 29.5 us  [spin_send(): return lax.ppermute(v, 'row', perm)]
    ppermute x12, waiting for transfers between devices: 25.2 us -> 15.9 us  [spin_send(): return lax.ppermute(v, 'row', perm)]
    ppermute x19 -> x20, waiting for transfers between devices: 16.5 us -> 21.8 us  [row_send(): return lax.ppermute(v, 'row', perm)]
    ppermute x9, starting transfers between devices: 10.3 us -> 14.1 us  [feat_send(): lax.ppermute(v, 'feat', [(i, (i >> 2 ^ dx) << 2 | i + dy & 3) for i in ra...]
    unnamed x18 -> x17, local copies, waits for them, and re-layouts: 3.31 us -> 4.61 us
    ppermute x19 -> x20, starting transfers between devices: 22.6 us -> 23.7 us  [row_send(): return lax.ppermute(v, 'row', perm)]
  transfers between devices with their start and end apart: 40 -> 41, of which waited for: 24 -> 19; matrix products, arithmetic and copies ran while one was open for 1% -> 2% of each run, Pallas kernels for 9% -> 10%
where the time goes in v1:
time: 150 us
  starting transfers between devices  67.2 us (45%)
  waiting for transfers between devices  56.1 us (37%)
  Pallas kernels  19.1 us (13%)
  local copies, waits for them, and re-layouts  5.23 us (3%)
  other arithmetic  1.78 us (1%)
    ppermute x12, starting transfers between devices, spin_send(): return lax.ppermute(v, 'row', perm)  29.5 us
    ppermute x20, starting transfers between devices, row_send(): return lax.ppermute(v, 'row', perm)  23.7 us
    ppermute x20, waiting for transfers between devices, row_send(): return lax.ppermute(v, 'row', perm)  21.8 us
    ppermute x9, waiting for transfers between devices, feat_send(): lax.ppermute(v, 'feat', [(i, (i >> 2 ^ dx) << 2 | i + dy & 3) for i in ra...  18.4 us
    ppermute x12, waiting for transfers between devices, spin_send(): return lax.ppermute(v, 'row', perm)  15.9 us
    ppermute x9, starting transfers between devices, feat_send(): lax.ppermute(v, 'feat', [(i, (i >> 2 ^ dx) << 2 | i + dy & 3) for i in ra...  14.1 us
    pallas_call x1, Pallas kernels, aggregate(): pl.pallas_call(agg_body, out_shape=(jax.ShapeDtypeStruct((2, B, B), f32),...  4.85 us
    unnamed x17, local copies, waits for them, and re-layouts  4.61 us
  transfers between devices with their start and end apart: 41, of which 19 were waited for; matrix products, arithmetic and copies ran while one was open for 2% of the time, Pallas kernels for 10%

profile of v1, /device:TPU:1, one launch (start us, length us, event | category | flops | bytes accessed | tf_op | source)
XLA Modules:
  0.0 150.3 jit_solution(3373206044149599090)
XLA Ops:
  0.6 3.3 %collective-permute-start.1 = (bf16[256,128]{1,0:T(8,128)(2,1)}, bf16[256,128]{1,0:T(8,128)(2,1)S(1)}, u32[]{:S(2)}, u32[]{:S(2)}) collective-permute-start(bf16[256,128]{1,0:T(8,128)(2,1)} %param.7), channel_id=1, source_target_pairs={{0,8},{8,0},{16,24},{24,16},{32,40},{40,32},{48,56},{56,48},{64,72... | collective-permute-start | bytes 196616 | tf_op jit(solution)/shard_map/ppermute | solution.py:25
  5.5 2.6 %collective-permute-start.4 = (bf16[512,128]{1,0:T(8,128)(2,1)S(1)}, bf16[512,128]{1,0:T(8,128)(2,1)S(1)}, u32[]{:S(2)}, u32[]{:S(2)}) collective-permute-start(bf16[512,128]{1,0:T(8,128)(2,1)S(1)} %constant_dynamic-update-slice_fusion), channel_id=1, source_target_pairs={{0,80},{8,56},{16,96},{24,72},{32,112},{40,88},{48,0},{56,104},{64... | collective-permute-start | bytes 393224 | tf_op jit(solution)/shard_map/ppermute | solution.py:41
  8.1 2.9 %collective-permute-start.6 = (bf16[512,128]{1,0:T(8,128)(2,1)S(1)}, bf16[512,128]{1,0:T(8,128)(2,1)S(1)}, u32[]{:S(2)}, u32[]{:S(2)}) collective-permute-start(bf16[512,128]{1,0:T(8,128)(2,1)S(1)} %constant_dynamic-update-slice_fusion), channel_id=1, source_target_pairs={{0,112},{8,24},{16,0},{24,40},{32,16},{40,56},{48,32},{56,72},{64,... | collective-permute-start | bytes 393224 | tf_op jit(solution)/shard_map/ppermute | solution.py:41
  11.0 1.2 collective-permute-start.7
  12.8 3.7 %collective-permute-start.5 = (bf16[256,128]{1,0:T(8,128)(2,1)S(1)}, bf16[256,128]{1,0:T(8,128)(2,1)S(1)}, u32[]{:S(2)}, u32[]{:S(2)}) collective-permute-start(bf16[256,128]{1,0:T(8,128)(2,1)S(1)} %slice.96), channel_id=1, source_target_pairs={{0,112},{8,24},{16,0},{24,40},{32,16},{40,56},{48,32},{56,72},{64,... | collective-permute-start | bytes 196616 | tf_op jit(solution)/shard_map/ppermute | solution.py:41
  17.2 1.5 collective-permute-start
  19.6 1.2 collective-permute-start.8
  20.9 0.9 copy-done.1
  24.1 2.5 %collective-permute-start.17 = (bf16[784,128]{1,0:T(8,128)(2,1)S(1)}, bf16[784,128]{1,0:T(8,128)(2,1)S(1)}, u32[]{:S(2)}, u32[]{:S(2)}) collective-permute-start(bf16[784,128]{1,0:T(8,128)(2,1)S(1)} %pack_up.1.a), channel_id=1, source_target_pairs={{0,4},{1,5},{2,6},{3,7},{4,0},{5,1},{6,2},{7,3},{8,12},{9,13},{10,... | collective-permute-start | bytes 602120 | tf_op jit(solution)/shard_map/ppermute | solution.py:29
  26.6 1.5 collective-permute-start.10
  29.5 3.5 %plan_tiles.1.plan.refs_4_ = s32[160]{0:T(256)S(1)} custom-call(s32[2]{0:T(128)S(1)} %pad_add_fusion.1.ids, s32[64]{0:T(128)S(1)} %copy-done.4, s32[64]{0:T(128)S(1)} %copy-done.5, s32[64]{0:T(128)S(1)} %get-tuple-element.41.c1, s32[64]{0:T(128)S(1)} %get-tuple-element.40.d1), custom_call_target="tpu_custom_call" | custom-call | flops 10000 | bytes 4096 | tf_op jit(solution)/shard_map/plan_tiles/pallas_call | solution.py:125
  33.0 2.5 %collective-permute-done.10.refs_1_ = bf16[512,128]{1,0:T(8,128)(2,1)S(1)} collective-permute-done((bf16[512,128]{1,0:T(8,128)(2,1)S(1)}, bf16[512,128]{1,0:T(8,128)(2,1)S(1)}, u32[]{:S(2)}, u32[]{:S(2)}) %collective-permute-start.10) | collective-permute-done | bytes 131104 | tf_op jit(solution)/shard_map/ppermute | solution.py:25
  35.5 2.8 %collective-permute-done.11.refs_2_ = bf16[512,128]{1,0:T(8,128)(2,1)S(1)} collective-permute-done((bf16[512,128]{1,0:T(8,128)(2,1)S(1)}, bf16[512,128]{1,0:T(8,128)(2,1)S(1)}, u32[]{:S(2)}, u32[]{:S(2)}) %collective-permute-start.11) | collective-permute-done | bytes 131104 | tf_op jit(solution)/shard_map/ppermute | solution.py:25
  38.3 1.4 collective-permute-start.18
  39.7 1.5 %collective-permute-start.19 = (bf16[1568,128]{1,0:T(8,128)(2,1)S(1)}, bf16[1568,128]{1,0:T(8,128)(2,1)S(1)}, u32[]{:S(2)}, u32[]{:S(2)}) collective-permute-start(bf16[1568,128]{1,0:T(8,128)(2,1)S(1)} %pair_up.1.refs_0_), channel_id=1, source_target_pairs={{0,3},{1,0},{2,1},{3,2},{4,7},{5,4},{6,5},{7,6},{8,11},{9,8},{10,9... | collective-permute-start | bytes 1204232 | tf_op jit(solution)/shard_map/ppermute | solution.py:29
  41.2 6.7 %collective-permute-done.18.refs_1_ = bf16[1568,128]{1,0:T(8,128)(2,1)S(1)} collective-permute-done((bf16[1568,128]{1,0:T(8,128)(2,1)S(1)}, bf16[1568,128]{1,0:T(8,128)(2,1)S(1)}, u32[]{:S(2)}, u32[]{:S(2)}) %collective-permute-start.18) | collective-permute-done | bytes 401440 | tf_op jit(solution)/shard_map/ppermute | solution.py:29
  48.0 2.7 %collective-permute-start.21 = (bf16[784,128]{1,0:T(8,128)(2,1)S(1)}, bf16[784,128]{1,0:T(8,128)(2,1)S(1)}, u32[]{:S(2)}, u32[]{:S(2)}) collective-permute-start(bf16[784,128]{1,0:T(8,128)(2,1)S(1)} %slice.98), channel_id=1, source_target_pairs={{0,3},{1,0},{2,1},{3,2},{4,7},{5,4},{6,5},{7,6},{8,11},{9,8},{10,9... | collective-permute-start | bytes 602120 | tf_op jit(solution)/shard_map/ppermute | solution.py:29
  50.7 3.0 %collective-permute-done.20.refs_3_ = bf16[784,128]{1,0:T(8,128)(2,1)S(1)} collective-permute-done((bf16[784,128]{1,0:T(8,128)(2,1)S(1)}, bf16[784,128]{1,0:T(8,128)(2,1)S(1)}, u32[]{:S(2)}, u32[]{:S(2)}) %collective-permute-start.20) | collective-permute-done | bytes 200736 | tf_op jit(solution)/shard_map/ppermute | solution.py:29
  53.7 1.4 lay_out.1
  55.2 4.7 %collective-permute-start.22 = (bf16[1024,512]{1,0:T(8,128)(2,1)S(1)}, bf16[1024,512]{1,0:T(8,128)(2,1)S(1)}, u32[]{:S(2)}, u32[]{:S(2)}) collective-permute-start(bf16[1024,512]{1,0:T(8,128)(2,1)S(1)} %get-tuple-element.24.w0), channel_id=1, source_target_pairs={{0,8},{8,0},{16,24},{24,16},{32,40},{40,32},{48,56},{56,48},{64,72... | collective-permute-start | bytes 3145736 | tf_op jit(solution)/shard_map/ppermute | solution.py:25
  59.9 1.5 %collective-permute-start.3 = (bf16[256,128]{1,0:T(8,128)(2,1)S(1)}, bf16[256,128]{1,0:T(8,128)(2,1)S(1)}, u32[]{:S(2)}, u32[]{:S(2)}) collective-permute-start(bf16[256,128]{1,0:T(8,128)(2,1)S(1)} %copy-done.7), channel_id=1, source_target_pairs={{0,128},{8,136},{16,144},{24,152},{32,160},{40,168},{48,176},{56,1... | collective-permute-start | bytes 196616 | tf_op jit(solution)/shard_map/ppermute | solution.py:25
  61.4 2.0 %collective-permute-done.3 = bf16[256,128]{1,0:T(8,128)(2,1)S(1)} collective-permute-done((bf16[256,128]{1,0:T(8,128)(2,1)S(1)}, bf16[256,128]{1,0:T(8,128)(2,1)S(1)}, u32[]{:S(2)}, u32[]{:S(2)}) %collective-permute-start.3) | collective-permute-done | bytes 65568 | tf_op jit(solution)/shard_map/ppermute | solution.py:25
  63.4 4.8 %aggregate.1 = (f32[2,128,128]{2,1,0:T(8,128)S(1)}, f32[2,128,128]{2,1,0:T(8,128)S(1)}) custom-call(s32[160]{0:T(256)S(1)} %plan_tiles.1.plan.refs_4_, bf16[64,128,128]{2,1,0:T(8,128)(2,1)S(1)} %copy-done, bf16[64,128,128]{2,1,0:T(8,128)(2,1)S(1)} %collective-permute-done.2.more, bf16[4,128,128]{2,1,0:T(8,128)(2,1)S(1)} %bitcast.30, ...), custom_call_target="tpu_custom_call" | custom-call | flops 268435456 | bytes 4194304 | tf_op jit(solution)/shard_map/aggregate/pallas_call | solution.py:176
  68.3 1.7 %collective-permute-start.12 = (f32[2,128,128]{2,1,0:T(8,128)S(1)}, f32[2,128,128]{2,1,0:T(8,128)S(1)}, u32[]{:S(2)}, u32[]{:S(2)}) collective-permute-start(f32[2,128,128]{2,1,0:T(8,128)S(1)} %get-tuple-element.23), channel_id=1, source_target_pairs={{0,8},{8,0},{16,24},{24,16},{32,40},{40,32},{48,56},{56,48},{64,72... | collective-permute-start | bytes 393224 | tf_op jit(solution)/shard_map/ppermute | solution.py:25
  70.0 1.0 collective-permute-done.12
  71.0 1.5 %collective-permute-start.13 = (bf16[256,128]{1,0:T(8,128)(2,1)S(1)}, bf16[256,128]{1,0:T(8,128)(2,1)S(1)}, u32[]{:S(2)}, u32[]{:S(2)}) collective-permute-start(bf16[256,128]{1,0:T(8,128)(2,1)S(1)} %bitcast.39), channel_id=1, source_target_pairs={{0,4},{1,5},{2,6},{3,7},{4,0},{5,1},{6,2},{7,3},{8,12},{9,13},{10,... | collective-permute-start | bytes 196616 | tf_op jit(solution)/shard_map/ppermute | solution.py:29
  72.5 3.2 %collective-permute-done.13 = bf16[256,128]{1,0:T(8,128)(2,1)S(1)} collective-permute-done((bf16[256,128]{1,0:T(8,128)(2,1)S(1)}, bf16[256,128]{1,0:T(8,128)(2,1)S(1)}, u32[]{:S(2)}, u32[]{:S(2)}) %collective-permute-start.13) | collective-permute-done | bytes 65568 | tf_op jit(solution)/shard_map/ppermute | solution.py:29
  76.6 2.4 %collective-permute-start.15 = (bf16[512,128]{1,0:T(8,128)(2,1)S(1)}, bf16[512,128]{1,0:T(8,128)(2,1)S(1)}, u32[]{:S(2)}, u32[]{:S(2)}) collective-permute-start(bf16[512,128]{1,0:T(8,128)(2,1)S(1)} %pad_maximum_fusion.2.p0), channel_id=1, source_target_pairs={{0,3},{1,0},{2,1},{3,2},{4,7},{5,4},{6,5},{7,6},{8,11},{9,8},{10,9... | collective-permute-start | bytes 393224 | tf_op jit(solution)/shard_map/ppermute | solution.py:29
  78.9 1.1 collective-permute-start.16
  80.0 1.2 collective-permute-done.14.p1
  81.2 4.4 %collective-permute-done.16.p3 = bf16[512,128]{1,0:T(8,128)(2,1)S(1)} collective-permute-done((bf16[512,128]{1,0:T(8,128)(2,1)S(1)}, bf16[512,128]{1,0:T(8,128)(2,1)S(1)}, u32[]{:S(2)}, u32[]{:S(2)}) %collective-permute-start.16) | collective-permute-done | bytes 131104 | tf_op jit(solution)/shard_map/ppermute | solution.py:29
  85.6 2.2 %middle.1 = (f32[256,128]{1,0:T(8,128)}, bf16[256,128]{1,0:T(8,128)(2,1)S(1)}, f32[64,1152]{1,0:T(8,128)S(1)}, f32[64,1152]{1,0:T(8,128)S(1)}) custom-call(s32[2]{0:T(128)S(1)} %pad_add_fusion.1.ids, bf16[512,128]{1,0:T(8,128)(2,1)S(1)} %pad_maximum_fusion.2.p0, bf16[512,128]{1,0:T(8,128)(2,1)S(1)} %collective-permute-done.14.p1, ...), custom_call_target="tpu_custom_call" | custom-call | flops 671088640 | bytes 5242880 | tf_op jit(solution)/shard_map/middle/pallas_call | solution.py:265
  87.8 2.2 %collective-permute-start.24 = (f32[64,1152]{1,0:T(8,128)S(1)}, f32[64,1152]{1,0:T(8,128)S(1)}, u32[]{:S(2)}, u32[]{:S(2)}) collective-permute-start(f32[64,1152]{1,0:T(8,128)S(1)} %get-tuple-element.30), channel_id=1, source_target_pairs={{0,8},{8,0},{16,24},{24,16},{32,40},{40,32},{48,56},{56,48},{64,72... | collective-permute-start | bytes 884744 | tf_op jit(solution)/shard_map/ppermute | solution.py:25
  90.0 1.2 collective-permute-done.24
  91.2 1.2 collective-permute-start.32
  92.4 4.2 %spread.1 = (f32[16,128,128]{2,1,0:T(8,128)S(1)}, bf16[2,128,128]{2,1,0:T(8,128)(2,1)S(1)}, bf16[14,128,128]{2,1,0:T(8,128)(2,1)S(1)}) custom-call(s32[160]{0:T(256)S(1)} %plan_tiles.1.plan.refs_4_, bf16[64,128,128]{2,1,0:T(8,128)(2,1)S(1)} %copy-done, bf16[64,128,128]{2,1,0:T(8,128)(2,1)S(1)} %collective-permute-done.2.more, ...), custom_call_target="tpu_custom_call" | custom-call | flops 268435456 | bytes 6291456 | tf_op jit(solution)/shard_map/spread/pallas_call | solution.py:306
  98.2 2.0 %collective-permute-start.33 = (bf16[32,1152]{1,0:T(8,128)(2,1)S(1)}, bf16[32,1152]{1,0:T(8,128)(2,1)S(1)}, u32[]{:S(2)}, u32[]{:S(2)}) collective-permute-start(bf16[32,1152]{1,0:T(8,128)(2,1)S(1)} %fusion.1.own), channel_id=1, source_target_pairs={{0,8},{8,0},{16,24},{24,16},{32,40},{40,32},{48,56},{56,48},{64,72... | collective-permute-start | bytes 221192 | tf_op jit(solution)/shard_map/ppermute | solution.py:25
  100.2 8.6 %collective-permute-done.28 = bf16[2,128,128]{2,1,0:T(8,128)(2,1)S(1)} collective-permute-done((bf16[2,128,128]{2,1,0:T(8,128)(2,1)S(1)}, bf16[2,128,128]{2,1,0:T(8,128)(2,1)S(1)}, u32[]{:S(2)}, u32[]{:S(2)}) %collective-permute-start.28) | collective-permute-done | bytes 65568 | tf_op jit(solution)/shard_map/ppermute | solution.py:25
  108.8 2.9 %collective-permute-start.29 = (bf16[2,128,128]{2,1,0:T(8,128)(2,1)S(1)}, bf16[2,128,128]{2,1,0:T(8,128)(2,1)S(1)}, u32[]{:S(2)}, u32[]{:S(2)}) collective-permute-start(bf16[2,128,128]{2,1,0:T(8,128)(2,1)S(1)} %add_convert_fusion), channel_id=1, source_target_pairs={{0,16},{8,120},{16,32},{24,8},{32,48},{40,24},{48,64},{56,40},{64,... | collective-permute-start | bytes 196616 | tf_op jit(solution)/shard_map/ppermute | solution.py:41
  111.9 1.4 collective-permute-start.35
  113.3 4.9 %collective-permute-start.36 = (bf16[64,1152]{1,0:T(8,128)(2,1)S(1)}, bf16[64,1152]{1,0:T(8,128)(2,1)S(1)}, u32[]{:S(2)}, u32[]{:S(2)}) collective-permute-start(bf16[64,1152]{1,0:T(8,128)(2,1)S(1)} %pad_maximum_fusion), channel_id=1, source_target_pairs={{0,80},{8,56},{16,96},{24,72},{32,112},{40,88},{48,0},{56,104},{64... | collective-permute-start | bytes 442376 | tf_op jit(solution)/shard_map/ppermute | solution.py:41
  119.3 7.2 %collective-permute-done.36.d3 = bf16[64,1152]{1,0:T(8,128)(2,1)S(1)} collective-permute-done((bf16[64,1152]{1,0:T(8,128)(2,1)S(1)}, bf16[64,1152]{1,0:T(8,128)(2,1)S(1)}, u32[]{:S(2)}, u32[]{:S(2)}) %collective-permute-start.36) | collective-permute-done | bytes 147488 | tf_op jit(solution)/shard_map/ppermute | solution.py:41
  126.9 5.8 %collective-permute-start.30 = (bf16[4,128,128]{2,1,0:T(8,128)(2,1)S(1)}, bf16[4,128,128]{2,1,0:T(8,128)(2,1)S(1)}, u32[]{:S(2)}, u32[]{:S(2)}) collective-permute-start(bf16[4,128,128]{2,1,0:T(8,128)(2,1)S(1)} %pad_maximum_fusion.3.t), channel_id=1, source_target_pairs={{0,48},{8,88},{16,64},{24,104},{32,80},{40,120},{48,96},{56,8},{64... | collective-permute-start | bytes 393224 | tf_op jit(solution)/shard_map/ppermute | solution.py:41
  132.7 2.5 %collective-permute-start.27 = (bf16[4,128,128]{2,1,0:T(8,128)(2,1)S(1)}, bf16[4,128,128]{2,1,0:T(8,128)(2,1)S(1)}, u32[]{:S(2)}, u32[]{:S(2)}) collective-permute-start(bf16[4,128,128]{2,1,0:T(8,128)(2,1)S(1)} %get-tuple-element.39), channel_id=1, source_target_pairs={{0,32},{8,104},{16,48},{24,120},{32,64},{40,8},{48,80},{56,24},{64... | collective-permute-start | bytes 393224 | tf_op jit(solution)/shard_map/ppermute | solution.py:41
  135.2 1.5 collective-permute-start.37
  136.7 6.3 %collective-permute-done.37.d4 = bf16[32,1152]{1,0:T(8,128)(2,1)S(1)} collective-permute-done((bf16[32,1152]{1,0:T(8,128)(2,1)S(1)}, bf16[32,1152]{1,0:T(8,128)(2,1)S(1)}, u32[]{:S(2)}, u32[]{:S(2)}) %collective-permute-start.37) | collective-permute-done | bytes 73760 | tf_op jit(solution)/shard_map/ppermute | solution.py:41
  144.1 2.8 %collective-permute-done.39 = bf16[32,1152]{1,0:T(8,128)(2,1)S(1)} collective-permute-done((bf16[32,1152]{1,0:T(8,128)(2,1)S(1)}, bf16[32,1152]{1,0:T(8,128)(2,1)S(1)}, u32[]{:S(2)}, u32[]{:S(2)}) %collective-permute-start.39) | collective-permute-done | bytes 73760 | tf_op jit(solution)/shard_map/ppermute | solution.py:25
  148.4 1.4 weight_out.1
  (86 shorter events, 14.8 us)
Async XLA Ops:
  0.6 4.4 %collective-permute-start.1 = (bf16[256,128]{1,0:T(8,128)(2,1)}, bf16[256,128]{1,0:T(8,128)(2,1)S(1)}, u32[]{:S(2)}, u32[]{:S(2)}) collective-permute-start(bf16[256,128]{1,0:T(8,128)(2,1)} %param.7), channel_id=1, source_target_pairs={{0,8},{8,0},{16,24},{24,16},{32,40},{40,32},{48,56},{56,48},{64,72... | collective-permute-start | bytes 196616 | tf_op jit(solution)/shard_map/ppermute | solution.py:25
  5.1 58.4 %collective-permute-start.2 = (bf16[64,128,128]{2,1,0:T(8,128)(2,1)}, bf16[64,128,128]{2,1,0:T(8,128)(2,1)S(1)}, u32[]{:S(2)}, u32[]{:S(2)}) collective-permute-start(bf16[64,128,128]{2,1,0:T(8,128)(2,1)} %tiles.3), channel_id=1, source_target_pairs={{0,8},{8,0},{16,24},{24,16},{32,40},{40,32},{48,56},{56,48},{64,72... | collective-permute-start | bytes 6291464 | tf_op jit(solution)/shard_map/ppermute | solution.py:25
  5.5 7.3 %collective-permute-start.4 = (bf16[512,128]{1,0:T(8,128)(2,1)S(1)}, bf16[512,128]{1,0:T(8,128)(2,1)S(1)}, u32[]{:S(2)}, u32[]{:S(2)}) collective-permute-start(bf16[512,128]{1,0:T(8,128)(2,1)S(1)} %constant_dynamic-update-slice_fusion), channel_id=1, source_target_pairs={{0,80},{8,56},{16,96},{24,72},{32,112},{40,88},{48,0},{56,104},{64... | collective-permute-start | bytes 393224 | tf_op jit(solution)/shard_map/ppermute | solution.py:41
  8.1 12.7 %collective-permute-start.6 = (bf16[512,128]{1,0:T(8,128)(2,1)S(1)}, bf16[512,128]{1,0:T(8,128)(2,1)S(1)}, u32[]{:S(2)}, u32[]{:S(2)}) collective-permute-start(bf16[512,128]{1,0:T(8,128)(2,1)S(1)} %constant_dynamic-update-slice_fusion), channel_id=1, source_target_pairs={{0,112},{8,24},{16,0},{24,40},{32,16},{40,56},{48,32},{56,72},{64,... | collective-permute-start | bytes 393224 | tf_op jit(solution)/shard_map/ppermute | solution.py:41
  11.0 9.9 %collective-permute-start.7 = (bf16[512,128]{1,0:T(8,128)(2,1)S(1)}, bf16[512,128]{1,0:T(8,128)(2,1)S(1)}, u32[]{:S(2)}, u32[]{:S(2)}) collective-permute-start(bf16[512,128]{1,0:T(8,128)(2,1)S(1)} %constant_dynamic-update-slice_fusion), channel_id=1, source_target_pairs={{0,96},{8,40},{16,112},{24,56},{32,0},{40,72},{48,16},{56,88},{64,... | collective-permute-start | bytes 393224 | tf_op jit(solution)/shard_map/ppermute | solution.py:41
  12.8 6.8 %collective-permute-start.5 = (bf16[256,128]{1,0:T(8,128)(2,1)S(1)}, bf16[256,128]{1,0:T(8,128)(2,1)S(1)}, u32[]{:S(2)}, u32[]{:S(2)}) collective-permute-start(bf16[256,128]{1,0:T(8,128)(2,1)S(1)} %slice.96), channel_id=1, source_target_pairs={{0,112},{8,24},{16,0},{24,40},{32,16},{40,56},{48,32},{56,72},{64,... | collective-permute-start | bytes 196616 | tf_op jit(solution)/shard_map/ppermute | solution.py:41
  17.2 9.4 %collective-permute-start = (s32[2,64]{1,0:T(2,128)S(1)}, s32[2,64]{1,0:T(2,128)S(1)}, u32[]{:S(2)}, u32[]{:S(2)}) collective-permute-start(s32[2,64]{1,0:T(2,128)S(1)} %pad_add_fusion), channel_id=1, source_target_pairs={{0,8},{8,0},{16,24},{24,16},{32,40},{40,32},{48,56},{56,48},{64,72... | collective-permute-start | bytes 1544 | tf_op jit(solution)/shard_map/ppermute | solution.py:25
  19.6 8.5 %collective-permute-start.8 = (bf16[256,128]{1,0:T(8,128)(2,1)S(1)}, bf16[256,128]{1,0:T(8,128)(2,1)S(1)}, u32[]{:S(2)}, u32[]{:S(2)}) collective-permute-start(bf16[256,128]{1,0:T(8,128)(2,1)S(1)} %collective-permute-done.5), channel_id=1, source_target_pairs={{0,128},{8,136},{16,144},{24,152},{32,160},{40,168},{48,176},{56,1... | collective-permute-start | bytes 196616 | tf_op jit(solution)/shard_map/ppermute | solution.py:25
  20.9 1.0 copy-start.1
  21.8 0.8 copy-start.3
  22.7 0.7 copy-start.6
  23.3 40.1 %copy-start = (bf16[64,128,128]{2,1,0:T(8,128)(2,1)S(1)}, bf16[64,128,128]{2,1,0:T(8,128)(2,1)}, u32[]{:S(2)}) copy-start(bf16[64,128,128]{2,1,0:T(8,128)(2,1)} %tiles.3) | copy-start | bytes 6291460
  24.1 14.2 %collective-permute-start.17 = (bf16[784,128]{1,0:T(8,128)(2,1)S(1)}, bf16[784,128]{1,0:T(8,128)(2,1)S(1)}, u32[]{:S(2)}, u32[]{:S(2)}) collective-permute-start(bf16[784,128]{1,0:T(8,128)(2,1)S(1)} %pack_up.1.a), channel_id=1, source_target_pairs={{0,4},{1,5},{2,6},{3,7},{4,0},{5,1},{6,2},{7,3},{8,12},{9,13},{10,... | collective-permute-start | bytes 602120 | tf_op jit(solution)/shard_map/ppermute | solution.py:29
  26.6 6.4 %collective-permute-start.9 = (bf16[512,128]{1,0:T(8,128)(2,1)S(1)}, bf16[512,128]{1,0:T(8,128)(2,1)S(1)}, u32[]{:S(2)}, u32[]{:S(2)}) collective-permute-start(bf16[512,128]{1,0:T(8,128)(2,1)S(1)} %collective-permute-done.6.refs_0_), channel_id=1, source_target_pairs={{0,128},{8,136},{16,144},{24,152},{32,160},{40,168},{48,176},{56,1... | collective-permute-start | bytes 393224 | tf_op jit(solution)/shard_map/ppermute | solution.py:25
  26.6 8.9 %collective-permute-start.10 = (bf16[512,128]{1,0:T(8,128)(2,1)S(1)}, bf16[512,128]{1,0:T(8,128)(2,1)S(1)}, u32[]{:S(2)}, u32[]{:S(2)}) collective-permute-start(bf16[512,128]{1,0:T(8,128)(2,1)S(1)} %collective-permute-done.7.refs_1_), channel_id=1, source_target_pairs={{0,128},{8,136},{16,144},{24,152},{32,160},{40,168},{48,176},{56,1... | collective-permute-start | bytes 393224 | tf_op jit(solution)/shard_map/ppermute | solution.py:25
  28.1 10.2 %collective-permute-start.11 = (bf16[512,128]{1,0:T(8,128)(2,1)S(1)}, bf16[512,128]{1,0:T(8,128)(2,1)S(1)}, u32[]{:S(2)}, u32[]{:S(2)}) collective-permute-start(bf16[512,128]{1,0:T(8,128)(2,1)S(1)} %collective-permute-done.4.refs_2_), channel_id=1, source_target_pairs={{0,128},{8,136},{16,144},{24,152},{32,160},{40,168},{48,176},{56,1... | collective-permute-start | bytes 393224 | tf_op jit(solution)/shard_map/ppermute | solution.py:25
  28.2 0.7 copy-start.4
  29.5 30.4 %copy-start.7 = (bf16[256,128]{1,0:T(8,128)(2,1)S(1)}, bf16[256,128]{1,0:T(8,128)(2,1)}, u32[]{:S(2)}) copy-start(bf16[256,128]{1,0:T(8,128)(2,1)} %param.7) | copy-start | bytes 196612
  38.3 9.6 %collective-permute-start.18 = (bf16[1568,128]{1,0:T(8,128)(2,1)S(1)}, bf16[1568,128]{1,0:T(8,128)(2,1)S(1)}, u32[]{:S(2)}, u32[]{:S(2)}) collective-permute-start(bf16[1568,128]{1,0:T(8,128)(2,1)S(1)} %pair_up.1.refs_0_), channel_id=1, source_target_pairs={{0,1},{1,2},{2,3},{3,0},{4,5},{5,6},{6,7},{7,4},{8,9},{9,10},{10,1... | collective-permute-start | bytes 1204232 | tf_op jit(solution)/shard_map/ppermute | solution.py:29
  39.7 8.3 %collective-permute-start.19 = (bf16[1568,128]{1,0:T(8,128)(2,1)S(1)}, bf16[1568,128]{1,0:T(8,128)(2,1)S(1)}, u32[]{:S(2)}, u32[]{:S(2)}) collective-permute-start(bf16[1568,128]{1,0:T(8,128)(2,1)S(1)} %pair_up.1.refs_0_), channel_id=1, source_target_pairs={{0,3},{1,0},{2,1},{3,2},{4,7},{5,4},{6,5},{7,6},{8,11},{9,8},{10,9... | collective-permute-start | bytes 1204232 | tf_op jit(solution)/shard_map/ppermute | solution.py:29
  47.9 5.9 %collective-permute-start.20 = (bf16[784,128]{1,0:T(8,128)(2,1)S(1)}, bf16[784,128]{1,0:T(8,128)(2,1)S(1)}, u32[]{:S(2)}, u32[]{:S(2)}) collective-permute-start(bf16[784,128]{1,0:T(8,128)(2,1)S(1)} %slice.97), channel_id=1, source_target_pairs={{0,1},{1,2},{2,3},{3,0},{4,5},{5,6},{6,7},{7,4},{8,9},{9,10},{10,1... | collective-permute-start | bytes 602120 | tf_op jit(solution)/shard_map/ppermute | solution.py:29
  48.0 5.7 %collective-permute-start.21 = (bf16[784,128]{1,0:T(8,128)(2,1)S(1)}, bf16[784,128]{1,0:T(8,128)(2,1)S(1)}, u32[]{:S(2)}, u32[]{:S(2)}) collective-permute-start(bf16[784,128]{1,0:T(8,128)(2,1)S(1)} %slice.98), channel_id=1, source_target_pairs={{0,3},{1,0},{2,1},{3,2},{4,7},{5,4},{6,5},{7,6},{8,11},{9,8},{10,9... | collective-permute-start | bytes 602120 | tf_op jit(solution)/shard_map/ppermute | solution.py:29
  55.2 24.9 %collective-permute-start.22 = (bf16[1024,512]{1,0:T(8,128)(2,1)S(1)}, bf16[1024,512]{1,0:T(8,128)(2,1)S(1)}, u32[]{:S(2)}, u32[]{:S(2)}) collective-permute-start(bf16[1024,512]{1,0:T(8,128)(2,1)S(1)} %get-tuple-element.24.w0), channel_id=1, source_target_pairs={{0,8},{8,0},{16,24},{24,16},{32,40},{40,32},{48,56},{56,48},{64,72... | collective-permute-start | bytes 3145736 | tf_op jit(solution)/shard_map/ppermute | solution.py:25
  59.9 3.5 %collective-permute-start.3 = (bf16[256,128]{1,0:T(8,128)(2,1)S(1)}, bf16[256,128]{1,0:T(8,128)(2,1)S(1)}, u32[]{:S(2)}, u32[]{:S(2)}) collective-permute-start(bf16[256,128]{1,0:T(8,128)(2,1)S(1)} %copy-done.7), channel_id=1, source_target_pairs={{0,128},{8,136},{16,144},{24,152},{32,160},{40,168},{48,176},{56,1... | collective-permute-start | bytes 196616 | tf_op jit(solution)/shard_map/ppermute | solution.py:25
  63.4 22.1 %copy-start.2 = (bf16[128,1024]{1,0:T(8,128)(2,1)S(1)}, bf16[128,1024]{1,0:T(8,128)(2,1)}, u32[]{:S(2)}) copy-start(bf16[128,1024]{1,0:T(8,128)(2,1)} %w_own.1) | copy-start | bytes 786436
  68.3 2.7 %collective-permute-start.12 = (f32[2,128,128]{2,1,0:T(8,128)S(1)}, f32[2,128,128]{2,1,0:T(8,128)S(1)}, u32[]{:S(2)}, u32[]{:S(2)}) collective-permute-start(f32[2,128,128]{2,1,0:T(8,128)S(1)} %get-tuple-element.23), channel_id=1, source_target_pairs={{0,8},{8,0},{16,24},{24,16},{32,40},{40,32},{48,56},{56,48},{64,72... | collective-permute-start | bytes 393224 | tf_op jit(solution)/shard_map/ppermute | solution.py:25
  71.0 4.7 %collective-permute-start.13 = (bf16[256,128]{1,0:T(8,128)(2,1)S(1)}, bf16[256,128]{1,0:T(8,128)(2,1)S(1)}, u32[]{:S(2)}, u32[]{:S(2)}) collective-permute-start(bf16[256,128]{1,0:T(8,128)(2,1)S(1)} %bitcast.39), channel_id=1, source_target_pairs={{0,4},{1,5},{2,6},{3,7},{4,0},{5,1},{6,2},{7,3},{8,12},{9,13},{10,... | collective-permute-start | bytes 196616 | tf_op jit(solution)/shard_map/ppermute | solution.py:29
  75.7 5.5 %collective-permute-start.14 = (bf16[512,128]{1,0:T(8,128)(2,1)S(1)}, bf16[512,128]{1,0:T(8,128)(2,1)S(1)}, u32[]{:S(2)}, u32[]{:S(2)}) collective-permute-start(bf16[512,128]{1,0:T(8,128)(2,1)S(1)} %pad_maximum_fusion.2.p0), channel_id=1, source_target_pairs={{0,1},{1,2},{2,3},{3,0},{4,5},{5,6},{6,7},{7,4},{8,9},{9,10},{10,1... | collective-permute-start | bytes 393224 | tf_op jit(solution)/shard_map/ppermute | solution.py:29
  76.6 4.6 %collective-permute-start.15 = (bf16[512,128]{1,0:T(8,128)(2,1)S(1)}, bf16[512,128]{1,0:T(8,128)(2,1)S(1)}, u32[]{:S(2)}, u32[]{:S(2)}) collective-permute-start(bf16[512,128]{1,0:T(8,128)(2,1)S(1)} %pad_maximum_fusion.2.p0), channel_id=1, source_target_pairs={{0,3},{1,0},{2,1},{3,2},{4,7},{5,4},{6,5},{7,6},{8,11},{9,8},{10,9... | collective-permute-start | bytes 393224 | tf_op jit(solution)/shard_map/ppermute | solution.py:29
  78.9 6.6 %collective-permute-start.16 = (bf16[512,128]{1,0:T(8,128)(2,1)S(1)}, bf16[512,128]{1,0:T(8,128)(2,1)S(1)}, u32[]{:S(2)}, u32[]{:S(2)}) collective-permute-start(bf16[512,128]{1,0:T(8,128)(2,1)S(1)} %pad_maximum_fusion.2.p0), channel_id=1, source_target_pairs={{0,2},{1,3},{2,0},{3,1},{4,6},{5,7},{6,4},{7,5},{8,10},{9,11},{10,... | collective-permute-start | bytes 393224 | tf_op jit(solution)/shard_map/ppermute | solution.py:29
  87.8 3.4 %collective-permute-start.24 = (f32[64,1152]{1,0:T(8,128)S(1)}, f32[64,1152]{1,0:T(8,128)S(1)}, u32[]{:S(2)}, u32[]{:S(2)}) collective-permute-start(f32[64,1152]{1,0:T(8,128)S(1)} %get-tuple-element.30), channel_id=1, source_target_pairs={{0,8},{8,0},{16,24},{24,16},{32,40},{40,32},{48,56},{56,48},{64,72... | collective-permute-start | bytes 884744 | tf_op jit(solution)/shard_map/ppermute | solution.py:25
  90.0 2.5 %collective-permute-start.23 = (bf16[2,128,128]{2,1,0:T(8,128)(2,1)S(1)}, bf16[2,128,128]{2,1,0:T(8,128)(2,1)S(1)}, u32[]{:S(2)}, u32[]{:S(2)}) collective-permute-start(bf16[2,128,128]{2,1,0:T(8,128)(2,1)S(1)} %bitcast.33), channel_id=1, source_target_pairs={{0,8},{8,0},{16,24},{24,16},{32,40},{40,32},{48,56},{56,48},{64,72... | collective-permute-start | bytes 196616 | tf_op jit(solution)/shard_map/ppermute | solution.py:25
  91.2 7.0 %collective-permute-start.32 = (bf16[32,1152]{1,0:T(8,128)(2,1)S(1)}, bf16[32,1152]{1,0:T(8,128)(2,1)S(1)}, u32[]{:S(2)}, u32[]{:S(2)}) collective-permute-start(bf16[32,1152]{1,0:T(8,128)(2,1)S(1)} %fusion.2.send), channel_id=1, source_target_pairs={{0,128},{8,136},{16,144},{24,152},{32,160},{40,168},{48,176},{56,1... | collective-permute-start | bytes 221192 | tf_op jit(solution)/shard_map/ppermute | solution.py:25
  96.6 21.6 %collective-permute-start.25 = (bf16[14,128,128]{2,1,0:T(8,128)(2,1)S(1)}, bf16[14,128,128]{2,1,0:T(8,128)(2,1)S(1)}, u32[]{:S(2)}, u32[]{:S(2)}) collective-permute-start(bf16[14,128,128]{2,1,0:T(8,128)(2,1)S(1)} %get-tuple-element.32), channel_id=1, source_target_pairs={{0,128},{8,136},{16,144},{24,152},{32,160},{40,168},{48,176},{56,1... | collective-permute-start | bytes 1376264 | tf_op jit(solution)/shard_map/ppermute | solution.py:25
  97.5 11.3 %collective-permute-start.28 = (bf16[2,128,128]{2,1,0:T(8,128)(2,1)S(1)}, bf16[2,128,128]{2,1,0:T(8,128)(2,1)S(1)}, u32[]{:S(2)}, u32[]{:S(2)}) collective-permute-start(bf16[2,128,128]{2,1,0:T(8,128)(2,1)S(1)} %get-tuple-element.33), channel_id=1, source_target_pairs={{0,128},{8,136},{16,144},{24,152},{32,160},{40,168},{48,176},{56,1... | collective-permute-start | bytes 196616 | tf_op jit(solution)/shard_map/ppermute | solution.py:25
  98.2 13.5 %collective-permute-start.33 = (bf16[32,1152]{1,0:T(8,128)(2,1)S(1)}, bf16[32,1152]{1,0:T(8,128)(2,1)S(1)}, u32[]{:S(2)}, u32[]{:S(2)}) collective-permute-start(bf16[32,1152]{1,0:T(8,128)(2,1)S(1)} %fusion.1.own), channel_id=1, source_target_pairs={{0,8},{8,0},{16,24},{24,16},{32,40},{40,32},{48,56},{56,48},{64,72... | collective-permute-start | bytes 221192 | tf_op jit(solution)/shard_map/ppermute | solution.py:25
  108.8 18.0 %collective-permute-start.29 = (bf16[2,128,128]{2,1,0:T(8,128)(2,1)S(1)}, bf16[2,128,128]{2,1,0:T(8,128)(2,1)S(1)}, u32[]{:S(2)}, u32[]{:S(2)}) collective-permute-start(bf16[2,128,128]{2,1,0:T(8,128)(2,1)S(1)} %add_convert_fusion), channel_id=1, source_target_pairs={{0,16},{8,120},{16,32},{24,8},{32,48},{40,24},{48,64},{56,40},{64,... | collective-permute-start | bytes 196616 | tf_op jit(solution)/shard_map/ppermute | solution.py:41
  111.8 7.5 %collective-permute-start.34 = (bf16[64,1152]{1,0:T(8,128)(2,1)S(1)}, bf16[64,1152]{1,0:T(8,128)(2,1)S(1)}, u32[]{:S(2)}, u32[]{:S(2)}) collective-permute-start(bf16[64,1152]{1,0:T(8,128)(2,1)S(1)} %pad_maximum_fusion), channel_id=1, source_target_pairs={{0,112},{8,24},{16,0},{24,40},{32,16},{40,56},{48,32},{56,72},{64,... | collective-permute-start | bytes 442376 | tf_op jit(solution)/shard_map/ppermute | solution.py:41
  111.9 7.4 %collective-permute-start.35 = (bf16[64,1152]{1,0:T(8,128)(2,1)S(1)}, bf16[64,1152]{1,0:T(8,128)(2,1)S(1)}, u32[]{:S(2)}, u32[]{:S(2)}) collective-permute-start(bf16[64,1152]{1,0:T(8,128)(2,1)S(1)} %pad_maximum_fusion), channel_id=1, source_target_pairs={{0,96},{8,40},{16,112},{24,56},{32,0},{40,72},{48,16},{56,88},{64,... | collective-permute-start | bytes 442376 | tf_op jit(solution)/shard_map/ppermute | solution.py:41
  113.3 13.2 %collective-permute-start.36 = (bf16[64,1152]{1,0:T(8,128)(2,1)S(1)}, bf16[64,1152]{1,0:T(8,128)(2,1)S(1)}, u32[]{:S(2)}, u32[]{:S(2)}) collective-permute-start(bf16[64,1152]{1,0:T(8,128)(2,1)S(1)} %pad_maximum_fusion), channel_id=1, source_target_pairs={{0,80},{8,56},{16,96},{24,72},{32,112},{40,88},{48,0},{56,104},{64... | collective-permute-start | bytes 442376 | tf_op jit(solution)/shard_map/ppermute | solution.py:41
  126.5 16.4 %collective-permute-start.38 = (bf16[96,1152]{1,0:T(8,128)(2,1)S(1)}, bf16[96,1152]{1,0:T(8,128)(2,1)S(1)}, u32[]{:S(2)}, u32[]{:S(2)}) collective-permute-start(bf16[96,1152]{1,0:T(8,128)(2,1)S(1)} %peer_rows.1), channel_id=1, source_target_pairs={{0,8},{8,0},{16,24},{24,16},{32,40},{40,32},{48,56},{56,48},{64,72... | collective-permute-start | bytes 663560 | tf_op jit(solution)/shard_map/ppermute | solution.py:25
  126.9 16.8 %collective-permute-start.30 = (bf16[4,128,128]{2,1,0:T(8,128)(2,1)S(1)}, bf16[4,128,128]{2,1,0:T(8,128)(2,1)S(1)}, u32[]{:S(2)}, u32[]{:S(2)}) collective-permute-start(bf16[4,128,128]{2,1,0:T(8,128)(2,1)S(1)} %pad_maximum_fusion.3.t), channel_id=1, source_target_pairs={{0,48},{8,88},{16,64},{24,104},{32,80},{40,120},{48,96},{56,8},{64... | collective-permute-start | bytes 393224 | tf_op jit(solution)/shard_map/ppermute | solution.py:41
  132.7 11.0 %collective-permute-start.27 = (bf16[4,128,128]{2,1,0:T(8,128)(2,1)S(1)}, bf16[4,128,128]{2,1,0:T(8,128)(2,1)S(1)}, u32[]{:S(2)}, u32[]{:S(2)}) collective-permute-start(bf16[4,128,128]{2,1,0:T(8,128)(2,1)S(1)} %get-tuple-element.39), channel_id=1, source_target_pairs={{0,32},{8,104},{16,48},{24,120},{32,64},{40,8},{48,80},{56,24},{64... | collective-permute-start | bytes 393224 | tf_op jit(solution)/shard_map/ppermute | solution.py:41
  135.2 8.6 %collective-permute-start.26 = (bf16[4,128,128]{2,1,0:T(8,128)(2,1)S(1)}, bf16[4,128,128]{2,1,0:T(8,128)(2,1)S(1)}, u32[]{:S(2)}, u32[]{:S(2)}) collective-permute-start(bf16[4,128,128]{2,1,0:T(8,128)(2,1)S(1)} %get-tuple-element.38), channel_id=1, source_target_pairs={{0,16},{8,120},{16,32},{24,8},{32,48},{40,24},{48,64},{56,40},{64,... | collective-permute-start | bytes 393224 | tf_op jit(solution)/shard_map/ppermute | solution.py:41
  135.2 7.7 %collective-permute-start.37 = (bf16[32,1152]{1,0:T(8,128)(2,1)S(1)}, bf16[32,1152]{1,0:T(8,128)(2,1)S(1)}, u32[]{:S(2)}, u32[]{:S(2)}) collective-permute-start(bf16[32,1152]{1,0:T(8,128)(2,1)S(1)} %slice.109), channel_id=1, source_target_pairs={{0,112},{8,24},{16,0},{24,40},{32,16},{40,56},{48,32},{56,72},{64,... | collective-permute-start | bytes 221192 | tf_op jit(solution)/shard_map/ppermute | solution.py:41
  143.6 3.3 %collective-permute-start.39 = (bf16[32,1152]{1,0:T(8,128)(2,1)S(1)}, bf16[32,1152]{1,0:T(8,128)(2,1)S(1)}, u32[]{:S(2)}, u32[]{:S(2)}) collective-permute-start(bf16[32,1152]{1,0:T(8,128)(2,1)S(1)} %sum_z.1), channel_id=1, source_target_pairs={{0,128},{8,136},{16,144},{24,152},{32,160},{40,168},{48,176},{56,1... | collective-permute-start | bytes 221192 | tf_op jit(solution)/shard_map/ppermute | solution.py:25
  143.8 3.2 %collective-permute-start.31 = (f32[2,128,128]{2,1,0:T(8,128)S(1)}, f32[2,128,128]{2,1,0:T(8,128)S(1)}, u32[]{:S(2)}, u32[]{:S(2)}) collective-permute-start(f32[2,128,128]{2,1,0:T(8,128)S(1)} %slice.107), channel_id=1, source_target_pairs={{0,8},{8,0},{16,24},{24,16},{32,40},{40,32},{48,56},{56,48},{64,72... | collective-permute-start | bytes 393224 | tf_op jit(solution)/shard_map/ppermute | solution.py:25
  146.9 1.5 collective-permute-start.40
  (1 other events, 0.7 us)

commit v2 on v1

--- a/solution.py
+++ b/solution.py
@@ -79,22 +79,42 @@
     )(ids, w, og, bias, *ready)
 
 
-def pair_body(a, b, *refs):
+def append_body(a, b, *refs):
     out = refs[-1]
-    out[0:784, :] = a[...]
-    out[784:1568, :] = b[...]
-
-
-def pair_up(a, b, *ready):
-    return pl.pallas_call(
-        pair_body,
-        out_shape=jax.ShapeDtypeStruct((1568, B), bf16),
+    rows = a.shape[0]
+    out[0:rows, :] = a[...]
+    out[rows:, :] = b[0 : out.shape[0] - rows, :]
+
+
+def append(n, a, b, *ready):
+    return pl.pallas_call(
+        append_body,
+        out_shape=jax.ShapeDtypeStruct((n, a.shape[1]), a.dtype),
         in_specs=[VM, VM] + [ANY] * len(ready),
         out_specs=VM,
         compiler_params=params(4),
-        cost_estimate=cost(0, 1 << 19),
-        name="pair_up",
+        cost_estimate=cost(0, 1 << 18),
+        name="append",
     )(a, b, *ready)
+
+
+def settle_body(mine, came, u, d, agg, a, b):
+    agg[...] = (mine[...] + came[...]).astype(bf16)
+    a[...] = u[0:784, :]
+    b[...] = d[784:1568, :]
+
+
+def settle(mine, came, u, d):
+    half = jax.ShapeDtypeStruct((784, B), bf16)
+    return pl.pallas_call(
+        settle_body,
+        out_shape=(jax.ShapeDtypeStruct((2, B, B), bf16), half, half),
+        in_specs=[VM] * 4,
+        out_specs=(VM, VM, VM),
+        compiler_params=params(4),
+        cost_estimate=cost(0, 1 << 18),
+        name="settle",
+    )(mine, came, u, d)
 
 
 def plan_body(ids, c0, d0, c1, d1, out):
@@ -115,7 +135,7 @@
             out[base + n] = i | (slot << 8) | ((dest[i] + 2 * side) << 16)
             return n + held
 
-        n = lax.fori_loop(0, 64, step, 0)
+        n = lax.fori_loop(0, 64, step, 0, unroll=8)
         for u in range(4):
             out[base + n + u] = (32 << 8) | (4 << 16)
         out[side] = (n + 3) >> 2
@@ -145,8 +165,8 @@
 
 
 def agg_body(plan, tiles, more, *refs):
-    pieces, mine, theirs, src, acc, sem = refs[0:10], refs[10], refs[11], refs[12], refs[13], refs[14]
-    both, x0, o4, o1, o2, o3, p4, p1, p2, p3 = pieces
+    mine, theirs, src, acc, sem = refs[8:]
+    both, x0, o14, o2, o3, p14, p2, p3 = refs[0:8]
     copies = []
 
     def put(dx, j, v):
@@ -155,8 +175,8 @@
         copies.append(pltpu.make_async_copy(v, src.at[at : at + n], sem.at[len(copies)]))
         copies[-1].start()
 
-    for dx, (v3, v2, v1, v4, v0) in enumerate(((o3, o2, o1, o4, both.at[0:2]), (p3, p2, p1, p4, x0))):
-        for j, v in ((0, v3), (2, v2), (4, v1), (6, v4), (7, v0)):
+    for dx, (v3, v2, v14, v0) in enumerate(((o3, o2, o14, both.at[0:2]), (p3, p2, p14, x0))):
+        for j, v in ((0, v3), (2, v2), (4, v14), (7, v0)):
             put(dx, j, v)
     acc[...] = jnp.zeros_like(acc)
     src[32] = jnp.zeros((B, B), bf16)
@@ -176,12 +196,12 @@
     return pl.pallas_call(
         agg_body,
         out_shape=(jax.ShapeDtypeStruct((2, B, B), f32), jax.ShapeDtypeStruct((2, B, B), f32)),
-        in_specs=[SM, VM, VM] + [HB] * 10,
+        in_specs=[SM, VM, VM] + [HB] * 8,
         out_specs=(VM, VM),
         scratch_shapes=[
             pltpu.VMEM((33, B, B), bf16),
             pltpu.VMEM((5, B, B), f32),
-            pltpu.SemaphoreType.DMA((10,)),
+            pltpu.SemaphoreType.DMA((8,)),
         ],
         compiler_params=params(12),
         cost_estimate=cost(2 * 64 * B**3, 4 << 20),
@@ -284,7 +304,7 @@
     )(ids, *pieces, w0, w1, og, bias, w_own)
 
 
-def spread_body(plan, tiles, more, prop, peer, send, near, first, rest, acc, both):
+def spread_body(plan, tiles, more, prop, peer, send, near, far, acc, both):
     acc[...] = jnp.zeros_like(acc)
     both[0:2] = prop[...]
     both[2:4] = peer[...]
@@ -297,9 +317,7 @@
 
     each_tile(plan, tiles, more, use)
     near[...] = acc[0:16]
-    first[...] = acc[28:30].astype(bf16)
-    rest[0:12] = acc[16:28].astype(bf16)
-    rest[12:14] = acc[30:32].astype(bf16)
+    far[...] = acc[16:32].astype(bf16)
 
 
 def spread(plan, tiles, more, prop, peer, send):
@@ -307,11 +325,10 @@
         spread_body,
         out_shape=(
             jax.ShapeDtypeStruct((16, B, B), f32),
-            jax.ShapeDtypeStruct((2, B, B), bf16),
-            jax.ShapeDtypeStruct((14, B, B), bf16),
+            jax.ShapeDtypeStruct((16, B, B), bf16),
         ),
         in_specs=[SM] + [VM] * 4 + [ANY],
-        out_specs=(VM, VM, VM),
+        out_specs=(VM, VM),
         scratch_shapes=[pltpu.VMEM((33, B, B), f32), pltpu.VMEM((5, B, B), bf16)],
         compiler_params=params(12),
         cost_estimate=cost(2 * 64 * B**3, 6 << 20),
@@ -319,6 +336,63 @@
     )(plan, tiles, more, prop, peer, send)
 
 
+def quarter_body(keep, got, came, far, out):
+    out[...] = (keep[0:32, :] + got[0:32, :] + came[...].astype(f32)).astype(bf16)
+
+
+def quarter_up(keep, got, came, far):
+    return pl.pallas_call(
+        quarter_body,
+        out_shape=jax.ShapeDtypeStruct((32, 1152), bf16),
+        in_specs=[VM] * 3 + [ANY],
+        out_specs=VM,
+        compiler_params=params(4),
+        cost_estimate=cost(0, 1 << 18),
+        name="quarter_up",
+    )(keep, got, came, far)
+
+
+def join_body(near, came, ready, t14, t2, t3, t0):
+    t3[...] = near[0:4] + came[0:4].astype(f32)
+    t2[...] = (near[4:8] + came[4:8].astype(f32)).astype(bf16)
+    t14[...] = (near[8:14] + came[8:14].astype(f32)).astype(bf16)
+    t0[...] = near[14:16] + came[14:16].astype(f32)
+
+
+def join(near, came, ready):
+    return pl.pallas_call(
+        join_body,
+        out_shape=(
+            jax.ShapeDtypeStruct((6, B, B), bf16),
+            jax.ShapeDtypeStruct((4, B, B), bf16),
+            jax.ShapeDtypeStruct((4, B, B), f32),
+            jax.ShapeDtypeStruct((2, B, B), f32),
+        ),
+        in_specs=[VM, VM, ANY],
+        out_specs=(VM, VM, VM, VM),
+        compiler_params=params(8),
+        cost_estimate=cost(0, 2 << 20),
+        name="join",
+    )(near, came, ready)
+
+
+def ride_body(t3, r14, ready, out):
+    out[0:2] = (t3[0:2] + r14[4:6].astype(f32)).astype(bf16)
+    out[2:4] = t3[2:4].astype(bf16)
+
+
+def ride(t3, r14, ready):
+    return pl.pallas_call(
+        ride_body,
+        out_shape=jax.ShapeDtypeStruct((4, B, B), bf16),
+        in_specs=[VM, VM, ANY],
+        out_specs=VM,
+        compiler_params=params(4),
+        cost_estimate=cost(0, 1 << 18),
+        name="ride",
+    )(t3, r14, ready)
+
+
 def rows_body(d1, d2, d3, t, out):
     for n, d in enumerate((d1, d2, d3)):
         out[32 * n : 32 * n + 32, :] = d[32:64, :]
@@ -336,10 +410,10 @@
     )(d1, d2, d3, t)
 
 
-def sum_body(scale, ids, own, d1, d2, d3, d4, e, t, out, buf):
+def sum_body(scale, ids, own, d1, d2, d3, e, t, out, buf):
     core, z = ids[0] & 1, (ids[0] >> 1) & 7
     buf[0] = own[...]
-    buf[4] = d4[...]
+    buf[4] = d1[64:96, :]
     for k, d in ((1, d1), (2, d2), (3, d3)):
         mine = jnp.where(core == 0, k, NZ - k)
         buf[mine] = d[0:32, :]
@@ -354,7 +428,7 @@
     return pl.pallas_call(
         functools.partial(sum_body, scale),
         out_shape=jax.ShapeDtypeStruct((32, 1152), bf16),
-        in_specs=[SM] + [VM] * 6 + [ANY],
+        in_specs=[SM] + [VM] * 5 + [ANY],
         out_specs=VM,
         scratch_shapes=[pltpu.VMEM((NZ, 32, 1152), bf16)],
         compiler_params=params(8),
@@ -394,21 +468,19 @@
     lists = row_send(jnp.stack([col_blocks, dest_blocks]), dc=1)
     swap, both_a = tie(adj_tiles, both)
     more = row_send(swap, dc=1)
-    o3 = spin_send(both, 3, -1)
-    o2 = spin_send(both, 2, -1)
-    o1 = spin_send(both, 1, -1)
-    o4 = spin_send(o3[:256], 1, -1)
-    p3, p2 = row_send(o3, dx=1), row_send(o2, dx=1)
-    p1, p4 = row_send(o1, dx=1), row_send(o4, dx=1)
+    o3, o2 = spin_send(both, 3, -1), spin_send(both, 2, -1)
     plan = plan_tiles(ids, col_blocks, dest_blocks, lists[0], lists[1])
-
-    pack = pack_up(ids, weight, out_grad, bias_vector[None, :], o1, o2, o3)
-    pair = pair_up(pack, feat_send(pack, dx=1), p1, p2, p3, p4, plan)
+    o14 = spin_send(append(768, both, o3, o2, x0, plan), 1, -1)
+    p3, p2, p14 = row_send(o3, dx=1), row_send(o2, dx=1), row_send(o14, dx=1)
+
+    pack = pack_up(ids, weight, out_grad, bias_vector[None, :], plan)
+    pair = append(1568, pack, feat_send(pack, dx=1), o14)
     wu, wd = feat_send(pair, dy=1), feat_send(pair, dy=-1)
-    wa, wb = feat_send(wu[:784], dy=1), feat_send(wd[784:], dy=-1)
-
-    mine, theirs = aggregate(plan, adj_tiles, more, (both_a, x0, o4, o1, o2, o3, p4, p1, p2, p3))
-    aggregated = (mine + row_send(theirs, dc=1)).astype(bf16).reshape(256, B)
+
+    mine, theirs = aggregate(plan, adj_tiles, more, (both_a, x0, o14, o2, o3, p14, p2, p3))
+    aggregated, wa, wb = settle(mine, row_send(theirs, dc=1), wu, wd)
+    aggregated = aggregated.reshape(256, B)
+    wa, wb = feat_send(wa, dy=1), feat_send(wb, dy=-1)
 
     q = jnp.concatenate([aggregated, feat_send(aggregated, dx=1)], axis=0)
     w0, og, bias = lay_out(ids, (pair, wu, wd, wa, wb))
@@ -420,29 +492,26 @@
     got = row_send(give, dc=1)
     send = (keep[32:] + got[32:]).astype(bf16)
     got_x = row_send(send, dx=1)
-    near, first, rest = spread(plan, adj_tiles, more, prop, peer, send)
-    came, came_rest = row_send(first, dx=1), row_send(rest, dx=1)
-    quarter = (keep[:32] + got[:32] + got_x.astype(f32)).astype(bf16)
-
-    r4 = spin_send((near[12:14] + came.astype(f32)).astype(bf16), 1)
+    near, far = spread(plan, adj_tiles, more, prop, peer, send)
+    came = row_send(far, dx=1)
+    quarter = quarter_up(keep, got, got_x, far)
     halves = jnp.concatenate([quarter, row_send(quarter, dc=1)], axis=0)
-    d3, d2, d1 = (spin_send(halves, k, -1) for k in (3, 2, 1))
-    d4 = spin_send(d3[:32], 1, -1)
-
-    t = near[:12] + came_rest[:12].astype(f32)
-    t0 = near[14:] + came_rest[12:].astype(f32)
-    low = t[4:12].astype(bf16)
-    r2, r1 = spin_send(low[:4], 2), spin_send(low[4:], 1)
-    t3 = jnp.concatenate([t[:2] + r4.astype(f32), t[2:4]], axis=0).astype(bf16)
+    d3, d2 = spin_send(halves, 3, -1), spin_send(halves, 2, -1)
+    last = append(96, halves, d3, d2)
+    d1 = spin_send(last, 1, -1)
+
+    t14, t2, t3, t0 = join(near, came, last)
+    r14, r2 = spin_send(t14, 1), spin_send(t2, 2)
+    t3 = ride(t3, r14, r2)
     r3 = spin_send(t3, 3)
 
-    e = row_send(peer_rows(d1, d2, d3, low), dc=1)
+    e = row_send(peer_rows(d1, d2, d3, t2), dc=1)
     scale = float(256 * lax.axis_size("row")) ** (-0.5)
-    total = sum_z(scale, ids, quarter, d1, d2, d3, d4, e, t3)
+    total = sum_z(scale, ids, quarter, d1, d2, d3, e, t3)
     two = jnp.concatenate([total, row_send(total, dx=1)], axis=0)
     weight_grad, bias_grad = weight_out(ids, two, row_send(two, dc=1))
 
-    r = r1.astype(f32) + r2.astype(f32) + r3.astype(f32)
+    r = r14[:4].astype(f32) + r2.astype(f32) + r3.astype(f32)
     out = t0 + r[:2] + row_send(r[2:], dc=1)
     return hidden, out.reshape(256, B), weight_grad, bias_grad[0]
 

time: 150 us -> 132 us (0.88)
  starting transfers between devices: 67.2 us -> 54.7 us
  waiting for transfers between devices: 56.1 us -> 48.7 us
  Pallas kernels: 19.1 us -> 20.6 us
    ppermute x12 -> x9, starting transfers between devices: 29.5 us -> 16.1 us  [spin_send(): return lax.ppermute(v, 'row', perm)]
    ppermute x20 -> x18, waiting for transfers between devices: 21.8 us -> 11 us  [row_send(): return lax.ppermute(v, 'row', perm)]
    ppermute x12 -> x9, waiting for transfers between devices: 15.9 us -> 20.3 us  [spin_send(): return lax.ppermute(v, 'row', perm)]
    ppermute x20 -> x18, starting transfers between devices: 23.7 us -> 24 us  [row_send(): return lax.ppermute(v, 'row', perm)]
    unnamed x17 -> x15, local copies, waits for them, and re-layouts: 4.61 us -> 4.6 us
  transfers between devices with their start and end apart: 41 -> 36, of which waited for: 19 -> 15; matrix products, arithmetic and copies ran while one was open for 2% -> 2% of each run, Pallas kernels for 10% -> 12%
where the time goes in v2:
time: 132 us
  starting transfers between devices  54.7 us (41%)
  waiting for transfers between devices  48.7 us (37%)
  Pallas kernels  20.6 us (16%)
  local copies, waits for them, and re-layouts  5.14 us (4%)
  other arithmetic  1.54 us (1%)
    ppermute x18, starting transfers between devices, row_send(): return lax.ppermute(v, 'row', perm)  24 us
    ppermute x9, waiting for transfers between devices, spin_send(): return lax.ppermute(v, 'row', perm)  20.3 us
    ppermute x9, waiting for transfers between devices, feat_send(): lax.ppermute(v, 'feat', [(i, (i >> 2 ^ dx) << 2 | i + dy & 3) for i in ra...  17.4 us
    ppermute x9, starting transfers between devices, spin_send(): return lax.ppermute(v, 'row', perm)  16.1 us
    ppermute x9, starting transfers between devices, feat_send(): lax.ppermute(v, 'feat', [(i, (i >> 2 ^ dx) << 2 | i + dy & 3) for i in ra...  14.6 us
    ppermute x18, waiting for transfers between devices, row_send(): return lax.ppermute(v, 'row', perm)  11 us
    pallas_call x1, Pallas kernels, aggregate(): pl.pallas_call(agg_body, out_shape=(jax.ShapeDtypeStruct((2, B, B), f32),...  5.86 us
    pallas_call x1, Pallas kernels, spread(): pl.pallas_call(spread_body, out_shape=(jax.ShapeDtypeStruct((16, B, B), f...  5.24 us
  transfers between devices with their start and end apart: 36, of which 15 were waited for; matrix products, arithmetic and copies ran while one was open for 2% of the time, Pallas kernels for 12%

profile of v2, /device:TPU:1, one launch (start us, length us, event | category | flops | bytes accessed | tf_op | source)
XLA Modules:
  0.0 131.5 jit_solution(5917815514583384743)
XLA Ops:
  0.6 3.3 %collective-permute-start.1 = (bf16[256,128]{1,0:T(8,128)(2,1)}, bf16[256,128]{1,0:T(8,128)(2,1)S(1)}, u32[]{:S(2)}, u32[]{:S(2)}) collective-permute-start(bf16[256,128]{1,0:T(8,128)(2,1)} %param.7), channel_id=1, source_target_pairs={{0,8},{8,0},{16,24},{24,16},{32,40},{40,32},{48,56},{56,48},{64,72... | collective-permute-start | bytes 196616 | tf_op jit(solution)/shard_map/ppermute | solution.py:25
  4.0 0.8 constant_dynamic-update-slice_fusion.1
  6.5 2.7 %collective-permute-start.5 = (bf16[512,128]{1,0:T(8,128)(2,1)S(1)}, bf16[512,128]{1,0:T(8,128)(2,1)S(1)}, u32[]{:S(2)}, u32[]{:S(2)}) collective-permute-start(bf16[512,128]{1,0:T(8,128)(2,1)S(1)} %constant_dynamic-update-slice_fusion.a), channel_id=1, source_target_pairs={{0,96},{8,40},{16,112},{24,56},{32,0},{40,72},{48,16},{56,88},{64,... | collective-permute-start | bytes 393224 | tf_op jit(solution)/shard_map/ppermute | solution.py:41
  9.2 4.7 %collective-permute-start.4 = (bf16[512,128]{1,0:T(8,128)(2,1)S(1)}, bf16[512,128]{1,0:T(8,128)(2,1)S(1)}, u32[]{:S(2)}, u32[]{:S(2)}) collective-permute-start(bf16[512,128]{1,0:T(8,128)(2,1)S(1)} %constant_dynamic-update-slice_fusion.a), channel_id=1, source_target_pairs={{0,80},{8,56},{16,96},{24,72},{32,112},{40,88},{48,0},{56,104},{64... | collective-permute-start | bytes 393224 | tf_op jit(solution)/shard_map/ppermute | solution.py:41
  15.2 2.7 %plan_tiles.1.refs_2_.plan.refs_0_ = s32[160]{0:T(256)S(1)} custom-call(s32[2]{0:T(128)S(1)} %pad_add_fusion.1.ids, s32[64]{0:T(128)S(1)} %copy-done.4, s32[64]{0:T(128)S(1)} %copy-done.5, s32[64]{0:T(128)S(1)} %get-tuple-element.49.c1, s32[64]{0:T(128)S(1)} %get-tuple-element.48.d1), custom_call_target="tpu_custom_call" | custom-call | flops 10000 | bytes 4096 | tf_op jit(solution)/shard_map/plan_tiles/pallas_call | solution.py:145
  17.9 0.9 copy-done.1
  18.9 0.8 copy-done.3
  20.4 0.7 pack_up.1.a
  21.1 2.5 %collective-permute-start.11 = (bf16[784,128]{1,0:T(8,128)(2,1)S(1)}, bf16[784,128]{1,0:T(8,128)(2,1)S(1)}, u32[]{:S(2)}, u32[]{:S(2)}) collective-permute-start(bf16[784,128]{1,0:T(8,128)(2,1)S(1)} %pack_up.1.a), channel_id=1, source_target_pairs={{0,4},{1,5},{2,6},{3,7},{4,0},{5,1},{6,2},{7,3},{8,12},{9,13},{10,... | collective-permute-start | bytes 602120 | tf_op jit(solution)/shard_map/ppermute | solution.py:29
  23.7 0.8 collective-permute-start.6
  24.5 5.0 %collective-permute-done.11.b = bf16[784,128]{1,0:T(8,128)(2,1)S(1)} collective-permute-done((bf16[784,128]{1,0:T(8,128)(2,1)S(1)}, bf16[784,128]{1,0:T(8,128)(2,1)S(1)}, u32[]{:S(2)}, u32[]{:S(2)}) %collective-permute-start.11) | collective-permute-done | bytes 200736 | tf_op jit(solution)/shard_map/ppermute | solution.py:29
  29.8 2.8 %collective-permute-start.13 = (bf16[1568,128]{1,0:T(8,128)(2,1)S(1)}, bf16[1568,128]{1,0:T(8,128)(2,1)S(1)}, u32[]{:S(2)}, u32[]{:S(2)}) collective-permute-start(bf16[1568,128]{1,0:T(8,128)(2,1)S(1)} %append.4.refs_0_), channel_id=1, source_target_pairs={{0,3},{1,0},{2,1},{3,2},{4,7},{5,4},{6,5},{7,6},{8,11},{9,8},{10,9... | collective-permute-start | bytes 1204232 | tf_op jit(solution)/shard_map/ppermute | solution.py:29
  32.6 1.5 %collective-permute-start.9 = (bf16[512,128]{1,0:T(8,128)(2,1)S(1)}, bf16[512,128]{1,0:T(8,128)(2,1)S(1)}, u32[]{:S(2)}, u32[]{:S(2)}) collective-permute-start(bf16[512,128]{1,0:T(8,128)(2,1)S(1)} %collective-permute-done.4.b), channel_id=1, source_target_pairs={{0,128},{8,136},{16,144},{24,152},{32,160},{40,168},{48,176},{56,1... | collective-permute-start | bytes 393224 | tf_op jit(solution)/shard_map/ppermute | solution.py:25
  34.1 7.0 %collective-permute-done.9 = bf16[512,128]{1,0:T(8,128)(2,1)S(1)} collective-permute-done((bf16[512,128]{1,0:T(8,128)(2,1)S(1)}, bf16[512,128]{1,0:T(8,128)(2,1)S(1)}, u32[]{:S(2)}, u32[]{:S(2)}) %collective-permute-start.9) | collective-permute-done | bytes 131104 | tf_op jit(solution)/shard_map/ppermute | solution.py:25
  41.1 5.9 %aggregate.1 = (f32[2,128,128]{2,1,0:T(8,128)S(1)}, f32[2,128,128]{2,1,0:T(8,128)S(1)}) custom-call(s32[160]{0:T(256)S(1)} %plan_tiles.1.refs_2_.plan.refs_0_, bf16[64,128,128]{2,1,0:T(8,128)(2,1)S(1)} %copy-done, bf16[64,128,128]{2,1,0:T(8,128)(2,1)} %collective-permute-done.2.more, bf16[4,128,128]{2,1,0:T(8,128)(2,1)S(1)} %bitcast.22, ...), custom_call_target="tpu_custom_call" | custom-call | flops 268435456 | bytes 4194304 | tf_op jit(solution)/shard_map/aggregate/pallas_call | solution.py:196
  47.0 2.5 %collective-permute-start.10 = (f32[2,128,128]{2,1,0:T(8,128)S(1)}, f32[2,128,128]{2,1,0:T(8,128)S(1)}, u32[]{:S(2)}, u32[]{:S(2)}) collective-permute-start(f32[2,128,128]{2,1,0:T(8,128)S(1)} %get-tuple-element.29), channel_id=1, source_target_pairs={{0,8},{8,0},{16,24},{24,16},{32,40},{40,32},{48,56},{56,48},{64,72... | collective-permute-start | bytes 393224 | tf_op jit(solution)/shard_map/ppermute | solution.py:25
  49.5 1.0 collective-permute-done.10.came
  50.6 2.7 %collective-permute-start.19 = (bf16[784,128]{1,0:T(8,128)(2,1)S(1)}, bf16[784,128]{1,0:T(8,128)(2,1)S(1)}, u32[]{:S(2)}, u32[]{:S(2)}) collective-permute-start(bf16[784,128]{1,0:T(8,128)(2,1)S(1)} %get-tuple-element.32), channel_id=1, source_target_pairs={{0,3},{1,0},{2,1},{3,2},{4,7},{5,4},{6,5},{7,6},{8,11},{9,8},{10,9... | collective-permute-start | bytes 602120 | tf_op jit(solution)/shard_map/ppermute | solution.py:29
  53.3 4.7 %collective-permute-done.18.refs_3_ = bf16[784,128]{1,0:T(8,128)(2,1)S(1)} collective-permute-done((bf16[784,128]{1,0:T(8,128)(2,1)S(1)}, bf16[784,128]{1,0:T(8,128)(2,1)S(1)}, u32[]{:S(2)}, u32[]{:S(2)}) %collective-permute-start.18) | collective-permute-done | bytes 200736 | tf_op jit(solution)/shard_map/ppermute | solution.py:29
  58.0 1.4 %lay_out.1 = (bf16[1024,512]{1,0:T(8,128)(2,1)S(1)}, bf16[256,1024]{1,0:T(8,128)(2,1)S(1)}, f32[8,1024]{1,0:T(8,128)S(1)}) custom-call(s32[2]{0:T(128)S(1)} %pad_add_fusion.1.ids, bf16[1568,128]{1,0:T(8,128)(2,1)S(1)} %append.4.refs_0_, bf16[1568,128]{1,0:T(8,128)(2,1)S(1)} %collective-permute-done.12.u.refs_1_, ...), custom_call_target="tpu_custom_call" | custom-call | bytes 3145728 | tf_op jit(solution)/shard_map/lay_out/pallas_call | solution.py:239
  59.4 1.5 %collective-permute-start.20 = (bf16[1024,512]{1,0:T(8,128)(2,1)S(1)}, bf16[1024,512]{1,0:T(8,128)(2,1)S(1)}, u32[]{:S(2)}, u32[]{:S(2)}) collective-permute-start(bf16[1024,512]{1,0:T(8,128)(2,1)S(1)} %get-tuple-element.33.w0), channel_id=1, source_target_pairs={{0,8},{8,0},{16,24},{24,16},{32,40},{40,32},{48,56},{56,48},{64,72... | collective-permute-start | bytes 3145736 | tf_op jit(solution)/shard_map/ppermute | solution.py:25
  60.9 2.2 %collective-permute-start.14 = (bf16[256,128]{1,0:T(8,128)(2,1)S(1)}, bf16[256,128]{1,0:T(8,128)(2,1)S(1)}, u32[]{:S(2)}, u32[]{:S(2)}) collective-permute-start(bf16[256,128]{1,0:T(8,128)(2,1)S(1)} %bitcast.32), channel_id=1, source_target_pairs={{0,4},{1,5},{2,6},{3,7},{4,0},{5,1},{6,2},{7,3},{8,12},{9,13},{10,... | collective-permute-start | bytes 196616 | tf_op jit(solution)/shard_map/ppermute | solution.py:29
  63.1 2.9 %collective-permute-done.14 = bf16[256,128]{1,0:T(8,128)(2,1)S(1)} collective-permute-done((bf16[256,128]{1,0:T(8,128)(2,1)S(1)}, bf16[256,128]{1,0:T(8,128)(2,1)S(1)}, u32[]{:S(2)}, u32[]{:S(2)}) %collective-permute-start.14) | collective-permute-done | bytes 65568 | tf_op jit(solution)/shard_map/ppermute | solution.py:29
  66.1 2.7 %collective-permute-start.17 = (bf16[512,128]{1,0:T(8,128)(2,1)S(1)}, bf16[512,128]{1,0:T(8,128)(2,1)S(1)}, u32[]{:S(2)}, u32[]{:S(2)}) collective-permute-start(bf16[512,128]{1,0:T(8,128)(2,1)S(1)} %pad_maximum_fusion.2.p0), channel_id=1, source_target_pairs={{0,2},{1,3},{2,0},{3,1},{4,6},{5,7},{6,4},{7,5},{8,10},{9,11},{10,... | collective-permute-start | bytes 393224 | tf_op jit(solution)/shard_map/ppermute | solution.py:29
  69.4 0.9 collective-permute-start.15
  70.3 1.5 %collective-permute-done.17.p3 = bf16[512,128]{1,0:T(8,128)(2,1)S(1)} collective-permute-done((bf16[512,128]{1,0:T(8,128)(2,1)S(1)}, bf16[512,128]{1,0:T(8,128)(2,1)S(1)}, u32[]{:S(2)}, u32[]{:S(2)}) %collective-permute-start.17) | collective-permute-done | bytes 131104 | tf_op jit(solution)/shard_map/ppermute | solution.py:29
  71.8 3.2 %collective-permute-done.16.p2 = bf16[512,128]{1,0:T(8,128)(2,1)S(1)} collective-permute-done((bf16[512,128]{1,0:T(8,128)(2,1)S(1)}, bf16[512,128]{1,0:T(8,128)(2,1)S(1)}, u32[]{:S(2)}, u32[]{:S(2)}) %collective-permute-start.16) | collective-permute-done | bytes 131104 | tf_op jit(solution)/shard_map/ppermute | solution.py:29
  75.0 2.2 %middle.1 = (f32[256,128]{1,0:T(8,128)}, bf16[256,128]{1,0:T(8,128)(2,1)S(1)}, f32[64,1152]{1,0:T(8,128)S(1)}, f32[64,1152]{1,0:T(8,128)S(1)}) custom-call(s32[2]{0:T(128)S(1)} %pad_add_fusion.1.ids, bf16[512,128]{1,0:T(8,128)(2,1)S(1)} %pad_maximum_fusion.2.p0, bf16[512,128]{1,0:T(8,128)(2,1)S(1)} %collective-permute-done.15.p1, ...), custom_call_target="tpu_custom_call" | custom-call | flops 671088640 | bytes 5242880 | tf_op jit(solution)/shard_map/middle/pallas_call | solution.py:285
  77.2 2.0 %collective-permute-start.22 = (f32[64,1152]{1,0:T(8,128)S(1)}, f32[64,1152]{1,0:T(8,128)S(1)}, u32[]{:S(2)}, u32[]{:S(2)}) collective-permute-start(f32[64,1152]{1,0:T(8,128)S(1)} %get-tuple-element.39), channel_id=1, source_target_pairs={{0,8},{8,0},{16,24},{24,16},{32,40},{40,32},{48,56},{56,48},{64,72... | collective-permute-start | bytes 884744 | tf_op jit(solution)/shard_map/ppermute | solution.py:25
  79.2 1.2 collective-permute-done.22.got
  80.6 5.2 %spread.1 = (f32[16,128,128]{2,1,0:T(8,128)S(1)}, bf16[16,128,128]{2,1,0:T(8,128)(2,1)S(1)}) custom-call(s32[160]{0:T(256)S(1)} %plan_tiles.1.refs_2_.plan.refs_0_, bf16[64,128,128]{2,1,0:T(8,128)(2,1)S(1)} %copy-done, bf16[64,128,128]{2,1,0:T(8,128)(2,1)} %collective-permute-done.2.more, bf16[2,128,128]{2,1,0:T(8,128)(2,1)S(1)} %bitcast.31, ...), custom_call_target="tpu_custom_call" | custom-call | flops 268435456 | bytes 6291456 | tf_op jit(solution)/shard_map/spread/pallas_call | solution.py:324
  85.9 1.4 %collective-permute-start.25 = (bf16[32,1152]{1,0:T(8,128)(2,1)S(1)}, bf16[32,1152]{1,0:T(8,128)(2,1)S(1)}, u32[]{:S(2)}, u32[]{:S(2)}) collective-permute-start(bf16[32,1152]{1,0:T(8,128)(2,1)S(1)} %quarter_up.1.own), channel_id=1, source_target_pairs={{0,8},{8,0},{16,24},{24,16},{32,40},{40,32},{48,56},{56,48},{64,72... | collective-permute-start | bytes 221192 | tf_op jit(solution)/shard_map/ppermute | solution.py:25
  87.2 1.3 collective-permute-start.23
  88.6 0.7 collective-permute-start.26
  89.3 9.4 %collective-permute-done.27.refs_0_.d2 = bf16[64,1152]{1,0:T(8,128)(2,1)S(1)} collective-permute-done((bf16[64,1152]{1,0:T(8,128)(2,1)S(1)}, bf16[64,1152]{1,0:T(8,128)(2,1)S(1)}, u32[]{:S(2)}, u32[]{:S(2)}) %collective-permute-start.27) | collective-permute-done | bytes 147488 | tf_op jit(solution)/shard_map/ppermute | solution.py:41
  98.8 2.8 %collective-permute-start.32 = (bf16[96,1152]{1,0:T(8,128)(2,1)S(1)}, bf16[96,1152]{1,0:T(8,128)(2,1)S(1)}, u32[]{:S(2)}, u32[]{:S(2)}) collective-permute-start(bf16[96,1152]{1,0:T(8,128)(2,1)S(1)} %append.5.ready), channel_id=1, source_target_pairs={{0,112},{8,24},{16,0},{24,40},{32,16},{40,56},{48,32},{56,72},{64,... | collective-permute-start | bytes 663560 | tf_op jit(solution)/shard_map/ppermute | solution.py:41
  101.7 3.1 %collective-permute-done.32.d1 = bf16[96,1152]{1,0:T(8,128)(2,1)S(1)} collective-permute-done((bf16[96,1152]{1,0:T(8,128)(2,1)S(1)}, bf16[96,1152]{1,0:T(8,128)(2,1)S(1)}, u32[]{:S(2)}, u32[]{:S(2)}) %collective-permute-start.32) | collective-permute-done | bytes 221216 | tf_op jit(solution)/shard_map/ppermute | solution.py:41
  104.8 2.1 %collective-permute-start.33 = (bf16[96,1152]{1,0:T(8,128)(2,1)S(1)}, bf16[96,1152]{1,0:T(8,128)(2,1)S(1)}, u32[]{:S(2)}, u32[]{:S(2)}) collective-permute-start(bf16[96,1152]{1,0:T(8,128)(2,1)S(1)} %peer_rows.1), channel_id=1, source_target_pairs={{0,8},{8,0},{16,24},{24,16},{32,40},{40,32},{48,56},{56,48},{64,72... | collective-permute-start | bytes 663560 | tf_op jit(solution)/shard_map/ppermute | solution.py:25
  106.9 3.4 %collective-permute-start.28 = (bf16[6,128,128]{2,1,0:T(8,128)(2,1)S(1)}, bf16[6,128,128]{2,1,0:T(8,128)(2,1)S(1)}, u32[]{:S(2)}, u32[]{:S(2)}) collective-permute-start(bf16[6,128,128]{2,1,0:T(8,128)(2,1)S(1)} %get-tuple-element.43), channel_id=1, source_target_pairs={{0,16},{8,120},{16,32},{24,8},{32,48},{40,24},{48,64},{56,40},{64,... | collective-permute-start | bytes 589832 | tf_op jit(solution)/shard_map/ppermute | solution.py:41
  110.3 6.1 %collective-permute-done.29.ready = bf16[4,128,128]{2,1,0:T(8,128)(2,1)S(1)} collective-permute-done((bf16[4,128,128]{2,1,0:T(8,128)(2,1)S(1)}, bf16[4,128,128]{2,1,0:T(8,128)(2,1)S(1)}, u32[]{:S(2)}, u32[]{:S(2)}) %collective-permute-start.29) | collective-permute-done | bytes 131104 | tf_op jit(solution)/shard_map/ppermute | solution.py:41
  116.5 0.7 sum_z.1
  117.2 0.9 collective-permute-start.34
  118.1 0.8 collective-permute-start.30
  118.9 1.6 %collective-permute-done.34 = bf16[32,1152]{1,0:T(8,128)(2,1)S(1)} collective-permute-done((bf16[32,1152]{1,0:T(8,128)(2,1)S(1)}, bf16[32,1152]{1,0:T(8,128)(2,1)S(1)}, u32[]{:S(2)}, u32[]{:S(2)}) %collective-permute-start.34) | collective-permute-done | bytes 73760 | tf_op jit(solution)/shard_map/ppermute | solution.py:25
  120.5 3.4 %collective-permute-start.35 = (bf16[64,1152]{1,0:T(8,128)(2,1)S(1)}, bf16[64,1152]{1,0:T(8,128)(2,1)S(1)}, u32[]{:S(2)}, u32[]{:S(2)}) collective-permute-start(bf16[64,1152]{1,0:T(8,128)(2,1)S(1)} %pad_maximum_fusion.1.mine), channel_id=1, source_target_pairs={{0,8},{8,0},{16,24},{24,16},{32,40},{40,32},{48,56},{56,48},{64,72... | collective-permute-start | bytes 442376 | tf_op jit(solution)/shard_map/ppermute | solution.py:25
  123.9 1.4 %collective-permute-done.30 = bf16[4,128,128]{2,1,0:T(8,128)(2,1)S(1)} collective-permute-done((bf16[4,128,128]{2,1,0:T(8,128)(2,1)S(1)}, bf16[4,128,128]{2,1,0:T(8,128)(2,1)S(1)}, u32[]{:S(2)}, u32[]{:S(2)}) %collective-permute-start.30) | collective-permute-done | bytes 131104 | tf_op jit(solution)/shard_map/ppermute | solution.py:41
  125.4 3.5 %collective-permute-start.31 = (f32[2,128,128]{2,1,0:T(8,128)S(1)}, f32[2,128,128]{2,1,0:T(8,128)S(1)}, u32[]{:S(2)}, u32[]{:S(2)}) collective-permute-start(f32[2,128,128]{2,1,0:T(8,128)S(1)} %slice.35), channel_id=1, source_target_pairs={{0,8},{8,0},{16,24},{24,16},{32,40},{40,32},{48,56},{56,48},{64,72... | collective-permute-start | bytes 393224 | tf_op jit(solution)/shard_map/ppermute | solution.py:25
  128.9 1.4 %weight_out.1 = (f32[128,1024]{1,0:T(8,128)}, f32[8,128]{1,0:T(8,128)S(1)}) custom-call(s32[2]{0:T(128)S(1)} %pad_add_fusion.1.ids, bf16[64,1152]{1,0:T(8,128)(2,1)S(1)} %pad_maximum_fusion.1.mine, bf16[64,1152]{1,0:T(8,128)(2,1)S(1)} %collective-permute-done.35.theirs), custom_call_target="tpu_custom_call" | custom-call | bytes 1048576 | tf_op jit(solution)/shard_map/weight_out/pallas_call | solution.py:451
  (67 shorter events, 6.4 us)
Async XLA Ops:
  0.6 40.5 %copy-start = (bf16[64,128,128]{2,1,0:T(8,128)(2,1)S(1)}, bf16[64,128,128]{2,1,0:T(8,128)(2,1)}, u32[]{:S(2)}) copy-start(bf16[64,128,128]{2,1,0:T(8,128)(2,1)} %tiles.3) | copy-start | bytes 6291460
  0.6 4.4 %collective-permute-start.1 = (bf16[256,128]{1,0:T(8,128)(2,1)}, bf16[256,128]{1,0:T(8,128)(2,1)S(1)}, u32[]{:S(2)}, u32[]{:S(2)}) collective-permute-start(bf16[256,128]{1,0:T(8,128)(2,1)} %param.7), channel_id=1, source_target_pairs={{0,8},{8,0},{16,24},{24,16},{32,40},{40,32},{48,56},{56,48},{64,72... | collective-permute-start | bytes 196616 | tf_op jit(solution)/shard_map/ppermute | solution.py:25
  5.1 36.0 %collective-permute-start.2 = (bf16[64,128,128]{2,1,0:T(8,128)(2,1)}, bf16[64,128,128]{2,1,0:T(8,128)(2,1)}, u32[]{:S(2)}, u32[]{:S(2)}) collective-permute-start(bf16[64,128,128]{2,1,0:T(8,128)(2,1)} %tiles.3), channel_id=1, source_target_pairs={{0,8},{8,0},{16,24},{24,16},{32,40},{40,32},{48,56},{56,48},{64,72... | collective-permute-start | bytes 6291464 | tf_op jit(solution)/shard_map/ppermute | solution.py:25
  5.5 18.1 %collective-permute-start.3 = (bf16[256,128]{1,0:T(8,128)(2,1)}, bf16[256,128]{1,0:T(8,128)(2,1)S(1)}, u32[]{:S(2)}, u32[]{:S(2)}) collective-permute-start(bf16[256,128]{1,0:T(8,128)(2,1)} %param.7), channel_id=1, source_target_pairs={{0,128},{8,136},{16,144},{24,152},{32,160},{40,168},{48,176},{56,1... | collective-permute-start | bytes 196616 | tf_op jit(solution)/shard_map/ppermute | solution.py:25
  6.2 7.6 %collective-permute-start = (s32[2,64]{1,0:T(2,128)S(1)}, s32[2,64]{1,0:T(2,128)S(1)}, u32[]{:S(2)}, u32[]{:S(2)}) collective-permute-start(s32[2,64]{1,0:T(2,128)S(1)} %pad_add_fusion), channel_id=1, source_target_pairs={{0,8},{8,0},{16,24},{24,16},{32,40},{40,32},{48,56},{56,48},{64,72... | collective-permute-start | bytes 1544 | tf_op jit(solution)/shard_map/ppermute | solution.py:25
  6.5 17.2 %collective-permute-start.5 = (bf16[512,128]{1,0:T(8,128)(2,1)S(1)}, bf16[512,128]{1,0:T(8,128)(2,1)S(1)}, u32[]{:S(2)}, u32[]{:S(2)}) collective-permute-start(bf16[512,128]{1,0:T(8,128)(2,1)S(1)} %constant_dynamic-update-slice_fusion.a), channel_id=1, source_target_pairs={{0,96},{8,40},{16,112},{24,56},{32,0},{40,72},{48,16},{56,88},{64,... | collective-permute-start | bytes 393224 | tf_op jit(solution)/shard_map/ppermute | solution.py:41
  9.2 14.5 %collective-permute-start.4 = (bf16[512,128]{1,0:T(8,128)(2,1)S(1)}, bf16[512,128]{1,0:T(8,128)(2,1)S(1)}, u32[]{:S(2)}, u32[]{:S(2)}) collective-permute-start(bf16[512,128]{1,0:T(8,128)(2,1)S(1)} %constant_dynamic-update-slice_fusion.a), channel_id=1, source_target_pairs={{0,80},{8,56},{16,96},{24,72},{32,112},{40,88},{48,0},{56,104},{64... | collective-permute-start | bytes 393224 | tf_op jit(solution)/shard_map/ppermute | solution.py:41
  13.9 0.7 copy-start.4
  14.5 0.7 copy-start.5
  17.9 1.0 copy-start.1
  18.9 0.8 copy-start.3
  19.7 0.7 copy-start.6
  21.1 8.4 %collective-permute-start.11 = (bf16[784,128]{1,0:T(8,128)(2,1)S(1)}, bf16[784,128]{1,0:T(8,128)(2,1)S(1)}, u32[]{:S(2)}, u32[]{:S(2)}) collective-permute-start(bf16[784,128]{1,0:T(8,128)(2,1)S(1)} %pack_up.1.a), channel_id=1, source_target_pairs={{0,4},{1,5},{2,6},{3,7},{4,0},{5,1},{6,2},{7,3},{8,12},{9,13},{10,... | collective-permute-start | bytes 602120 | tf_op jit(solution)/shard_map/ppermute | solution.py:29
  23.7 6.1 %collective-permute-start.6 = (bf16[768,128]{1,0:T(8,128)(2,1)S(1)}, bf16[768,128]{1,0:T(8,128)(2,1)S(1)}, u32[]{:S(2)}, u32[]{:S(2)}) collective-permute-start(bf16[768,128]{1,0:T(8,128)(2,1)S(1)} %append.3), channel_id=1, source_target_pairs={{0,112},{8,24},{16,0},{24,40},{32,16},{40,56},{48,32},{56,72},{64,... | collective-permute-start | bytes 589832 | tf_op jit(solution)/shard_map/ppermute | solution.py:41
  24.5 8.1 %collective-permute-start.8 = (bf16[512,128]{1,0:T(8,128)(2,1)S(1)}, bf16[512,128]{1,0:T(8,128)(2,1)S(1)}, u32[]{:S(2)}, u32[]{:S(2)}) collective-permute-start(bf16[512,128]{1,0:T(8,128)(2,1)S(1)} %collective-permute-done.5.refs_0_), channel_id=1, source_target_pairs={{0,128},{8,136},{16,144},{24,152},{32,160},{40,168},{48,176},{56,1... | collective-permute-start | bytes 393224 | tf_op jit(solution)/shard_map/ppermute | solution.py:25
  29.8 19.7 %collective-permute-start.13 = (bf16[1568,128]{1,0:T(8,128)(2,1)S(1)}, bf16[1568,128]{1,0:T(8,128)(2,1)S(1)}, u32[]{:S(2)}, u32[]{:S(2)}) collective-permute-start(bf16[1568,128]{1,0:T(8,128)(2,1)S(1)} %append.4.refs_0_), channel_id=1, source_target_pairs={{0,3},{1,0},{2,1},{3,2},{4,7},{5,4},{6,5},{7,6},{8,11},{9,8},{10,9... | collective-permute-start | bytes 1204232 | tf_op jit(solution)/shard_map/ppermute | solution.py:29
  32.6 16.9 %collective-permute-start.12 = (bf16[1568,128]{1,0:T(8,128)(2,1)S(1)}, bf16[1568,128]{1,0:T(8,128)(2,1)S(1)}, u32[]{:S(2)}, u32[]{:S(2)}) collective-permute-start(bf16[1568,128]{1,0:T(8,128)(2,1)S(1)} %append.4.refs_0_), channel_id=1, source_target_pairs={{0,1},{1,2},{2,3},{3,0},{4,5},{5,6},{6,7},{7,4},{8,9},{9,10},{10,1... | collective-permute-start | bytes 1204232 | tf_op jit(solution)/shard_map/ppermute | solution.py:29
  32.6 8.5 %collective-permute-start.7 = (bf16[768,128]{1,0:T(8,128)(2,1)S(1)}, bf16[768,128]{1,0:T(8,128)(2,1)S(1)}, u32[]{:S(2)}, u32[]{:S(2)}) collective-permute-start(bf16[768,128]{1,0:T(8,128)(2,1)S(1)} %collective-permute-done.6.refs_0_), channel_id=1, source_target_pairs={{0,128},{8,136},{16,144},{24,152},{32,160},{40,168},{48,176},{56,1... | collective-permute-start | bytes 589832 | tf_op jit(solution)/shard_map/ppermute | solution.py:25
  32.6 8.4 %collective-permute-start.9 = (bf16[512,128]{1,0:T(8,128)(2,1)S(1)}, bf16[512,128]{1,0:T(8,128)(2,1)S(1)}, u32[]{:S(2)}, u32[]{:S(2)}) collective-permute-start(bf16[512,128]{1,0:T(8,128)(2,1)S(1)} %collective-permute-done.4.b), channel_id=1, source_target_pairs={{0,128},{8,136},{16,144},{24,152},{32,160},{40,168},{48,176},{56,1... | collective-permute-start | bytes 393224 | tf_op jit(solution)/shard_map/ppermute | solution.py:25
  47.0 28.1 %copy-start.2 = (bf16[128,1024]{1,0:T(8,128)(2,1)S(1)}, bf16[128,1024]{1,0:T(8,128)(2,1)}, u32[]{:S(2)}) copy-start(bf16[128,1024]{1,0:T(8,128)(2,1)} %w_own.1) | copy-start | bytes 786436
  47.0 3.5 %collective-permute-start.10 = (f32[2,128,128]{2,1,0:T(8,128)S(1)}, f32[2,128,128]{2,1,0:T(8,128)S(1)}, u32[]{:S(2)}, u32[]{:S(2)}) collective-permute-start(f32[2,128,128]{2,1,0:T(8,128)S(1)} %get-tuple-element.29), channel_id=1, source_target_pairs={{0,8},{8,0},{16,24},{24,16},{32,40},{40,32},{48,56},{56,48},{64,72... | collective-permute-start | bytes 393224 | tf_op jit(solution)/shard_map/ppermute | solution.py:25
  50.5 7.5 %collective-permute-start.18 = (bf16[784,128]{1,0:T(8,128)(2,1)S(1)}, bf16[784,128]{1,0:T(8,128)(2,1)S(1)}, u32[]{:S(2)}, u32[]{:S(2)}) collective-permute-start(bf16[784,128]{1,0:T(8,128)(2,1)S(1)} %get-tuple-element.31), channel_id=1, source_target_pairs={{0,1},{1,2},{2,3},{3,0},{4,5},{5,6},{6,7},{7,4},{8,9},{9,10},{10,1... | collective-permute-start | bytes 602120 | tf_op jit(solution)/shard_map/ppermute | solution.py:29
  50.6 7.4 %collective-permute-start.19 = (bf16[784,128]{1,0:T(8,128)(2,1)S(1)}, bf16[784,128]{1,0:T(8,128)(2,1)S(1)}, u32[]{:S(2)}, u32[]{:S(2)}) collective-permute-start(bf16[784,128]{1,0:T(8,128)(2,1)S(1)} %get-tuple-element.32), channel_id=1, source_target_pairs={{0,3},{1,0},{2,1},{3,2},{4,7},{5,4},{6,5},{7,6},{8,11},{9,8},{10,9... | collective-permute-start | bytes 602120 | tf_op jit(solution)/shard_map/ppermute | solution.py:29
  59.4 15.6 %collective-permute-start.20 = (bf16[1024,512]{1,0:T(8,128)(2,1)S(1)}, bf16[1024,512]{1,0:T(8,128)(2,1)S(1)}, u32[]{:S(2)}, u32[]{:S(2)}) collective-permute-start(bf16[1024,512]{1,0:T(8,128)(2,1)S(1)} %get-tuple-element.33.w0), channel_id=1, source_target_pairs={{0,8},{8,0},{16,24},{24,16},{32,40},{40,32},{48,56},{56,48},{64,72... | collective-permute-start | bytes 3145736 | tf_op jit(solution)/shard_map/ppermute | solution.py:25
  60.9 5.2 %collective-permute-start.14 = (bf16[256,128]{1,0:T(8,128)(2,1)S(1)}, bf16[256,128]{1,0:T(8,128)(2,1)S(1)}, u32[]{:S(2)}, u32[]{:S(2)}) collective-permute-start(bf16[256,128]{1,0:T(8,128)(2,1)S(1)} %bitcast.32), channel_id=1, source_target_pairs={{0,4},{1,5},{2,6},{3,7},{4,0},{5,1},{6,2},{7,3},{8,12},{9,13},{10,... | collective-permute-start | bytes 196616 | tf_op jit(solution)/shard_map/ppermute | solution.py:29
  66.1 5.7 %collective-permute-start.17 = (bf16[512,128]{1,0:T(8,128)(2,1)S(1)}, bf16[512,128]{1,0:T(8,128)(2,1)S(1)}, u32[]{:S(2)}, u32[]{:S(2)}) collective-permute-start(bf16[512,128]{1,0:T(8,128)(2,1)S(1)} %pad_maximum_fusion.2.p0), channel_id=1, source_target_pairs={{0,2},{1,3},{2,0},{3,1},{4,6},{5,7},{6,4},{7,5},{8,10},{9,11},{10,... | collective-permute-start | bytes 393224 | tf_op jit(solution)/shard_map/ppermute | solution.py:29
  68.8 6.2 %collective-permute-start.16 = (bf16[512,128]{1,0:T(8,128)(2,1)S(1)}, bf16[512,128]{1,0:T(8,128)(2,1)S(1)}, u32[]{:S(2)}, u32[]{:S(2)}) collective-permute-start(bf16[512,128]{1,0:T(8,128)(2,1)S(1)} %pad_maximum_fusion.2.p0), channel_id=1, source_target_pairs={{0,3},{1,0},{2,1},{3,2},{4,7},{5,4},{6,5},{7,6},{8,11},{9,8},{10,9... | collective-permute-start | bytes 393224 | tf_op jit(solution)/shard_map/ppermute | solution.py:29
  69.4 5.6 %collective-permute-start.15 = (bf16[512,128]{1,0:T(8,128)(2,1)S(1)}, bf16[512,128]{1,0:T(8,128)(2,1)S(1)}, u32[]{:S(2)}, u32[]{:S(2)}) collective-permute-start(bf16[512,128]{1,0:T(8,128)(2,1)S(1)} %pad_maximum_fusion.2.p0), channel_id=1, source_target_pairs={{0,1},{1,2},{2,3},{3,0},{4,5},{5,6},{6,7},{7,4},{8,9},{9,10},{10,1... | collective-permute-start | bytes 393224 | tf_op jit(solution)/shard_map/ppermute | solution.py:29
  77.2 3.2 %collective-permute-start.22 = (f32[64,1152]{1,0:T(8,128)S(1)}, f32[64,1152]{1,0:T(8,128)S(1)}, u32[]{:S(2)}, u32[]{:S(2)}) collective-permute-start(f32[64,1152]{1,0:T(8,128)S(1)} %get-tuple-element.39), channel_id=1, source_target_pairs={{0,8},{8,0},{16,24},{24,16},{32,40},{40,32},{48,56},{56,48},{64,72... | collective-permute-start | bytes 884744 | tf_op jit(solution)/shard_map/ppermute | solution.py:25
  79.2 1.3 %collective-permute-start.21 = (bf16[2,128,128]{2,1,0:T(8,128)(2,1)S(1)}, bf16[2,128,128]{2,1,0:T(8,128)(2,1)S(1)}, u32[]{:S(2)}, u32[]{:S(2)}) collective-permute-start(bf16[2,128,128]{2,1,0:T(8,128)(2,1)S(1)} %bitcast.30), channel_id=1, source_target_pairs={{0,8},{8,0},{16,24},{24,16},{32,40},{40,32},{48,56},{56,48},{64,72... | collective-permute-start | bytes 196616 | tf_op jit(solution)/shard_map/ppermute | solution.py:25
  80.5 5.4 %collective-permute-start.24 = (bf16[32,1152]{1,0:T(8,128)(2,1)S(1)}, bf16[32,1152]{1,0:T(8,128)(2,1)S(1)}, u32[]{:S(2)}, u32[]{:S(2)}) collective-permute-start(bf16[32,1152]{1,0:T(8,128)(2,1)S(1)} %fusion.send), channel_id=1, source_target_pairs={{0,128},{8,136},{16,144},{24,152},{32,160},{40,168},{48,176},{56,1... | collective-permute-start | bytes 221192 | tf_op jit(solution)/shard_map/ppermute | solution.py:25
  85.9 2.7 %collective-permute-start.25 = (bf16[32,1152]{1,0:T(8,128)(2,1)S(1)}, bf16[32,1152]{1,0:T(8,128)(2,1)S(1)}, u32[]{:S(2)}, u32[]{:S(2)}) collective-permute-start(bf16[32,1152]{1,0:T(8,128)(2,1)S(1)} %quarter_up.1.own), channel_id=1, source_target_pairs={{0,8},{8,0},{16,24},{24,16},{32,40},{40,32},{48,56},{56,48},{64,72... | collective-permute-start | bytes 221192 | tf_op jit(solution)/shard_map/ppermute | solution.py:25
  87.2 14.4 %collective-permute-start.23 = (bf16[16,128,128]{2,1,0:T(8,128)(2,1)S(1)}, bf16[16,128,128]{2,1,0:T(8,128)(2,1)S(1)}, u32[]{:S(2)}, u32[]{:S(2)}) collective-permute-start(bf16[16,128,128]{2,1,0:T(8,128)(2,1)S(1)} %get-tuple-element.41.far), channel_id=1, source_target_pairs={{0,128},{8,136},{16,144},{24,152},{32,160},{40,168},{48,176},{56,1... | collective-permute-start | bytes 1572872 | tf_op jit(solution)/shard_map/ppermute | solution.py:25
  88.5 10.2 %collective-permute-start.27 = (bf16[64,1152]{1,0:T(8,128)(2,1)S(1)}, bf16[64,1152]{1,0:T(8,128)(2,1)S(1)}, u32[]{:S(2)}, u32[]{:S(2)}) collective-permute-start(bf16[64,1152]{1,0:T(8,128)(2,1)S(1)} %pad_maximum_fusion.a), channel_id=1, source_target_pairs={{0,96},{8,40},{16,112},{24,56},{32,0},{40,72},{48,16},{56,88},{64,... | collective-permute-start | bytes 442376 | tf_op jit(solution)/shard_map/ppermute | solution.py:41
  88.6 10.1 %collective-permute-start.26 = (bf16[64,1152]{1,0:T(8,128)(2,1)S(1)}, bf16[64,1152]{1,0:T(8,128)(2,1)S(1)}, u32[]{:S(2)}, u32[]{:S(2)}) collective-permute-start(bf16[64,1152]{1,0:T(8,128)(2,1)S(1)} %pad_maximum_fusion.a), channel_id=1, source_target_pairs={{0,80},{8,56},{16,96},{24,72},{32,112},{40,88},{48,0},{56,104},{64... | collective-permute-start | bytes 442376 | tf_op jit(solution)/shard_map/ppermute | solution.py:41
  98.8 6.1 %collective-permute-start.32 = (bf16[96,1152]{1,0:T(8,128)(2,1)S(1)}, bf16[96,1152]{1,0:T(8,128)(2,1)S(1)}, u32[]{:S(2)}, u32[]{:S(2)}) collective-permute-start(bf16[96,1152]{1,0:T(8,128)(2,1)S(1)} %append.5.ready), channel_id=1, source_target_pairs={{0,112},{8,24},{16,0},{24,40},{32,16},{40,56},{48,32},{56,72},{64,... | collective-permute-start | bytes 663560 | tf_op jit(solution)/shard_map/ppermute | solution.py:41
  104.8 11.7 %collective-permute-start.33 = (bf16[96,1152]{1,0:T(8,128)(2,1)S(1)}, bf16[96,1152]{1,0:T(8,128)(2,1)S(1)}, u32[]{:S(2)}, u32[]{:S(2)}) collective-permute-start(bf16[96,1152]{1,0:T(8,128)(2,1)S(1)} %peer_rows.1), channel_id=1, source_target_pairs={{0,8},{8,0},{16,24},{24,16},{32,40},{40,32},{48,56},{56,48},{64,72... | collective-permute-start | bytes 663560 | tf_op jit(solution)/shard_map/ppermute | solution.py:25
  106.9 9.5 %collective-permute-start.28 = (bf16[6,128,128]{2,1,0:T(8,128)(2,1)S(1)}, bf16[6,128,128]{2,1,0:T(8,128)(2,1)S(1)}, u32[]{:S(2)}, u32[]{:S(2)}) collective-permute-start(bf16[6,128,128]{2,1,0:T(8,128)(2,1)S(1)} %get-tuple-element.43), channel_id=1, source_target_pairs={{0,16},{8,120},{16,32},{24,8},{32,48},{40,24},{48,64},{56,40},{64,... | collective-permute-start | bytes 589832 | tf_op jit(solution)/shard_map/ppermute | solution.py:41
  110.3 6.1 %collective-permute-start.29 = (bf16[4,128,128]{2,1,0:T(8,128)(2,1)S(1)}, bf16[4,128,128]{2,1,0:T(8,128)(2,1)S(1)}, u32[]{:S(2)}, u32[]{:S(2)}) collective-permute-start(bf16[4,128,128]{2,1,0:T(8,128)(2,1)S(1)} %get-tuple-element.44.t), channel_id=1, source_target_pairs={{0,32},{8,104},{16,48},{24,120},{32,64},{40,8},{48,80},{56,24},{64... | collective-permute-start | bytes 393224 | tf_op jit(solution)/shard_map/ppermute | solution.py:41
  117.2 3.3 %collective-permute-start.34 = (bf16[32,1152]{1,0:T(8,128)(2,1)S(1)}, bf16[32,1152]{1,0:T(8,128)(2,1)S(1)}, u32[]{:S(2)}, u32[]{:S(2)}) collective-permute-start(bf16[32,1152]{1,0:T(8,128)(2,1)S(1)} %sum_z.1), channel_id=1, source_target_pairs={{0,128},{8,136},{16,144},{24,152},{32,160},{40,168},{48,176},{56,1... | collective-permute-start | bytes 221192 | tf_op jit(solution)/shard_map/ppermute | solution.py:25
  118.1 7.2 %collective-permute-start.30 = (bf16[4,128,128]{2,1,0:T(8,128)(2,1)S(1)}, bf16[4,128,128]{2,1,0:T(8,128)(2,1)S(1)}, u32[]{:S(2)}, u32[]{:S(2)}) collective-permute-start(bf16[4,128,128]{2,1,0:T(8,128)(2,1)S(1)} %ride.1.t), channel_id=1, source_target_pairs={{0,48},{8,88},{16,64},{24,104},{32,80},{40,120},{48,96},{56,8},{64... | collective-permute-start | bytes 393224 | tf_op jit(solution)/shard_map/ppermute | solution.py:41
  120.5 8.4 %collective-permute-start.35 = (bf16[64,1152]{1,0:T(8,128)(2,1)S(1)}, bf16[64,1152]{1,0:T(8,128)(2,1)S(1)}, u32[]{:S(2)}, u32[]{:S(2)}) collective-permute-start(bf16[64,1152]{1,0:T(8,128)(2,1)S(1)} %pad_maximum_fusion.1.mine), channel_id=1, source_target_pairs={{0,8},{8,0},{16,24},{24,16},{32,40},{40,32},{48,56},{56,48},{64,72... | collective-permute-start | bytes 442376 | tf_op jit(solution)/shard_map/ppermute | solution.py:25
  125.4 5.5 %collective-permute-start.31 = (f32[2,128,128]{2,1,0:T(8,128)S(1)}, f32[2,128,128]{2,1,0:T(8,128)S(1)}, u32[]{:S(2)}, u32[]{:S(2)}) collective-permute-start(f32[2,128,128]{2,1,0:T(8,128)S(1)} %slice.35), channel_id=1, source_target_pairs={{0,8},{8,0},{16,24},{24,16},{32,40},{40,32},{48,56},{56,48},{64,72... | collective-permute-start | bytes 393224 | tf_op jit(solution)/shard_map/ppermute | solution.py:25

commit v3 on v2

--- a/solution.py
+++ b/solution.py
@@ -211,7 +211,7 @@
 
 def lay_body(ids, *refs):
     own = refs[0:5]
-    w_out, og_out, bias_out, rows, sem = refs[5:10]
+    w_out, og_out, bias_out, rows, sem = refs[6:11]
     yy, xx = ids[1] & 3, ids[1] >> 2
     copies, cols = [], []
 
@@ -235,7 +235,7 @@
         bias_out[:, pl.ds(cols[k], B)] = rows[k].astype(f32)[0:8]
 
 
-def lay_out(ids, own):
+def lay_out(ids, own, ready):
     return pl.pallas_call(
         lay_body,
         out_shape=(
@@ -243,13 +243,13 @@
             jax.ShapeDtypeStruct((256, 1024), bf16),
             jax.ShapeDtypeStruct((8, 1024), f32),
         ),
-        in_specs=[SM] + [HB] * 5,
+        in_specs=[SM] + [HB] * 5 + [ANY],
         out_specs=(VM, VM, VM),
         scratch_shapes=[pltpu.VMEM((8, 16, B), bf16), pltpu.SemaphoreType.DMA((48,))],
         compiler_params=params(8),
         cost_estimate=cost(0, 3 << 20),
         name="lay_out",
-    )(ids, *own)
+    )(ids, *own, ready)
 
 
 def mid_body(ids, p0, p1, p2, p3, w0, w1, og, bias, w_own, hidden, prop, keep, give, agg, pre, gp, wp):
@@ -470,11 +470,12 @@
     more = row_send(swap, dc=1)
     o3, o2 = spin_send(both, 3, -1), spin_send(both, 2, -1)
     plan = plan_tiles(ids, col_blocks, dest_blocks, lists[0], lists[1])
-    o14 = spin_send(append(768, both, o3, o2, x0, plan), 1, -1)
+    ext = append(768, both, o3, o2, x0, plan)
+    o14 = spin_send(ext, 1, -1)
     p3, p2, p14 = row_send(o3, dx=1), row_send(o2, dx=1), row_send(o14, dx=1)
 
-    pack = pack_up(ids, weight, out_grad, bias_vector[None, :], plan)
-    pair = append(1568, pack, feat_send(pack, dx=1), o14)
+    pack = pack_up(ids, weight, out_grad, bias_vector[None, :], ext)
+    pair = append(1568, pack, feat_send(pack, dx=1), p3, p2, p14)
     wu, wd = feat_send(pair, dy=1), feat_send(pair, dy=-1)
 
     mine, theirs = aggregate(plan, adj_tiles, more, (both_a, x0, o14, o2, o3, p14, p2, p3))
@@ -483,7 +484,7 @@
     wa, wb = feat_send(wa, dy=1), feat_send(wb, dy=-1)
 
     q = jnp.concatenate([aggregated, feat_send(aggregated, dx=1)], axis=0)
-    w0, og, bias = lay_out(ids, (pair, wu, wd, wa, wb))
+    w0, og, bias = lay_out(ids, (pair, wu, wd, wa, wb), q)
     pieces = (q, feat_send(q, dy=1), feat_send(q, dy=-1), feat_send(q, dy=2))
     hidden, prop, keep, give = middle(ids, pieces, w0, row_send(w0, dc=1), og, bias, weight)
     prop = prop.reshape(2, B, B)
@@ -505,7 +506,7 @@
     t3 = ride(t3, r14, r2)
     r3 = spin_send(t3, 3)
 
-    e = row_send(peer_rows(d1, d2, d3, t2), dc=1)
+    e = row_send(peer_rows(d1, d2, d3, t3), dc=1)
     scale = float(256 * lax.axis_size("row")) ** (-0.5)
     total = sum_z(scale, ids, quarter, d1, d2, d3, e, t3)
     two = jnp.concatenate([total, row_send(total, dx=1)], axis=0)

time: 132 us -> 130 us (0.985)
  waiting for transfers between devices: 48.7 us -> 39.1 us
  starting transfers between devices: 54.7 us -> 60.9 us
    ppermute x9, starting transfers between devices: 16.1 us -> 26.5 us  [spin_send(): return lax.ppermute(v, 'row', perm)]
    ppermute x9, waiting for transfers between devices: 20.3 us -> 12.1 us  [spin_send(): return lax.ppermute(v, 'row', perm)]
    ppermute x9, waiting for transfers between devices: 17.4 us -> 11.6 us  [feat_send(): lax.ppermute(v, 'feat', [(i, (i >> 2 ^ dx) << 2 | i + dy & 3) for i in ra...]
    ppermute x18, waiting for transfers between devices: 11 us -> 15.4 us  [row_send(): return lax.ppermute(v, 'row', perm)]
    ppermute x9, starting transfers between devices: 14.6 us -> 11.4 us  [feat_send(): lax.ppermute(v, 'feat', [(i, (i >> 2 ^ dx) << 2 | i + dy & 3) for i in ra...]
  transfers between devices with their start and end apart: 36 -> 36, of which waited for: 15 -> 17; matrix products, arithmetic and copies ran while one was open for 2% -> 2% of each run, Pallas kernels for 12% -> 13%
where the time goes in v3:
time: 130 us; the launch traced here: 129 us
  starting transfers between devices  60.9 us (47%)
  waiting for transfers between devices  39.1 us (30%)
  Pallas kernels  21.8 us (17%)
  local copies, waits for them, and re-layouts  5.14 us (4%)
  other arithmetic  1.53 us (1%)
    ppermute x9, starting transfers between devices, spin_send(): return lax.ppermute(v, 'row', perm)  26.5 us
    ppermute x18, starting transfers between devices, row_send(): return lax.ppermute(v, 'row', perm)  23 us
    ppermute x18, waiting for transfers between devices, row_send(): return lax.ppermute(v, 'row', perm)  15.4 us
    ppermute x9, waiting for transfers between devices, spin_send(): return lax.ppermute(v, 'row', perm)  12.1 us
    ppermute x9, waiting for transfers between devices, feat_send(): lax.ppermute(v, 'feat', [(i, (i >> 2 ^ dx) << 2 | i + dy & 3) for i in ra...  11.6 us
    ppermute x9, starting transfers between devices, feat_send(): lax.ppermute(v, 'feat', [(i, (i >> 2 ^ dx) << 2 | i + dy & 3) for i in ra...  11.4 us
    pallas_call x1, Pallas kernels, aggregate(): pl.pallas_call(agg_body, out_shape=(jax.ShapeDtypeStruct((2, B, B), f32),...  6.41 us
    pallas_call x1, Pallas kernels, spread(): pl.pallas_call(spread_body, out_shape=(jax.ShapeDtypeStruct((16, B, B), f...  5.9 us
  transfers between devices with their start and end apart: 36, of which 17 were waited for; matrix products, arithmetic and copies ran while one was open for 2% of the time, Pallas kernels for 13%

profile of v3, /device:TPU:1, one launch (start us, length us, event | category | flops | bytes accessed | tf_op | source)
XLA Modules:
  0.0 129.4 jit_solution(1441661622775915994)
XLA Ops:
  0.6 3.3 %collective-permute-start.1 = (bf16[256,128]{1,0:T(8,128)(2,1)}, bf16[256,128]{1,0:T(8,128)(2,1)S(1)}, u32[]{:S(2)}, u32[]{:S(2)}) collective-permute-start(bf16[256,128]{1,0:T(8,128)(2,1)} %param.7), channel_id=1, source_target_pairs={{0,8},{8,0},{16,24},{24,16},{32,40},{40,32},{48,56},{56,48},{64,72... | collective-permute-start | bytes 196616 | tf_op jit(solution)/shard_map/ppermute | solution.py:25
  4.0 0.8 constant_dynamic-update-slice_fusion.1
  5.5 0.7 pad_add_fusion
  6.5 2.7 %collective-permute-start.5 = (bf16[512,128]{1,0:T(8,128)(2,1)S(1)}, bf16[512,128]{1,0:T(8,128)(2,1)S(1)}, u32[]{:S(2)}, u32[]{:S(2)}) collective-permute-start(bf16[512,128]{1,0:T(8,128)(2,1)S(1)} %constant_dynamic-update-slice_fusion.a), channel_id=1, source_target_pairs={{0,96},{8,40},{16,112},{24,56},{32,0},{40,72},{48,16},{56,88},{64,... | collective-permute-start | bytes 393224 | tf_op jit(solution)/shard_map/ppermute | solution.py:41
  9.2 4.7 %collective-permute-start.4 = (bf16[512,128]{1,0:T(8,128)(2,1)S(1)}, bf16[512,128]{1,0:T(8,128)(2,1)S(1)}, u32[]{:S(2)}, u32[]{:S(2)}) collective-permute-start(bf16[512,128]{1,0:T(8,128)(2,1)S(1)} %constant_dynamic-update-slice_fusion.a), channel_id=1, source_target_pairs={{0,80},{8,56},{16,96},{24,72},{32,112},{40,88},{48,0},{56,104},{64... | collective-permute-start | bytes 393224 | tf_op jit(solution)/shard_map/ppermute | solution.py:41
  15.2 2.7 %plan_tiles.1.refs_2_.plan = s32[160]{0:T(256)S(1)} custom-call(s32[2]{0:T(128)S(1)} %pad_add_fusion.1.ids, s32[64]{0:T(128)S(1)} %copy-done.4, s32[64]{0:T(128)S(1)} %copy-done.5, s32[64]{0:T(128)S(1)} %get-tuple-element.49.c1, s32[64]{0:T(128)S(1)} %get-tuple-element.48.d1), custom_call_target="tpu_custom_call" | custom-call | flops 10000 | bytes 4096 | tf_op jit(solution)/shard_map/plan_tiles/pallas_call | solution.py:145
  17.9 2.5 %collective-permute-done.4.b = bf16[512,128]{1,0:T(8,128)(2,1)S(1)} collective-permute-done((bf16[512,128]{1,0:T(8,128)(2,1)S(1)}, bf16[512,128]{1,0:T(8,128)(2,1)S(1)}, u32[]{:S(2)}, u32[]{:S(2)}) %collective-permute-start.4) | collective-permute-done | bytes 131104 | tf_op jit(solution)/shard_map/ppermute | solution.py:41
  20.6 0.9 copy-done.1
  21.5 0.8 copy-done.3
  23.0 0.7 pack_up.1.a
  23.7 2.5 %collective-permute-start.11 = (bf16[784,128]{1,0:T(8,128)(2,1)S(1)}, bf16[784,128]{1,0:T(8,128)(2,1)S(1)}, u32[]{:S(2)}, u32[]{:S(2)}) collective-permute-start(bf16[784,128]{1,0:T(8,128)(2,1)S(1)} %pack_up.1.a), channel_id=1, source_target_pairs={{0,4},{1,5},{2,6},{3,7},{4,0},{5,1},{6,2},{7,3},{8,12},{9,13},{10,... | collective-permute-start | bytes 602120 | tf_op jit(solution)/shard_map/ppermute | solution.py:29
  26.5 1.2 collective-permute-start.8
  28.0 8.5 %collective-permute-done.8.refs_1_ = bf16[512,128]{1,0:T(8,128)(2,1)S(1)} collective-permute-done((bf16[512,128]{1,0:T(8,128)(2,1)S(1)}, bf16[512,128]{1,0:T(8,128)(2,1)S(1)}, u32[]{:S(2)}, u32[]{:S(2)}) %collective-permute-start.8) | collective-permute-done | bytes 131104 | tf_op jit(solution)/shard_map/ppermute | solution.py:25
  36.5 2.8 %collective-permute-done.9.refs_0_ = bf16[512,128]{1,0:T(8,128)(2,1)S(1)} collective-permute-done((bf16[512,128]{1,0:T(8,128)(2,1)S(1)}, bf16[512,128]{1,0:T(8,128)(2,1)S(1)}, u32[]{:S(2)}, u32[]{:S(2)}) %collective-permute-start.9) | collective-permute-done | bytes 131104 | tf_op jit(solution)/shard_map/ppermute | solution.py:25
  39.4 2.8 %collective-permute-start.13 = (bf16[1568,128]{1,0:T(8,128)(2,1)S(1)}, bf16[1568,128]{1,0:T(8,128)(2,1)S(1)}, u32[]{:S(2)}, u32[]{:S(2)}) collective-permute-start(bf16[1568,128]{1,0:T(8,128)(2,1)S(1)} %append.4.refs_0_), channel_id=1, source_target_pairs={{0,3},{1,0},{2,1},{3,2},{4,7},{5,4},{6,5},{7,6},{8,11},{9,8},{10,9... | collective-permute-start | bytes 1204232 | tf_op jit(solution)/shard_map/ppermute | solution.py:29
  42.2 6.4 %aggregate.1 = (f32[2,128,128]{2,1,0:T(8,128)S(1)}, f32[2,128,128]{2,1,0:T(8,128)S(1)}) custom-call(s32[160]{0:T(256)S(1)} %plan_tiles.1.refs_2_.plan, bf16[64,128,128]{2,1,0:T(8,128)(2,1)S(1)} %copy-done, bf16[64,128,128]{2,1,0:T(8,128)(2,1)} %collective-permute-done.2.more, bf16[4,128,128]{2,1,0:T(8,128)(2,1)S(1)} %bitcast.22, ...), custom_call_target="tpu_custom_call" | custom-call | flops 268435456 | bytes 4194304 | tf_op jit(solution)/shard_map/aggregate/pallas_call | solution.py:196
  48.6 2.4 %collective-permute-start.10 = (f32[2,128,128]{2,1,0:T(8,128)S(1)}, f32[2,128,128]{2,1,0:T(8,128)S(1)}, u32[]{:S(2)}, u32[]{:S(2)}) collective-permute-start(f32[2,128,128]{2,1,0:T(8,128)S(1)} %get-tuple-element.29), channel_id=1, source_target_pairs={{0,8},{8,0},{16,24},{24,16},{32,40},{40,32},{48,56},{56,48},{64,72... | collective-permute-start | bytes 393224 | tf_op jit(solution)/shard_map/ppermute | solution.py:25
  51.3 0.8 collective-permute-done.10.came
  52.5 2.7 %collective-permute-start.19 = (bf16[784,128]{1,0:T(8,128)(2,1)S(1)}, bf16[784,128]{1,0:T(8,128)(2,1)S(1)}, u32[]{:S(2)}, u32[]{:S(2)}) collective-permute-start(bf16[784,128]{1,0:T(8,128)(2,1)S(1)} %get-tuple-element.32), channel_id=1, source_target_pairs={{0,3},{1,0},{2,1},{3,2},{4,7},{5,4},{6,5},{7,6},{8,11},{9,8},{10,9... | collective-permute-start | bytes 602120 | tf_op jit(solution)/shard_map/ppermute | solution.py:29
  55.2 1.5 %collective-permute-start.14 = (bf16[256,128]{1,0:T(8,128)(2,1)S(1)}, bf16[256,128]{1,0:T(8,128)(2,1)S(1)}, u32[]{:S(2)}, u32[]{:S(2)}) collective-permute-start(bf16[256,128]{1,0:T(8,128)(2,1)S(1)} %bitcast.32), channel_id=1, source_target_pairs={{0,4},{1,5},{2,6},{3,7},{4,0},{5,1},{6,2},{7,3},{8,12},{9,13},{10,... | collective-permute-start | bytes 196616 | tf_op jit(solution)/shard_map/ppermute | solution.py:29
  56.7 3.2 %collective-permute-done.14 = bf16[256,128]{1,0:T(8,128)(2,1)S(1)} collective-permute-done((bf16[256,128]{1,0:T(8,128)(2,1)S(1)}, bf16[256,128]{1,0:T(8,128)(2,1)S(1)}, u32[]{:S(2)}, u32[]{:S(2)}) %collective-permute-start.14) | collective-permute-done | bytes 65568 | tf_op jit(solution)/shard_map/ppermute | solution.py:29
  59.9 1.4 %lay_out.1 = (bf16[1024,512]{1,0:T(8,128)(2,1)S(1)}, bf16[256,1024]{1,0:T(8,128)(2,1)S(1)}, f32[8,1024]{1,0:T(8,128)S(1)}) custom-call(s32[2]{0:T(128)S(1)} %pad_add_fusion.1.ids, bf16[1568,128]{1,0:T(8,128)(2,1)S(1)} %append.4.refs_0_, bf16[1568,128]{1,0:T(8,128)(2,1)S(1)} %collective-permute-done.12.u.refs_1_, ...), custom_call_target="tpu_custom_call" | custom-call | bytes 3145728 | tf_op jit(solution)/shard_map/lay_out/pallas_call | solution.py:239
  61.3 4.5 %collective-permute-start.20 = (bf16[1024,512]{1,0:T(8,128)(2,1)S(1)}, bf16[1024,512]{1,0:T(8,128)(2,1)S(1)}, u32[]{:S(2)}, u32[]{:S(2)}) collective-permute-start(bf16[1024,512]{1,0:T(8,128)(2,1)S(1)} %get-tuple-element.33.w0), channel_id=1, source_target_pairs={{0,8},{8,0},{16,24},{24,16},{32,40},{40,32},{48,56},{56,48},{64,72... | collective-permute-start | bytes 3145736 | tf_op jit(solution)/shard_map/ppermute | solution.py:25
  65.8 1.0 collective-permute-start.16
  67.3 5.1 %collective-permute-done.17.p3 = bf16[512,128]{1,0:T(8,128)(2,1)S(1)} collective-permute-done((bf16[512,128]{1,0:T(8,128)(2,1)S(1)}, bf16[512,128]{1,0:T(8,128)(2,1)S(1)}, u32[]{:S(2)}, u32[]{:S(2)}) %collective-permute-start.17) | collective-permute-done | bytes 131104 | tf_op jit(solution)/shard_map/ppermute | solution.py:29
  72.4 1.3 collective-permute-done.16.p2
  73.7 1.9 %collective-permute-done.15.p1 = bf16[512,128]{1,0:T(8,128)(2,1)S(1)} collective-permute-done((bf16[512,128]{1,0:T(8,128)(2,1)S(1)}, bf16[512,128]{1,0:T(8,128)(2,1)S(1)}, u32[]{:S(2)}, u32[]{:S(2)}) %collective-permute-start.15) | collective-permute-done | bytes 131104 | tf_op jit(solution)/shard_map/ppermute | solution.py:29
  75.6 2.2 %middle.1 = (f32[256,128]{1,0:T(8,128)}, bf16[256,128]{1,0:T(8,128)(2,1)S(1)}, f32[64,1152]{1,0:T(8,128)S(1)}, f32[64,1152]{1,0:T(8,128)S(1)}) custom-call(s32[2]{0:T(128)S(1)} %pad_add_fusion.1.ids, bf16[512,128]{1,0:T(8,128)(2,1)S(1)} %pad_maximum_fusion.2.refs_5_.p0, bf16[512,128]{1,0:T(8,128)(2,1)S(1)} %collective-permute-done.15.p1, ...), custom_call_target="tpu_custom_call" | custom-call | flops 671088640 | bytes 5242880 | tf_op jit(solution)/shard_map/middle/pallas_call | solution.py:285
  78.3 1.2 collective-permute-done.22.got
  79.5 1.6 %collective-permute-start.24 = (bf16[32,1152]{1,0:T(8,128)(2,1)S(1)}, bf16[32,1152]{1,0:T(8,128)(2,1)S(1)}, u32[]{:S(2)}, u32[]{:S(2)}) collective-permute-start(bf16[32,1152]{1,0:T(8,128)(2,1)S(1)} %fusion.send), channel_id=1, source_target_pairs={{0,128},{8,136},{16,144},{24,152},{32,160},{40,168},{48,176},{56,1... | collective-permute-start | bytes 221192 | tf_op jit(solution)/shard_map/ppermute | solution.py:25
  81.1 5.9 %spread.1 = (f32[16,128,128]{2,1,0:T(8,128)S(1)}, bf16[16,128,128]{2,1,0:T(8,128)(2,1)S(1)}) custom-call(s32[160]{0:T(256)S(1)} %plan_tiles.1.refs_2_.plan, bf16[64,128,128]{2,1,0:T(8,128)(2,1)S(1)} %copy-done, bf16[64,128,128]{2,1,0:T(8,128)(2,1)} %collective-permute-done.2.more, bf16[2,128,128]{2,1,0:T(8,128)(2,1)S(1)} %bitcast.31, ...), custom_call_target="tpu_custom_call" | custom-call | flops 268435456 | bytes 6291456 | tf_op jit(solution)/shard_map/spread/pallas_call | solution.py:324
  87.1 0.7 collective-permute-start.25
  87.9 0.9 collective-permute-done.25
  88.8 5.3 %collective-permute-start.27 = (bf16[64,1152]{1,0:T(8,128)(2,1)S(1)}, bf16[64,1152]{1,0:T(8,128)(2,1)S(1)}, u32[]{:S(2)}, u32[]{:S(2)}) collective-permute-start(bf16[64,1152]{1,0:T(8,128)(2,1)S(1)} %pad_maximum_fusion.a), channel_id=1, source_target_pairs={{0,96},{8,40},{16,112},{24,56},{32,0},{40,72},{48,16},{56,88},{64,... | collective-permute-start | bytes 442376 | tf_op jit(solution)/shard_map/ppermute | solution.py:41
  94.1 2.7 %collective-permute-start.26 = (bf16[64,1152]{1,0:T(8,128)(2,1)S(1)}, bf16[64,1152]{1,0:T(8,128)(2,1)S(1)}, u32[]{:S(2)}, u32[]{:S(2)}) collective-permute-start(bf16[64,1152]{1,0:T(8,128)(2,1)S(1)} %pad_maximum_fusion.a), channel_id=1, source_target_pairs={{0,80},{8,56},{16,96},{24,72},{32,112},{40,88},{48,0},{56,104},{64... | collective-permute-start | bytes 442376 | tf_op jit(solution)/shard_map/ppermute | solution.py:41
  97.0 4.4 %collective-permute-done.26.b.d3 = bf16[64,1152]{1,0:T(8,128)(2,1)S(1)} collective-permute-done((bf16[64,1152]{1,0:T(8,128)(2,1)S(1)}, bf16[64,1152]{1,0:T(8,128)(2,1)S(1)}, u32[]{:S(2)}, u32[]{:S(2)}) %collective-permute-start.26) | collective-permute-done | bytes 147488 | tf_op jit(solution)/shard_map/ppermute | solution.py:41
  101.4 2.7 %collective-permute-start.32 = (bf16[96,1152]{1,0:T(8,128)(2,1)S(1)}, bf16[96,1152]{1,0:T(8,128)(2,1)S(1)}, u32[]{:S(2)}, u32[]{:S(2)}) collective-permute-start(bf16[96,1152]{1,0:T(8,128)(2,1)S(1)} %append.5.ready), channel_id=1, source_target_pairs={{0,112},{8,24},{16,0},{24,40},{32,16},{40,56},{48,32},{56,72},{64,... | collective-permute-start | bytes 663560 | tf_op jit(solution)/shard_map/ppermute | solution.py:41
  104.4 5.0 %collective-permute-start.29 = (bf16[4,128,128]{2,1,0:T(8,128)(2,1)S(1)}, bf16[4,128,128]{2,1,0:T(8,128)(2,1)S(1)}, u32[]{:S(2)}, u32[]{:S(2)}) collective-permute-start(bf16[4,128,128]{2,1,0:T(8,128)(2,1)S(1)} %get-tuple-element.44), channel_id=1, source_target_pairs={{0,32},{8,104},{16,48},{24,120},{32,64},{40,8},{48,80},{56,24},{64... | collective-permute-start | bytes 393224 | tf_op jit(solution)/shard_map/ppermute | solution.py:41
  109.4 2.7 %collective-permute-done.29.ready = bf16[4,128,128]{2,1,0:T(8,128)(2,1)S(1)} collective-permute-done((bf16[4,128,128]{2,1,0:T(8,128)(2,1)S(1)}, bf16[4,128,128]{2,1,0:T(8,128)(2,1)S(1)}, u32[]{:S(2)}, u32[]{:S(2)}) %collective-permute-start.29) | collective-permute-done | bytes 131104 | tf_op jit(solution)/shard_map/ppermute | solution.py:41
  112.1 3.4 %collective-permute-start.33 = (bf16[96,1152]{1,0:T(8,128)(2,1)S(1)}, bf16[96,1152]{1,0:T(8,128)(2,1)S(1)}, u32[]{:S(2)}, u32[]{:S(2)}) collective-permute-start(bf16[96,1152]{1,0:T(8,128)(2,1)S(1)} %peer_rows.1), channel_id=1, source_target_pairs={{0,8},{8,0},{16,24},{24,16},{32,40},{40,32},{48,56},{56,48},{64,72... | collective-permute-start | bytes 663560 | tf_op jit(solution)/shard_map/ppermute | solution.py:25
  115.5 3.3 %collective-permute-start.30 = (bf16[4,128,128]{2,1,0:T(8,128)(2,1)S(1)}, bf16[4,128,128]{2,1,0:T(8,128)(2,1)S(1)}, u32[]{:S(2)}, u32[]{:S(2)}) collective-permute-start(bf16[4,128,128]{2,1,0:T(8,128)(2,1)S(1)} %ride.1.t), channel_id=1, source_target_pairs={{0,48},{8,88},{16,64},{24,104},{32,80},{40,120},{48,96},{56,8},{64... | collective-permute-start | bytes 393224 | tf_op jit(solution)/shard_map/ppermute | solution.py:41
  118.8 0.7 sum_z.1
  119.5 1.1 collective-permute-start.34
  120.5 2.3 %collective-permute-done.30 = bf16[4,128,128]{2,1,0:T(8,128)(2,1)S(1)} collective-permute-done((bf16[4,128,128]{2,1,0:T(8,128)(2,1)S(1)}, bf16[4,128,128]{2,1,0:T(8,128)(2,1)S(1)}, u32[]{:S(2)}, u32[]{:S(2)}) %collective-permute-start.30) | collective-permute-done | bytes 131104 | tf_op jit(solution)/shard_map/ppermute | solution.py:41
  122.9 2.9 %collective-permute-start.31 = (f32[2,128,128]{2,1,0:T(8,128)S(1)}, f32[2,128,128]{2,1,0:T(8,128)S(1)}, u32[]{:S(2)}, u32[]{:S(2)}) collective-permute-start(f32[2,128,128]{2,1,0:T(8,128)S(1)} %slice.35), channel_id=1, source_target_pairs={{0,8},{8,0},{16,24},{24,16},{32,40},{40,32},{48,56},{56,48},{64,72... | collective-permute-start | bytes 393224 | tf_op jit(solution)/shard_map/ppermute | solution.py:25
  125.9 0.9 collective-permute-done.31
  126.7 0.7 fusion.1
  127.4 1.4 %weight_out.1 = (f32[128,1024]{1,0:T(8,128)}, f32[8,128]{1,0:T(8,128)S(1)}) custom-call(s32[2]{0:T(128)S(1)} %pad_add_fusion.1.ids, bf16[64,1152]{1,0:T(8,128)(2,1)S(1)} %pad_maximum_fusion.1.mine, bf16[64,1152]{1,0:T(8,128)(2,1)S(1)} %collective-permute-done.35.theirs), custom_call_target="tpu_custom_call" | custom-call | bytes 1048576 | tf_op jit(solution)/shard_map/weight_out/pallas_call | solution.py:451
  (67 shorter events, 6.6 us)
Async XLA Ops:
  0.6 41.6 %copy-start = (bf16[64,128,128]{2,1,0:T(8,128)(2,1)S(1)}, bf16[64,128,128]{2,1,0:T(8,128)(2,1)}, u32[]{:S(2)}) copy-start(bf16[64,128,128]{2,1,0:T(8,128)(2,1)} %tiles.3) | copy-start | bytes 6291460
  0.6 4.4 %collective-permute-start.1 = (bf16[256,128]{1,0:T(8,128)(2,1)}, bf16[256,128]{1,0:T(8,128)(2,1)S(1)}, u32[]{:S(2)}, u32[]{:S(2)}) collective-permute-start(bf16[256,128]{1,0:T(8,128)(2,1)} %param.7), channel_id=1, source_target_pairs={{0,8},{8,0},{16,24},{24,16},{32,40},{40,32},{48,56},{56,48},{64,72... | collective-permute-start | bytes 196616 | tf_op jit(solution)/shard_map/ppermute | solution.py:25
  5.1 37.1 %collective-permute-start.2 = (bf16[64,128,128]{2,1,0:T(8,128)(2,1)}, bf16[64,128,128]{2,1,0:T(8,128)(2,1)}, u32[]{:S(2)}, u32[]{:S(2)}) collective-permute-start(bf16[64,128,128]{2,1,0:T(8,128)(2,1)} %tiles.3), channel_id=1, source_target_pairs={{0,8},{8,0},{16,24},{24,16},{32,40},{40,32},{48,56},{56,48},{64,72... | collective-permute-start | bytes 6291464 | tf_op jit(solution)/shard_map/ppermute | solution.py:25
  5.5 12.4 %collective-permute-start.3 = (bf16[256,128]{1,0:T(8,128)(2,1)}, bf16[256,128]{1,0:T(8,128)(2,1)S(1)}, u32[]{:S(2)}, u32[]{:S(2)}) collective-permute-start(bf16[256,128]{1,0:T(8,128)(2,1)} %param.7), channel_id=1, source_target_pairs={{0,128},{8,136},{16,144},{24,152},{32,160},{40,168},{48,176},{56,1... | collective-permute-start | bytes 196616 | tf_op jit(solution)/shard_map/ppermute | solution.py:25
  6.2 7.6 %collective-permute-start = (s32[2,64]{1,0:T(2,128)S(1)}, s32[2,64]{1,0:T(2,128)S(1)}, u32[]{:S(2)}, u32[]{:S(2)}) collective-permute-start(s32[2,64]{1,0:T(2,128)S(1)} %pad_add_fusion), channel_id=1, source_target_pairs={{0,8},{8,0},{16,24},{24,16},{32,40},{40,32},{48,56},{56,48},{64,72... | collective-permute-start | bytes 1544 | tf_op jit(solution)/shard_map/ppermute | solution.py:25
  6.5 11.5 %collective-permute-start.5 = (bf16[512,128]{1,0:T(8,128)(2,1)S(1)}, bf16[512,128]{1,0:T(8,128)(2,1)S(1)}, u32[]{:S(2)}, u32[]{:S(2)}) collective-permute-start(bf16[512,128]{1,0:T(8,128)(2,1)S(1)} %constant_dynamic-update-slice_fusion.a), channel_id=1, source_target_pairs={{0,96},{8,40},{16,112},{24,56},{32,0},{40,72},{48,16},{56,88},{64,... | collective-permute-start | bytes 393224 | tf_op jit(solution)/shard_map/ppermute | solution.py:41
  9.2 11.2 %collective-permute-start.4 = (bf16[512,128]{1,0:T(8,128)(2,1)S(1)}, bf16[512,128]{1,0:T(8,128)(2,1)S(1)}, u32[]{:S(2)}, u32[]{:S(2)}) collective-permute-start(bf16[512,128]{1,0:T(8,128)(2,1)S(1)} %constant_dynamic-update-slice_fusion.a), channel_id=1, source_target_pairs={{0,80},{8,56},{16,96},{24,72},{32,112},{40,88},{48,0},{56,104},{64... | collective-permute-start | bytes 393224 | tf_op jit(solution)/shard_map/ppermute | solution.py:41
  13.9 0.7 copy-start.4
  14.5 0.7 copy-start.5
  20.4 5.8 %collective-permute-start.6 = (bf16[768,128]{1,0:T(8,128)(2,1)S(1)}, bf16[768,128]{1,0:T(8,128)(2,1)S(1)}, u32[]{:S(2)}, u32[]{:S(2)}) collective-permute-start(bf16[768,128]{1,0:T(8,128)(2,1)S(1)} %append.3.refs_0_), channel_id=1, source_target_pairs={{0,112},{8,24},{16,0},{24,40},{32,16},{40,56},{48,32},{56,72},{64,... | collective-permute-start | bytes 589832 | tf_op jit(solution)/shard_map/ppermute | solution.py:41
  20.5 1.0 copy-start.1
  21.5 0.8 copy-start.3
  22.3 0.7 copy-start.6
  23.7 15.6 %collective-permute-start.11 = (bf16[784,128]{1,0:T(8,128)(2,1)S(1)}, bf16[784,128]{1,0:T(8,128)(2,1)S(1)}, u32[]{:S(2)}, u32[]{:S(2)}) collective-permute-start(bf16[784,128]{1,0:T(8,128)(2,1)S(1)} %pack_up.1.a), channel_id=1, source_target_pairs={{0,4},{1,5},{2,6},{3,7},{4,0},{5,1},{6,2},{7,3},{8,12},{9,13},{10,... | collective-permute-start | bytes 602120 | tf_op jit(solution)/shard_map/ppermute | solution.py:29
  26.3 13.1 %collective-permute-start.7 = (bf16[768,128]{1,0:T(8,128)(2,1)S(1)}, bf16[768,128]{1,0:T(8,128)(2,1)S(1)}, u32[]{:S(2)}, u32[]{:S(2)}) collective-permute-start(bf16[768,128]{1,0:T(8,128)(2,1)S(1)} %collective-permute-done.6), channel_id=1, source_target_pairs={{0,128},{8,136},{16,144},{24,152},{32,160},{40,168},{48,176},{56,1... | collective-permute-start | bytes 589832 | tf_op jit(solution)/shard_map/ppermute | solution.py:25
  26.5 10.0 %collective-permute-start.8 = (bf16[512,128]{1,0:T(8,128)(2,1)S(1)}, bf16[512,128]{1,0:T(8,128)(2,1)S(1)}, u32[]{:S(2)}, u32[]{:S(2)}) collective-permute-start(bf16[512,128]{1,0:T(8,128)(2,1)S(1)} %collective-permute-done.5.refs_0_), channel_id=1, source_target_pairs={{0,128},{8,136},{16,144},{24,152},{32,160},{40,168},{48,176},{56,1... | collective-permute-start | bytes 393224 | tf_op jit(solution)/shard_map/ppermute | solution.py:25
  27.7 11.6 %collective-permute-start.9 = (bf16[512,128]{1,0:T(8,128)(2,1)S(1)}, bf16[512,128]{1,0:T(8,128)(2,1)S(1)}, u32[]{:S(2)}, u32[]{:S(2)}) collective-permute-start(bf16[512,128]{1,0:T(8,128)(2,1)S(1)} %collective-permute-done.4.b), channel_id=1, source_target_pairs={{0,128},{8,136},{16,144},{24,152},{32,160},{40,168},{48,176},{56,1... | collective-permute-start | bytes 393224 | tf_op jit(solution)/shard_map/ppermute | solution.py:25
  39.4 11.7 %collective-permute-start.13 = (bf16[1568,128]{1,0:T(8,128)(2,1)S(1)}, bf16[1568,128]{1,0:T(8,128)(2,1)S(1)}, u32[]{:S(2)}, u32[]{:S(2)}) collective-permute-start(bf16[1568,128]{1,0:T(8,128)(2,1)S(1)} %append.4.refs_0_), channel_id=1, source_target_pairs={{0,3},{1,0},{2,1},{3,2},{4,7},{5,4},{6,5},{7,6},{8,11},{9,8},{10,9... | collective-permute-start | bytes 1204232 | tf_op jit(solution)/shard_map/ppermute | solution.py:29
  42.2 9.1 %collective-permute-start.12 = (bf16[1568,128]{1,0:T(8,128)(2,1)S(1)}, bf16[1568,128]{1,0:T(8,128)(2,1)S(1)}, u32[]{:S(2)}, u32[]{:S(2)}) collective-permute-start(bf16[1568,128]{1,0:T(8,128)(2,1)S(1)} %append.4.refs_0_), channel_id=1, source_target_pairs={{0,1},{1,2},{2,3},{3,0},{4,5},{5,6},{6,7},{7,4},{8,9},{9,10},{10,1... | collective-permute-start | bytes 1204232 | tf_op jit(solution)/shard_map/ppermute | solution.py:29
  48.6 26.9 %copy-start.2 = (bf16[128,1024]{1,0:T(8,128)(2,1)S(1)}, bf16[128,1024]{1,0:T(8,128)(2,1)}, u32[]{:S(2)}) copy-start(bf16[128,1024]{1,0:T(8,128)(2,1)} %w_own.1) | copy-start | bytes 786436
  48.6 3.4 %collective-permute-start.10 = (f32[2,128,128]{2,1,0:T(8,128)S(1)}, f32[2,128,128]{2,1,0:T(8,128)S(1)}, u32[]{:S(2)}, u32[]{:S(2)}) collective-permute-start(f32[2,128,128]{2,1,0:T(8,128)S(1)} %get-tuple-element.29), channel_id=1, source_target_pairs={{0,8},{8,0},{16,24},{24,16},{32,40},{40,32},{48,56},{56,48},{64,72... | collective-permute-start | bytes 393224 | tf_op jit(solution)/shard_map/ppermute | solution.py:25
  52.1 7.8 %collective-permute-start.18 = (bf16[784,128]{1,0:T(8,128)(2,1)S(1)}, bf16[784,128]{1,0:T(8,128)(2,1)S(1)}, u32[]{:S(2)}, u32[]{:S(2)}) collective-permute-start(bf16[784,128]{1,0:T(8,128)(2,1)S(1)} %get-tuple-element.31), channel_id=1, source_target_pairs={{0,1},{1,2},{2,3},{3,0},{4,5},{5,6},{6,7},{7,4},{8,9},{9,10},{10,1... | collective-permute-start | bytes 602120 | tf_op jit(solution)/shard_map/ppermute | solution.py:29
  52.5 7.4 %collective-permute-start.19 = (bf16[784,128]{1,0:T(8,128)(2,1)S(1)}, bf16[784,128]{1,0:T(8,128)(2,1)S(1)}, u32[]{:S(2)}, u32[]{:S(2)}) collective-permute-start(bf16[784,128]{1,0:T(8,128)(2,1)S(1)} %get-tuple-element.32), channel_id=1, source_target_pairs={{0,3},{1,0},{2,1},{3,2},{4,7},{5,4},{6,5},{7,6},{8,11},{9,8},{10,9... | collective-permute-start | bytes 602120 | tf_op jit(solution)/shard_map/ppermute | solution.py:29
  55.2 4.6 %collective-permute-start.14 = (bf16[256,128]{1,0:T(8,128)(2,1)S(1)}, bf16[256,128]{1,0:T(8,128)(2,1)S(1)}, u32[]{:S(2)}, u32[]{:S(2)}) collective-permute-start(bf16[256,128]{1,0:T(8,128)(2,1)S(1)} %bitcast.32), channel_id=1, source_target_pairs={{0,4},{1,5},{2,6},{3,7},{4,0},{5,1},{6,2},{7,3},{8,12},{9,13},{10,... | collective-permute-start | bytes 196616 | tf_op jit(solution)/shard_map/ppermute | solution.py:29
  61.3 14.2 %collective-permute-start.20 = (bf16[1024,512]{1,0:T(8,128)(2,1)S(1)}, bf16[1024,512]{1,0:T(8,128)(2,1)S(1)}, u32[]{:S(2)}, u32[]{:S(2)}) collective-permute-start(bf16[1024,512]{1,0:T(8,128)(2,1)S(1)} %get-tuple-element.33.w0), channel_id=1, source_target_pairs={{0,8},{8,0},{16,24},{24,16},{32,40},{40,32},{48,56},{56,48},{64,72... | collective-permute-start | bytes 3145736 | tf_op jit(solution)/shard_map/ppermute | solution.py:25
  65.8 6.6 %collective-permute-start.17 = (bf16[512,128]{1,0:T(8,128)(2,1)S(1)}, bf16[512,128]{1,0:T(8,128)(2,1)S(1)}, u32[]{:S(2)}, u32[]{:S(2)}) collective-permute-start(bf16[512,128]{1,0:T(8,128)(2,1)S(1)} %pad_maximum_fusion.2.refs_5_.p0), channel_id=1, source_target_pairs={{0,2},{1,3},{2,0},{3,1},{4,6},{5,7},{6,4},{7,5},{8,10},{9,11},{10,... | collective-permute-start | bytes 393224 | tf_op jit(solution)/shard_map/ppermute | solution.py:29
  65.8 7.9 %collective-permute-start.16 = (bf16[512,128]{1,0:T(8,128)(2,1)S(1)}, bf16[512,128]{1,0:T(8,128)(2,1)S(1)}, u32[]{:S(2)}, u32[]{:S(2)}) collective-permute-start(bf16[512,128]{1,0:T(8,128)(2,1)S(1)} %pad_maximum_fusion.2.refs_5_.p0), channel_id=1, source_target_pairs={{0,3},{1,0},{2,1},{3,2},{4,7},{5,4},{6,5},{7,6},{8,11},{9,8},{10,9... | collective-permute-start | bytes 393224 | tf_op jit(solution)/shard_map/ppermute | solution.py:29
  66.8 8.7 %collective-permute-start.15 = (bf16[512,128]{1,0:T(8,128)(2,1)S(1)}, bf16[512,128]{1,0:T(8,128)(2,1)S(1)}, u32[]{:S(2)}, u32[]{:S(2)}) collective-permute-start(bf16[512,128]{1,0:T(8,128)(2,1)S(1)} %pad_maximum_fusion.2.refs_5_.p0), channel_id=1, source_target_pairs={{0,1},{1,2},{2,3},{3,0},{4,5},{5,6},{6,7},{7,4},{8,9},{9,10},{10,1... | collective-permute-start | bytes 393224 | tf_op jit(solution)/shard_map/ppermute | solution.py:29
  77.8 1.7 %collective-permute-start.22 = (f32[64,1152]{1,0:T(8,128)S(1)}, f32[64,1152]{1,0:T(8,128)S(1)}, u32[]{:S(2)}, u32[]{:S(2)}) collective-permute-start(f32[64,1152]{1,0:T(8,128)S(1)} %get-tuple-element.39), channel_id=1, source_target_pairs={{0,8},{8,0},{16,24},{24,16},{32,40},{40,32},{48,56},{56,48},{64,72... | collective-permute-start | bytes 884744 | tf_op jit(solution)/shard_map/ppermute | solution.py:25
  78.2 2.8 %collective-permute-start.21 = (bf16[2,128,128]{2,1,0:T(8,128)(2,1)S(1)}, bf16[2,128,128]{2,1,0:T(8,128)(2,1)S(1)}, u32[]{:S(2)}, u32[]{:S(2)}) collective-permute-start(bf16[2,128,128]{2,1,0:T(8,128)(2,1)S(1)} %bitcast.30), channel_id=1, source_target_pairs={{0,8},{8,0},{16,24},{24,16},{32,40},{40,32},{48,56},{56,48},{64,72... | collective-permute-start | bytes 196616 | tf_op jit(solution)/shard_map/ppermute | solution.py:25
  79.5 7.6 %collective-permute-start.24 = (bf16[32,1152]{1,0:T(8,128)(2,1)S(1)}, bf16[32,1152]{1,0:T(8,128)(2,1)S(1)}, u32[]{:S(2)}, u32[]{:S(2)}) collective-permute-start(bf16[32,1152]{1,0:T(8,128)(2,1)S(1)} %fusion.send), channel_id=1, source_target_pairs={{0,128},{8,136},{16,144},{24,152},{32,160},{40,168},{48,176},{56,1... | collective-permute-start | bytes 221192 | tf_op jit(solution)/shard_map/ppermute | solution.py:25
  87.0 17.2 %collective-permute-start.23 = (bf16[16,128,128]{2,1,0:T(8,128)(2,1)S(1)}, bf16[16,128,128]{2,1,0:T(8,128)(2,1)S(1)}, u32[]{:S(2)}, u32[]{:S(2)}) collective-permute-start(bf16[16,128,128]{2,1,0:T(8,128)(2,1)S(1)} %get-tuple-element.41.far), channel_id=1, source_target_pairs={{0,128},{8,136},{16,144},{24,152},{32,160},{40,168},{48,176},{56,1... | collective-permute-start | bytes 1572872 | tf_op jit(solution)/shard_map/ppermute | solution.py:25
  87.1 1.6 %collective-permute-start.25 = (bf16[32,1152]{1,0:T(8,128)(2,1)S(1)}, bf16[32,1152]{1,0:T(8,128)(2,1)S(1)}, u32[]{:S(2)}, u32[]{:S(2)}) collective-permute-start(bf16[32,1152]{1,0:T(8,128)(2,1)S(1)} %quarter_up.1.own), channel_id=1, source_target_pairs={{0,8},{8,0},{16,24},{24,16},{32,40},{40,32},{48,56},{56,48},{64,72... | collective-permute-start | bytes 221192 | tf_op jit(solution)/shard_map/ppermute | solution.py:25
  88.8 8.2 %collective-permute-start.27 = (bf16[64,1152]{1,0:T(8,128)(2,1)S(1)}, bf16[64,1152]{1,0:T(8,128)(2,1)S(1)}, u32[]{:S(2)}, u32[]{:S(2)}) collective-permute-start(bf16[64,1152]{1,0:T(8,128)(2,1)S(1)} %pad_maximum_fusion.a), channel_id=1, source_target_pairs={{0,96},{8,40},{16,112},{24,56},{32,0},{40,72},{48,16},{56,88},{64,... | collective-permute-start | bytes 442376 | tf_op jit(solution)/shard_map/ppermute | solution.py:41
  94.1 7.3 %collective-permute-start.26 = (bf16[64,1152]{1,0:T(8,128)(2,1)S(1)}, bf16[64,1152]{1,0:T(8,128)(2,1)S(1)}, u32[]{:S(2)}, u32[]{:S(2)}) collective-permute-start(bf16[64,1152]{1,0:T(8,128)(2,1)S(1)} %pad_maximum_fusion.a), channel_id=1, source_target_pairs={{0,80},{8,56},{16,96},{24,72},{32,112},{40,88},{48,0},{56,104},{64... | collective-permute-start | bytes 442376 | tf_op jit(solution)/shard_map/ppermute | solution.py:41
  101.4 10.6 %collective-permute-start.32 = (bf16[96,1152]{1,0:T(8,128)(2,1)S(1)}, bf16[96,1152]{1,0:T(8,128)(2,1)S(1)}, u32[]{:S(2)}, u32[]{:S(2)}) collective-permute-start(bf16[96,1152]{1,0:T(8,128)(2,1)S(1)} %append.5.ready), channel_id=1, source_target_pairs={{0,112},{8,24},{16,0},{24,40},{32,16},{40,56},{48,32},{56,72},{64,... | collective-permute-start | bytes 663560 | tf_op jit(solution)/shard_map/ppermute | solution.py:41
  104.3 7.7 %collective-permute-start.28 = (bf16[6,128,128]{2,1,0:T(8,128)(2,1)S(1)}, bf16[6,128,128]{2,1,0:T(8,128)(2,1)S(1)}, u32[]{:S(2)}, u32[]{:S(2)}) collective-permute-start(bf16[6,128,128]{2,1,0:T(8,128)(2,1)S(1)} %get-tuple-element.43), channel_id=1, source_target_pairs={{0,16},{8,120},{16,32},{24,8},{32,48},{40,24},{48,64},{56,40},{64,... | collective-permute-start | bytes 589832 | tf_op jit(solution)/shard_map/ppermute | solution.py:41
  104.4 7.6 %collective-permute-start.29 = (bf16[4,128,128]{2,1,0:T(8,128)(2,1)S(1)}, bf16[4,128,128]{2,1,0:T(8,128)(2,1)S(1)}, u32[]{:S(2)}, u32[]{:S(2)}) collective-permute-start(bf16[4,128,128]{2,1,0:T(8,128)(2,1)S(1)} %get-tuple-element.44), channel_id=1, source_target_pairs={{0,32},{8,104},{16,48},{24,120},{32,64},{40,8},{48,80},{56,24},{64... | collective-permute-start | bytes 393224 | tf_op jit(solution)/shard_map/ppermute | solution.py:41
  112.1 6.7 %collective-permute-start.33 = (bf16[96,1152]{1,0:T(8,128)(2,1)S(1)}, bf16[96,1152]{1,0:T(8,128)(2,1)S(1)}, u32[]{:S(2)}, u32[]{:S(2)}) collective-permute-start(bf16[96,1152]{1,0:T(8,128)(2,1)S(1)} %peer_rows.1), channel_id=1, source_target_pairs={{0,8},{8,0},{16,24},{24,16},{32,40},{40,32},{48,56},{56,48},{64,72... | collective-permute-start | bytes 663560 | tf_op jit(solution)/shard_map/ppermute | solution.py:25
  115.5 7.3 %collective-permute-start.30 = (bf16[4,128,128]{2,1,0:T(8,128)(2,1)S(1)}, bf16[4,128,128]{2,1,0:T(8,128)(2,1)S(1)}, u32[]{:S(2)}, u32[]{:S(2)}) collective-permute-start(bf16[4,128,128]{2,1,0:T(8,128)(2,1)S(1)} %ride.1.t), channel_id=1, source_target_pairs={{0,48},{8,88},{16,64},{24,104},{32,80},{40,120},{48,96},{56,8},{64... | collective-permute-start | bytes 393224 | tf_op jit(solution)/shard_map/ppermute | solution.py:41
  119.5 6.3 %collective-permute-start.34 = (bf16[32,1152]{1,0:T(8,128)(2,1)S(1)}, bf16[32,1152]{1,0:T(8,128)(2,1)S(1)}, u32[]{:S(2)}, u32[]{:S(2)}) collective-permute-start(bf16[32,1152]{1,0:T(8,128)(2,1)S(1)} %sum_z.1), channel_id=1, source_target_pairs={{0,128},{8,136},{16,144},{24,152},{32,160},{40,168},{48,176},{56,1... | collective-permute-start | bytes 221192 | tf_op jit(solution)/shard_map/ppermute | solution.py:25
  122.9 3.9 %collective-permute-start.31 = (f32[2,128,128]{2,1,0:T(8,128)S(1)}, f32[2,128,128]{2,1,0:T(8,128)S(1)}, u32[]{:S(2)}, u32[]{:S(2)}) collective-permute-start(f32[2,128,128]{2,1,0:T(8,128)S(1)} %slice.35), channel_id=1, source_target_pairs={{0,8},{8,0},{16,24},{24,16},{32,40},{40,32},{48,56},{56,48},{64,72... | collective-permute-start | bytes 393224 | tf_op jit(solution)/shard_map/ppermute | solution.py:25
  125.8 1.7 %collective-permute-start.35 = (bf16[64,1152]{1,0:T(8,128)(2,1)S(1)}, bf16[64,1152]{1,0:T(8,128)(2,1)S(1)}, u32[]{:S(2)}, u32[]{:S(2)}) collective-permute-start(bf16[64,1152]{1,0:T(8,128)(2,1)S(1)} %pad_maximum_fusion.1.mine), channel_id=1, source_target_pairs={{0,8},{8,0},{16,24},{24,16},{32,40},{40,32},{48,56},{56,48},{64,72... | collective-permute-start | bytes 442376 | tf_op jit(solution)/shard_map/ppermute | solution.py:25

commit v4 on v3

--- a/solution.py
+++ b/solution.py
@@ -73,7 +73,7 @@
         in_specs=[SM, HB, HB, VM] + [ANY] * len(ready),
         out_specs=VM,
         scratch_shapes=[pltpu.SemaphoreType.DMA((5,))],
-        compiler_params=params(4),
+        compiler_params=params(60),
         cost_estimate=cost(0, 1 << 19),
         name="pack_up",
     )(ids, w, og, bias, *ready)
@@ -98,23 +98,38 @@
     )(a, b, *ready)
 
 
-def settle_body(mine, came, u, d, agg, a, b):
-    agg[...] = (mine[...] + came[...]).astype(bf16)
+def turn_body(u, d, a, b):
     a[...] = u[0:784, :]
     b[...] = d[784:1568, :]
 
 
-def settle(mine, came, u, d):
+def turn(u, d):
     half = jax.ShapeDtypeStruct((784, B), bf16)
     return pl.pallas_call(
+        turn_body,
+        out_shape=(half, half),
+        in_specs=[VM, VM],
+        out_specs=(VM, VM),
+        compiler_params=params(4),
+        cost_estimate=cost(0, 1 << 18),
+        name="turn",
+    )(u, d)
+
+
+def settle_body(mine, came, a, b, agg):
+    agg[...] = (mine[...] + came[...]).astype(bf16)
+
+
+def settle(mine, came, a, b):
+    return pl.pallas_call(
         settle_body,
-        out_shape=(jax.ShapeDtypeStruct((2, B, B), bf16), half, half),
-        in_specs=[VM] * 4,
-        out_specs=(VM, VM, VM),
+        out_shape=jax.ShapeDtypeStruct((2, B, B), bf16),
+        in_specs=[VM, VM, ANY, ANY],
+        out_specs=VM,
         compiler_params=params(4),
         cost_estimate=cost(0, 1 << 18),
         name="settle",
-    )(mine, came, u, d)
+    )(mine, came, a, b)
 
 
 def plan_body(ids, c0, d0, c1, d1, out):
@@ -165,7 +180,7 @@
 
 
 def agg_body(plan, tiles, more, *refs):
-    mine, theirs, src, acc, sem = refs[8:]
+    mine, theirs, src, acc, sem = refs[10:]
     both, x0, o14, o2, o3, p14, p2, p3 = refs[0:8]
     copies = []
 
@@ -191,12 +206,12 @@
     theirs[...] = acc[2:4]
 
 
-def aggregate(plan, tiles, more, pieces):
+def aggregate(plan, tiles, more, pieces, *ready):
     parts = [v.reshape(-1, B, B) for v in pieces]
     return pl.pallas_call(
         agg_body,
         out_shape=(jax.ShapeDtypeStruct((2, B, B), f32), jax.ShapeDtypeStruct((2, B, B), f32)),
-        in_specs=[SM, VM, VM] + [HB] * 8,
+        in_specs=[SM, VM, VM] + [HB] * 8 + [ANY] * 2,
         out_specs=(VM, VM),
         scratch_shapes=[
             pltpu.VMEM((33, B, B), bf16),
@@ -206,7 +221,7 @@
         compiler_params=params(12),
         cost_estimate=cost(2 * 64 * B**3, 4 << 20),
         name="aggregate",
-    )(plan, tiles, more, *parts)
+    )(plan, tiles, more, *parts, *ready)
 
 
 def lay_body(ids, *refs):
@@ -376,21 +391,21 @@
     )(near, came, ready)
 
 
-def ride_body(t3, r14, ready, out):
+def ride_body(t3, r14, out):
     out[0:2] = (t3[0:2] + r14[4:6].astype(f32)).astype(bf16)
     out[2:4] = t3[2:4].astype(bf16)
 
 
-def ride(t3, r14, ready):
+def ride(t3, r14):
     return pl.pallas_call(
         ride_body,
         out_shape=jax.ShapeDtypeStruct((4, B, B), bf16),
-        in_specs=[VM, VM, ANY],
+        in_specs=[VM, VM],
         out_specs=VM,
         compiler_params=params(4),
         cost_estimate=cost(0, 1 << 18),
         name="ride",
-    )(t3, r14, ready)
+    )(t3, r14)
 
 
 def rows_body(d1, d2, d3, t, out):
@@ -470,18 +485,20 @@
     more = row_send(swap, dc=1)
     o3, o2 = spin_send(both, 3, -1), spin_send(both, 2, -1)
     plan = plan_tiles(ids, col_blocks, dest_blocks, lists[0], lists[1])
-    ext = append(768, both, o3, o2, x0, plan)
+
+    pack = pack_up(ids, weight, out_grad, bias_vector[None, :])
+    pack_x = feat_send(pack, dx=1)
+
+    pair = append(1568, pack, pack_x)
+    ext = append(768, both, o3, o2, x0, plan, pair)
     o14 = spin_send(ext, 1, -1)
     p3, p2, p14 = row_send(o3, dx=1), row_send(o2, dx=1), row_send(o14, dx=1)
-
-    pack = pack_up(ids, weight, out_grad, bias_vector[None, :], ext)
-    pair = append(1568, pack, feat_send(pack, dx=1), p3, p2, p14)
     wu, wd = feat_send(pair, dy=1), feat_send(pair, dy=-1)
 
-    mine, theirs = aggregate(plan, adj_tiles, more, (both_a, x0, o14, o2, o3, p14, p2, p3))
-    aggregated, wa, wb = settle(mine, row_send(theirs, dc=1), wu, wd)
-    aggregated = aggregated.reshape(256, B)
+    wa, wb = turn(wu, wd)
+    mine, theirs = aggregate(plan, adj_tiles, more, (both_a, x0, o14, o2, o3, p14, p2, p3), wa, wb)
     wa, wb = feat_send(wa, dy=1), feat_send(wb, dy=-1)
+    aggregated = settle(mine, row_send(theirs, dc=1), wa, wb).reshape(256, B)
 
     q = jnp.concatenate([aggregated, feat_send(aggregated, dx=1)], axis=0)
     w0, og, bias = lay_out(ids, (pair, wu, wd, wa, wb), q)
@@ -503,10 +520,10 @@
 
     t14, t2, t3, t0 = join(near, came, last)
     r14, r2 = spin_send(t14, 1), spin_send(t2, 2)
-    t3 = ride(t3, r14, r2)
+    t3 = ride(t3, r14)
     r3 = spin_send(t3, 3)
 
-    e = row_send(peer_rows(d1, d2, d3, t3), dc=1)
+    e = row_send(peer_rows(d1, d2, d3, r2), dc=1)
     scale = float(256 * lax.axis_size("row")) ** (-0.5)
     total = sum_z(scale, ids, quarter, d1, d2, d3, e, t3)
     two = jnp.concatenate([total, row_send(total, dx=1)], axis=0)

time: 130 us -> 124 us (0.954)
  starting transfers between devices: 60.9 us -> 52.8 us
  waiting for transfers between devices: 39.1 us -> 41.8 us
    ppermute x9, waiting for transfers between devices: 12.1 us -> 22.3 us  [spin_send(): return lax.ppermute(v, 'row', perm)]
    ppermute x18, waiting for transfers between devices: 15.4 us -> 7.11 us  [row_send(): return lax.ppermute(v, 'row', perm)]
    ppermute x9, starting transfers between devices: 26.5 us -> 19.2 us  [spin_send(): return lax.ppermute(v, 'row', perm)]
    pallas_call x1, Pallas kernels: 0.73 us -> 2.31 us  [pack_up(): pl.pallas_call(pack_body, out_shape=jax.ShapeDtypeStruct((784, B), bf16),...]
  transfers between devices with their start and end apart: 36 -> 36, of which waited for: 17 -> 17; matrix products, arithmetic and copies ran while one was open for 2% -> 2% of each run, Pallas kernels for 13% -> 14%
where the time goes in v4:
time: 124 us
  starting transfers between devices  52.8 us (43%)
  waiting for transfers between devices  41.8 us (34%)
  Pallas kernels  22.1 us (18%)
  local copies, waits for them, and re-layouts  4.29 us (3%)
  other arithmetic  2.04 us (2%)
    ppermute x18, starting transfers between devices, row_send(): return lax.ppermute(v, 'row', perm)  22.4 us
    ppermute x9, waiting for transfers between devices, spin_send(): return lax.ppermute(v, 'row', perm)  22.3 us
    ppermute x9, starting transfers between devices, spin_send(): return lax.ppermute(v, 'row', perm)  19.2 us
    ppermute x9, waiting for transfers between devices, feat_send(): lax.ppermute(v, 'feat', [(i, (i >> 2 ^ dx) << 2 | i + dy & 3) for i in ra...  12.4 us
    ppermute x9, starting transfers between devices, feat_send(): lax.ppermute(v, 'feat', [(i, (i >> 2 ^ dx) << 2 | i + dy & 3) for i in ra...  11.1 us
    ppermute x18, waiting for transfers between devices, row_send(): return lax.ppermute(v, 'row', perm)  7.11 us
    pallas_call x1, Pallas kernels, aggregate(): pl.pallas_call(agg_body, out_shape=(jax.ShapeDtypeStruct((2, B, B), f32),...  5.86 us
    pallas_call x1, Pallas kernels, spread(): pl.pallas_call(spread_body, out_shape=(jax.ShapeDtypeStruct((16, B, B), f...  5.24 us
  transfers between devices with their start and end apart: 36, of which 17 were waited for; matrix products, arithmetic and copies ran while one was open for 2% of the time, Pallas kernels for 14%

profile of v4, /device:TPU:1, one launch (start us, length us, event | category | flops | bytes accessed | tf_op | source)
XLA Modules:
  0.0 123.9 jit_solution(15578553281734269777)
XLA Ops:
  0.6 3.3 %collective-permute-start.1 = (bf16[256,128]{1,0:T(8,128)(2,1)}, bf16[256,128]{1,0:T(8,128)(2,1)S(1)}, u32[]{:S(2)}, u32[]{:S(2)}) collective-permute-start(bf16[256,128]{1,0:T(8,128)(2,1)} %param.7), channel_id=1, source_target_pairs={{0,8},{8,0},{16,24},{24,16},{32,40},{40,32},{48,56},{56,48},{64,72... | collective-permute-start | bytes 196616 | tf_op jit(solution)/shard_map/ppermute | solution.py:25
  4.0 0.8 constant_dynamic-update-slice_fusion.1
  6.1 2.3 %pack_up.1.a = bf16[784,128]{1,0:T(8,128)(2,1)} custom-call(s32[2]{0:T(128)} %pad_add_fusion.1.ids, bf16[128,1024]{1,0:T(8,128)(2,1)} %w_own.1, bf16[256,128]{1,0:T(8,128)(2,1)} %og.1, bf16[1,128]{1,0:T(2,128)(2,1)} %bitcast.37), custom_call_target="tpu_custom_call" | custom-call | bytes 524288 | tf_op jit(solution)/shard_map/pack_up/pallas_call | solution.py:70
  8.4 1.1 collective-permute-start.6
  10.5 0.7 collective-permute-start
  11.2 3.0 %collective-permute-start.5 = (bf16[512,128]{1,0:T(8,128)(2,1)S(1)}, bf16[512,128]{1,0:T(8,128)(2,1)S(1)}, u32[]{:S(2)}, u32[]{:S(2)}) collective-permute-start(bf16[512,128]{1,0:T(8,128)(2,1)S(1)} %constant_dynamic-update-slice_fusion.a), channel_id=1, source_target_pairs={{0,96},{8,40},{16,112},{24,56},{32,0},{40,72},{48,16},{56,88},{64,... | collective-permute-start | bytes 393224 | tf_op jit(solution)/shard_map/ppermute | solution.py:41
  14.2 2.4 %collective-permute-done.6.b = bf16[784,128]{1,0:T(8,128)(2,1)S(1)} collective-permute-done((bf16[784,128]{1,0:T(8,128)(2,1)}, bf16[784,128]{1,0:T(8,128)(2,1)S(1)}, u32[]{:S(2)}, u32[]{:S(2)}) %collective-permute-start.6) | collective-permute-done | bytes 200736 | tf_op jit(solution)/shard_map/ppermute | solution.py:29
  16.7 2.6 %collective-permute-start.4 = (bf16[512,128]{1,0:T(8,128)(2,1)S(1)}, bf16[512,128]{1,0:T(8,128)(2,1)S(1)}, u32[]{:S(2)}, u32[]{:S(2)}) collective-permute-start(bf16[512,128]{1,0:T(8,128)(2,1)S(1)} %constant_dynamic-update-slice_fusion.a), channel_id=1, source_target_pairs={{0,80},{8,56},{16,96},{24,72},{32,112},{40,88},{48,0},{56,104},{64... | collective-permute-start | bytes 393224 | tf_op jit(solution)/shard_map/ppermute | solution.py:41
  19.3 0.9 copy-done.2
  20.3 2.8 %collective-permute-start.12 = (bf16[1568,128]{1,0:T(8,128)(2,1)S(1)}, bf16[1568,128]{1,0:T(8,128)(2,1)S(1)}, u32[]{:S(2)}, u32[]{:S(2)}) collective-permute-start(bf16[1568,128]{1,0:T(8,128)(2,1)S(1)} %append.3.refs_3_.refs_0_), channel_id=1, source_target_pairs={{0,3},{1,0},{2,1},{3,2},{4,7},{5,4},{6,5},{7,6},{8,11},{9,8},{10,9... | collective-permute-start | bytes 1204232 | tf_op jit(solution)/shard_map/ppermute | solution.py:29
  25.1 2.7 %plan_tiles.1.refs_2_.plan = s32[160]{0:T(256)S(1)} custom-call(s32[2]{0:T(128)S(1)} %copy-done.3, s32[64]{0:T(128)S(1)} %copy-done.5, s32[64]{0:T(128)S(1)} %copy-done.6, s32[64]{0:T(128)S(1)} %get-tuple-element.47.c1, s32[64]{0:T(128)S(1)} %get-tuple-element.46.d1), custom_call_target="tpu_custom_call" | custom-call | flops 10000 | bytes 4096 | tf_op jit(solution)/shard_map/plan_tiles/pallas_call | solution.py:160
  27.8 2.9 %collective-permute-start.7 = (bf16[768,128]{1,0:T(8,128)(2,1)S(1)}, bf16[768,128]{1,0:T(8,128)(2,1)S(1)}, u32[]{:S(2)}, u32[]{:S(2)}) collective-permute-start(bf16[768,128]{1,0:T(8,128)(2,1)S(1)} %append.4), channel_id=1, source_target_pairs={{0,112},{8,24},{16,0},{24,40},{32,16},{40,56},{48,32},{56,72},{64,... | collective-permute-start | bytes 589832 | tf_op jit(solution)/shard_map/ppermute | solution.py:41
  30.8 3.2 %collective-permute-done.7 = bf16[768,128]{1,0:T(8,128)(2,1)S(1)} collective-permute-done((bf16[768,128]{1,0:T(8,128)(2,1)S(1)}, bf16[768,128]{1,0:T(8,128)(2,1)S(1)}, u32[]{:S(2)}, u32[]{:S(2)}) %collective-permute-start.7) | collective-permute-done | bytes 196640 | tf_op jit(solution)/shard_map/ppermute | solution.py:41
  34.0 1.2 collective-permute-start.8
  35.4 1.2 collective-permute-start.10
  36.8 3.1 %collective-permute-done.9 = bf16[512,128]{1,0:T(8,128)(2,1)S(1)} collective-permute-done((bf16[512,128]{1,0:T(8,128)(2,1)S(1)}, bf16[512,128]{1,0:T(8,128)(2,1)S(1)}, u32[]{:S(2)}, u32[]{:S(2)}) %collective-permute-start.9) | collective-permute-done | bytes 131104 | tf_op jit(solution)/shard_map/ppermute | solution.py:25
  39.9 2.4 %collective-permute-start.15 = (bf16[784,128]{1,0:T(8,128)(2,1)S(1)}, bf16[784,128]{1,0:T(8,128)(2,1)S(1)}, u32[]{:S(2)}, u32[]{:S(2)}) collective-permute-start(bf16[784,128]{1,0:T(8,128)(2,1)S(1)} %get-tuple-element.28.refs_9_), channel_id=1, source_target_pairs={{0,3},{1,0},{2,1},{3,2},{4,7},{5,4},{6,5},{7,6},{8,11},{9,8},{10,9... | collective-permute-start | bytes 602120 | tf_op jit(solution)/shard_map/ppermute | solution.py:29
  42.3 5.9 %aggregate.1 = (f32[2,128,128]{2,1,0:T(8,128)S(1)}, f32[2,128,128]{2,1,0:T(8,128)S(1)}) custom-call(s32[160]{0:T(256)S(1)} %plan_tiles.1.refs_2_.plan, bf16[64,128,128]{2,1,0:T(8,128)(2,1)S(1)} %copy-done, bf16[64,128,128]{2,1,0:T(8,128)(2,1)} %collective-permute-done.2.more, bf16[4,128,128]{2,1,0:T(8,128)(2,1)S(1)} %bitcast.22, ...), custom_call_target="tpu_custom_call" | custom-call | flops 268435456 | bytes 4194304 | tf_op jit(solution)/shard_map/aggregate/pallas_call | solution.py:211
  48.2 6.5 %collective-permute-start.13 = (f32[2,128,128]{2,1,0:T(8,128)S(1)}, f32[2,128,128]{2,1,0:T(8,128)S(1)}, u32[]{:S(2)}, u32[]{:S(2)}) collective-permute-start(f32[2,128,128]{2,1,0:T(8,128)S(1)} %get-tuple-element.30), channel_id=1, source_target_pairs={{0,8},{8,0},{16,24},{24,16},{32,40},{40,32},{48,56},{56,48},{64,72... | collective-permute-start | bytes 393224 | tf_op jit(solution)/shard_map/ppermute | solution.py:25
  54.7 1.0 collective-permute-done.13.came
  55.7 3.0 %collective-permute-start.16 = (bf16[256,128]{1,0:T(8,128)(2,1)S(1)}, bf16[256,128]{1,0:T(8,128)(2,1)S(1)}, u32[]{:S(2)}, u32[]{:S(2)}) collective-permute-start(bf16[256,128]{1,0:T(8,128)(2,1)S(1)} %bitcast.26), channel_id=1, source_target_pairs={{0,4},{1,5},{2,6},{3,7},{4,0},{5,1},{6,2},{7,3},{8,12},{9,13},{10,... | collective-permute-start | bytes 196616 | tf_op jit(solution)/shard_map/ppermute | solution.py:29
  58.7 1.9 %collective-permute-done.16 = bf16[256,128]{1,0:T(8,128)(2,1)S(1)} collective-permute-done((bf16[256,128]{1,0:T(8,128)(2,1)S(1)}, bf16[256,128]{1,0:T(8,128)(2,1)S(1)}, u32[]{:S(2)}, u32[]{:S(2)}) %collective-permute-start.16) | collective-permute-done | bytes 65568 | tf_op jit(solution)/shard_map/ppermute | solution.py:29
  60.6 1.4 %lay_out.1 = (bf16[1024,512]{1,0:T(8,128)(2,1)S(1)}, bf16[256,1024]{1,0:T(8,128)(2,1)S(1)}, f32[8,1024]{1,0:T(8,128)S(1)}) custom-call(s32[2]{0:T(128)S(1)} %copy-done.4, bf16[1568,128]{1,0:T(8,128)(2,1)S(1)} %append.3.refs_3_.refs_0_, bf16[1568,128]{1,0:T(8,128)(2,1)S(1)} %collective-permute-done.11.u.refs_1_, ...), custom_call_target="tpu_custom_call" | custom-call | bytes 3145728 | tf_op jit(solution)/shard_map/lay_out/pallas_call | solution.py:254
  62.0 1.6 %collective-permute-start.20 = (bf16[1024,512]{1,0:T(8,128)(2,1)S(1)}, bf16[1024,512]{1,0:T(8,128)(2,1)S(1)}, u32[]{:S(2)}, u32[]{:S(2)}) collective-permute-start(bf16[1024,512]{1,0:T(8,128)(2,1)S(1)} %get-tuple-element.31.w0), channel_id=1, source_target_pairs={{0,8},{8,0},{16,24},{24,16},{32,40},{40,32},{48,56},{56,48},{64,72... | collective-permute-start | bytes 3145736 | tf_op jit(solution)/shard_map/ppermute | solution.py:25
  63.7 1.4 %collective-permute-start.18 = (bf16[512,128]{1,0:T(8,128)(2,1)S(1)}, bf16[512,128]{1,0:T(8,128)(2,1)S(1)}, u32[]{:S(2)}, u32[]{:S(2)}) collective-permute-start(bf16[512,128]{1,0:T(8,128)(2,1)S(1)} %pad_maximum_fusion.2.refs_5_.p0), channel_id=1, source_target_pairs={{0,3},{1,0},{2,1},{3,2},{4,7},{5,4},{6,5},{7,6},{8,11},{9,8},{10,9... | collective-permute-start | bytes 393224 | tf_op jit(solution)/shard_map/ppermute | solution.py:29
  65.4 4.8 %collective-permute-done.19.p3 = bf16[512,128]{1,0:T(8,128)(2,1)S(1)} collective-permute-done((bf16[512,128]{1,0:T(8,128)(2,1)S(1)}, bf16[512,128]{1,0:T(8,128)(2,1)S(1)}, u32[]{:S(2)}, u32[]{:S(2)}) %collective-permute-start.19) | collective-permute-done | bytes 131104 | tf_op jit(solution)/shard_map/ppermute | solution.py:29
  70.2 1.6 %collective-permute-done.18.p2 = bf16[512,128]{1,0:T(8,128)(2,1)S(1)} collective-permute-done((bf16[512,128]{1,0:T(8,128)(2,1)S(1)}, bf16[512,128]{1,0:T(8,128)(2,1)S(1)}, u32[]{:S(2)}, u32[]{:S(2)}) %collective-permute-start.18) | collective-permute-done | bytes 131104 | tf_op jit(solution)/shard_map/ppermute | solution.py:29
  71.8 1.6 %collective-permute-done.17.p1 = bf16[512,128]{1,0:T(8,128)(2,1)S(1)} collective-permute-done((bf16[512,128]{1,0:T(8,128)(2,1)S(1)}, bf16[512,128]{1,0:T(8,128)(2,1)S(1)}, u32[]{:S(2)}, u32[]{:S(2)}) %collective-permute-start.17) | collective-permute-done | bytes 131104 | tf_op jit(solution)/shard_map/ppermute | solution.py:29
  73.4 2.1 %middle.1 = (f32[256,128]{1,0:T(8,128)}, bf16[256,128]{1,0:T(8,128)(2,1)S(1)}, f32[64,1152]{1,0:T(8,128)S(1)}, f32[64,1152]{1,0:T(8,128)S(1)}) custom-call(s32[2]{0:T(128)S(1)} %copy-done.4, bf16[512,128]{1,0:T(8,128)(2,1)S(1)} %pad_maximum_fusion.2.refs_5_.p0, bf16[512,128]{1,0:T(8,128)(2,1)S(1)} %collective-permute-done.17.p1, ...), custom_call_target="tpu_custom_call" | custom-call | flops 671088640 | bytes 5242880 | tf_op jit(solution)/shard_map/middle/pallas_call | solution.py:300
  76.1 1.2 collective-permute-done.22.got
  77.3 1.1 collective-permute-start.24
  78.4 5.2 %spread.1 = (f32[16,128,128]{2,1,0:T(8,128)S(1)}, bf16[16,128,128]{2,1,0:T(8,128)(2,1)S(1)}) custom-call(s32[160]{0:T(256)S(1)} %plan_tiles.1.refs_2_.plan, bf16[64,128,128]{2,1,0:T(8,128)(2,1)S(1)} %copy-done, bf16[64,128,128]{2,1,0:T(8,128)(2,1)} %collective-permute-done.2.more, bf16[2,128,128]{2,1,0:T(8,128)(2,1)S(1)} %bitcast.33, ...), custom_call_target="tpu_custom_call" | custom-call | flops 268435456 | bytes 6291456 | tf_op jit(solution)/shard_map/spread/pallas_call | solution.py:339
  83.7 1.4 %collective-permute-start.25 = (bf16[32,1152]{1,0:T(8,128)(2,1)S(1)}, bf16[32,1152]{1,0:T(8,128)(2,1)S(1)}, u32[]{:S(2)}, u32[]{:S(2)}) collective-permute-start(bf16[32,1152]{1,0:T(8,128)(2,1)S(1)} %quarter_up.1.own), channel_id=1, source_target_pairs={{0,8},{8,0},{16,24},{24,16},{32,40},{40,32},{48,56},{56,48},{64,72... | collective-permute-start | bytes 221192 | tf_op jit(solution)/shard_map/ppermute | solution.py:25
  86.0 2.3 %collective-permute-start.27 = (bf16[64,1152]{1,0:T(8,128)(2,1)S(1)}, bf16[64,1152]{1,0:T(8,128)(2,1)S(1)}, u32[]{:S(2)}, u32[]{:S(2)}) collective-permute-start(bf16[64,1152]{1,0:T(8,128)(2,1)S(1)} %pad_maximum_fusion.a), channel_id=1, source_target_pairs={{0,96},{8,40},{16,112},{24,56},{32,0},{40,72},{48,16},{56,88},{64,... | collective-permute-start | bytes 442376 | tf_op jit(solution)/shard_map/ppermute | solution.py:41
  88.3 1.0 collective-permute-start.26
  89.3 3.0 %collective-permute-done.27.refs_0_.d2 = bf16[64,1152]{1,0:T(8,128)(2,1)S(1)} collective-permute-done((bf16[64,1152]{1,0:T(8,128)(2,1)S(1)}, bf16[64,1152]{1,0:T(8,128)(2,1)S(1)}, u32[]{:S(2)}, u32[]{:S(2)}) %collective-permute-start.27) | collective-permute-done | bytes 147488 | tf_op jit(solution)/shard_map/ppermute | solution.py:41
  92.3 6.9 %collective-permute-done.26.b.d3 = bf16[64,1152]{1,0:T(8,128)(2,1)S(1)} collective-permute-done((bf16[64,1152]{1,0:T(8,128)(2,1)S(1)}, bf16[64,1152]{1,0:T(8,128)(2,1)S(1)}, u32[]{:S(2)}, u32[]{:S(2)}) %collective-permute-start.26) | collective-permute-done | bytes 147488 | tf_op jit(solution)/shard_map/ppermute | solution.py:41
  99.4 1.4 %collective-permute-start.29 = (bf16[4,128,128]{2,1,0:T(8,128)(2,1)S(1)}, bf16[4,128,128]{2,1,0:T(8,128)(2,1)S(1)}, u32[]{:S(2)}, u32[]{:S(2)}) collective-permute-start(bf16[4,128,128]{2,1,0:T(8,128)(2,1)S(1)} %get-tuple-element.42), channel_id=1, source_target_pairs={{0,32},{8,104},{16,48},{24,120},{32,64},{40,8},{48,80},{56,24},{64... | collective-permute-start | bytes 393224 | tf_op jit(solution)/shard_map/ppermute | solution.py:41
  100.8 2.1 %collective-permute-start.28 = (bf16[6,128,128]{2,1,0:T(8,128)(2,1)S(1)}, bf16[6,128,128]{2,1,0:T(8,128)(2,1)S(1)}, u32[]{:S(2)}, u32[]{:S(2)}) collective-permute-start(bf16[6,128,128]{2,1,0:T(8,128)(2,1)S(1)} %get-tuple-element.41), channel_id=1, source_target_pairs={{0,16},{8,120},{16,32},{24,8},{32,48},{40,24},{48,64},{56,40},{64,... | collective-permute-start | bytes 589832 | tf_op jit(solution)/shard_map/ppermute | solution.py:41
  102.9 3.9 %collective-permute-done.32.d1 = bf16[96,1152]{1,0:T(8,128)(2,1)S(1)} collective-permute-done((bf16[96,1152]{1,0:T(8,128)(2,1)S(1)}, bf16[96,1152]{1,0:T(8,128)(2,1)S(1)}, u32[]{:S(2)}, u32[]{:S(2)}) %collective-permute-start.32) | collective-permute-done | bytes 221216 | tf_op jit(solution)/shard_map/ppermute | solution.py:41
  107.3 2.1 %collective-permute-done.28.r14 = bf16[6,128,128]{2,1,0:T(8,128)(2,1)S(1)} collective-permute-done((bf16[6,128,128]{2,1,0:T(8,128)(2,1)S(1)}, bf16[6,128,128]{2,1,0:T(8,128)(2,1)S(1)}, u32[]{:S(2)}, u32[]{:S(2)}) %collective-permute-start.28) | collective-permute-done | bytes 196640 | tf_op jit(solution)/shard_map/ppermute | solution.py:41
  109.4 3.9 %collective-permute-start.30 = (bf16[4,128,128]{2,1,0:T(8,128)(2,1)S(1)}, bf16[4,128,128]{2,1,0:T(8,128)(2,1)S(1)}, u32[]{:S(2)}, u32[]{:S(2)}) collective-permute-start(bf16[4,128,128]{2,1,0:T(8,128)(2,1)S(1)} %ride.1.t), channel_id=1, source_target_pairs={{0,48},{8,88},{16,64},{24,104},{32,80},{40,120},{48,96},{56,8},{64... | collective-permute-start | bytes 393224 | tf_op jit(solution)/shard_map/ppermute | solution.py:41
  113.3 0.7 sum_z.1
  114.0 0.7 collective-permute-start.34
  114.7 3.3 %collective-permute-done.30 = bf16[4,128,128]{2,1,0:T(8,128)(2,1)S(1)} collective-permute-done((bf16[4,128,128]{2,1,0:T(8,128)(2,1)S(1)}, bf16[4,128,128]{2,1,0:T(8,128)(2,1)S(1)}, u32[]{:S(2)}, u32[]{:S(2)}) %collective-permute-start.30) | collective-permute-done | bytes 131104 | tf_op jit(solution)/shard_map/ppermute | solution.py:41
  118.0 2.3 %collective-permute-start.31 = (f32[2,128,128]{2,1,0:T(8,128)S(1)}, f32[2,128,128]{2,1,0:T(8,128)S(1)}, u32[]{:S(2)}, u32[]{:S(2)}) collective-permute-start(f32[2,128,128]{2,1,0:T(8,128)S(1)} %slice.35), channel_id=1, source_target_pairs={{0,8},{8,0},{16,24},{24,16},{32,40},{40,32},{48,56},{56,48},{64,72... | collective-permute-start | bytes 393224 | tf_op jit(solution)/shard_map/ppermute | solution.py:25
  120.4 0.9 collective-permute-done.31
  122.0 1.4 %weight_out.1 = (f32[128,1024]{1,0:T(8,128)}, f32[8,128]{1,0:T(8,128)S(1)}) custom-call(s32[2]{0:T(128)S(1)} %copy-done.4, bf16[64,1152]{1,0:T(8,128)(2,1)S(1)} %pad_maximum_fusion.1.mine, bf16[64,1152]{1,0:T(8,128)(2,1)S(1)} %collective-permute-done.35.theirs), custom_call_target="tpu_custom_call" | custom-call | bytes 1048576 | tf_op jit(solution)/shard_map/weight_out/pallas_call | solution.py:466
  (68 shorter events, 8.7 us)
Async XLA Ops:
  0.6 41.6 %copy-start = (bf16[64,128,128]{2,1,0:T(8,128)(2,1)S(1)}, bf16[64,128,128]{2,1,0:T(8,128)(2,1)}, u32[]{:S(2)}) copy-start(bf16[64,128,128]{2,1,0:T(8,128)(2,1)} %tiles.3) | copy-start | bytes 6291460
  0.6 4.4 %collective-permute-start.1 = (bf16[256,128]{1,0:T(8,128)(2,1)}, bf16[256,128]{1,0:T(8,128)(2,1)S(1)}, u32[]{:S(2)}, u32[]{:S(2)}) collective-permute-start(bf16[256,128]{1,0:T(8,128)(2,1)} %param.7), channel_id=1, source_target_pairs={{0,8},{8,0},{16,24},{24,16},{32,40},{40,32},{48,56},{56,48},{64,72... | collective-permute-start | bytes 196616 | tf_op jit(solution)/shard_map/ppermute | solution.py:25
  5.1 37.2 %collective-permute-start.2 = (bf16[64,128,128]{2,1,0:T(8,128)(2,1)}, bf16[64,128,128]{2,1,0:T(8,128)(2,1)}, u32[]{:S(2)}, u32[]{:S(2)}) collective-permute-start(bf16[64,128,128]{2,1,0:T(8,128)(2,1)} %tiles.3), channel_id=1, source_target_pairs={{0,8},{8,0},{16,24},{24,16},{32,40},{40,32},{48,56},{56,48},{64,72... | collective-permute-start | bytes 6291464 | tf_op jit(solution)/shard_map/ppermute | solution.py:25
  8.4 8.2 %collective-permute-start.6 = (bf16[784,128]{1,0:T(8,128)(2,1)}, bf16[784,128]{1,0:T(8,128)(2,1)S(1)}, u32[]{:S(2)}, u32[]{:S(2)}) collective-permute-start(bf16[784,128]{1,0:T(8,128)(2,1)} %pack_up.1.a), channel_id=1, source_target_pairs={{0,4},{1,5},{2,6},{3,7},{4,0},{5,1},{6,2},{7,3},{8,12},{9,13},{10,... | collective-permute-start | bytes 602120 | tf_op jit(solution)/shard_map/ppermute | solution.py:29
  9.5 13.5 %collective-permute-start.3 = (bf16[256,128]{1,0:T(8,128)(2,1)}, bf16[256,128]{1,0:T(8,128)(2,1)S(1)}, u32[]{:S(2)}, u32[]{:S(2)}) collective-permute-start(bf16[256,128]{1,0:T(8,128)(2,1)} %param.7), channel_id=1, source_target_pairs={{0,128},{8,136},{16,144},{24,152},{32,160},{40,168},{48,176},{56,1... | collective-permute-start | bytes 196616 | tf_op jit(solution)/shard_map/ppermute | solution.py:25
  10.5 9.7 %collective-permute-start = (s32[2,64]{1,0:T(2,128)S(1)}, s32[2,64]{1,0:T(2,128)S(1)}, u32[]{:S(2)}, u32[]{:S(2)}) collective-permute-start(s32[2,64]{1,0:T(2,128)S(1)} %pad_add_fusion), channel_id=1, source_target_pairs={{0,8},{8,0},{16,24},{24,16},{32,40},{40,32},{48,56},{56,48},{64,72... | collective-permute-start | bytes 1544 | tf_op jit(solution)/shard_map/ppermute | solution.py:25
  11.2 16.6 %collective-permute-start.5 = (bf16[512,128]{1,0:T(8,128)(2,1)S(1)}, bf16[512,128]{1,0:T(8,128)(2,1)S(1)}, u32[]{:S(2)}, u32[]{:S(2)}) collective-permute-start(bf16[512,128]{1,0:T(8,128)(2,1)S(1)} %constant_dynamic-update-slice_fusion.a), channel_id=1, source_target_pairs={{0,96},{8,40},{16,112},{24,56},{32,0},{40,72},{48,16},{56,88},{64,... | collective-permute-start | bytes 393224 | tf_op jit(solution)/shard_map/ppermute | solution.py:41
  16.7 11.1 %collective-permute-start.4 = (bf16[512,128]{1,0:T(8,128)(2,1)S(1)}, bf16[512,128]{1,0:T(8,128)(2,1)S(1)}, u32[]{:S(2)}, u32[]{:S(2)}) collective-permute-start(bf16[512,128]{1,0:T(8,128)(2,1)S(1)} %constant_dynamic-update-slice_fusion.a), channel_id=1, source_target_pairs={{0,80},{8,56},{16,96},{24,72},{32,112},{40,88},{48,0},{56,104},{64... | collective-permute-start | bytes 393224 | tf_op jit(solution)/shard_map/ppermute | solution.py:41
  19.3 0.9 copy-start.2
  20.3 15.2 %collective-permute-start.12 = (bf16[1568,128]{1,0:T(8,128)(2,1)S(1)}, bf16[1568,128]{1,0:T(8,128)(2,1)S(1)}, u32[]{:S(2)}, u32[]{:S(2)}) collective-permute-start(bf16[1568,128]{1,0:T(8,128)(2,1)S(1)} %append.3.refs_3_.refs_0_), channel_id=1, source_target_pairs={{0,3},{1,0},{2,1},{3,2},{4,7},{5,4},{6,5},{7,6},{8,11},{9,8},{10,9... | collective-permute-start | bytes 1204232 | tf_op jit(solution)/shard_map/ppermute | solution.py:29
  23.1 13.6 %collective-permute-start.11 = (bf16[1568,128]{1,0:T(8,128)(2,1)S(1)}, bf16[1568,128]{1,0:T(8,128)(2,1)S(1)}, u32[]{:S(2)}, u32[]{:S(2)}) collective-permute-start(bf16[1568,128]{1,0:T(8,128)(2,1)S(1)} %append.3.refs_3_.refs_0_), channel_id=1, source_target_pairs={{0,1},{1,2},{2,3},{3,0},{4,5},{5,6},{6,7},{7,4},{8,9},{9,10},{10,1... | collective-permute-start | bytes 1204232 | tf_op jit(solution)/shard_map/ppermute | solution.py:29
  23.1 0.7 copy-start.3
  23.7 0.7 copy-start.5
  24.4 0.7 copy-start.6
  27.8 6.1 %collective-permute-start.7 = (bf16[768,128]{1,0:T(8,128)(2,1)S(1)}, bf16[768,128]{1,0:T(8,128)(2,1)S(1)}, u32[]{:S(2)}, u32[]{:S(2)}) collective-permute-start(bf16[768,128]{1,0:T(8,128)(2,1)S(1)} %append.4), channel_id=1, source_target_pairs={{0,112},{8,24},{16,0},{24,40},{32,16},{40,56},{48,32},{56,72},{64,... | collective-permute-start | bytes 589832 | tf_op jit(solution)/shard_map/ppermute | solution.py:41
  34.0 8.3 %collective-permute-start.8 = (bf16[768,128]{1,0:T(8,128)(2,1)S(1)}, bf16[768,128]{1,0:T(8,128)(2,1)S(1)}, u32[]{:S(2)}, u32[]{:S(2)}) collective-permute-start(bf16[768,128]{1,0:T(8,128)(2,1)S(1)} %collective-permute-done.7), channel_id=1, source_target_pairs={{0,128},{8,136},{16,144},{24,152},{32,160},{40,168},{48,176},{56,1... | collective-permute-start | bytes 589832 | tf_op jit(solution)/shard_map/ppermute | solution.py:25
  35.2 4.7 %collective-permute-start.9 = (bf16[512,128]{1,0:T(8,128)(2,1)S(1)}, bf16[512,128]{1,0:T(8,128)(2,1)S(1)}, u32[]{:S(2)}, u32[]{:S(2)}) collective-permute-start(bf16[512,128]{1,0:T(8,128)(2,1)S(1)} %collective-permute-done.5.refs_0_), channel_id=1, source_target_pairs={{0,128},{8,136},{16,144},{24,152},{32,160},{40,168},{48,176},{56,1... | collective-permute-start | bytes 393224 | tf_op jit(solution)/shard_map/ppermute | solution.py:25
  35.4 6.8 %collective-permute-start.10 = (bf16[512,128]{1,0:T(8,128)(2,1)S(1)}, bf16[512,128]{1,0:T(8,128)(2,1)S(1)}, u32[]{:S(2)}, u32[]{:S(2)}) collective-permute-start(bf16[512,128]{1,0:T(8,128)(2,1)S(1)} %collective-permute-done.4.b), channel_id=1, source_target_pairs={{0,128},{8,136},{16,144},{24,152},{32,160},{40,168},{48,176},{56,1... | collective-permute-start | bytes 393224 | tf_op jit(solution)/shard_map/ppermute | solution.py:25
  36.7 18.0 %collective-permute-start.14 = (bf16[784,128]{1,0:T(8,128)(2,1)S(1)}, bf16[784,128]{1,0:T(8,128)(2,1)S(1)}, u32[]{:S(2)}, u32[]{:S(2)}) collective-permute-start(bf16[784,128]{1,0:T(8,128)(2,1)S(1)} %get-tuple-element.27.refs_8_), channel_id=1, source_target_pairs={{0,1},{1,2},{2,3},{3,0},{4,5},{5,6},{6,7},{7,4},{8,9},{9,10},{10,1... | collective-permute-start | bytes 602120 | tf_op jit(solution)/shard_map/ppermute | solution.py:29
  39.9 14.8 %collective-permute-start.15 = (bf16[784,128]{1,0:T(8,128)(2,1)S(1)}, bf16[784,128]{1,0:T(8,128)(2,1)S(1)}, u32[]{:S(2)}, u32[]{:S(2)}) collective-permute-start(bf16[784,128]{1,0:T(8,128)(2,1)S(1)} %get-tuple-element.28.refs_9_), channel_id=1, source_target_pairs={{0,3},{1,0},{2,1},{3,2},{4,7},{5,4},{6,5},{7,6},{8,11},{9,8},{10,9... | collective-permute-start | bytes 602120 | tf_op jit(solution)/shard_map/ppermute | solution.py:29
  42.3 18.3 %copy-start.4 = (s32[2]{0:T(128)S(1)}, s32[2]{0:T(128)}, u32[]{:S(2)}) copy-start(s32[2]{0:T(128)} %pad_add_fusion.1.ids) | copy-start | bytes 28
  48.2 25.2 %copy-start.1 = (bf16[128,1024]{1,0:T(8,128)(2,1)S(1)}, bf16[128,1024]{1,0:T(8,128)(2,1)}, u32[]{:S(2)}) copy-start(bf16[128,1024]{1,0:T(8,128)(2,1)} %w_own.1) | copy-start | bytes 786436
  48.2 7.5 %collective-permute-start.13 = (f32[2,128,128]{2,1,0:T(8,128)S(1)}, f32[2,128,128]{2,1,0:T(8,128)S(1)}, u32[]{:S(2)}, u32[]{:S(2)}) collective-permute-start(f32[2,128,128]{2,1,0:T(8,128)S(1)} %get-tuple-element.30), channel_id=1, source_target_pairs={{0,8},{8,0},{16,24},{24,16},{32,40},{40,32},{48,56},{56,48},{64,72... | collective-permute-start | bytes 393224 | tf_op jit(solution)/shard_map/ppermute | solution.py:25
  55.7 4.9 %collective-permute-start.16 = (bf16[256,128]{1,0:T(8,128)(2,1)S(1)}, bf16[256,128]{1,0:T(8,128)(2,1)S(1)}, u32[]{:S(2)}, u32[]{:S(2)}) collective-permute-start(bf16[256,128]{1,0:T(8,128)(2,1)S(1)} %bitcast.26), channel_id=1, source_target_pairs={{0,4},{1,5},{2,6},{3,7},{4,0},{5,1},{6,2},{7,3},{8,12},{9,13},{10,... | collective-permute-start | bytes 196616 | tf_op jit(solution)/shard_map/ppermute | solution.py:29
  62.0 11.4 %collective-permute-start.20 = (bf16[1024,512]{1,0:T(8,128)(2,1)S(1)}, bf16[1024,512]{1,0:T(8,128)(2,1)S(1)}, u32[]{:S(2)}, u32[]{:S(2)}) collective-permute-start(bf16[1024,512]{1,0:T(8,128)(2,1)S(1)} %get-tuple-element.31.w0), channel_id=1, source_target_pairs={{0,8},{8,0},{16,24},{24,16},{32,40},{40,32},{48,56},{56,48},{64,72... | collective-permute-start | bytes 3145736 | tf_op jit(solution)/shard_map/ppermute | solution.py:25
  63.6 6.6 %collective-permute-start.19 = (bf16[512,128]{1,0:T(8,128)(2,1)S(1)}, bf16[512,128]{1,0:T(8,128)(2,1)S(1)}, u32[]{:S(2)}, u32[]{:S(2)}) collective-permute-start(bf16[512,128]{1,0:T(8,128)(2,1)S(1)} %pad_maximum_fusion.2.refs_5_.p0), channel_id=1, source_target_pairs={{0,2},{1,3},{2,0},{3,1},{4,6},{5,7},{6,4},{7,5},{8,10},{9,11},{10,... | collective-permute-start | bytes 393224 | tf_op jit(solution)/shard_map/ppermute | solution.py:29
  63.7 8.0 %collective-permute-start.18 = (bf16[512,128]{1,0:T(8,128)(2,1)S(1)}, bf16[512,128]{1,0:T(8,128)(2,1)S(1)}, u32[]{:S(2)}, u32[]{:S(2)}) collective-permute-start(bf16[512,128]{1,0:T(8,128)(2,1)S(1)} %pad_maximum_fusion.2.refs_5_.p0), channel_id=1, source_target_pairs={{0,3},{1,0},{2,1},{3,2},{4,7},{5,4},{6,5},{7,6},{8,11},{9,8},{10,9... | collective-permute-start | bytes 393224 | tf_op jit(solution)/shard_map/ppermute | solution.py:29
  65.1 8.2 %collective-permute-start.17 = (bf16[512,128]{1,0:T(8,128)(2,1)S(1)}, bf16[512,128]{1,0:T(8,128)(2,1)S(1)}, u32[]{:S(2)}, u32[]{:S(2)}) collective-permute-start(bf16[512,128]{1,0:T(8,128)(2,1)S(1)} %pad_maximum_fusion.2.refs_5_.p0), channel_id=1, source_target_pairs={{0,1},{1,2},{2,3},{3,0},{4,5},{5,6},{6,7},{7,4},{8,9},{9,10},{10,1... | collective-permute-start | bytes 393224 | tf_op jit(solution)/shard_map/ppermute | solution.py:29
  75.5 1.7 %collective-permute-start.22 = (f32[64,1152]{1,0:T(8,128)S(1)}, f32[64,1152]{1,0:T(8,128)S(1)}, u32[]{:S(2)}, u32[]{:S(2)}) collective-permute-start(f32[64,1152]{1,0:T(8,128)S(1)} %get-tuple-element.37), channel_id=1, source_target_pairs={{0,8},{8,0},{16,24},{24,16},{32,40},{40,32},{48,56},{56,48},{64,72... | collective-permute-start | bytes 884744 | tf_op jit(solution)/shard_map/ppermute | solution.py:25
  76.0 2.4 %collective-permute-start.21 = (bf16[2,128,128]{2,1,0:T(8,128)(2,1)S(1)}, bf16[2,128,128]{2,1,0:T(8,128)(2,1)S(1)}, u32[]{:S(2)}, u32[]{:S(2)}) collective-permute-start(bf16[2,128,128]{2,1,0:T(8,128)(2,1)S(1)} %bitcast.32), channel_id=1, source_target_pairs={{0,8},{8,0},{16,24},{24,16},{32,40},{40,32},{48,56},{56,48},{64,72... | collective-permute-start | bytes 196616 | tf_op jit(solution)/shard_map/ppermute | solution.py:25
  77.3 6.4 %collective-permute-start.24 = (bf16[32,1152]{1,0:T(8,128)(2,1)S(1)}, bf16[32,1152]{1,0:T(8,128)(2,1)S(1)}, u32[]{:S(2)}, u32[]{:S(2)}) collective-permute-start(bf16[32,1152]{1,0:T(8,128)(2,1)S(1)} %fusion.send), channel_id=1, source_target_pairs={{0,128},{8,136},{16,144},{24,152},{32,160},{40,168},{48,176},{56,1... | collective-permute-start | bytes 221192 | tf_op jit(solution)/shard_map/ppermute | solution.py:25
  83.7 2.3 %collective-permute-start.25 = (bf16[32,1152]{1,0:T(8,128)(2,1)S(1)}, bf16[32,1152]{1,0:T(8,128)(2,1)S(1)}, u32[]{:S(2)}, u32[]{:S(2)}) collective-permute-start(bf16[32,1152]{1,0:T(8,128)(2,1)S(1)} %quarter_up.1.own), channel_id=1, source_target_pairs={{0,8},{8,0},{16,24},{24,16},{32,40},{40,32},{48,56},{56,48},{64,72... | collective-permute-start | bytes 221192 | tf_op jit(solution)/shard_map/ppermute | solution.py:25
  85.1 14.2 %collective-permute-start.23 = (bf16[16,128,128]{2,1,0:T(8,128)(2,1)S(1)}, bf16[16,128,128]{2,1,0:T(8,128)(2,1)S(1)}, u32[]{:S(2)}, u32[]{:S(2)}) collective-permute-start(bf16[16,128,128]{2,1,0:T(8,128)(2,1)S(1)} %get-tuple-element.39.far), channel_id=1, source_target_pairs={{0,128},{8,136},{16,144},{24,152},{32,160},{40,168},{48,176},{56,1... | collective-permute-start | bytes 1572872 | tf_op jit(solution)/shard_map/ppermute | solution.py:25
  86.0 6.3 %collective-permute-start.27 = (bf16[64,1152]{1,0:T(8,128)(2,1)S(1)}, bf16[64,1152]{1,0:T(8,128)(2,1)S(1)}, u32[]{:S(2)}, u32[]{:S(2)}) collective-permute-start(bf16[64,1152]{1,0:T(8,128)(2,1)S(1)} %pad_maximum_fusion.a), channel_id=1, source_target_pairs={{0,96},{8,40},{16,112},{24,56},{32,0},{40,72},{48,16},{56,88},{64,... | collective-permute-start | bytes 442376 | tf_op jit(solution)/shard_map/ppermute | solution.py:41
  88.3 10.9 %collective-permute-start.26 = (bf16[64,1152]{1,0:T(8,128)(2,1)S(1)}, bf16[64,1152]{1,0:T(8,128)(2,1)S(1)}, u32[]{:S(2)}, u32[]{:S(2)}) collective-permute-start(bf16[64,1152]{1,0:T(8,128)(2,1)S(1)} %pad_maximum_fusion.a), channel_id=1, source_target_pairs={{0,80},{8,56},{16,96},{24,72},{32,112},{40,88},{48,0},{56,104},{64... | collective-permute-start | bytes 442376 | tf_op jit(solution)/shard_map/ppermute | solution.py:41
  99.2 7.6 %collective-permute-start.32 = (bf16[96,1152]{1,0:T(8,128)(2,1)S(1)}, bf16[96,1152]{1,0:T(8,128)(2,1)S(1)}, u32[]{:S(2)}, u32[]{:S(2)}) collective-permute-start(bf16[96,1152]{1,0:T(8,128)(2,1)S(1)} %append.5.ready), channel_id=1, source_target_pairs={{0,112},{8,24},{16,0},{24,40},{32,16},{40,56},{48,32},{56,72},{64,... | collective-permute-start | bytes 663560 | tf_op jit(solution)/shard_map/ppermute | solution.py:41
  99.4 7.3 %collective-permute-start.29 = (bf16[4,128,128]{2,1,0:T(8,128)(2,1)S(1)}, bf16[4,128,128]{2,1,0:T(8,128)(2,1)S(1)}, u32[]{:S(2)}, u32[]{:S(2)}) collective-permute-start(bf16[4,128,128]{2,1,0:T(8,128)(2,1)S(1)} %get-tuple-element.42), channel_id=1, source_target_pairs={{0,32},{8,104},{16,48},{24,120},{32,64},{40,8},{48,80},{56,24},{64... | collective-permute-start | bytes 393224 | tf_op jit(solution)/shard_map/ppermute | solution.py:41
  100.8 8.6 %collective-permute-start.28 = (bf16[6,128,128]{2,1,0:T(8,128)(2,1)S(1)}, bf16[6,128,128]{2,1,0:T(8,128)(2,1)S(1)}, u32[]{:S(2)}, u32[]{:S(2)}) collective-permute-start(bf16[6,128,128]{2,1,0:T(8,128)(2,1)S(1)} %get-tuple-element.41), channel_id=1, source_target_pairs={{0,16},{8,120},{16,32},{24,8},{32,48},{40,24},{48,64},{56,40},{64,... | collective-permute-start | bytes 589832 | tf_op jit(solution)/shard_map/ppermute | solution.py:41
  106.8 6.5 %collective-permute-start.33 = (bf16[96,1152]{1,0:T(8,128)(2,1)S(1)}, bf16[96,1152]{1,0:T(8,128)(2,1)S(1)}, u32[]{:S(2)}, u32[]{:S(2)}) collective-permute-start(bf16[96,1152]{1,0:T(8,128)(2,1)S(1)} %peer_rows.1), channel_id=1, source_target_pairs={{0,8},{8,0},{16,24},{24,16},{32,40},{40,32},{48,56},{56,48},{64,72... | collective-permute-start | bytes 663560 | tf_op jit(solution)/shard_map/ppermute | solution.py:25
  109.4 8.5 %collective-permute-start.30 = (bf16[4,128,128]{2,1,0:T(8,128)(2,1)S(1)}, bf16[4,128,128]{2,1,0:T(8,128)(2,1)S(1)}, u32[]{:S(2)}, u32[]{:S(2)}) collective-permute-start(bf16[4,128,128]{2,1,0:T(8,128)(2,1)S(1)} %ride.1.t), channel_id=1, source_target_pairs={{0,48},{8,88},{16,64},{24,104},{32,80},{40,120},{48,96},{56,8},{64... | collective-permute-start | bytes 393224 | tf_op jit(solution)/shard_map/ppermute | solution.py:41
  114.0 6.3 %collective-permute-start.34 = (bf16[32,1152]{1,0:T(8,128)(2,1)S(1)}, bf16[32,1152]{1,0:T(8,128)(2,1)S(1)}, u32[]{:S(2)}, u32[]{:S(2)}) collective-permute-start(bf16[32,1152]{1,0:T(8,128)(2,1)S(1)} %sum_z.1), channel_id=1, source_target_pairs={{0,128},{8,136},{16,144},{24,152},{32,160},{40,168},{48,176},{56,1... | collective-permute-start | bytes 221192 | tf_op jit(solution)/shard_map/ppermute | solution.py:25
  118.0 3.2 %collective-permute-start.31 = (f32[2,128,128]{2,1,0:T(8,128)S(1)}, f32[2,128,128]{2,1,0:T(8,128)S(1)}, u32[]{:S(2)}, u32[]{:S(2)}) collective-permute-start(f32[2,128,128]{2,1,0:T(8,128)S(1)} %slice.35), channel_id=1, source_target_pairs={{0,8},{8,0},{16,24},{24,16},{32,40},{40,32},{48,56},{56,48},{64,72... | collective-permute-start | bytes 393224 | tf_op jit(solution)/shard_map/ppermute | solution.py:25
  120.3 1.7 %collective-permute-start.35 = (bf16[64,1152]{1,0:T(8,128)(2,1)S(1)}, bf16[64,1152]{1,0:T(8,128)(2,1)S(1)}, u32[]{:S(2)}, u32[]{:S(2)}) collective-permute-start(bf16[64,1152]{1,0:T(8,128)(2,1)S(1)} %pad_maximum_fusion.1.mine), channel_id=1, source_target_pairs={{0,8},{8,0},{16,24},{24,16},{32,40},{40,32},{48,56},{56,48},{64,72... | collective-permute-start | bytes 442376 | tf_op jit(solution)/shard_map/ppermute | solution.py:25

commit v5 on v4

--- a/solution.py
+++ b/solution.py
@@ -98,29 +98,29 @@
     )(a, b, *ready)
 
 
-def turn_body(u, d, a, b):
+def turn_body(u, d, r0, r1, a, b):
     a[...] = u[0:784, :]
     b[...] = d[784:1568, :]
 
 
-def turn(u, d):
+def turn(u, d, *ready):
     half = jax.ShapeDtypeStruct((784, B), bf16)
     return pl.pallas_call(
         turn_body,
         out_shape=(half, half),
-        in_specs=[VM, VM],
+        in_specs=[VM, VM, ANY, ANY],
         out_specs=(VM, VM),
         compiler_params=params(4),
         cost_estimate=cost(0, 1 << 18),
         name="turn",
-    )(u, d)
-
-
-def settle_body(mine, came, a, b, agg):
+    )(u, d, *ready)
+
+
+def settle_body(mine, came, r0, r1, agg):
     agg[...] = (mine[...] + came[...]).astype(bf16)
 
 
-def settle(mine, came, a, b):
+def settle(mine, came, *ready):
     return pl.pallas_call(
         settle_body,
         out_shape=jax.ShapeDtypeStruct((2, B, B), bf16),
@@ -129,7 +129,7 @@
         compiler_params=params(4),
         cost_estimate=cost(0, 1 << 18),
         name="settle",
-    )(mine, came, a, b)
+    )(mine, came, *ready)
 
 
 def plan_body(ids, c0, d0, c1, d1, out):
@@ -180,8 +180,8 @@
 
 
 def agg_body(plan, tiles, more, *refs):
-    mine, theirs, src, acc, sem = refs[10:]
-    both, x0, o14, o2, o3, p14, p2, p3 = refs[0:8]
+    mine, theirs, src, acc, sem = refs[12:]
+    both, x0, o4, o1, o2, o3, p4, p1, p2, p3 = refs[0:10]
     copies = []
 
     def put(dx, j, v):
@@ -190,8 +190,8 @@
         copies.append(pltpu.make_async_copy(v, src.at[at : at + n], sem.at[len(copies)]))
         copies[-1].start()
 
-    for dx, (v3, v2, v14, v0) in enumerate(((o3, o2, o14, both.at[0:2]), (p3, p2, p14, x0))):
-        for j, v in ((0, v3), (2, v2), (4, v14), (7, v0)):
+    for dx, (v3, v2, v1, v4, v0) in enumerate(((o3, o2, o1, o4, both.at[0:2]), (p3, p2, p1, p4, x0))):
+        for j, v in ((0, v3), (2, v2), (4, v1), (6, v4), (7, v0)):
             put(dx, j, v)
     acc[...] = jnp.zeros_like(acc)
     src[32] = jnp.zeros((B, B), bf16)
@@ -211,12 +211,12 @@
     return pl.pallas_call(
         agg_body,
         out_shape=(jax.ShapeDtypeStruct((2, B, B), f32), jax.ShapeDtypeStruct((2, B, B), f32)),
-        in_specs=[SM, VM, VM] + [HB] * 8 + [ANY] * 2,
+        in_specs=[SM, VM, VM] + [HB] * 10 + [ANY] * 2,
         out_specs=(VM, VM),
         scratch_shapes=[
             pltpu.VMEM((33, B, B), bf16),
             pltpu.VMEM((5, B, B), f32),
-            pltpu.SemaphoreType.DMA((8,)),
+            pltpu.SemaphoreType.DMA((10,)),
         ],
         compiler_params=params(12),
         cost_estimate=cost(2 * 64 * B**3, 4 << 20),
@@ -368,10 +368,9 @@
 
 
 def join_body(near, came, ready, t14, t2, t3, t0):
-    t3[...] = near[0:4] + came[0:4].astype(f32)
-    t2[...] = (near[4:8] + came[4:8].astype(f32)).astype(bf16)
-    t14[...] = (near[8:14] + came[8:14].astype(f32)).astype(bf16)
-    t0[...] = near[14:16] + came[14:16].astype(f32)
+    for ref, n in ((t3, 0), (t2, 4), (t14, 8), (t0, 14)):
+        m = n + ref.shape[0]
+        ref[...] = (near[n:m] + came[n:m].astype(f32)).astype(ref.dtype)
 
 
 def join(near, came, ready):
@@ -384,28 +383,28 @@
             jax.ShapeDtypeStruct((2, B, B), f32),
         ),
         in_specs=[VM, VM, ANY],
-        out_specs=(VM, VM, VM, VM),
+        out_specs=(VM,) * 4,
         compiler_params=params(8),
         cost_estimate=cost(0, 2 << 20),
         name="join",
     )(near, came, ready)
 
 
-def ride_body(t3, r14, out):
+def ride_body(t3, r14, ready, out):
     out[0:2] = (t3[0:2] + r14[4:6].astype(f32)).astype(bf16)
     out[2:4] = t3[2:4].astype(bf16)
 
 
-def ride(t3, r14):
+def ride(t3, r14, ready):
     return pl.pallas_call(
         ride_body,
         out_shape=jax.ShapeDtypeStruct((4, B, B), bf16),
-        in_specs=[VM, VM],
+        in_specs=[VM, VM, ANY],
         out_specs=VM,
         compiler_params=params(4),
         cost_estimate=cost(0, 1 << 18),
         name="ride",
-    )(t3, r14)
+    )(t3, r14, ready)
 
 
 def rows_body(d1, d2, d3, t, out):
@@ -483,20 +482,19 @@
     lists = row_send(jnp.stack([col_blocks, dest_blocks]), dc=1)
     swap, both_a = tie(adj_tiles, both)
     more = row_send(swap, dc=1)
-    o3, o2 = spin_send(both, 3, -1), spin_send(both, 2, -1)
+    o3, o2, o1 = (spin_send(both, k, -1) for k in (3, 2, 1))
+    o4 = row_send(features, dz=4)
     plan = plan_tiles(ids, col_blocks, dest_blocks, lists[0], lists[1])
 
     pack = pack_up(ids, weight, out_grad, bias_vector[None, :])
     pack_x = feat_send(pack, dx=1)
 
-    pair = append(1568, pack, pack_x)
-    ext = append(768, both, o3, o2, x0, plan, pair)
-    o14 = spin_send(ext, 1, -1)
-    p3, p2, p14 = row_send(o3, dx=1), row_send(o2, dx=1), row_send(o14, dx=1)
+    p3, p2, p1, p4 = (row_send(v, dx=1) for v in (o3, o2, o1, o4))
+    pair = append(1568, pack, pack_x, o1, o4, x0, p3, p2, plan)
     wu, wd = feat_send(pair, dy=1), feat_send(pair, dy=-1)
 
-    wa, wb = turn(wu, wd)
-    mine, theirs = aggregate(plan, adj_tiles, more, (both_a, x0, o14, o2, o3, p14, p2, p3), wa, wb)
+    wa, wb = turn(wu, wd, p1, p4)
+    mine, theirs = aggregate(plan, adj_tiles, more, (both_a, x0, o4, o1, o2, o3, p4, p1, p2, p3), wa, wb)
     wa, wb = feat_send(wa, dy=1), feat_send(wb, dy=-1)
     aggregated = settle(mine, row_send(theirs, dc=1), wa, wb).reshape(256, B)
 
@@ -520,10 +518,10 @@
 
     t14, t2, t3, t0 = join(near, came, last)
     r14, r2 = spin_send(t14, 1), spin_send(t2, 2)
-    t3 = ride(t3, r14)
+    t3 = ride(t3, r14, r2)
     r3 = spin_send(t3, 3)
 
-    e = row_send(peer_rows(d1, d2, d3, r2), dc=1)
+    e = row_send(peer_rows(d1, d2, d3, r14), dc=1)
     scale = float(256 * lax.axis_size("row")) ** (-0.5)
     total = sum_z(scale, ids, quarter, d1, d2, d3, e, t3)
     two = jnp.concatenate([total, row_send(total, dx=1)], axis=0)

time: 124 us -> 131 us (1.056)
  starting transfers between devices: 52.8 us -> 55.9 us
  waiting for transfers between devices: 41.8 us -> 43.3 us
    ppermute x9, waiting for transfers between devices: 22.3 us -> 18.5 us  [spin_send(): return lax.ppermute(v, 'row', perm)]
    ppermute x9, waiting for transfers between devices: 12.4 us -> 15.8 us  [feat_send(): lax.ppermute(v, 'feat', [(i, (i >> 2 ^ dx) << 2 | i + dy & 3) for i in ra...]
    ppermute x18 -> x20, starting transfers between devices: 22.4 us -> 24.5 us  [row_send(): return lax.ppermute(v, 'row', perm)]
    ppermute x9, starting transfers between devices: 19.2 us -> 21.2 us  [spin_send(): return lax.ppermute(v, 'row', perm)]
    ppermute x18 -> x20, waiting for transfers between devices: 7.11 us -> 8.94 us  [row_send(): return lax.ppermute(v, 'row', perm)]
  transfers between devices with their start and end apart: 36 -> 38, of which waited for: 17 -> 17; matrix products, arithmetic and copies ran while one was open for 2% -> 2% of each run, Pallas kernels for 14% -> 14%
where the time goes in v5:
time: 131 us; the launch traced here: 130 us
  starting transfers between devices  55.9 us (43%)
  waiting for transfers between devices  43.3 us (33%)
  Pallas kernels  23.4 us (18%)
  local copies, waits for them, and re-layouts  4.29 us (3%)
  other arithmetic  2.04 us (2%)
    ppermute x20, starting transfers between devices, row_send(): return lax.ppermute(v, 'row', perm)  24.5 us
    ppermute x9, starting transfers between devices, spin_send(): return lax.ppermute(v, 'row', perm)  21.2 us
    ppermute x9, waiting for transfers between devices, spin_send(): return lax.ppermute(v, 'row', perm)  18.5 us
    ppermute x9, waiting for transfers between devices, feat_send(): lax.ppermute(v, 'feat', [(i, (i >> 2 ^ dx) << 2 | i + dy & 3) for i in ra...  15.8 us
    ppermute x9, starting transfers between devices, feat_send(): lax.ppermute(v, 'feat', [(i, (i >> 2 ^ dx) << 2 | i + dy & 3) for i in ra...  10.3 us
    ppermute x20, waiting for transfers between devices, row_send(): return lax.ppermute(v, 'row', perm)  8.94 us
    pallas_call x1, Pallas kernels, aggregate(): pl.pallas_call(agg_body, out_shape=(jax.ShapeDtypeStruct((2, B, B), f32),...  6.44 us
    pallas_call x1, Pallas kernels, spread(): pl.pallas_call(spread_body, out_shape=(jax.ShapeDtypeStruct((16, B, B), f...  5.91 us
  transfers between devices with their start and end apart: 38, of which 17 were waited for; matrix products, arithmetic and copies ran while one was open for 2% of the time, Pallas kernels for 14%

profile of v5, /device:TPU:1, one launch (start us, length us, event | category | flops | bytes accessed | tf_op | source)
XLA Modules:
  0.0 129.8 jit_solution(10060433695984016883)
XLA Ops:
  0.6 3.3 %collective-permute-start.1 = (bf16[256,128]{1,0:T(8,128)(2,1)}, bf16[256,128]{1,0:T(8,128)(2,1)S(1)}, u32[]{:S(2)}, u32[]{:S(2)}) collective-permute-start(bf16[256,128]{1,0:T(8,128)(2,1)} %param.7), channel_id=1, source_target_pairs={{0,8},{8,0},{16,24},{24,16},{32,40},{40,32},{48,56},{56,48},{64,72... | collective-permute-start | bytes 196616 | tf_op jit(solution)/shard_map/ppermute | solution.py:25
  4.0 0.8 constant_dynamic-update-slice_fusion.1
  5.5 2.6 %collective-permute-start.7 = (bf16[512,128]{1,0:T(8,128)(2,1)S(1)}, bf16[512,128]{1,0:T(8,128)(2,1)S(1)}, u32[]{:S(2)}, u32[]{:S(2)}) collective-permute-start(bf16[512,128]{1,0:T(8,128)(2,1)S(1)} %constant_dynamic-update-slice_fusion), channel_id=1, source_target_pairs={{0,80},{8,56},{16,96},{24,72},{32,112},{40,88},{48,0},{56,104},{64... | collective-permute-start | bytes 393224 | tf_op jit(solution)/shard_map/ppermute | solution.py:41
  8.1 3.3 %collective-permute-start.6 = (bf16[512,128]{1,0:T(8,128)(2,1)S(1)}, bf16[512,128]{1,0:T(8,128)(2,1)S(1)}, u32[]{:S(2)}, u32[]{:S(2)}) collective-permute-start(bf16[512,128]{1,0:T(8,128)(2,1)S(1)} %constant_dynamic-update-slice_fusion), channel_id=1, source_target_pairs={{0,96},{8,40},{16,112},{24,56},{32,0},{40,72},{48,16},{56,88},{64,... | collective-permute-start | bytes 393224 | tf_op jit(solution)/shard_map/ppermute | solution.py:41
  12.1 4.0 %collective-permute-start.4 = (bf16[256,128]{1,0:T(8,128)(2,1)}, bf16[256,128]{1,0:T(8,128)(2,1)S(1)}, u32[]{:S(2)}, u32[]{:S(2)}) collective-permute-start(bf16[256,128]{1,0:T(8,128)(2,1)} %param.7), channel_id=1, source_target_pairs={{0,64},{8,72},{16,80},{24,88},{32,96},{40,104},{48,112},{56,120},{... | collective-permute-start | bytes 196616 | tf_op jit(solution)/shard_map/ppermute | solution.py:25
  16.2 1.2 collective-permute-start.3
  18.0 2.3 %pack_up.1.a = bf16[784,128]{1,0:T(8,128)(2,1)} custom-call(s32[2]{0:T(128)} %pad_add_fusion.1.ids, bf16[128,1024]{1,0:T(8,128)(2,1)} %w_own.1, bf16[256,128]{1,0:T(8,128)(2,1)} %og.1, bf16[1,128]{1,0:T(2,128)(2,1)} %bitcast.41), custom_call_target="tpu_custom_call" | custom-call | bytes 524288 | tf_op jit(solution)/shard_map/pack_up/pallas_call | solution.py:70
  20.3 2.5 %collective-permute-start.12 = (bf16[784,128]{1,0:T(8,128)(2,1)}, bf16[784,128]{1,0:T(8,128)(2,1)S(1)}, u32[]{:S(2)}, u32[]{:S(2)}) collective-permute-start(bf16[784,128]{1,0:T(8,128)(2,1)} %pack_up.1.a), channel_id=1, source_target_pairs={{0,4},{1,5},{2,6},{3,7},{4,0},{5,1},{6,2},{7,3},{8,12},{9,13},{10,... | collective-permute-start | bytes 602120 | tf_op jit(solution)/shard_map/ppermute | solution.py:29
  22.8 2.3 %collective-permute-start.5 = (bf16[512,128]{1,0:T(8,128)(2,1)S(1)}, bf16[512,128]{1,0:T(8,128)(2,1)S(1)}, u32[]{:S(2)}, u32[]{:S(2)}) collective-permute-start(bf16[512,128]{1,0:T(8,128)(2,1)S(1)} %constant_dynamic-update-slice_fusion), channel_id=1, source_target_pairs={{0,112},{8,24},{16,0},{24,40},{32,16},{40,56},{48,32},{56,72},{64,... | collective-permute-start | bytes 393224 | tf_op jit(solution)/shard_map/ppermute | solution.py:41
  25.4 1.2 collective-permute-start.10
  28.5 2.7 %plan_tiles.1.refs_5_.plan = s32[160]{0:T(256)S(1)} custom-call(s32[2]{0:T(128)S(1)} %copy-done.3, s32[64]{0:T(128)S(1)} %copy-done.5, s32[64]{0:T(128)S(1)} %copy-done.6, s32[64]{0:T(128)S(1)} %get-tuple-element.47.c1, s32[64]{0:T(128)S(1)} %get-tuple-element.46.d1), custom_call_target="tpu_custom_call" | custom-call | flops 10000 | bytes 4096 | tf_op jit(solution)/shard_map/plan_tiles/pallas_call | solution.py:160
  31.3 1.3 %collective-permute-done.10.refs_4_ = bf16[512,128]{1,0:T(8,128)(2,1)S(1)} collective-permute-done((bf16[512,128]{1,0:T(8,128)(2,1)S(1)}, bf16[512,128]{1,0:T(8,128)(2,1)S(1)}, u32[]{:S(2)}, u32[]{:S(2)}) %collective-permute-start.10) | collective-permute-done | bytes 131104 | tf_op jit(solution)/shard_map/ppermute | solution.py:25
  32.7 0.9 copy-done.2
  33.6 2.8 %collective-permute-start.14 = (bf16[1568,128]{1,0:T(8,128)(2,1)S(1)}, bf16[1568,128]{1,0:T(8,128)(2,1)S(1)}, u32[]{:S(2)}, u32[]{:S(2)}) collective-permute-start(bf16[1568,128]{1,0:T(8,128)(2,1)S(1)} %append.2.refs_0_), channel_id=1, source_target_pairs={{0,3},{1,0},{2,1},{3,2},{4,7},{5,4},{6,5},{7,6},{8,11},{9,8},{10,9... | collective-permute-start | bytes 1204232 | tf_op jit(solution)/shard_map/ppermute | solution.py:29
  36.4 1.5 %collective-permute-start.8 = (bf16[256,128]{1,0:T(8,128)(2,1)S(1)}, bf16[256,128]{1,0:T(8,128)(2,1)S(1)}, u32[]{:S(2)}, u32[]{:S(2)}) collective-permute-start(bf16[256,128]{1,0:T(8,128)(2,1)S(1)} %collective-permute-done.4.refs_1_), channel_id=1, source_target_pairs={{0,128},{8,136},{16,144},{24,152},{32,160},{40,168},{48,176},{56,1... | collective-permute-start | bytes 196616 | tf_op jit(solution)/shard_map/ppermute | solution.py:25
  37.9 3.3 %collective-permute-done.8.r1 = bf16[256,128]{1,0:T(8,128)(2,1)S(1)} collective-permute-done((bf16[256,128]{1,0:T(8,128)(2,1)S(1)}, bf16[256,128]{1,0:T(8,128)(2,1)S(1)}, u32[]{:S(2)}, u32[]{:S(2)}) %collective-permute-start.8) | collective-permute-done | bytes 65568 | tf_op jit(solution)/shard_map/ppermute | solution.py:25
  41.7 3.1 %collective-permute-done.13.u.refs_1_ = bf16[1568,128]{1,0:T(8,128)(2,1)S(1)} collective-permute-done((bf16[1568,128]{1,0:T(8,128)(2,1)S(1)}, bf16[1568,128]{1,0:T(8,128)(2,1)S(1)}, u32[]{:S(2)}, u32[]{:S(2)}) %collective-permute-start.13) | collective-permute-done | bytes 401440 | tf_op jit(solution)/shard_map/ppermute | solution.py:29
  45.0 2.7 %collective-permute-start.17 = (bf16[784,128]{1,0:T(8,128)(2,1)S(1)}, bf16[784,128]{1,0:T(8,128)(2,1)S(1)}, u32[]{:S(2)}, u32[]{:S(2)}) collective-permute-start(bf16[784,128]{1,0:T(8,128)(2,1)S(1)} %get-tuple-element.28.refs_11_), channel_id=1, source_target_pairs={{0,3},{1,0},{2,1},{3,2},{4,7},{5,4},{6,5},{7,6},{8,11},{9,8},{10,9... | collective-permute-start | bytes 602120 | tf_op jit(solution)/shard_map/ppermute | solution.py:29
  47.6 6.4 %aggregate.1 = (f32[2,128,128]{2,1,0:T(8,128)S(1)}, f32[2,128,128]{2,1,0:T(8,128)S(1)}) custom-call(s32[160]{0:T(256)S(1)} %plan_tiles.1.refs_5_.plan, bf16[64,128,128]{2,1,0:T(8,128)(2,1)S(1)} %copy-done, bf16[64,128,128]{2,1,0:T(8,128)(2,1)} %collective-permute-done.2.more, bf16[4,128,128]{2,1,0:T(8,128)(2,1)S(1)} %bitcast.28, ...), custom_call_target="tpu_custom_call" | custom-call | flops 268435456 | bytes 4194304 | tf_op jit(solution)/shard_map/aggregate/pallas_call | solution.py:211
  54.1 5.0 %collective-permute-start.15 = (f32[2,128,128]{2,1,0:T(8,128)S(1)}, f32[2,128,128]{2,1,0:T(8,128)S(1)}, u32[]{:S(2)}, u32[]{:S(2)}) collective-permute-start(f32[2,128,128]{2,1,0:T(8,128)S(1)} %get-tuple-element.30), channel_id=1, source_target_pairs={{0,8},{8,0},{16,24},{24,16},{32,40},{40,32},{48,56},{56,48},{64,72... | collective-permute-start | bytes 393224 | tf_op jit(solution)/shard_map/ppermute | solution.py:25
  59.1 1.0 collective-permute-done.15.came
  60.1 0.7 collective-permute-start.18
  60.8 4.0 %collective-permute-done.18 = bf16[256,128]{1,0:T(8,128)(2,1)S(1)} collective-permute-done((bf16[256,128]{1,0:T(8,128)(2,1)S(1)}, bf16[256,128]{1,0:T(8,128)(2,1)S(1)}, u32[]{:S(2)}, u32[]{:S(2)}) %collective-permute-start.18) | collective-permute-done | bytes 65568 | tf_op jit(solution)/shard_map/ppermute | solution.py:29
  64.8 1.4 %lay_out.1 = (bf16[1024,512]{1,0:T(8,128)(2,1)S(1)}, bf16[256,1024]{1,0:T(8,128)(2,1)S(1)}, f32[8,1024]{1,0:T(8,128)S(1)}) custom-call(s32[2]{0:T(128)S(1)} %copy-done.4, bf16[1568,128]{1,0:T(8,128)(2,1)S(1)} %append.2.refs_0_, bf16[1568,128]{1,0:T(8,128)(2,1)S(1)} %collective-permute-done.13.u.refs_1_, ...), custom_call_target="tpu_custom_call" | custom-call | bytes 3145728 | tf_op jit(solution)/shard_map/lay_out/pallas_call | solution.py:254
  66.3 1.6 %collective-permute-start.22 = (bf16[1024,512]{1,0:T(8,128)(2,1)S(1)}, bf16[1024,512]{1,0:T(8,128)(2,1)S(1)}, u32[]{:S(2)}, u32[]{:S(2)}) collective-permute-start(bf16[1024,512]{1,0:T(8,128)(2,1)S(1)} %get-tuple-element.31.w0), channel_id=1, source_target_pairs={{0,8},{8,0},{16,24},{24,16},{32,40},{40,32},{48,56},{56,48},{64,72... | collective-permute-start | bytes 3145736 | tf_op jit(solution)/shard_map/ppermute | solution.py:25
  67.9 1.0 collective-permute-start.20
  69.3 5.1 %collective-permute-done.21.p3 = bf16[512,128]{1,0:T(8,128)(2,1)S(1)} collective-permute-done((bf16[512,128]{1,0:T(8,128)(2,1)S(1)}, bf16[512,128]{1,0:T(8,128)(2,1)S(1)}, u32[]{:S(2)}, u32[]{:S(2)}) %collective-permute-start.21) | collective-permute-done | bytes 131104 | tf_op jit(solution)/shard_map/ppermute | solution.py:29
  74.6 3.0 %collective-permute-done.19.p1 = bf16[512,128]{1,0:T(8,128)(2,1)S(1)} collective-permute-done((bf16[512,128]{1,0:T(8,128)(2,1)S(1)}, bf16[512,128]{1,0:T(8,128)(2,1)S(1)}, u32[]{:S(2)}, u32[]{:S(2)}) %collective-permute-start.19) | collective-permute-done | bytes 131104 | tf_op jit(solution)/shard_map/ppermute | solution.py:29
  77.6 2.2 %middle.1 = (f32[256,128]{1,0:T(8,128)}, bf16[256,128]{1,0:T(8,128)(2,1)S(1)}, f32[64,1152]{1,0:T(8,128)S(1)}, f32[64,1152]{1,0:T(8,128)S(1)}) custom-call(s32[2]{0:T(128)S(1)} %copy-done.4, bf16[512,128]{1,0:T(8,128)(2,1)S(1)} %pad_maximum_fusion.2.refs_5_.p0, bf16[512,128]{1,0:T(8,128)(2,1)S(1)} %collective-permute-done.19.p1, ...), custom_call_target="tpu_custom_call" | custom-call | flops 671088640 | bytes 5242880 | tf_op jit(solution)/shard_map/middle/pallas_call | solution.py:300
  80.3 1.2 collective-permute-done.24.got
  81.5 1.3 %collective-permute-start.26 = (bf16[32,1152]{1,0:T(8,128)(2,1)S(1)}, bf16[32,1152]{1,0:T(8,128)(2,1)S(1)}, u32[]{:S(2)}, u32[]{:S(2)}) collective-permute-start(bf16[32,1152]{1,0:T(8,128)(2,1)S(1)} %fusion.send), channel_id=1, source_target_pairs={{0,128},{8,136},{16,144},{24,152},{32,160},{40,168},{48,176},{56,1... | collective-permute-start | bytes 221192 | tf_op jit(solution)/shard_map/ppermute | solution.py:25
  82.8 5.9 %spread.1 = (f32[16,128,128]{2,1,0:T(8,128)S(1)}, bf16[16,128,128]{2,1,0:T(8,128)(2,1)S(1)}) custom-call(s32[160]{0:T(256)S(1)} %plan_tiles.1.refs_5_.plan, bf16[64,128,128]{2,1,0:T(8,128)(2,1)S(1)} %copy-done, bf16[64,128,128]{2,1,0:T(8,128)(2,1)} %collective-permute-done.2.more, bf16[2,128,128]{2,1,0:T(8,128)(2,1)S(1)} %bitcast.37, ...), custom_call_target="tpu_custom_call" | custom-call | flops 268435456 | bytes 6291456 | tf_op jit(solution)/shard_map/spread/pallas_call | solution.py:339
  88.9 0.8 collective-permute-start.27
  89.7 0.9 collective-permute-done.27
  90.6 4.0 %collective-permute-start.29 = (bf16[64,1152]{1,0:T(8,128)(2,1)S(1)}, bf16[64,1152]{1,0:T(8,128)(2,1)S(1)}, u32[]{:S(2)}, u32[]{:S(2)}) collective-permute-start(bf16[64,1152]{1,0:T(8,128)(2,1)S(1)} %pad_maximum_fusion.a), channel_id=1, source_target_pairs={{0,96},{8,40},{16,112},{24,56},{32,0},{40,72},{48,16},{56,88},{64,... | collective-permute-start | bytes 442376 | tf_op jit(solution)/shard_map/ppermute | solution.py:41
  94.7 1.5 %collective-permute-start.28 = (bf16[64,1152]{1,0:T(8,128)(2,1)S(1)}, bf16[64,1152]{1,0:T(8,128)(2,1)S(1)}, u32[]{:S(2)}, u32[]{:S(2)}) collective-permute-start(bf16[64,1152]{1,0:T(8,128)(2,1)S(1)} %pad_maximum_fusion.a), channel_id=1, source_target_pairs={{0,80},{8,56},{16,96},{24,72},{32,112},{40,88},{48,0},{56,104},{64... | collective-permute-start | bytes 442376 | tf_op jit(solution)/shard_map/ppermute | solution.py:41
  96.1 3.0 %collective-permute-done.29.refs_0_.d2 = bf16[64,1152]{1,0:T(8,128)(2,1)S(1)} collective-permute-done((bf16[64,1152]{1,0:T(8,128)(2,1)S(1)}, bf16[64,1152]{1,0:T(8,128)(2,1)S(1)}, u32[]{:S(2)}, u32[]{:S(2)}) %collective-permute-start.29) | collective-permute-done | bytes 147488 | tf_op jit(solution)/shard_map/ppermute | solution.py:41
  99.2 7.2 %collective-permute-done.28.b.d3 = bf16[64,1152]{1,0:T(8,128)(2,1)S(1)} collective-permute-done((bf16[64,1152]{1,0:T(8,128)(2,1)S(1)}, bf16[64,1152]{1,0:T(8,128)(2,1)S(1)}, u32[]{:S(2)}, u32[]{:S(2)}) %collective-permute-start.28) | collective-permute-done | bytes 147488 | tf_op jit(solution)/shard_map/ppermute | solution.py:41
  106.6 2.7 %collective-permute-start.30 = (bf16[6,128,128]{2,1,0:T(8,128)(2,1)S(1)}, bf16[6,128,128]{2,1,0:T(8,128)(2,1)S(1)}, u32[]{:S(2)}, u32[]{:S(2)}) collective-permute-start(bf16[6,128,128]{2,1,0:T(8,128)(2,1)S(1)} %get-tuple-element.41), channel_id=1, source_target_pairs={{0,16},{8,120},{16,32},{24,8},{32,48},{40,24},{48,64},{56,40},{64,... | collective-permute-start | bytes 589832 | tf_op jit(solution)/shard_map/ppermute | solution.py:41
  110.0 5.6 %collective-permute-done.34.d1 = bf16[96,1152]{1,0:T(8,128)(2,1)S(1)} collective-permute-done((bf16[96,1152]{1,0:T(8,128)(2,1)S(1)}, bf16[96,1152]{1,0:T(8,128)(2,1)S(1)}, u32[]{:S(2)}, u32[]{:S(2)}) %collective-permute-start.34) | collective-permute-done | bytes 221216 | tf_op jit(solution)/shard_map/ppermute | solution.py:41
  116.0 4.0 %collective-permute-start.32 = (bf16[4,128,128]{2,1,0:T(8,128)(2,1)S(1)}, bf16[4,128,128]{2,1,0:T(8,128)(2,1)S(1)}, u32[]{:S(2)}, u32[]{:S(2)}) collective-permute-start(bf16[4,128,128]{2,1,0:T(8,128)(2,1)S(1)} %ride.1.t), channel_id=1, source_target_pairs={{0,48},{8,88},{16,64},{24,104},{32,80},{40,120},{48,96},{56,8},{64... | collective-permute-start | bytes 393224 | tf_op jit(solution)/shard_map/ppermute | solution.py:41
  120.0 0.7 sum_z.1
  120.7 1.3 collective-permute-start.36
  122.0 2.7 %collective-permute-done.32 = bf16[4,128,128]{2,1,0:T(8,128)(2,1)S(1)} collective-permute-done((bf16[4,128,128]{2,1,0:T(8,128)(2,1)S(1)}, bf16[4,128,128]{2,1,0:T(8,128)(2,1)S(1)}, u32[]{:S(2)}, u32[]{:S(2)}) %collective-permute-start.32) | collective-permute-done | bytes 131104 | tf_op jit(solution)/shard_map/ppermute | solution.py:41
  124.7 1.5 %collective-permute-start.33 = (f32[2,128,128]{2,1,0:T(8,128)S(1)}, f32[2,128,128]{2,1,0:T(8,128)S(1)}, u32[]{:S(2)}, u32[]{:S(2)}) collective-permute-start(f32[2,128,128]{2,1,0:T(8,128)S(1)} %slice.35), channel_id=1, source_target_pairs={{0,8},{8,0},{16,24},{24,16},{32,40},{40,32},{48,56},{56,48},{64,72... | collective-permute-start | bytes 393224 | tf_op jit(solution)/shard_map/ppermute | solution.py:25
  126.3 0.9 collective-permute-done.33
  127.2 0.7 fusion.1
  127.9 1.4 %weight_out.1 = (f32[128,1024]{1,0:T(8,128)}, f32[8,128]{1,0:T(8,128)S(1)}) custom-call(s32[2]{0:T(128)S(1)} %copy-done.4, bf16[64,1152]{1,0:T(8,128)(2,1)S(1)} %pad_maximum_fusion.1.mine, bf16[64,1152]{1,0:T(8,128)(2,1)S(1)} %collective-permute-done.37.theirs), custom_call_target="tpu_custom_call" | custom-call | bytes 1048576 | tf_op jit(solution)/shard_map/weight_out/pallas_call | solution.py:465
  (71 shorter events, 8.1 us)
Async XLA Ops:
  0.6 47.0 %copy-start = (bf16[64,128,128]{2,1,0:T(8,128)(2,1)S(1)}, bf16[64,128,128]{2,1,0:T(8,128)(2,1)}, u32[]{:S(2)}) copy-start(bf16[64,128,128]{2,1,0:T(8,128)(2,1)} %tiles.3) | copy-start | bytes 6291460
  0.6 4.4 %collective-permute-start.1 = (bf16[256,128]{1,0:T(8,128)(2,1)}, bf16[256,128]{1,0:T(8,128)(2,1)S(1)}, u32[]{:S(2)}, u32[]{:S(2)}) collective-permute-start(bf16[256,128]{1,0:T(8,128)(2,1)} %param.7), channel_id=1, source_target_pairs={{0,8},{8,0},{16,24},{24,16},{32,40},{40,32},{48,56},{56,48},{64,72... | collective-permute-start | bytes 196616 | tf_op jit(solution)/shard_map/ppermute | solution.py:25
  5.1 42.5 %collective-permute-start.2 = (bf16[64,128,128]{2,1,0:T(8,128)(2,1)}, bf16[64,128,128]{2,1,0:T(8,128)(2,1)}, u32[]{:S(2)}, u32[]{:S(2)}) collective-permute-start(bf16[64,128,128]{2,1,0:T(8,128)(2,1)} %tiles.3), channel_id=1, source_target_pairs={{0,8},{8,0},{16,24},{24,16},{32,40},{40,32},{48,56},{56,48},{64,72... | collective-permute-start | bytes 6291464 | tf_op jit(solution)/shard_map/ppermute | solution.py:25
  5.5 19.6 %collective-permute-start.7 = (bf16[512,128]{1,0:T(8,128)(2,1)S(1)}, bf16[512,128]{1,0:T(8,128)(2,1)S(1)}, u32[]{:S(2)}, u32[]{:S(2)}) collective-permute-start(bf16[512,128]{1,0:T(8,128)(2,1)S(1)} %constant_dynamic-update-slice_fusion), channel_id=1, source_target_pairs={{0,80},{8,56},{16,96},{24,72},{32,112},{40,88},{48,0},{56,104},{64... | collective-permute-start | bytes 393224 | tf_op jit(solution)/shard_map/ppermute | solution.py:41
  8.1 17.3 %collective-permute-start.6 = (bf16[512,128]{1,0:T(8,128)(2,1)S(1)}, bf16[512,128]{1,0:T(8,128)(2,1)S(1)}, u32[]{:S(2)}, u32[]{:S(2)}) collective-permute-start(bf16[512,128]{1,0:T(8,128)(2,1)S(1)} %constant_dynamic-update-slice_fusion), channel_id=1, source_target_pairs={{0,96},{8,40},{16,112},{24,56},{32,0},{40,72},{48,16},{56,88},{64,... | collective-permute-start | bytes 393224 | tf_op jit(solution)/shard_map/ppermute | solution.py:41
  12.1 4.0 %collective-permute-start = (s32[2,64]{1,0:T(2,128)S(1)}, s32[2,64]{1,0:T(2,128)S(1)}, u32[]{:S(2)}, u32[]{:S(2)}) collective-permute-start(s32[2,64]{1,0:T(2,128)S(1)} %pad_add_fusion), channel_id=1, source_target_pairs={{0,8},{8,0},{16,24},{24,16},{32,40},{40,32},{48,56},{56,48},{64,72... | collective-permute-start | bytes 1544 | tf_op jit(solution)/shard_map/ppermute | solution.py:25
  12.1 8.1 %collective-permute-start.4 = (bf16[256,128]{1,0:T(8,128)(2,1)}, bf16[256,128]{1,0:T(8,128)(2,1)S(1)}, u32[]{:S(2)}, u32[]{:S(2)}) collective-permute-start(bf16[256,128]{1,0:T(8,128)(2,1)} %param.7), channel_id=1, source_target_pairs={{0,64},{8,72},{16,80},{24,88},{32,96},{40,104},{48,112},{56,120},{... | collective-permute-start | bytes 196616 | tf_op jit(solution)/shard_map/ppermute | solution.py:25
  16.2 6.7 %collective-permute-start.3 = (bf16[256,128]{1,0:T(8,128)(2,1)}, bf16[256,128]{1,0:T(8,128)(2,1)S(1)}, u32[]{:S(2)}, u32[]{:S(2)}) collective-permute-start(bf16[256,128]{1,0:T(8,128)(2,1)} %param.7), channel_id=1, source_target_pairs={{0,128},{8,136},{16,144},{24,152},{32,160},{40,168},{48,176},{56,1... | collective-permute-start | bytes 196616 | tf_op jit(solution)/shard_map/ppermute | solution.py:25
  20.3 11.0 %collective-permute-start.12 = (bf16[784,128]{1,0:T(8,128)(2,1)}, bf16[784,128]{1,0:T(8,128)(2,1)S(1)}, u32[]{:S(2)}, u32[]{:S(2)}) collective-permute-start(bf16[784,128]{1,0:T(8,128)(2,1)} %pack_up.1.a), channel_id=1, source_target_pairs={{0,4},{1,5},{2,6},{3,7},{4,0},{5,1},{6,2},{7,3},{8,12},{9,13},{10,... | collective-permute-start | bytes 602120 | tf_op jit(solution)/shard_map/ppermute | solution.py:29
  22.8 8.5 %collective-permute-start.5 = (bf16[512,128]{1,0:T(8,128)(2,1)S(1)}, bf16[512,128]{1,0:T(8,128)(2,1)S(1)}, u32[]{:S(2)}, u32[]{:S(2)}) collective-permute-start(bf16[512,128]{1,0:T(8,128)(2,1)S(1)} %constant_dynamic-update-slice_fusion), channel_id=1, source_target_pairs={{0,112},{8,24},{16,0},{24,40},{32,16},{40,56},{48,32},{56,72},{64,... | collective-permute-start | bytes 393224 | tf_op jit(solution)/shard_map/ppermute | solution.py:41
  25.1 6.2 %collective-permute-start.11 = (bf16[512,128]{1,0:T(8,128)(2,1)S(1)}, bf16[512,128]{1,0:T(8,128)(2,1)S(1)}, u32[]{:S(2)}, u32[]{:S(2)}) collective-permute-start(bf16[512,128]{1,0:T(8,128)(2,1)S(1)} %collective-permute-done.7), channel_id=1, source_target_pairs={{0,128},{8,136},{16,144},{24,152},{32,160},{40,168},{48,176},{56,1... | collective-permute-start | bytes 393224 | tf_op jit(solution)/shard_map/ppermute | solution.py:25
  25.4 7.2 %collective-permute-start.10 = (bf16[512,128]{1,0:T(8,128)(2,1)S(1)}, bf16[512,128]{1,0:T(8,128)(2,1)S(1)}, u32[]{:S(2)}, u32[]{:S(2)}) collective-permute-start(bf16[512,128]{1,0:T(8,128)(2,1)S(1)} %collective-permute-done.6), channel_id=1, source_target_pairs={{0,128},{8,136},{16,144},{24,152},{32,160},{40,168},{48,176},{56,1... | collective-permute-start | bytes 393224 | tf_op jit(solution)/shard_map/ppermute | solution.py:25
  26.6 0.7 copy-start.3
  27.2 0.7 copy-start.5
  27.9 0.7 copy-start.6
  32.7 0.9 copy-start.2
  33.6 8.1 %collective-permute-start.14 = (bf16[1568,128]{1,0:T(8,128)(2,1)S(1)}, bf16[1568,128]{1,0:T(8,128)(2,1)S(1)}, u32[]{:S(2)}, u32[]{:S(2)}) collective-permute-start(bf16[1568,128]{1,0:T(8,128)(2,1)S(1)} %append.2.refs_0_), channel_id=1, source_target_pairs={{0,3},{1,0},{2,1},{3,2},{4,7},{5,4},{6,5},{7,6},{8,11},{9,8},{10,9... | collective-permute-start | bytes 1204232 | tf_op jit(solution)/shard_map/ppermute | solution.py:29
  36.4 8.4 %collective-permute-start.13 = (bf16[1568,128]{1,0:T(8,128)(2,1)S(1)}, bf16[1568,128]{1,0:T(8,128)(2,1)S(1)}, u32[]{:S(2)}, u32[]{:S(2)}) collective-permute-start(bf16[1568,128]{1,0:T(8,128)(2,1)S(1)} %append.2.refs_0_), channel_id=1, source_target_pairs={{0,1},{1,2},{2,3},{3,0},{4,5},{5,6},{6,7},{7,4},{8,9},{9,10},{10,1... | collective-permute-start | bytes 1204232 | tf_op jit(solution)/shard_map/ppermute | solution.py:29
  36.4 4.8 %collective-permute-start.9 = (bf16[512,128]{1,0:T(8,128)(2,1)S(1)}, bf16[512,128]{1,0:T(8,128)(2,1)S(1)}, u32[]{:S(2)}, u32[]{:S(2)}) collective-permute-start(bf16[512,128]{1,0:T(8,128)(2,1)S(1)} %collective-permute-done.5.refs_0_), channel_id=1, source_target_pairs={{0,128},{8,136},{16,144},{24,152},{32,160},{40,168},{48,176},{56,1... | collective-permute-start | bytes 393224 | tf_op jit(solution)/shard_map/ppermute | solution.py:25
  36.4 4.8 %collective-permute-start.8 = (bf16[256,128]{1,0:T(8,128)(2,1)S(1)}, bf16[256,128]{1,0:T(8,128)(2,1)S(1)}, u32[]{:S(2)}, u32[]{:S(2)}) collective-permute-start(bf16[256,128]{1,0:T(8,128)(2,1)S(1)} %collective-permute-done.4.refs_1_), channel_id=1, source_target_pairs={{0,128},{8,136},{16,144},{24,152},{32,160},{40,168},{48,176},{56,1... | collective-permute-start | bytes 196616 | tf_op jit(solution)/shard_map/ppermute | solution.py:25
  44.9 14.2 %collective-permute-start.16 = (bf16[784,128]{1,0:T(8,128)(2,1)S(1)}, bf16[784,128]{1,0:T(8,128)(2,1)S(1)}, u32[]{:S(2)}, u32[]{:S(2)}) collective-permute-start(bf16[784,128]{1,0:T(8,128)(2,1)S(1)} %get-tuple-element.27.refs_10_), channel_id=1, source_target_pairs={{0,1},{1,2},{2,3},{3,0},{4,5},{5,6},{6,7},{7,4},{8,9},{9,10},{10,1... | collective-permute-start | bytes 602120 | tf_op jit(solution)/shard_map/ppermute | solution.py:29
  45.0 14.1 %collective-permute-start.17 = (bf16[784,128]{1,0:T(8,128)(2,1)S(1)}, bf16[784,128]{1,0:T(8,128)(2,1)S(1)}, u32[]{:S(2)}, u32[]{:S(2)}) collective-permute-start(bf16[784,128]{1,0:T(8,128)(2,1)S(1)} %get-tuple-element.28.refs_11_), channel_id=1, source_target_pairs={{0,3},{1,0},{2,1},{3,2},{4,7},{5,4},{6,5},{7,6},{8,11},{9,8},{10,9... | collective-permute-start | bytes 602120 | tf_op jit(solution)/shard_map/ppermute | solution.py:29
  47.6 17.2 %copy-start.4 = (s32[2]{0:T(128)S(1)}, s32[2]{0:T(128)}, u32[]{:S(2)}) copy-start(s32[2]{0:T(128)} %pad_add_fusion.1.ids) | copy-start | bytes 28
  54.1 23.5 %copy-start.1 = (bf16[128,1024]{1,0:T(8,128)(2,1)S(1)}, bf16[128,1024]{1,0:T(8,128)(2,1)}, u32[]{:S(2)}) copy-start(bf16[128,1024]{1,0:T(8,128)(2,1)} %w_own.1) | copy-start | bytes 786436
  54.1 6.0 %collective-permute-start.15 = (f32[2,128,128]{2,1,0:T(8,128)S(1)}, f32[2,128,128]{2,1,0:T(8,128)S(1)}, u32[]{:S(2)}, u32[]{:S(2)}) collective-permute-start(f32[2,128,128]{2,1,0:T(8,128)S(1)} %get-tuple-element.30), channel_id=1, source_target_pairs={{0,8},{8,0},{16,24},{24,16},{32,40},{40,32},{48,56},{56,48},{64,72... | collective-permute-start | bytes 393224 | tf_op jit(solution)/shard_map/ppermute | solution.py:25
  60.1 4.7 %collective-permute-start.18 = (bf16[256,128]{1,0:T(8,128)(2,1)S(1)}, bf16[256,128]{1,0:T(8,128)(2,1)S(1)}, u32[]{:S(2)}, u32[]{:S(2)}) collective-permute-start(bf16[256,128]{1,0:T(8,128)(2,1)S(1)} %bitcast.32), channel_id=1, source_target_pairs={{0,4},{1,5},{2,6},{3,7},{4,0},{5,1},{6,2},{7,3},{8,12},{9,13},{10,... | collective-permute-start | bytes 196616 | tf_op jit(solution)/shard_map/ppermute | solution.py:29
  66.3 11.4 %collective-permute-start.22 = (bf16[1024,512]{1,0:T(8,128)(2,1)S(1)}, bf16[1024,512]{1,0:T(8,128)(2,1)S(1)}, u32[]{:S(2)}, u32[]{:S(2)}) collective-permute-start(bf16[1024,512]{1,0:T(8,128)(2,1)S(1)} %get-tuple-element.31.w0), channel_id=1, source_target_pairs={{0,8},{8,0},{16,24},{24,16},{32,40},{40,32},{48,56},{56,48},{64,72... | collective-permute-start | bytes 3145736 | tf_op jit(solution)/shard_map/ppermute | solution.py:25
  67.9 6.6 %collective-permute-start.21 = (bf16[512,128]{1,0:T(8,128)(2,1)S(1)}, bf16[512,128]{1,0:T(8,128)(2,1)S(1)}, u32[]{:S(2)}, u32[]{:S(2)}) collective-permute-start(bf16[512,128]{1,0:T(8,128)(2,1)S(1)} %pad_maximum_fusion.2.refs_5_.p0), channel_id=1, source_target_pairs={{0,2},{1,3},{2,0},{3,1},{4,6},{5,7},{6,4},{7,5},{8,10},{9,11},{10,... | collective-permute-start | bytes 393224 | tf_op jit(solution)/shard_map/ppermute | solution.py:29
  67.9 6.7 %collective-permute-start.20 = (bf16[512,128]{1,0:T(8,128)(2,1)S(1)}, bf16[512,128]{1,0:T(8,128)(2,1)S(1)}, u32[]{:S(2)}, u32[]{:S(2)}) collective-permute-start(bf16[512,128]{1,0:T(8,128)(2,1)S(1)} %pad_maximum_fusion.2.refs_5_.p0), channel_id=1, source_target_pairs={{0,3},{1,0},{2,1},{3,2},{4,7},{5,4},{6,5},{7,6},{8,11},{9,8},{10,9... | collective-permute-start | bytes 393224 | tf_op jit(solution)/shard_map/ppermute | solution.py:29
  68.9 8.7 %collective-permute-start.19 = (bf16[512,128]{1,0:T(8,128)(2,1)S(1)}, bf16[512,128]{1,0:T(8,128)(2,1)S(1)}, u32[]{:S(2)}, u32[]{:S(2)}) collective-permute-start(bf16[512,128]{1,0:T(8,128)(2,1)S(1)} %pad_maximum_fusion.2.refs_5_.p0), channel_id=1, source_target_pairs={{0,1},{1,2},{2,3},{3,0},{4,5},{5,6},{6,7},{7,4},{8,9},{9,10},{10,1... | collective-permute-start | bytes 393224 | tf_op jit(solution)/shard_map/ppermute | solution.py:29
  79.8 1.7 %collective-permute-start.24 = (f32[64,1152]{1,0:T(8,128)S(1)}, f32[64,1152]{1,0:T(8,128)S(1)}, u32[]{:S(2)}, u32[]{:S(2)}) collective-permute-start(f32[64,1152]{1,0:T(8,128)S(1)} %get-tuple-element.37), channel_id=1, source_target_pairs={{0,8},{8,0},{16,24},{24,16},{32,40},{40,32},{48,56},{56,48},{64,72... | collective-permute-start | bytes 884744 | tf_op jit(solution)/shard_map/ppermute | solution.py:25
  80.3 2.5 %collective-permute-start.23 = (bf16[2,128,128]{2,1,0:T(8,128)(2,1)S(1)}, bf16[2,128,128]{2,1,0:T(8,128)(2,1)S(1)}, u32[]{:S(2)}, u32[]{:S(2)}) collective-permute-start(bf16[2,128,128]{2,1,0:T(8,128)(2,1)S(1)} %bitcast.36), channel_id=1, source_target_pairs={{0,8},{8,0},{16,24},{24,16},{32,40},{40,32},{48,56},{56,48},{64,72... | collective-permute-start | bytes 196616 | tf_op jit(solution)/shard_map/ppermute | solution.py:25
  81.5 7.3 %collective-permute-start.26 = (bf16[32,1152]{1,0:T(8,128)(2,1)S(1)}, bf16[32,1152]{1,0:T(8,128)(2,1)S(1)}, u32[]{:S(2)}, u32[]{:S(2)}) collective-permute-start(bf16[32,1152]{1,0:T(8,128)(2,1)S(1)} %fusion.send), channel_id=1, source_target_pairs={{0,128},{8,136},{16,144},{24,152},{32,160},{40,168},{48,176},{56,1... | collective-permute-start | bytes 221192 | tf_op jit(solution)/shard_map/ppermute | solution.py:25
  88.8 17.7 %collective-permute-start.25 = (bf16[16,128,128]{2,1,0:T(8,128)(2,1)S(1)}, bf16[16,128,128]{2,1,0:T(8,128)(2,1)S(1)}, u32[]{:S(2)}, u32[]{:S(2)}) collective-permute-start(bf16[16,128,128]{2,1,0:T(8,128)(2,1)S(1)} %get-tuple-element.39.far), channel_id=1, source_target_pairs={{0,128},{8,136},{16,144},{24,152},{32,160},{40,168},{48,176},{56,1... | collective-permute-start | bytes 1572872 | tf_op jit(solution)/shard_map/ppermute | solution.py:25
  88.9 1.7 %collective-permute-start.27 = (bf16[32,1152]{1,0:T(8,128)(2,1)S(1)}, bf16[32,1152]{1,0:T(8,128)(2,1)S(1)}, u32[]{:S(2)}, u32[]{:S(2)}) collective-permute-start(bf16[32,1152]{1,0:T(8,128)(2,1)S(1)} %quarter_up.1.own), channel_id=1, source_target_pairs={{0,8},{8,0},{16,24},{24,16},{32,40},{40,32},{48,56},{56,48},{64,72... | collective-permute-start | bytes 221192 | tf_op jit(solution)/shard_map/ppermute | solution.py:25
  90.6 8.5 %collective-permute-start.29 = (bf16[64,1152]{1,0:T(8,128)(2,1)S(1)}, bf16[64,1152]{1,0:T(8,128)(2,1)S(1)}, u32[]{:S(2)}, u32[]{:S(2)}) collective-permute-start(bf16[64,1152]{1,0:T(8,128)(2,1)S(1)} %pad_maximum_fusion.a), channel_id=1, source_target_pairs={{0,96},{8,40},{16,112},{24,56},{32,0},{40,72},{48,16},{56,88},{64,... | collective-permute-start | bytes 442376 | tf_op jit(solution)/shard_map/ppermute | solution.py:41
  94.7 11.7 %collective-permute-start.28 = (bf16[64,1152]{1,0:T(8,128)(2,1)S(1)}, bf16[64,1152]{1,0:T(8,128)(2,1)S(1)}, u32[]{:S(2)}, u32[]{:S(2)}) collective-permute-start(bf16[64,1152]{1,0:T(8,128)(2,1)S(1)} %pad_maximum_fusion.a), channel_id=1, source_target_pairs={{0,80},{8,56},{16,96},{24,72},{32,112},{40,88},{48,0},{56,104},{64... | collective-permute-start | bytes 442376 | tf_op jit(solution)/shard_map/ppermute | solution.py:41
  106.4 9.2 %collective-permute-start.34 = (bf16[96,1152]{1,0:T(8,128)(2,1)S(1)}, bf16[96,1152]{1,0:T(8,128)(2,1)S(1)}, u32[]{:S(2)}, u32[]{:S(2)}) collective-permute-start(bf16[96,1152]{1,0:T(8,128)(2,1)S(1)} %append.3.ready), channel_id=1, source_target_pairs={{0,112},{8,24},{16,0},{24,40},{32,16},{40,56},{48,32},{56,72},{64,... | collective-permute-start | bytes 663560 | tf_op jit(solution)/shard_map/ppermute | solution.py:41
  106.6 9.0 %collective-permute-start.30 = (bf16[6,128,128]{2,1,0:T(8,128)(2,1)S(1)}, bf16[6,128,128]{2,1,0:T(8,128)(2,1)S(1)}, u32[]{:S(2)}, u32[]{:S(2)}) collective-permute-start(bf16[6,128,128]{2,1,0:T(8,128)(2,1)S(1)} %get-tuple-element.41), channel_id=1, source_target_pairs={{0,16},{8,120},{16,32},{24,8},{32,48},{40,24},{48,64},{56,40},{64,... | collective-permute-start | bytes 589832 | tf_op jit(solution)/shard_map/ppermute | solution.py:41
  109.3 6.7 %collective-permute-start.31 = (bf16[4,128,128]{2,1,0:T(8,128)(2,1)S(1)}, bf16[4,128,128]{2,1,0:T(8,128)(2,1)S(1)}, u32[]{:S(2)}, u32[]{:S(2)}) collective-permute-start(bf16[4,128,128]{2,1,0:T(8,128)(2,1)S(1)} %get-tuple-element.42), channel_id=1, source_target_pairs={{0,32},{8,104},{16,48},{24,120},{32,64},{40,8},{48,80},{56,24},{64... | collective-permute-start | bytes 393224 | tf_op jit(solution)/shard_map/ppermute | solution.py:41
  115.6 4.3 %collective-permute-start.35 = (bf16[96,1152]{1,0:T(8,128)(2,1)S(1)}, bf16[96,1152]{1,0:T(8,128)(2,1)S(1)}, u32[]{:S(2)}, u32[]{:S(2)}) collective-permute-start(bf16[96,1152]{1,0:T(8,128)(2,1)S(1)} %peer_rows.1), channel_id=1, source_target_pairs={{0,8},{8,0},{16,24},{24,16},{32,40},{40,32},{48,56},{56,48},{64,72... | collective-permute-start | bytes 663560 | tf_op jit(solution)/shard_map/ppermute | solution.py:25
  116.0 8.6 %collective-permute-start.32 = (bf16[4,128,128]{2,1,0:T(8,128)(2,1)S(1)}, bf16[4,128,128]{2,1,0:T(8,128)(2,1)S(1)}, u32[]{:S(2)}, u32[]{:S(2)}) collective-permute-start(bf16[4,128,128]{2,1,0:T(8,128)(2,1)S(1)} %ride.1.t), channel_id=1, source_target_pairs={{0,48},{8,88},{16,64},{24,104},{32,80},{40,120},{48,96},{56,8},{64... | collective-permute-start | bytes 393224 | tf_op jit(solution)/shard_map/ppermute | solution.py:41
  120.7 5.5 %collective-permute-start.36 = (bf16[32,1152]{1,0:T(8,128)(2,1)S(1)}, bf16[32,1152]{1,0:T(8,128)(2,1)S(1)}, u32[]{:S(2)}, u32[]{:S(2)}) collective-permute-start(bf16[32,1152]{1,0:T(8,128)(2,1)S(1)} %sum_z.1), channel_id=1, source_target_pairs={{0,128},{8,136},{16,144},{24,152},{32,160},{40,168},{48,176},{56,1... | collective-permute-start | bytes 221192 | tf_op jit(solution)/shard_map/ppermute | solution.py:25
  124.7 2.5 %collective-permute-start.33 = (f32[2,128,128]{2,1,0:T(8,128)S(1)}, f32[2,128,128]{2,1,0:T(8,128)S(1)}, u32[]{:S(2)}, u32[]{:S(2)}) collective-permute-start(f32[2,128,128]{2,1,0:T(8,128)S(1)} %slice.35), channel_id=1, source_target_pairs={{0,8},{8,0},{16,24},{24,16},{32,40},{40,32},{48,56},{56,48},{64,72... | collective-permute-start | bytes 393224 | tf_op jit(solution)/shard_map/ppermute | solution.py:25
  126.2 1.7 %collective-permute-start.37 = (bf16[64,1152]{1,0:T(8,128)(2,1)S(1)}, bf16[64,1152]{1,0:T(8,128)(2,1)S(1)}, u32[]{:S(2)}, u32[]{:S(2)}) collective-permute-start(bf16[64,1152]{1,0:T(8,128)(2,1)S(1)} %pad_maximum_fusion.1.mine), channel_id=1, source_target_pairs={{0,8},{8,0},{16,24},{24,16},{32,40},{40,32},{48,56},{56,48},{64,72... | collective-permute-start | bytes 442376 | tf_op jit(solution)/shard_map/ppermute | solution.py:25

commit v6 on v4

--- a/solution.py
+++ b/solution.py
@@ -98,26 +98,27 @@
     )(a, b, *ready)
 
 
-def turn_body(u, d, a, b):
+def turn_body(u, d, *refs):
+    a, b = refs[-2:]
     a[...] = u[0:784, :]
     b[...] = d[784:1568, :]
 
 
-def turn(u, d):
+def turn(u, d, *ready):
     half = jax.ShapeDtypeStruct((784, B), bf16)
     return pl.pallas_call(
         turn_body,
         out_shape=(half, half),
-        in_specs=[VM, VM],
+        in_specs=[VM, VM] + [ANY] * len(ready),
         out_specs=(VM, VM),
         compiler_params=params(4),
         cost_estimate=cost(0, 1 << 18),
         name="turn",
-    )(u, d)
+    )(u, d, *ready)
 
 
 def settle_body(mine, came, a, b, agg):
-    agg[...] = (mine[...] + came[...]).astype(bf16)
+    agg[...] = (mine[0:2] + came[...]).astype(bf16)
 
 
 def settle(mine, came, a, b):
@@ -136,9 +137,9 @@
     me = ids[0]
     mx, mz, mc = me >> 4, (me >> 1) & 7, me & 1
     for side, (cols, dest) in enumerate(((c0, d0), (c1, d1))):
-        base = 8 + 72 * side
-
-        def step(i, n, cols=cols, dest=dest, base=base, side=side):
+        base = 8 + 144 * side
+
+        def step(i, count, cols=cols, dest=dest, base=base, side=side):
             b = cols[i]
             o = b >> 1
             dx, dz, dc = (o >> 4) ^ mx, ((o >> 1) - mz) & 7, (o & 1) ^ mc
@@ -146,20 +147,22 @@
             edge = (dz & 3) == 0
             held = jnp.where(edge, 1 - dc, jnp.where(k <= 3, 1, 0))
             j = jnp.where(edge, jnp.where(dz == 0, 7, 6), (3 - k) * 2 + dc)
-            slot = dx * 16 + j * 2 + (b & 1)
-            out[base + n] = i | (slot << 8) | ((dest[i] + 2 * side) << 16)
-            return n + held
-
-        n = lax.fori_loop(0, 64, step, 0, unroll=8)
-        for u in range(4):
-            out[base + n + u] = (32 << 8) | (4 << 16)
-        out[side] = (n + 3) >> 2
+            slot = j * 2 + (b & 1)
+            n = jnp.where(dx == 0, count[0], count[1])
+            out[base + dx * 72 + n] = i | (slot << 8) | ((dest[i] + 2 * side) << 16)
+            return count[0] + held * (1 - dx), count[1] + held * dx
+
+        count = lax.fori_loop(0, 64, step, (0, 0), unroll=8)
+        for dx in range(2):
+            for u in range(4):
+                out[base + dx * 72 + count[dx] + u] = (16 << 8) | (4 << 16)
+            out[side * 2 + dx] = (count[dx] + 3) >> 2
 
 
 def plan_tiles(ids, c0, d0, c1, d1):
     return pl.pallas_call(
         plan_body,
-        out_shape=jax.ShapeDtypeStruct((160,), jnp.int32),
+        out_shape=jax.ShapeDtypeStruct((304,), jnp.int32),
         in_specs=[SM] * 5,
         out_specs=SM,
         compiler_params=params(4),
@@ -168,60 +171,57 @@
     )(ids, c0, d0, c1, d1)
 
 
-def each_tile(plan, tiles, more, use):
+def each_tile(plan, dx, tiles, more, use):
     for side, ref in enumerate((tiles, more)):
-        def step(g, carry, side=side, ref=ref):
+        base = 8 + 144 * side + 72 * dx
+
+        def step(g, carry, base=base, ref=ref):
             for u in range(4):
-                e = plan[8 + 72 * side + g * 4 + u]
+                e = plan[base + g * 4 + u]
                 use(ref[e & 255], (e >> 8) & 255, e >> 16)
             return carry
 
-        lax.fori_loop(0, plan[side], step, 0)
-
-
-def agg_body(plan, tiles, more, *refs):
-    mine, theirs, src, acc, sem = refs[10:]
-    both, x0, o14, o2, o3, p14, p2, p3 = refs[0:8]
+        lax.fori_loop(0, plan[side * 2 + dx], step, 0)
+
+
+def agg_body(dx, plan, tiles, more, v3, v2, v14, v0, *refs):
+    start, out, src, acc, sem = refs[0], *refs[-4:]
     copies = []
-
-    def put(dx, j, v):
-        n = v.shape[0]
-        at = dx * 16 + j * 2
-        copies.append(pltpu.make_async_copy(v, src.at[at : at + n], sem.at[len(copies)]))
+    for n, v in ((0, v3), (4, v2), (8, v14), (14, v0.at[0:2])):
+        at = src.at[n : n + v.shape[0]]
+        copies.append(pltpu.make_async_copy(v, at, sem.at[len(copies)]))
         copies[-1].start()
-
-    for dx, (v3, v2, v14, v0) in enumerate(((o3, o2, o14, both.at[0:2]), (p3, p2, p14, x0))):
-        for j, v in ((0, v3), (2, v2), (4, v14), (7, v0)):
-            put(dx, j, v)
-    acc[...] = jnp.zeros_like(acc)
-    src[32] = jnp.zeros((B, B), bf16)
+    if dx == 0:
+        acc[...] = jnp.zeros_like(acc)
+    else:
+        acc[0:4] = start[...]
+    src[16] = jnp.zeros((B, B), bf16)
     for c in copies:
         c.wait()
 
     def use(tile, slot, dest):
         acc[dest] += jnp.dot(tile, src[slot], preferred_element_type=f32)
 
-    each_tile(plan, tiles, more, use)
-    mine[...] = acc[0:2]
-    theirs[...] = acc[2:4]
-
-
-def aggregate(plan, tiles, more, pieces, *ready):
+    each_tile(plan, dx, tiles, more, use)
+    out[...] = acc[0:4]
+
+
+def aggregate(dx, plan, tiles, more, pieces, start, *ready):
     parts = [v.reshape(-1, B, B) for v in pieces]
     return pl.pallas_call(
-        agg_body,
-        out_shape=(jax.ShapeDtypeStruct((2, B, B), f32), jax.ShapeDtypeStruct((2, B, B), f32)),
-        in_specs=[SM, VM, VM] + [HB] * 8 + [ANY] * 2,
-        out_specs=(VM, VM),
+        functools.partial(agg_body, dx),
+        out_shape=jax.ShapeDtypeStruct((4, B, B), f32),
+        in_specs=[SM, VM, VM] + [HB] * 4 + [VM if dx else ANY] + [ANY] * len(ready),
+        out_specs=VM,
         scratch_shapes=[
-            pltpu.VMEM((33, B, B), bf16),
+            pltpu.VMEM((17, B, B), bf16),
             pltpu.VMEM((5, B, B), f32),
-            pltpu.SemaphoreType.DMA((8,)),
+            pltpu.SemaphoreType.DMA((4,)),
         ],
-        compiler_params=params(12),
-        cost_estimate=cost(2 * 64 * B**3, 4 << 20),
+        compiler_params=params(8),
+        cost_estimate=cost(2 * 32 * B**3, 3 << 20),
         name="aggregate",
-    )(plan, tiles, more, *parts, *ready)
+    )(plan, tiles, more, *parts, start, *ready)
 
 
 def lay_body(ids, *refs):
@@ -319,7 +319,7 @@
     )(ids, *pieces, w0, w1, og, bias, w_own)
 
 
-def spread_body(plan, tiles, more, prop, peer, send, near, far, acc, both):
+def spread_body(dx, plan, tiles, more, prop, peer, ready, out, acc, both):
     acc[...] = jnp.zeros_like(acc)
     both[0:2] = prop[...]
     both[2:4] = peer[...]
@@ -330,25 +330,21 @@
             tile, both[dest], (((0,), (0,)), ((), ())), preferred_element_type=f32
         )
 
-    each_tile(plan, tiles, more, use)
-    near[...] = acc[0:16]
-    far[...] = acc[16:32].astype(bf16)
-
-
-def spread(plan, tiles, more, prop, peer, send):
-    return pl.pallas_call(
-        spread_body,
-        out_shape=(
-            jax.ShapeDtypeStruct((16, B, B), f32),
-            jax.ShapeDtypeStruct((16, B, B), bf16),
-        ),
+    each_tile(plan, dx, tiles, more, use)
+    out[...] = acc[0:16].astype(out.dtype)
+
+
+def spread(dx, plan, tiles, more, prop, peer, ready):
+    return pl.pallas_call(
+        functools.partial(spread_body, dx),
+        out_shape=jax.ShapeDtypeStruct((16, B, B), bf16 if dx else f32),
         in_specs=[SM] + [VM] * 4 + [ANY],
-        out_specs=(VM, VM),
-        scratch_shapes=[pltpu.VMEM((33, B, B), f32), pltpu.VMEM((5, B, B), bf16)],
-        compiler_params=params(12),
-        cost_estimate=cost(2 * 64 * B**3, 6 << 20),
+        out_specs=VM,
+        scratch_shapes=[pltpu.VMEM((17, B, B), f32), pltpu.VMEM((5, B, B), bf16)],
+        compiler_params=params(8),
+        cost_estimate=cost(2 * 32 * B**3, 4 << 20),
         name="spread",
-    )(plan, tiles, more, prop, peer, send)
+    )(plan, tiles, more, prop, peer, ready)
 
 
 def quarter_body(keep, got, came, far, out):
@@ -489,16 +485,16 @@
     pack = pack_up(ids, weight, out_grad, bias_vector[None, :])
     pack_x = feat_send(pack, dx=1)
 
-    pair = append(1568, pack, pack_x)
-    ext = append(768, both, o3, o2, x0, plan, pair)
-    o14 = spin_send(ext, 1, -1)
+    pair = append(1568, pack, pack_x, o3, o2, x0)
+    o14 = spin_send(append(768, both, o3), 1, -1)
     p3, p2, p14 = row_send(o3, dx=1), row_send(o2, dx=1), row_send(o14, dx=1)
     wu, wd = feat_send(pair, dy=1), feat_send(pair, dy=-1)
 
-    wa, wb = turn(wu, wd)
-    mine, theirs = aggregate(plan, adj_tiles, more, (both_a, x0, o14, o2, o3, p14, p2, p3), wa, wb)
+    wa, wb = turn(wu, wd, plan, p3, p2)
+    sums = aggregate(0, plan, adj_tiles, more, (o3, o2, o14, both_a), ids)
+    sums = aggregate(1, plan, adj_tiles, more, (p3, p2, p14, x0), sums, wa, wb)
     wa, wb = feat_send(wa, dy=1), feat_send(wb, dy=-1)
-    aggregated = settle(mine, row_send(theirs, dc=1), wa, wb).reshape(256, B)
+    aggregated = settle(sums, row_send(sums[2:], dc=1), wa, wb).reshape(256, B)
 
     q = jnp.concatenate([aggregated, feat_send(aggregated, dx=1)], axis=0)
     w0, og, bias = lay_out(ids, (pair, wu, wd, wa, wb), q)
@@ -510,9 +506,10 @@
     got = row_send(give, dc=1)
     send = (keep[32:] + got[32:]).astype(bf16)
     got_x = row_send(send, dx=1)
-    near, far = spread(plan, adj_tiles, more, prop, peer, send)
+    far = spread(1, plan, adj_tiles, more, prop, peer, send)
     came = row_send(far, dx=1)
-    quarter = quarter_up(keep, got, got_x, far)
+    near = spread(0, plan, adj_tiles, more, prop, peer, far)
+    quarter = quarter_up(keep, got, got_x, near)
     halves = jnp.concatenate([quarter, row_send(quarter, dc=1)], axis=0)
     d3, d2 = spin_send(halves, 3, -1), spin_send(halves, 2, -1)
     last = append(96, halves, d3, d2)

time: 124 us -> 128 us (1.032)
  waiting for transfers between devices: 41.8 us -> 34.9 us
  starting transfers between devices: 52.8 us -> 58.7 us
  Pallas kernels: 22.1 us -> 26.9 us
    ppermute x9, waiting for transfers between devices: 22.3 us -> 15.1 us  [spin_send(): return lax.ppermute(v, 'row', perm)]
    ppermute x9, starting transfers between devices: 19.2 us -> 25.9 us  [spin_send(): return lax.ppermute(v, 'row', perm)]
    pallas_call x4 -> x6, Pallas kernels: 13.9 us -> 18.7 us  [the longest x2 8.07 us: aggregate(): pl.pallas_call(functools.partial(agg_body, dx), out_shape=jax.ShapeDtypeS...]
    ppermute x18, waiting for transfers between devices: 7.11 us -> 8.58 us  [row_send(): return lax.ppermute(v, 'row', perm)]
  transfers between devices with their start and end apart: 36 -> 36, of which waited for: 17 -> 17; matrix products, arithmetic and copies ran while one was open for 2% -> 2% of each run, Pallas kernels for 14% -> 17%
where the time goes in v6:
time: 128 us
  starting transfers between devices  58.7 us (46%)
  waiting for transfers between devices  34.9 us (27%)
  Pallas kernels  26.9 us (21%)
  local copies, waits for them, and re-layouts  4.3 us (3%)
  other arithmetic  2.05 us (2%)
    ppermute x9, starting transfers between devices, spin_send(): return lax.ppermute(v, 'row', perm)  25.9 us
    ppermute x18, starting transfers between devices, row_send(): return lax.ppermute(v, 'row', perm)  22.3 us
    ppermute x9, waiting for transfers between devices, spin_send(): return lax.ppermute(v, 'row', perm)  15.1 us
    ppermute x9, waiting for transfers between devices, feat_send(): lax.ppermute(v, 'feat', [(i, (i >> 2 ^ dx) << 2 | i + dy & 3) for i in ra...  11.2 us
    ppermute x9, starting transfers between devices, feat_send(): lax.ppermute(v, 'feat', [(i, (i >> 2 ^ dx) << 2 | i + dy & 3) for i in ra...  10.5 us
    ppermute x18, waiting for transfers between devices, row_send(): return lax.ppermute(v, 'row', perm)  8.58 us
    pallas_call x2, Pallas kernels, aggregate(): pl.pallas_call(functools.partial(agg_body, dx), out_shape=jax.ShapeDtypeS...  8.07 us
    pallas_call x2, Pallas kernels, spread(): pl.pallas_call(functools.partial(spread_body, dx), out_shape=jax.ShapeDty...  7.53 us
  transfers between devices with their start and end apart: 36, of which 17 were waited for; matrix products, arithmetic and copies ran while one was open for 2% of the time, Pallas kernels for 17%

profile of v6, /device:TPU:1, one launch (start us, length us, event | category | flops | bytes accessed | tf_op | source)
XLA Modules:
  0.0 127.7 jit_solution(8188500924454421033)
XLA Ops:
  0.6 3.3 %collective-permute-start.1 = (bf16[256,128]{1,0:T(8,128)(2,1)}, bf16[256,128]{1,0:T(8,128)(2,1)S(1)}, u32[]{:S(2)}, u32[]{:S(2)}) collective-permute-start(bf16[256,128]{1,0:T(8,128)(2,1)} %param.7), channel_id=1, source_target_pairs={{0,8},{8,0},{16,24},{24,16},{32,40},{40,32},{48,56},{56,48},{64,72... | collective-permute-start | bytes 196616 | tf_op jit(solution)/shard_map/ppermute | solution.py:25
  4.0 0.8 constant_dynamic-update-slice_fusion.1
  6.1 2.3 %pack_up.1.a = bf16[784,128]{1,0:T(8,128)(2,1)} custom-call(s32[2]{0:T(128)} %pad_add_fusion.1.ids.refs_0_, bf16[128,1024]{1,0:T(8,128)(2,1)} %w_own.1, bf16[256,128]{1,0:T(8,128)(2,1)} %og.1, bf16[1,128]{1,0:T(2,128)(2,1)} %bitcast.38), custom_call_target="tpu_custom_call" | custom-call | bytes 524288 | tf_op jit(solution)/shard_map/pack_up/pallas_call | solution.py:70
  8.4 1.1 collective-permute-start.10
  9.5 4.3 %collective-permute-start.3 = (bf16[512,128]{1,0:T(8,128)(2,1)S(1)}, bf16[512,128]{1,0:T(8,128)(2,1)S(1)}, u32[]{:S(2)}, u32[]{:S(2)}) collective-permute-start(bf16[512,128]{1,0:T(8,128)(2,1)S(1)} %constant_dynamic-update-slice_fusion.a), channel_id=1, source_target_pairs={{0,80},{8,56},{16,96},{24,72},{32,112},{40,88},{48,0},{56,104},{64... | collective-permute-start | bytes 393224 | tf_op jit(solution)/shard_map/ppermute | solution.py:41
  13.9 3.3 %collective-permute-start.5 = (bf16[512,128]{1,0:T(8,128)(2,1)S(1)}, bf16[512,128]{1,0:T(8,128)(2,1)S(1)}, u32[]{:S(2)}, u32[]{:S(2)}) collective-permute-start(bf16[512,128]{1,0:T(8,128)(2,1)S(1)} %constant_dynamic-update-slice_fusion.a), channel_id=1, source_target_pairs={{0,96},{8,40},{16,112},{24,56},{32,0},{40,72},{48,16},{56,88},{64,... | collective-permute-start | bytes 393224 | tf_op jit(solution)/shard_map/ppermute | solution.py:41
  17.5 1.0 collective-permute-done.3.b.refs_0_
  18.6 4.4 %collective-permute-start.7 = (bf16[768,128]{1,0:T(8,128)(2,1)S(1)}, bf16[768,128]{1,0:T(8,128)(2,1)S(1)}, u32[]{:S(2)}, u32[]{:S(2)}) collective-permute-start(bf16[768,128]{1,0:T(8,128)(2,1)S(1)} %append.3), channel_id=1, source_target_pairs={{0,112},{8,24},{16,0},{24,40},{32,16},{40,56},{48,32},{56,72},{64,... | collective-permute-start | bytes 589832 | tf_op jit(solution)/shard_map/ppermute | solution.py:41
  23.5 0.9 copy-done.2
  24.4 2.8 %collective-permute-start.12 = (bf16[1568,128]{1,0:T(8,128)(2,1)S(1)}, bf16[1568,128]{1,0:T(8,128)(2,1)S(1)}, u32[]{:S(2)}, u32[]{:S(2)}) collective-permute-start(bf16[1568,128]{1,0:T(8,128)(2,1)S(1)} %append.4.refs_0_), channel_id=1, source_target_pairs={{0,3},{1,0},{2,1},{3,2},{4,7},{5,4},{6,5},{7,6},{8,11},{9,8},{10,9... | collective-permute-start | bytes 1204232 | tf_op jit(solution)/shard_map/ppermute | solution.py:29
  27.9 1.7 %collective-permute-start = (s32[2,64]{1,0:T(2,128)S(1)}, s32[2,64]{1,0:T(2,128)S(1)}, u32[]{:S(2)}, u32[]{:S(2)}) collective-permute-start(s32[2,64]{1,0:T(2,128)S(1)} %pad_add_fusion), channel_id=1, source_target_pairs={{0,8},{8,0},{16,24},{24,16},{32,40},{40,32},{48,56},{56,48},{64,72... | collective-permute-start | bytes 1544 | tf_op jit(solution)/shard_map/ppermute | solution.py:25
  29.6 0.8 collective-permute-done
  30.7 4.5 %collective-permute-done.6.refs_2_ = bf16[512,128]{1,0:T(8,128)(2,1)S(1)} collective-permute-done((bf16[512,128]{1,0:T(8,128)(2,1)S(1)}, bf16[512,128]{1,0:T(8,128)(2,1)S(1)}, u32[]{:S(2)}, u32[]{:S(2)}) %collective-permute-start.6) | collective-permute-done | bytes 131104 | tf_op jit(solution)/shard_map/ppermute | solution.py:25
  35.5 1.2 collective-permute-start.8
  38.6 3.1 %plan_tiles.1.plan.refs_0_ = s32[304]{0:T(512)S(1)} custom-call(s32[2]{0:T(128)S(1)} %copy-done.3, s32[64]{0:T(128)S(1)} %copy-done.5, s32[64]{0:T(128)S(1)} %copy-done.6, s32[64]{0:T(128)S(1)} %get-tuple-element.39.c1, s32[64]{0:T(128)S(1)} %get-tuple-element.38.d1), custom_call_target="tpu_custom_call" | custom-call | flops 10000 | bytes 4096 | tf_op jit(solution)/shard_map/plan_tiles/pallas_call | solution.py:163
  42.2 2.7 %collective-permute-start.15 = (bf16[784,128]{1,0:T(8,128)(2,1)S(1)}, bf16[784,128]{1,0:T(8,128)(2,1)S(1)}, u32[]{:S(2)}, u32[]{:S(2)}) collective-permute-start(bf16[784,128]{1,0:T(8,128)(2,1)S(1)} %get-tuple-element.24.refs_2_), channel_id=1, source_target_pairs={{0,3},{1,0},{2,1},{3,2},{4,7},{5,4},{6,5},{7,6},{8,11},{9,8},{10,9... | collective-permute-start | bytes 602120 | tf_op jit(solution)/shard_map/ppermute | solution.py:29
  44.9 4.2 %aggregate.2.refs_0_ = f32[4,128,128]{2,1,0:T(8,128)S(1)} custom-call(s32[304]{0:T(512)S(1)} %plan_tiles.1.plan.refs_0_, bf16[64,128,128]{2,1,0:T(8,128)(2,1)S(1)} %copy-done, bf16[64,128,128]{2,1,0:T(8,128)(2,1)} %collective-permute-done.2.more, bf16[4,128,128]{2,1,0:T(8,128)(2,1)S(1)} %bitcast.22, bf16[4,128,128]{2,1,0:T(8,128)(2,1)S(1)} %bitcast.24, ...), custom_call_target="tpu_custom_call" | custom-call | flops 134217728 | bytes 3145728 | tf_op jit(solution)/shard_map/aggregate/pallas_call | solution.py:211
  49.1 3.8 %aggregate.3.mine = f32[4,128,128]{2,1,0:T(8,128)S(1)} custom-call(s32[304]{0:T(512)S(1)} %plan_tiles.1.plan.refs_0_, bf16[64,128,128]{2,1,0:T(8,128)(2,1)S(1)} %copy-done, bf16[64,128,128]{2,1,0:T(8,128)(2,1)} %collective-permute-done.2.more, bf16[4,128,128]{2,1,0:T(8,128)(2,1)S(1)} %bitcast.26, bf16[4,128,128]{2,1,0:T(8,128)(2,1)S(1)} %bitcast.25, ...), custom_call_target="tpu_custom_call" | custom-call | flops 134217728 | bytes 3145728 | tf_op jit(solution)/shard_map/aggregate/pallas_call | solution.py:211
  53.0 1.9 %collective-permute-start.13 = (f32[2,128,128]{2,1,0:T(8,128)S(1)}, f32[2,128,128]{2,1,0:T(8,128)S(1)}, u32[]{:S(2)}, u32[]{:S(2)}) collective-permute-start(f32[2,128,128]{2,1,0:T(8,128)S(1)} %slice.36), channel_id=1, source_target_pairs={{0,8},{8,0},{16,24},{24,16},{32,40},{40,32},{48,56},{56,48},{64,72... | collective-permute-start | bytes 393224 | tf_op jit(solution)/shard_map/ppermute | solution.py:25
  54.9 1.0 collective-permute-done.13.came
  55.9 0.8 collective-permute-start.16
  56.8 4.0 %collective-permute-done.16 = bf16[256,128]{1,0:T(8,128)(2,1)S(1)} collective-permute-done((bf16[256,128]{1,0:T(8,128)(2,1)S(1)}, bf16[256,128]{1,0:T(8,128)(2,1)S(1)}, u32[]{:S(2)}, u32[]{:S(2)}) %collective-permute-start.16) | collective-permute-done | bytes 65568 | tf_op jit(solution)/shard_map/ppermute | solution.py:29
  60.8 1.4 %lay_out.1 = (bf16[1024,512]{1,0:T(8,128)(2,1)S(1)}, bf16[256,1024]{1,0:T(8,128)(2,1)S(1)}, f32[8,1024]{1,0:T(8,128)S(1)}) custom-call(s32[2]{0:T(128)S(1)} %copy-done.4, bf16[1568,128]{1,0:T(8,128)(2,1)S(1)} %append.4.refs_0_, bf16[1568,128]{1,0:T(8,128)(2,1)S(1)} %collective-permute-done.11.u.refs_1_, ...), custom_call_target="tpu_custom_call" | custom-call | bytes 3145728 | tf_op jit(solution)/shard_map/lay_out/pallas_call | solution.py:254
  62.3 1.6 %collective-permute-start.20 = (bf16[1024,512]{1,0:T(8,128)(2,1)S(1)}, bf16[1024,512]{1,0:T(8,128)(2,1)S(1)}, u32[]{:S(2)}, u32[]{:S(2)}) collective-permute-start(bf16[1024,512]{1,0:T(8,128)(2,1)S(1)} %get-tuple-element.25.w0), channel_id=1, source_target_pairs={{0,8},{8,0},{16,24},{24,16},{32,40},{40,32},{48,56},{56,48},{64,72... | collective-permute-start | bytes 3145736 | tf_op jit(solution)/shard_map/ppermute | solution.py:25
  63.9 1.1 collective-permute-start.19
  65.5 0.9 collective-permute-start.17
  66.4 4.0 %collective-permute-done.19.p3 = bf16[512,128]{1,0:T(8,128)(2,1)S(1)} collective-permute-done((bf16[512,128]{1,0:T(8,128)(2,1)S(1)}, bf16[512,128]{1,0:T(8,128)(2,1)S(1)}, u32[]{:S(2)}, u32[]{:S(2)}) %collective-permute-start.19) | collective-permute-done | bytes 131104 | tf_op jit(solution)/shard_map/ppermute | solution.py:29
  70.4 2.1 %collective-permute-done.18.p2 = bf16[512,128]{1,0:T(8,128)(2,1)S(1)} collective-permute-done((bf16[512,128]{1,0:T(8,128)(2,1)S(1)}, bf16[512,128]{1,0:T(8,128)(2,1)S(1)}, u32[]{:S(2)}, u32[]{:S(2)}) %collective-permute-start.18) | collective-permute-done | bytes 131104 | tf_op jit(solution)/shard_map/ppermute | solution.py:29
  72.5 1.1 collective-permute-done.17.p1
  73.6 2.1 %middle.1 = (f32[256,128]{1,0:T(8,128)}, bf16[256,128]{1,0:T(8,128)(2,1)S(1)}, f32[64,1152]{1,0:T(8,128)S(1)}, f32[64,1152]{1,0:T(8,128)S(1)}) custom-call(s32[2]{0:T(128)S(1)} %copy-done.4, bf16[512,128]{1,0:T(8,128)(2,1)S(1)} %pad_maximum_fusion.2.refs_5_.p0, bf16[512,128]{1,0:T(8,128)(2,1)S(1)} %collective-permute-done.17.p1, ...), custom_call_target="tpu_custom_call" | custom-call | flops 671088640 | bytes 5242880 | tf_op jit(solution)/shard_map/middle/pallas_call | solution.py:300
  76.3 1.2 collective-permute-done.22.got
  77.9 3.5 %spread.2.ready = bf16[16,128,128]{2,1,0:T(8,128)(2,1)S(1)} custom-call(s32[304]{0:T(512)S(1)} %plan_tiles.1.plan.refs_0_, bf16[64,128,128]{2,1,0:T(8,128)(2,1)S(1)} %copy-done, bf16[64,128,128]{2,1,0:T(8,128)(2,1)} %collective-permute-done.2.more, bf16[2,128,128]{2,1,0:T(8,128)(2,1)S(1)} %bitcast.28, bf16[2,128,128]{2,1,0:T(8,128)(2,1)S(1)} %collective-permute-done.21.peer, ...), custom_call_target="tpu_custom_call" | custom-call | flops 134217728 | bytes 4194304 | tf_op jit(solution)/shard_map/spread/pallas_call | solution.py:338
  81.4 4.0 %spread.3.far.near = f32[16,128,128]{2,1,0:T(8,128)S(1)} custom-call(s32[304]{0:T(512)S(1)} %plan_tiles.1.plan.refs_0_, bf16[64,128,128]{2,1,0:T(8,128)(2,1)S(1)} %copy-done, bf16[64,128,128]{2,1,0:T(8,128)(2,1)} %collective-permute-done.2.more, bf16[2,128,128]{2,1,0:T(8,128)(2,1)S(1)} %bitcast.29, bf16[2,128,128]{2,1,0:T(8,128)(2,1)S(1)} %collective-permute-done.21.peer, ...), custom_call_target="tpu_custom_call" | custom-call | flops 134217728 | bytes 4194304 | tf_op jit(solution)/shard_map/spread/pallas_call | solution.py:338
  86.0 1.2 collective-permute-start.23
  87.2 2.1 %collective-permute-start.27 = (bf16[64,1152]{1,0:T(8,128)(2,1)S(1)}, bf16[64,1152]{1,0:T(8,128)(2,1)S(1)}, u32[]{:S(2)}, u32[]{:S(2)}) collective-permute-start(bf16[64,1152]{1,0:T(8,128)(2,1)S(1)} %pad_maximum_fusion.a), channel_id=1, source_target_pairs={{0,96},{8,40},{16,112},{24,56},{32,0},{40,72},{48,16},{56,88},{64,... | collective-permute-start | bytes 442376 | tf_op jit(solution)/shard_map/ppermute | solution.py:41
  89.3 2.8 %collective-permute-start.26 = (bf16[64,1152]{1,0:T(8,128)(2,1)S(1)}, bf16[64,1152]{1,0:T(8,128)(2,1)S(1)}, u32[]{:S(2)}, u32[]{:S(2)}) collective-permute-start(bf16[64,1152]{1,0:T(8,128)(2,1)S(1)} %pad_maximum_fusion.a), channel_id=1, source_target_pairs={{0,80},{8,56},{16,96},{24,72},{32,112},{40,88},{48,0},{56,104},{64... | collective-permute-start | bytes 442376 | tf_op jit(solution)/shard_map/ppermute | solution.py:41
  92.0 5.1 %collective-permute-done.27.refs_0_.d2 = bf16[64,1152]{1,0:T(8,128)(2,1)S(1)} collective-permute-done((bf16[64,1152]{1,0:T(8,128)(2,1)S(1)}, bf16[64,1152]{1,0:T(8,128)(2,1)S(1)}, u32[]{:S(2)}, u32[]{:S(2)}) %collective-permute-start.27) | collective-permute-done | bytes 147488 | tf_op jit(solution)/shard_map/ppermute | solution.py:41
  97.1 1.0 collective-permute-done.26.b.d3
  98.1 2.7 %collective-permute-start.32 = (bf16[96,1152]{1,0:T(8,128)(2,1)S(1)}, bf16[96,1152]{1,0:T(8,128)(2,1)S(1)}, u32[]{:S(2)}, u32[]{:S(2)}) collective-permute-start(bf16[96,1152]{1,0:T(8,128)(2,1)S(1)} %append.5.ready), channel_id=1, source_target_pairs={{0,112},{8,24},{16,0},{24,40},{32,16},{40,56},{48,32},{56,72},{64,... | collective-permute-start | bytes 663560 | tf_op jit(solution)/shard_map/ppermute | solution.py:41
  100.9 3.4 %collective-permute-start.29 = (bf16[4,128,128]{2,1,0:T(8,128)(2,1)S(1)}, bf16[4,128,128]{2,1,0:T(8,128)(2,1)S(1)}, u32[]{:S(2)}, u32[]{:S(2)}) collective-permute-start(bf16[4,128,128]{2,1,0:T(8,128)(2,1)S(1)} %get-tuple-element.34), channel_id=1, source_target_pairs={{0,32},{8,104},{16,48},{24,120},{32,64},{40,8},{48,80},{56,24},{64... | collective-permute-start | bytes 393224 | tf_op jit(solution)/shard_map/ppermute | solution.py:41
  105.7 2.7 %collective-permute-done.29.t = bf16[4,128,128]{2,1,0:T(8,128)(2,1)S(1)} collective-permute-done((bf16[4,128,128]{2,1,0:T(8,128)(2,1)S(1)}, bf16[4,128,128]{2,1,0:T(8,128)(2,1)S(1)}, u32[]{:S(2)}, u32[]{:S(2)}) %collective-permute-start.29) | collective-permute-done | bytes 131104 | tf_op jit(solution)/shard_map/ppermute | solution.py:41
  108.4 4.2 %collective-permute-start.33 = (bf16[96,1152]{1,0:T(8,128)(2,1)S(1)}, bf16[96,1152]{1,0:T(8,128)(2,1)S(1)}, u32[]{:S(2)}, u32[]{:S(2)}) collective-permute-start(bf16[96,1152]{1,0:T(8,128)(2,1)S(1)} %peer_rows.1), channel_id=1, source_target_pairs={{0,8},{8,0},{16,24},{24,16},{32,40},{40,32},{48,56},{56,48},{64,72... | collective-permute-start | bytes 663560 | tf_op jit(solution)/shard_map/ppermute | solution.py:25
  112.6 2.3 %collective-permute-start.30 = (bf16[4,128,128]{2,1,0:T(8,128)(2,1)S(1)}, bf16[4,128,128]{2,1,0:T(8,128)(2,1)S(1)}, u32[]{:S(2)}, u32[]{:S(2)}) collective-permute-start(bf16[4,128,128]{2,1,0:T(8,128)(2,1)S(1)} %ride.1.t), channel_id=1, source_target_pairs={{0,48},{8,88},{16,64},{24,104},{32,80},{40,120},{48,96},{56,8},{64... | collective-permute-start | bytes 393224 | tf_op jit(solution)/shard_map/ppermute | solution.py:41
  115.5 1.3 %collective-permute-start.34 = (bf16[32,1152]{1,0:T(8,128)(2,1)S(1)}, bf16[32,1152]{1,0:T(8,128)(2,1)S(1)}, u32[]{:S(2)}, u32[]{:S(2)}) collective-permute-start(bf16[32,1152]{1,0:T(8,128)(2,1)S(1)} %sum_z.1), channel_id=1, source_target_pairs={{0,128},{8,136},{16,144},{24,152},{32,160},{40,168},{48,176},{56,1... | collective-permute-start | bytes 221192 | tf_op jit(solution)/shard_map/ppermute | solution.py:25
  116.9 4.0 %collective-permute-done.30 = bf16[4,128,128]{2,1,0:T(8,128)(2,1)S(1)} collective-permute-done((bf16[4,128,128]{2,1,0:T(8,128)(2,1)S(1)}, bf16[4,128,128]{2,1,0:T(8,128)(2,1)S(1)}, u32[]{:S(2)}, u32[]{:S(2)}) %collective-permute-start.30) | collective-permute-done | bytes 131104 | tf_op jit(solution)/shard_map/ppermute | solution.py:41
  121.0 3.1 %collective-permute-start.31 = (f32[2,128,128]{2,1,0:T(8,128)S(1)}, f32[2,128,128]{2,1,0:T(8,128)S(1)}, u32[]{:S(2)}, u32[]{:S(2)}) collective-permute-start(f32[2,128,128]{2,1,0:T(8,128)S(1)} %slice.40), channel_id=1, source_target_pairs={{0,8},{8,0},{16,24},{24,16},{32,40},{40,32},{48,56},{56,48},{64,72... | collective-permute-start | bytes 393224 | tf_op jit(solution)/shard_map/ppermute | solution.py:25
  124.2 0.9 collective-permute-done.31
  125.8 1.4 %weight_out.1 = (f32[128,1024]{1,0:T(8,128)}, f32[8,128]{1,0:T(8,128)S(1)}) custom-call(s32[2]{0:T(128)S(1)} %copy-done.4, bf16[64,1152]{1,0:T(8,128)(2,1)S(1)} %pad_maximum_fusion.1.mine, bf16[64,1152]{1,0:T(8,128)(2,1)S(1)} %collective-permute-done.35.theirs), custom_call_target="tpu_custom_call" | custom-call | bytes 1048576 | tf_op jit(solution)/shard_map/weight_out/pallas_call | solution.py:462
  (71 shorter events, 11.6 us)
Async XLA Ops:
  0.6 44.3 %copy-start = (bf16[64,128,128]{2,1,0:T(8,128)(2,1)S(1)}, bf16[64,128,128]{2,1,0:T(8,128)(2,1)}, u32[]{:S(2)}) copy-start(bf16[64,128,128]{2,1,0:T(8,128)(2,1)} %tiles.7) | copy-start | bytes 6291460
  0.6 4.4 %collective-permute-start.1 = (bf16[256,128]{1,0:T(8,128)(2,1)}, bf16[256,128]{1,0:T(8,128)(2,1)S(1)}, u32[]{:S(2)}, u32[]{:S(2)}) collective-permute-start(bf16[256,128]{1,0:T(8,128)(2,1)} %param.7), channel_id=1, source_target_pairs={{0,8},{8,0},{16,24},{24,16},{32,40},{40,32},{48,56},{56,48},{64,72... | collective-permute-start | bytes 196616 | tf_op jit(solution)/shard_map/ppermute | solution.py:25
  5.1 39.8 %collective-permute-start.2 = (bf16[64,128,128]{2,1,0:T(8,128)(2,1)}, bf16[64,128,128]{2,1,0:T(8,128)(2,1)}, u32[]{:S(2)}, u32[]{:S(2)}) collective-permute-start(bf16[64,128,128]{2,1,0:T(8,128)(2,1)} %tiles.7), channel_id=1, source_target_pairs={{0,8},{8,0},{16,24},{24,16},{32,40},{40,32},{48,56},{56,48},{64,72... | collective-permute-start | bytes 6291464 | tf_op jit(solution)/shard_map/ppermute | solution.py:25
  8.4 15.0 %collective-permute-start.10 = (bf16[784,128]{1,0:T(8,128)(2,1)}, bf16[784,128]{1,0:T(8,128)(2,1)S(1)}, u32[]{:S(2)}, u32[]{:S(2)}) collective-permute-start(bf16[784,128]{1,0:T(8,128)(2,1)} %pack_up.1.a), channel_id=1, source_target_pairs={{0,4},{1,5},{2,6},{3,7},{4,0},{5,1},{6,2},{7,3},{8,12},{9,13},{10,... | collective-permute-start | bytes 602120 | tf_op jit(solution)/shard_map/ppermute | solution.py:29
  9.5 9.0 %collective-permute-start.3 = (bf16[512,128]{1,0:T(8,128)(2,1)S(1)}, bf16[512,128]{1,0:T(8,128)(2,1)S(1)}, u32[]{:S(2)}, u32[]{:S(2)}) collective-permute-start(bf16[512,128]{1,0:T(8,128)(2,1)S(1)} %constant_dynamic-update-slice_fusion.a), channel_id=1, source_target_pairs={{0,80},{8,56},{16,96},{24,72},{32,112},{40,88},{48,0},{56,104},{64... | collective-permute-start | bytes 393224 | tf_op jit(solution)/shard_map/ppermute | solution.py:41
  13.9 9.6 %collective-permute-start.5 = (bf16[512,128]{1,0:T(8,128)(2,1)S(1)}, bf16[512,128]{1,0:T(8,128)(2,1)S(1)}, u32[]{:S(2)}, u32[]{:S(2)}) collective-permute-start(bf16[512,128]{1,0:T(8,128)(2,1)S(1)} %constant_dynamic-update-slice_fusion.a), channel_id=1, source_target_pairs={{0,96},{8,40},{16,112},{24,56},{32,0},{40,72},{48,16},{56,88},{64,... | collective-permute-start | bytes 393224 | tf_op jit(solution)/shard_map/ppermute | solution.py:41
  17.2 5.8 %collective-permute-start.9 = (bf16[256,128]{1,0:T(8,128)(2,1)}, bf16[256,128]{1,0:T(8,128)(2,1)S(1)}, u32[]{:S(2)}, u32[]{:S(2)}) collective-permute-start(bf16[256,128]{1,0:T(8,128)(2,1)} %param.7), channel_id=1, source_target_pairs={{0,128},{8,136},{16,144},{24,152},{32,160},{40,168},{48,176},{56,1... | collective-permute-start | bytes 196616 | tf_op jit(solution)/shard_map/ppermute | solution.py:25
  18.6 16.9 %collective-permute-start.7 = (bf16[768,128]{1,0:T(8,128)(2,1)S(1)}, bf16[768,128]{1,0:T(8,128)(2,1)S(1)}, u32[]{:S(2)}, u32[]{:S(2)}) collective-permute-start(bf16[768,128]{1,0:T(8,128)(2,1)S(1)} %append.3), channel_id=1, source_target_pairs={{0,112},{8,24},{16,0},{24,40},{32,16},{40,56},{48,32},{56,72},{64,... | collective-permute-start | bytes 589832 | tf_op jit(solution)/shard_map/ppermute | solution.py:41
  23.5 0.9 copy-start.2
  24.4 20.5 %copy-start.4 = (s32[2]{0:T(128)S(1)}, s32[2]{0:T(128)}, u32[]{:S(2)}) copy-start(s32[2]{0:T(128)} %pad_add_fusion.1.ids.refs_0_) | copy-start | bytes 28
  24.4 17.3 %collective-permute-start.12 = (bf16[1568,128]{1,0:T(8,128)(2,1)S(1)}, bf16[1568,128]{1,0:T(8,128)(2,1)S(1)}, u32[]{:S(2)}, u32[]{:S(2)}) collective-permute-start(bf16[1568,128]{1,0:T(8,128)(2,1)S(1)} %append.4.refs_0_), channel_id=1, source_target_pairs={{0,3},{1,0},{2,1},{3,2},{4,7},{5,4},{6,5},{7,6},{8,11},{9,8},{10,9... | collective-permute-start | bytes 1204232 | tf_op jit(solution)/shard_map/ppermute | solution.py:29
  27.2 14.5 %collective-permute-start.11 = (bf16[1568,128]{1,0:T(8,128)(2,1)S(1)}, bf16[1568,128]{1,0:T(8,128)(2,1)S(1)}, u32[]{:S(2)}, u32[]{:S(2)}) collective-permute-start(bf16[1568,128]{1,0:T(8,128)(2,1)S(1)} %append.4.refs_0_), channel_id=1, source_target_pairs={{0,1},{1,2},{2,3},{3,0},{4,5},{5,6},{6,7},{7,4},{8,9},{9,10},{10,1... | collective-permute-start | bytes 1204232 | tf_op jit(solution)/shard_map/ppermute | solution.py:29
  27.9 2.5 %collective-permute-start = (s32[2,64]{1,0:T(2,128)S(1)}, s32[2,64]{1,0:T(2,128)S(1)}, u32[]{:S(2)}, u32[]{:S(2)}) collective-permute-start(s32[2,64]{1,0:T(2,128)S(1)} %pad_add_fusion), channel_id=1, source_target_pairs={{0,8},{8,0},{16,24},{24,16},{32,40},{40,32},{48,56},{56,48},{64,72... | collective-permute-start | bytes 1544 | tf_op jit(solution)/shard_map/ppermute | solution.py:25
  30.4 4.8 %collective-permute-start.6 = (bf16[512,128]{1,0:T(8,128)(2,1)S(1)}, bf16[512,128]{1,0:T(8,128)(2,1)S(1)}, u32[]{:S(2)}, u32[]{:S(2)}) collective-permute-start(bf16[512,128]{1,0:T(8,128)(2,1)S(1)} %collective-permute-done.5.refs_1_), channel_id=1, source_target_pairs={{0,128},{8,136},{16,144},{24,152},{32,160},{40,168},{48,176},{56,1... | collective-permute-start | bytes 393224 | tf_op jit(solution)/shard_map/ppermute | solution.py:25
  35.2 6.5 %collective-permute-start.4 = (bf16[512,128]{1,0:T(8,128)(2,1)S(1)}, bf16[512,128]{1,0:T(8,128)(2,1)S(1)}, u32[]{:S(2)}, u32[]{:S(2)}) collective-permute-start(bf16[512,128]{1,0:T(8,128)(2,1)S(1)} %collective-permute-done.3.b.refs_0_), channel_id=1, source_target_pairs={{0,128},{8,136},{16,144},{24,152},{32,160},{40,168},{48,176},{56,1... | collective-permute-start | bytes 393224 | tf_op jit(solution)/shard_map/ppermute | solution.py:25
  35.5 13.6 %collective-permute-start.8 = (bf16[768,128]{1,0:T(8,128)(2,1)S(1)}, bf16[768,128]{1,0:T(8,128)(2,1)S(1)}, u32[]{:S(2)}, u32[]{:S(2)}) collective-permute-start(bf16[768,128]{1,0:T(8,128)(2,1)S(1)} %collective-permute-done.7), channel_id=1, source_target_pairs={{0,128},{8,136},{16,144},{24,152},{32,160},{40,168},{48,176},{56,1... | collective-permute-start | bytes 589832 | tf_op jit(solution)/shard_map/ppermute | solution.py:25
  36.7 0.7 copy-start.3
  37.3 0.7 copy-start.5
  38.0 0.7 copy-start.6
  41.8 13.1 %collective-permute-start.14 = (bf16[784,128]{1,0:T(8,128)(2,1)S(1)}, bf16[784,128]{1,0:T(8,128)(2,1)S(1)}, u32[]{:S(2)}, u32[]{:S(2)}) collective-permute-start(bf16[784,128]{1,0:T(8,128)(2,1)S(1)} %get-tuple-element.23.refs_1_), channel_id=1, source_target_pairs={{0,1},{1,2},{2,3},{3,0},{4,5},{5,6},{6,7},{7,4},{8,9},{9,10},{10,1... | collective-permute-start | bytes 602120 | tf_op jit(solution)/shard_map/ppermute | solution.py:29
  42.2 12.8 %collective-permute-start.15 = (bf16[784,128]{1,0:T(8,128)(2,1)S(1)}, bf16[784,128]{1,0:T(8,128)(2,1)S(1)}, u32[]{:S(2)}, u32[]{:S(2)}) collective-permute-start(bf16[784,128]{1,0:T(8,128)(2,1)S(1)} %get-tuple-element.24.refs_2_), channel_id=1, source_target_pairs={{0,3},{1,0},{2,1},{3,2},{4,7},{5,4},{6,5},{7,6},{8,11},{9,8},{10,9... | collective-permute-start | bytes 602120 | tf_op jit(solution)/shard_map/ppermute | solution.py:29
  53.0 20.6 %copy-start.1 = (bf16[128,1024]{1,0:T(8,128)(2,1)S(1)}, bf16[128,1024]{1,0:T(8,128)(2,1)}, u32[]{:S(2)}) copy-start(bf16[128,1024]{1,0:T(8,128)(2,1)} %w_own.1) | copy-start | bytes 786436
  53.0 2.9 %collective-permute-start.13 = (f32[2,128,128]{2,1,0:T(8,128)S(1)}, f32[2,128,128]{2,1,0:T(8,128)S(1)}, u32[]{:S(2)}, u32[]{:S(2)}) collective-permute-start(f32[2,128,128]{2,1,0:T(8,128)S(1)} %slice.36), channel_id=1, source_target_pairs={{0,8},{8,0},{16,24},{24,16},{32,40},{40,32},{48,56},{56,48},{64,72... | collective-permute-start | bytes 393224 | tf_op jit(solution)/shard_map/ppermute | solution.py:25
  55.9 4.9 %collective-permute-start.16 = (bf16[256,128]{1,0:T(8,128)(2,1)S(1)}, bf16[256,128]{1,0:T(8,128)(2,1)S(1)}, u32[]{:S(2)}, u32[]{:S(2)}) collective-permute-start(bf16[256,128]{1,0:T(8,128)(2,1)S(1)} %bitcast.31), channel_id=1, source_target_pairs={{0,4},{1,5},{2,6},{3,7},{4,0},{5,1},{6,2},{7,3},{8,12},{9,13},{10,... | collective-permute-start | bytes 196616 | tf_op jit(solution)/shard_map/ppermute | solution.py:29
  62.3 11.4 %collective-permute-start.20 = (bf16[1024,512]{1,0:T(8,128)(2,1)S(1)}, bf16[1024,512]{1,0:T(8,128)(2,1)S(1)}, u32[]{:S(2)}, u32[]{:S(2)}) collective-permute-start(bf16[1024,512]{1,0:T(8,128)(2,1)S(1)} %get-tuple-element.25.w0), channel_id=1, source_target_pairs={{0,8},{8,0},{16,24},{24,16},{32,40},{40,32},{48,56},{56,48},{64,72... | collective-permute-start | bytes 3145736 | tf_op jit(solution)/shard_map/ppermute | solution.py:25
  63.9 6.6 %collective-permute-start.19 = (bf16[512,128]{1,0:T(8,128)(2,1)S(1)}, bf16[512,128]{1,0:T(8,128)(2,1)S(1)}, u32[]{:S(2)}, u32[]{:S(2)}) collective-permute-start(bf16[512,128]{1,0:T(8,128)(2,1)S(1)} %pad_maximum_fusion.2.refs_5_.p0), channel_id=1, source_target_pairs={{0,2},{1,3},{2,0},{3,1},{4,6},{5,7},{6,4},{7,5},{8,10},{9,11},{10,... | collective-permute-start | bytes 393224 | tf_op jit(solution)/shard_map/ppermute | solution.py:29
  65.0 7.6 %collective-permute-start.18 = (bf16[512,128]{1,0:T(8,128)(2,1)S(1)}, bf16[512,128]{1,0:T(8,128)(2,1)S(1)}, u32[]{:S(2)}, u32[]{:S(2)}) collective-permute-start(bf16[512,128]{1,0:T(8,128)(2,1)S(1)} %pad_maximum_fusion.2.refs_5_.p0), channel_id=1, source_target_pairs={{0,3},{1,0},{2,1},{3,2},{4,7},{5,4},{6,5},{7,6},{8,11},{9,8},{10,9... | collective-permute-start | bytes 393224 | tf_op jit(solution)/shard_map/ppermute | solution.py:29
  65.5 8.1 %collective-permute-start.17 = (bf16[512,128]{1,0:T(8,128)(2,1)S(1)}, bf16[512,128]{1,0:T(8,128)(2,1)S(1)}, u32[]{:S(2)}, u32[]{:S(2)}) collective-permute-start(bf16[512,128]{1,0:T(8,128)(2,1)S(1)} %pad_maximum_fusion.2.refs_5_.p0), channel_id=1, source_target_pairs={{0,1},{1,2},{2,3},{3,0},{4,5},{5,6},{6,7},{7,4},{8,9},{9,10},{10,1... | collective-permute-start | bytes 393224 | tf_op jit(solution)/shard_map/ppermute | solution.py:29
  75.8 1.7 %collective-permute-start.22 = (f32[64,1152]{1,0:T(8,128)S(1)}, f32[64,1152]{1,0:T(8,128)S(1)}, u32[]{:S(2)}, u32[]{:S(2)}) collective-permute-start(f32[64,1152]{1,0:T(8,128)S(1)} %get-tuple-element.31), channel_id=1, source_target_pairs={{0,8},{8,0},{16,24},{24,16},{32,40},{40,32},{48,56},{56,48},{64,72... | collective-permute-start | bytes 884744 | tf_op jit(solution)/shard_map/ppermute | solution.py:25
  76.2 1.6 %collective-permute-start.21 = (bf16[2,128,128]{2,1,0:T(8,128)(2,1)S(1)}, bf16[2,128,128]{2,1,0:T(8,128)(2,1)S(1)}, u32[]{:S(2)}, u32[]{:S(2)}) collective-permute-start(bf16[2,128,128]{2,1,0:T(8,128)(2,1)S(1)} %bitcast.27), channel_id=1, source_target_pairs={{0,8},{8,0},{16,24},{24,16},{32,40},{40,32},{48,56},{56,48},{64,72... | collective-permute-start | bytes 196616 | tf_op jit(solution)/shard_map/ppermute | solution.py:25
  77.5 8.0 %collective-permute-start.24 = (bf16[32,1152]{1,0:T(8,128)(2,1)S(1)}, bf16[32,1152]{1,0:T(8,128)(2,1)S(1)}, u32[]{:S(2)}, u32[]{:S(2)}) collective-permute-start(bf16[32,1152]{1,0:T(8,128)(2,1)S(1)} %fusion.ready), channel_id=1, source_target_pairs={{0,128},{8,136},{16,144},{24,152},{32,160},{40,168},{48,176},{56,1... | collective-permute-start | bytes 221192 | tf_op jit(solution)/shard_map/ppermute | solution.py:25
  85.5 1.7 %collective-permute-start.25 = (bf16[32,1152]{1,0:T(8,128)(2,1)S(1)}, bf16[32,1152]{1,0:T(8,128)(2,1)S(1)}, u32[]{:S(2)}, u32[]{:S(2)}) collective-permute-start(bf16[32,1152]{1,0:T(8,128)(2,1)S(1)} %quarter_up.1.own), channel_id=1, source_target_pairs={{0,8},{8,0},{16,24},{24,16},{32,40},{40,32},{48,56},{56,48},{64,72... | collective-permute-start | bytes 221192 | tf_op jit(solution)/shard_map/ppermute | solution.py:25
  86.0 14.8 %collective-permute-start.23 = (bf16[16,128,128]{2,1,0:T(8,128)(2,1)S(1)}, bf16[16,128,128]{2,1,0:T(8,128)(2,1)S(1)}, u32[]{:S(2)}, u32[]{:S(2)}) collective-permute-start(bf16[16,128,128]{2,1,0:T(8,128)(2,1)S(1)} %spread.2.ready), channel_id=1, source_target_pairs={{0,128},{8,136},{16,144},{24,152},{32,160},{40,168},{48,176},{56,1... | collective-permute-start | bytes 1572872 | tf_op jit(solution)/shard_map/ppermute | solution.py:25
  87.2 9.9 %collective-permute-start.27 = (bf16[64,1152]{1,0:T(8,128)(2,1)S(1)}, bf16[64,1152]{1,0:T(8,128)(2,1)S(1)}, u32[]{:S(2)}, u32[]{:S(2)}) collective-permute-start(bf16[64,1152]{1,0:T(8,128)(2,1)S(1)} %pad_maximum_fusion.a), channel_id=1, source_target_pairs={{0,96},{8,40},{16,112},{24,56},{32,0},{40,72},{48,16},{56,88},{64,... | collective-permute-start | bytes 442376 | tf_op jit(solution)/shard_map/ppermute | solution.py:41
  89.3 8.8 %collective-permute-start.26 = (bf16[64,1152]{1,0:T(8,128)(2,1)S(1)}, bf16[64,1152]{1,0:T(8,128)(2,1)S(1)}, u32[]{:S(2)}, u32[]{:S(2)}) collective-permute-start(bf16[64,1152]{1,0:T(8,128)(2,1)S(1)} %pad_maximum_fusion.a), channel_id=1, source_target_pairs={{0,80},{8,56},{16,96},{24,72},{32,112},{40,88},{48,0},{56,104},{64... | collective-permute-start | bytes 442376 | tf_op jit(solution)/shard_map/ppermute | solution.py:41
  98.1 7.6 %collective-permute-start.32 = (bf16[96,1152]{1,0:T(8,128)(2,1)S(1)}, bf16[96,1152]{1,0:T(8,128)(2,1)S(1)}, u32[]{:S(2)}, u32[]{:S(2)}) collective-permute-start(bf16[96,1152]{1,0:T(8,128)(2,1)S(1)} %append.5.ready), channel_id=1, source_target_pairs={{0,112},{8,24},{16,0},{24,40},{32,16},{40,56},{48,32},{56,72},{64,... | collective-permute-start | bytes 663560 | tf_op jit(solution)/shard_map/ppermute | solution.py:41
  100.9 7.5 %collective-permute-start.29 = (bf16[4,128,128]{2,1,0:T(8,128)(2,1)S(1)}, bf16[4,128,128]{2,1,0:T(8,128)(2,1)S(1)}, u32[]{:S(2)}, u32[]{:S(2)}) collective-permute-start(bf16[4,128,128]{2,1,0:T(8,128)(2,1)S(1)} %get-tuple-element.34), channel_id=1, source_target_pairs={{0,32},{8,104},{16,48},{24,120},{32,64},{40,8},{48,80},{56,24},{64... | collective-permute-start | bytes 393224 | tf_op jit(solution)/shard_map/ppermute | solution.py:41
  104.3 8.3 %collective-permute-start.28 = (bf16[6,128,128]{2,1,0:T(8,128)(2,1)S(1)}, bf16[6,128,128]{2,1,0:T(8,128)(2,1)S(1)}, u32[]{:S(2)}, u32[]{:S(2)}) collective-permute-start(bf16[6,128,128]{2,1,0:T(8,128)(2,1)S(1)} %get-tuple-element.33), channel_id=1, source_target_pairs={{0,16},{8,120},{16,32},{24,8},{32,48},{40,24},{48,64},{56,40},{64,... | collective-permute-start | bytes 589832 | tf_op jit(solution)/shard_map/ppermute | solution.py:41
  108.4 6.5 %collective-permute-start.33 = (bf16[96,1152]{1,0:T(8,128)(2,1)S(1)}, bf16[96,1152]{1,0:T(8,128)(2,1)S(1)}, u32[]{:S(2)}, u32[]{:S(2)}) collective-permute-start(bf16[96,1152]{1,0:T(8,128)(2,1)S(1)} %peer_rows.1), channel_id=1, source_target_pairs={{0,8},{8,0},{16,24},{24,16},{32,40},{40,32},{48,56},{56,48},{64,72... | collective-permute-start | bytes 663560 | tf_op jit(solution)/shard_map/ppermute | solution.py:25
  112.6 8.3 %collective-permute-start.30 = (bf16[4,128,128]{2,1,0:T(8,128)(2,1)S(1)}, bf16[4,128,128]{2,1,0:T(8,128)(2,1)S(1)}, u32[]{:S(2)}, u32[]{:S(2)}) collective-permute-start(bf16[4,128,128]{2,1,0:T(8,128)(2,1)S(1)} %ride.1.t), channel_id=1, source_target_pairs={{0,48},{8,88},{16,64},{24,104},{32,80},{40,120},{48,96},{56,8},{64... | collective-permute-start | bytes 393224 | tf_op jit(solution)/shard_map/ppermute | solution.py:41
  115.5 8.6 %collective-permute-start.34 = (bf16[32,1152]{1,0:T(8,128)(2,1)S(1)}, bf16[32,1152]{1,0:T(8,128)(2,1)S(1)}, u32[]{:S(2)}, u32[]{:S(2)}) collective-permute-start(bf16[32,1152]{1,0:T(8,128)(2,1)S(1)} %sum_z.1), channel_id=1, source_target_pairs={{0,128},{8,136},{16,144},{24,152},{32,160},{40,168},{48,176},{56,1... | collective-permute-start | bytes 221192 | tf_op jit(solution)/shard_map/ppermute | solution.py:25
  121.0 4.1 %collective-permute-start.31 = (f32[2,128,128]{2,1,0:T(8,128)S(1)}, f32[2,128,128]{2,1,0:T(8,128)S(1)}, u32[]{:S(2)}, u32[]{:S(2)}) collective-permute-start(f32[2,128,128]{2,1,0:T(8,128)S(1)} %slice.40), channel_id=1, source_target_pairs={{0,8},{8,0},{16,24},{24,16},{32,40},{40,32},{48,56},{56,48},{64,72... | collective-permute-start | bytes 393224 | tf_op jit(solution)/shard_map/ppermute | solution.py:25
  124.1 1.7 %collective-permute-start.35 = (bf16[64,1152]{1,0:T(8,128)(2,1)S(1)}, bf16[64,1152]{1,0:T(8,128)(2,1)S(1)}, u32[]{:S(2)}, u32[]{:S(2)}) collective-permute-start(bf16[64,1152]{1,0:T(8,128)(2,1)S(1)} %pad_maximum_fusion.1.mine), channel_id=1, source_target_pairs={{0,8},{8,0},{16,24},{24,16},{32,40},{40,32},{48,56},{56,48},{64,72... | collective-permute-start | bytes 442376 | tf_op jit(solution)/shard_map/ppermute | solution.py:25

commit v7 on v4

--- a/solution.py
+++ b/solution.py
@@ -98,22 +98,39 @@
     )(a, b, *ready)
 
 
-def turn_body(u, d, a, b):
+def turn_body(u, d, *refs):
+    a, b = refs[-2:]
     a[...] = u[0:784, :]
     b[...] = d[784:1568, :]
 
 
-def turn(u, d):
+def turn(u, d, *ready):
     half = jax.ShapeDtypeStruct((784, B), bf16)
     return pl.pallas_call(
         turn_body,
         out_shape=(half, half),
-        in_specs=[VM, VM],
+        in_specs=[VM, VM] + [ANY] * len(ready),
         out_specs=(VM, VM),
         compiler_params=params(4),
         cost_estimate=cost(0, 1 << 18),
         name="turn",
-    )(u, d)
+    )(u, d, *ready)
+
+
+def hold_body(v, r0, r1, out):
+    out[...] = v[...]
+
+
+def hold(v, *ready):
+    return pl.pallas_call(
+        hold_body,
+        out_shape=jax.ShapeDtypeStruct(v.shape, v.dtype),
+        in_specs=[VM, ANY, ANY],
+        out_specs=VM,
+        compiler_params=params(4),
+        cost_estimate=cost(0, 1 << 18),
+        name="hold",
+    )(v, *ready)
 
 
 def settle_body(mine, came, a, b, agg):
@@ -489,13 +506,13 @@
     pack = pack_up(ids, weight, out_grad, bias_vector[None, :])
     pack_x = feat_send(pack, dx=1)
 
-    pair = append(1568, pack, pack_x)
-    ext = append(768, both, o3, o2, x0, plan, pair)
-    o14 = spin_send(ext, 1, -1)
-    p3, p2, p14 = row_send(o3, dx=1), row_send(o2, dx=1), row_send(o14, dx=1)
+    pair = append(1568, pack, pack_x, o3, o2, x0)
+    o14 = spin_send(append(768, both, o3, lists), 1, -1)
+    p3, p2 = row_send(o3, dx=1), row_send(o2, dx=1)
+    p14 = row_send(hold(o14, p3, p2), dx=1)
     wu, wd = feat_send(pair, dy=1), feat_send(pair, dy=-1)
 
-    wa, wb = turn(wu, wd)
+    wa, wb = turn(wu, wd, p14, plan)
     mine, theirs = aggregate(plan, adj_tiles, more, (both_a, x0, o14, o2, o3, p14, p2, p3), wa, wb)
     wa, wb = feat_send(wa, dy=1), feat_send(wb, dy=-1)
     aggregated = settle(mine, row_send(theirs, dc=1), wa, wb).reshape(256, B)
@@ -518,7 +535,7 @@
     last = append(96, halves, d3, d2)
     d1 = spin_send(last, 1, -1)
 
-    t14, t2, t3, t0 = join(near, came, last)
+    t14, t2, t3, t0 = join(near, came, halves)
     r14, r2 = spin_send(t14, 1), spin_send(t2, 2)
     t3 = ride(t3, r14)
     r3 = spin_send(t3, 3)

time: 124 us -> 122 us (0.984)
  starting transfers between devices: 52.8 us -> 50.6 us
    ppermute x9, starting transfers between devices: 19.2 us -> 13.6 us  [spin_send(): return lax.ppermute(v, 'row', perm)]
    ppermute x18, starting transfers between devices: 22.4 us -> 25 us  [row_send(): return lax.ppermute(v, 'row', perm)]
    ppermute x9, waiting for transfers between devices: 12.4 us -> 11 us  [feat_send(): lax.ppermute(v, 'feat', [(i, (i >> 2 ^ dx) << 2 | i + dy & 3) for i in ra...]
  transfers between devices with their start and end apart: 36 -> 36, of which waited for: 17 -> 19; matrix products, arithmetic and copies ran while one was open for 2% -> 2% of each run, Pallas kernels for 14% -> 15%
where the time goes in v7:
time: 122 us
  starting transfers between devices  50.6 us (41%)
  waiting for transfers between devices  41.2 us (34%)
  Pallas kernels  22.9 us (19%)
  local copies, waits for them, and re-layouts  4.29 us (4%)
  other arithmetic  2.04 us (2%)
    ppermute x18, starting transfers between devices, row_send(): return lax.ppermute(v, 'row', perm)  25 us
    ppermute x9, waiting for transfers between devices, spin_send(): return lax.ppermute(v, 'row', perm)  21.9 us
    ppermute x9, starting transfers between devices, spin_send(): return lax.ppermute(v, 'row', perm)  13.6 us
    ppermute x9, starting transfers between devices, feat_send(): lax.ppermute(v, 'feat', [(i, (i >> 2 ^ dx) << 2 | i + dy & 3) for i in ra...  12 us
    ppermute x9, waiting for transfers between devices, feat_send(): lax.ppermute(v, 'feat', [(i, (i >> 2 ^ dx) << 2 | i + dy & 3) for i in ra...  11 us
    ppermute x18, waiting for transfers between devices, row_send(): return lax.ppermute(v, 'row', perm)  8.31 us
    pallas_call x1, Pallas kernels, aggregate(): pl.pallas_call(agg_body, out_shape=(jax.ShapeDtypeStruct((2, B, B), f32),...  6.23 us
    pallas_call x1, Pallas kernels, spread(): pl.pallas_call(spread_body, out_shape=(jax.ShapeDtypeStruct((16, B, B), f...  5.68 us
  transfers between devices with their start and end apart: 36, of which 19 were waited for; matrix products, arithmetic and copies ran while one was open for 2% of the time, Pallas kernels for 15%

profile of v7, /device:TPU:1, one launch (start us, length us, event | category | flops | bytes accessed | tf_op | source)
XLA Modules:
  0.0 121.9 jit_solution(1350017283750675289)
XLA Ops:
  0.6 3.3 %collective-permute-start.1 = (bf16[256,128]{1,0:T(8,128)(2,1)}, bf16[256,128]{1,0:T(8,128)(2,1)S(1)}, u32[]{:S(2)}, u32[]{:S(2)}) collective-permute-start(bf16[256,128]{1,0:T(8,128)(2,1)} %param.7), channel_id=1, source_target_pairs={{0,8},{8,0},{16,24},{24,16},{32,40},{40,32},{48,56},{56,48},{64,72... | collective-permute-start | bytes 196616 | tf_op jit(solution)/shard_map/ppermute | solution.py:25
  4.0 0.8 constant_dynamic-update-slice_fusion.1
  5.5 1.3 %collective-permute-start.6 = (bf16[512,128]{1,0:T(8,128)(2,1)S(1)}, bf16[512,128]{1,0:T(8,128)(2,1)S(1)}, u32[]{:S(2)}, u32[]{:S(2)}) collective-permute-start(bf16[512,128]{1,0:T(8,128)(2,1)S(1)} %constant_dynamic-update-slice_fusion.a), channel_id=1, source_target_pairs={{0,96},{8,40},{16,112},{24,56},{32,0},{40,72},{48,16},{56,88},{64,... | collective-permute-start | bytes 393224 | tf_op jit(solution)/shard_map/ppermute | solution.py:41
  7.4 2.3 %pack_up.1.a = bf16[784,128]{1,0:T(8,128)(2,1)} custom-call(s32[2]{0:T(128)} %pad_add_fusion.1.ids, bf16[128,1024]{1,0:T(8,128)(2,1)} %w_own.1, bf16[256,128]{1,0:T(8,128)(2,1)} %og.1, bf16[1,128]{1,0:T(2,128)(2,1)} %bitcast.37), custom_call_target="tpu_custom_call" | custom-call | bytes 524288 | tf_op jit(solution)/shard_map/pack_up/pallas_call | solution.py:70
  9.7 2.8 %collective-permute-start.10 = (bf16[784,128]{1,0:T(8,128)(2,1)}, bf16[784,128]{1,0:T(8,128)(2,1)S(1)}, u32[]{:S(2)}, u32[]{:S(2)}) collective-permute-start(bf16[784,128]{1,0:T(8,128)(2,1)} %pack_up.1.a), channel_id=1, source_target_pairs={{0,4},{1,5},{2,6},{3,7},{4,0},{5,1},{6,2},{7,3},{8,12},{9,13},{10,... | collective-permute-start | bytes 602120 | tf_op jit(solution)/shard_map/ppermute | solution.py:29
  12.5 4.7 %collective-permute-start.4 = (bf16[512,128]{1,0:T(8,128)(2,1)S(1)}, bf16[512,128]{1,0:T(8,128)(2,1)S(1)}, u32[]{:S(2)}, u32[]{:S(2)}) collective-permute-start(bf16[512,128]{1,0:T(8,128)(2,1)S(1)} %constant_dynamic-update-slice_fusion.a), channel_id=1, source_target_pairs={{0,80},{8,56},{16,96},{24,72},{32,112},{40,88},{48,0},{56,104},{64... | collective-permute-start | bytes 393224 | tf_op jit(solution)/shard_map/ppermute | solution.py:41
  17.5 0.7 pad_add_fusion
  18.5 0.8 collective-permute-done.refs_0_
  19.4 1.2 collective-permute-start.3
  20.5 1.9 %collective-permute-done.4.b.refs_0_ = bf16[512,128]{1,0:T(8,128)(2,1)S(1)} collective-permute-done((bf16[512,128]{1,0:T(8,128)(2,1)S(1)}, bf16[512,128]{1,0:T(8,128)(2,1)S(1)}, u32[]{:S(2)}, u32[]{:S(2)}) %collective-permute-start.4) | collective-permute-done | bytes 131104 | tf_op jit(solution)/shard_map/ppermute | solution.py:41
  22.5 1.2 collective-permute-start.5
  24.2 0.9 copy-done.2
  25.1 2.8 %collective-permute-start.12 = (bf16[1568,128]{1,0:T(8,128)(2,1)S(1)}, bf16[1568,128]{1,0:T(8,128)(2,1)S(1)}, u32[]{:S(2)}, u32[]{:S(2)}) collective-permute-start(bf16[1568,128]{1,0:T(8,128)(2,1)S(1)} %append.4.refs_0_), channel_id=1, source_target_pairs={{0,3},{1,0},{2,1},{3,2},{4,7},{5,4},{6,5},{7,6},{8,11},{9,8},{10,9... | collective-permute-start | bytes 1204232 | tf_op jit(solution)/shard_map/ppermute | solution.py:29
  28.0 0.7 collective-permute-start.7
  28.7 3.1 %collective-permute-done.7.r0 = bf16[512,128]{1,0:T(8,128)(2,1)S(1)} collective-permute-done((bf16[512,128]{1,0:T(8,128)(2,1)S(1)}, bf16[512,128]{1,0:T(8,128)(2,1)S(1)}, u32[]{:S(2)}, u32[]{:S(2)}) %collective-permute-start.7) | collective-permute-done | bytes 131104 | tf_op jit(solution)/shard_map/ppermute | solution.py:25
  31.8 1.1 collective-permute-start.9
  34.9 2.7 %plan_tiles.1.refs_1_.plan = s32[160]{0:T(256)S(1)} custom-call(s32[2]{0:T(128)S(1)} %copy-done.3, s32[64]{0:T(128)S(1)} %copy-done.5, s32[64]{0:T(128)S(1)} %copy-done.6, s32[64]{0:T(128)S(1)} %get-tuple-element.47.c1, s32[64]{0:T(128)S(1)} %get-tuple-element.46.d1), custom_call_target="tpu_custom_call" | custom-call | flops 10000 | bytes 4096 | tf_op jit(solution)/shard_map/plan_tiles/pallas_call | solution.py:177
  38.1 2.7 %collective-permute-start.15 = (bf16[784,128]{1,0:T(8,128)(2,1)S(1)}, bf16[784,128]{1,0:T(8,128)(2,1)S(1)}, u32[]{:S(2)}, u32[]{:S(2)}) collective-permute-start(bf16[784,128]{1,0:T(8,128)(2,1)S(1)} %get-tuple-element.28.refs_9_), channel_id=1, source_target_pairs={{0,3},{1,0},{2,1},{3,2},{4,7},{5,4},{6,5},{7,6},{8,11},{9,8},{10,9... | collective-permute-start | bytes 602120 | tf_op jit(solution)/shard_map/ppermute | solution.py:29
  40.8 6.2 %aggregate.1 = (f32[2,128,128]{2,1,0:T(8,128)S(1)}, f32[2,128,128]{2,1,0:T(8,128)S(1)}) custom-call(s32[160]{0:T(256)S(1)} %plan_tiles.1.refs_1_.plan, bf16[64,128,128]{2,1,0:T(8,128)(2,1)S(1)} %copy-done, bf16[64,128,128]{2,1,0:T(8,128)(2,1)} %collective-permute-done.2.more, bf16[4,128,128]{2,1,0:T(8,128)(2,1)S(1)} %bitcast.23, ...), custom_call_target="tpu_custom_call" | custom-call | flops 268435456 | bytes 4194304 | tf_op jit(solution)/shard_map/aggregate/pallas_call | solution.py:228
  47.1 6.8 %collective-permute-start.13 = (f32[2,128,128]{2,1,0:T(8,128)S(1)}, f32[2,128,128]{2,1,0:T(8,128)S(1)}, u32[]{:S(2)}, u32[]{:S(2)}) collective-permute-start(f32[2,128,128]{2,1,0:T(8,128)S(1)} %get-tuple-element.30), channel_id=1, source_target_pairs={{0,8},{8,0},{16,24},{24,16},{32,40},{40,32},{48,56},{56,48},{64,72... | collective-permute-start | bytes 393224 | tf_op jit(solution)/shard_map/ppermute | solution.py:25
  53.8 1.0 collective-permute-done.13.came
  54.8 1.2 collective-permute-start.16
  56.0 3.7 %collective-permute-done.16 = bf16[256,128]{1,0:T(8,128)(2,1)S(1)} collective-permute-done((bf16[256,128]{1,0:T(8,128)(2,1)S(1)}, bf16[256,128]{1,0:T(8,128)(2,1)S(1)}, u32[]{:S(2)}, u32[]{:S(2)}) %collective-permute-start.16) | collective-permute-done | bytes 65568 | tf_op jit(solution)/shard_map/ppermute | solution.py:29
  59.7 1.4 %lay_out.1 = (bf16[1024,512]{1,0:T(8,128)(2,1)S(1)}, bf16[256,1024]{1,0:T(8,128)(2,1)S(1)}, f32[8,1024]{1,0:T(8,128)S(1)}) custom-call(s32[2]{0:T(128)S(1)} %copy-done.4, bf16[1568,128]{1,0:T(8,128)(2,1)S(1)} %append.4.refs_0_, bf16[1568,128]{1,0:T(8,128)(2,1)S(1)} %collective-permute-done.11.u.refs_1_, ...), custom_call_target="tpu_custom_call" | custom-call | bytes 3145728 | tf_op jit(solution)/shard_map/lay_out/pallas_call | solution.py:271
  61.2 1.6 %collective-permute-start.20 = (bf16[1024,512]{1,0:T(8,128)(2,1)S(1)}, bf16[1024,512]{1,0:T(8,128)(2,1)S(1)}, u32[]{:S(2)}, u32[]{:S(2)}) collective-permute-start(bf16[1024,512]{1,0:T(8,128)(2,1)S(1)} %get-tuple-element.31.w0), channel_id=1, source_target_pairs={{0,8},{8,0},{16,24},{24,16},{32,40},{40,32},{48,56},{56,48},{64,72... | collective-permute-start | bytes 3145736 | tf_op jit(solution)/shard_map/ppermute | solution.py:25
  62.8 1.0 collective-permute-start.19
  64.3 0.9 collective-permute-start.17
  65.2 4.1 %collective-permute-done.19.p3 = bf16[512,128]{1,0:T(8,128)(2,1)S(1)} collective-permute-done((bf16[512,128]{1,0:T(8,128)(2,1)S(1)}, bf16[512,128]{1,0:T(8,128)(2,1)S(1)}, u32[]{:S(2)}, u32[]{:S(2)}) %collective-permute-start.19) | collective-permute-done | bytes 131104 | tf_op jit(solution)/shard_map/ppermute | solution.py:29
  69.3 2.0 %collective-permute-done.18.p2 = bf16[512,128]{1,0:T(8,128)(2,1)S(1)} collective-permute-done((bf16[512,128]{1,0:T(8,128)(2,1)S(1)}, bf16[512,128]{1,0:T(8,128)(2,1)S(1)}, u32[]{:S(2)}, u32[]{:S(2)}) %collective-permute-start.18) | collective-permute-done | bytes 131104 | tf_op jit(solution)/shard_map/ppermute | solution.py:29
  71.3 1.2 %collective-permute-done.17.p1 = bf16[512,128]{1,0:T(8,128)(2,1)S(1)} collective-permute-done((bf16[512,128]{1,0:T(8,128)(2,1)S(1)}, bf16[512,128]{1,0:T(8,128)(2,1)S(1)}, u32[]{:S(2)}, u32[]{:S(2)}) %collective-permute-start.17) | collective-permute-done | bytes 131104 | tf_op jit(solution)/shard_map/ppermute | solution.py:29
  72.5 2.1 %middle.1 = (f32[256,128]{1,0:T(8,128)}, bf16[256,128]{1,0:T(8,128)(2,1)S(1)}, f32[64,1152]{1,0:T(8,128)S(1)}, f32[64,1152]{1,0:T(8,128)S(1)}) custom-call(s32[2]{0:T(128)S(1)} %copy-done.4, bf16[512,128]{1,0:T(8,128)(2,1)S(1)} %pad_maximum_fusion.2.refs_5_.p0, bf16[512,128]{1,0:T(8,128)(2,1)S(1)} %collective-permute-done.17.p1, ...), custom_call_target="tpu_custom_call" | custom-call | flops 671088640 | bytes 5242880 | tf_op jit(solution)/shard_map/middle/pallas_call | solution.py:317
  75.2 1.2 collective-permute-done.22.got
  76.4 1.1 collective-permute-start.24
  77.5 5.7 %spread.1 = (f32[16,128,128]{2,1,0:T(8,128)S(1)}, bf16[16,128,128]{2,1,0:T(8,128)(2,1)S(1)}) custom-call(s32[160]{0:T(256)S(1)} %plan_tiles.1.refs_1_.plan, bf16[64,128,128]{2,1,0:T(8,128)(2,1)S(1)} %copy-done, bf16[64,128,128]{2,1,0:T(8,128)(2,1)} %collective-permute-done.2.more, bf16[2,128,128]{2,1,0:T(8,128)(2,1)S(1)} %bitcast.33, ...), custom_call_target="tpu_custom_call" | custom-call | flops 268435456 | bytes 6291456 | tf_op jit(solution)/shard_map/spread/pallas_call | solution.py:356
  83.7 0.7 collective-permute-start.23
  84.7 1.5 %collective-permute-start.30 = (bf16[64,1152]{1,0:T(8,128)(2,1)S(1)}, bf16[64,1152]{1,0:T(8,128)(2,1)S(1)}, u32[]{:S(2)}, u32[]{:S(2)}) collective-permute-start(bf16[64,1152]{1,0:T(8,128)(2,1)S(1)} %pad_maximum_fusion.ready.a), channel_id=1, source_target_pairs={{0,80},{8,56},{16,96},{24,72},{32,112},{40,88},{48,0},{56,104},{64... | collective-permute-start | bytes 442376 | tf_op jit(solution)/shard_map/ppermute | solution.py:41
  86.2 9.3 %collective-permute-done.31.refs_0_.d2 = bf16[64,1152]{1,0:T(8,128)(2,1)S(1)} collective-permute-done((bf16[64,1152]{1,0:T(8,128)(2,1)S(1)}, bf16[64,1152]{1,0:T(8,128)(2,1)S(1)}, u32[]{:S(2)}, u32[]{:S(2)}) %collective-permute-start.31) | collective-permute-done | bytes 147488 | tf_op jit(solution)/shard_map/ppermute | solution.py:41
  95.6 2.8 %collective-permute-start.32 = (bf16[96,1152]{1,0:T(8,128)(2,1)S(1)}, bf16[96,1152]{1,0:T(8,128)(2,1)S(1)}, u32[]{:S(2)}, u32[]{:S(2)}) collective-permute-start(bf16[96,1152]{1,0:T(8,128)(2,1)S(1)} %append.5), channel_id=1, source_target_pairs={{0,112},{8,24},{16,0},{24,40},{32,16},{40,56},{48,32},{56,72},{64,... | collective-permute-start | bytes 663560 | tf_op jit(solution)/shard_map/ppermute | solution.py:41
  98.8 2.9 %collective-permute-done.32.d1 = bf16[96,1152]{1,0:T(8,128)(2,1)S(1)} collective-permute-done((bf16[96,1152]{1,0:T(8,128)(2,1)S(1)}, bf16[96,1152]{1,0:T(8,128)(2,1)S(1)}, u32[]{:S(2)}, u32[]{:S(2)}) %collective-permute-start.32) | collective-permute-done | bytes 221216 | tf_op jit(solution)/shard_map/ppermute | solution.py:41
  101.6 4.7 %collective-permute-done.27.t = bf16[4,128,128]{2,1,0:T(8,128)(2,1)S(1)} collective-permute-done((bf16[4,128,128]{2,1,0:T(8,128)(2,1)S(1)}, bf16[4,128,128]{2,1,0:T(8,128)(2,1)S(1)}, u32[]{:S(2)}, u32[]{:S(2)}) %collective-permute-start.27) | collective-permute-done | bytes 131104 | tf_op jit(solution)/shard_map/ppermute | solution.py:41
  107.0 1.8 %collective-permute-start.28 = (bf16[4,128,128]{2,1,0:T(8,128)(2,1)S(1)}, bf16[4,128,128]{2,1,0:T(8,128)(2,1)S(1)}, u32[]{:S(2)}, u32[]{:S(2)}) collective-permute-start(bf16[4,128,128]{2,1,0:T(8,128)(2,1)S(1)} %ride.1.t), channel_id=1, source_target_pairs={{0,48},{8,88},{16,64},{24,104},{32,80},{40,120},{48,96},{56,8},{64... | collective-permute-start | bytes 393224 | tf_op jit(solution)/shard_map/ppermute | solution.py:41
  108.9 0.7 sum_z.1
  109.5 0.8 collective-permute-start.34
  110.4 2.5 %collective-permute-done.28 = bf16[4,128,128]{2,1,0:T(8,128)(2,1)S(1)} collective-permute-done((bf16[4,128,128]{2,1,0:T(8,128)(2,1)S(1)}, bf16[4,128,128]{2,1,0:T(8,128)(2,1)S(1)}, u32[]{:S(2)}, u32[]{:S(2)}) %collective-permute-start.28) | collective-permute-done | bytes 131104 | tf_op jit(solution)/shard_map/ppermute | solution.py:41
  112.9 5.4 %collective-permute-start.29 = (f32[2,128,128]{2,1,0:T(8,128)S(1)}, f32[2,128,128]{2,1,0:T(8,128)S(1)}, u32[]{:S(2)}, u32[]{:S(2)}) collective-permute-start(f32[2,128,128]{2,1,0:T(8,128)S(1)} %slice.35), channel_id=1, source_target_pairs={{0,8},{8,0},{16,24},{24,16},{32,40},{40,32},{48,56},{56,48},{64,72... | collective-permute-start | bytes 393224 | tf_op jit(solution)/shard_map/ppermute | solution.py:25
  118.4 0.9 collective-permute-done.29
  119.3 0.7 fusion.1
  120.0 1.4 %weight_out.1 = (f32[128,1024]{1,0:T(8,128)}, f32[8,128]{1,0:T(8,128)S(1)}) custom-call(s32[2]{0:T(128)S(1)} %copy-done.4, bf16[64,1152]{1,0:T(8,128)(2,1)S(1)} %pad_maximum_fusion.1.mine, bf16[64,1152]{1,0:T(8,128)(2,1)S(1)} %collective-permute-done.35.theirs), custom_call_target="tpu_custom_call" | custom-call | bytes 1048576 | tf_op jit(solution)/shard_map/weight_out/pallas_call | solution.py:483
  (69 shorter events, 8.7 us)
Async XLA Ops:
  0.6 40.2 %copy-start = (bf16[64,128,128]{2,1,0:T(8,128)(2,1)S(1)}, bf16[64,128,128]{2,1,0:T(8,128)(2,1)}, u32[]{:S(2)}) copy-start(bf16[64,128,128]{2,1,0:T(8,128)(2,1)} %tiles.3) | copy-start | bytes 6291460
  0.6 4.4 %collective-permute-start.1 = (bf16[256,128]{1,0:T(8,128)(2,1)}, bf16[256,128]{1,0:T(8,128)(2,1)S(1)}, u32[]{:S(2)}, u32[]{:S(2)}) collective-permute-start(bf16[256,128]{1,0:T(8,128)(2,1)} %param.7), channel_id=1, source_target_pairs={{0,8},{8,0},{16,24},{24,16},{32,40},{40,32},{48,56},{56,48},{64,72... | collective-permute-start | bytes 196616 | tf_op jit(solution)/shard_map/ppermute | solution.py:25
  5.1 35.7 %collective-permute-start.2 = (bf16[64,128,128]{2,1,0:T(8,128)(2,1)}, bf16[64,128,128]{2,1,0:T(8,128)(2,1)}, u32[]{:S(2)}, u32[]{:S(2)}) collective-permute-start(bf16[64,128,128]{2,1,0:T(8,128)(2,1)} %tiles.3), channel_id=1, source_target_pairs={{0,8},{8,0},{16,24},{24,16},{32,40},{40,32},{48,56},{56,48},{64,72... | collective-permute-start | bytes 6291464 | tf_op jit(solution)/shard_map/ppermute | solution.py:25
  5.5 11.6 %collective-permute-start.6 = (bf16[512,128]{1,0:T(8,128)(2,1)S(1)}, bf16[512,128]{1,0:T(8,128)(2,1)S(1)}, u32[]{:S(2)}, u32[]{:S(2)}) collective-permute-start(bf16[512,128]{1,0:T(8,128)(2,1)S(1)} %constant_dynamic-update-slice_fusion.a), channel_id=1, source_target_pairs={{0,96},{8,40},{16,112},{24,56},{32,0},{40,72},{48,16},{56,88},{64,... | collective-permute-start | bytes 393224 | tf_op jit(solution)/shard_map/ppermute | solution.py:41
  9.7 14.5 %collective-permute-start.10 = (bf16[784,128]{1,0:T(8,128)(2,1)}, bf16[784,128]{1,0:T(8,128)(2,1)S(1)}, u32[]{:S(2)}, u32[]{:S(2)}) collective-permute-start(bf16[784,128]{1,0:T(8,128)(2,1)} %pack_up.1.a), channel_id=1, source_target_pairs={{0,4},{1,5},{2,6},{3,7},{4,0},{5,1},{6,2},{7,3},{8,12},{9,13},{10,... | collective-permute-start | bytes 602120 | tf_op jit(solution)/shard_map/ppermute | solution.py:29
  12.5 9.9 %collective-permute-start.4 = (bf16[512,128]{1,0:T(8,128)(2,1)S(1)}, bf16[512,128]{1,0:T(8,128)(2,1)S(1)}, u32[]{:S(2)}, u32[]{:S(2)}) collective-permute-start(bf16[512,128]{1,0:T(8,128)(2,1)S(1)} %constant_dynamic-update-slice_fusion.a), channel_id=1, source_target_pairs={{0,80},{8,56},{16,96},{24,72},{32,112},{40,88},{48,0},{56,104},{64... | collective-permute-start | bytes 393224 | tf_op jit(solution)/shard_map/ppermute | solution.py:41
  17.2 10.8 %collective-permute-start.8 = (bf16[512,128]{1,0:T(8,128)(2,1)S(1)}, bf16[512,128]{1,0:T(8,128)(2,1)S(1)}, u32[]{:S(2)}, u32[]{:S(2)}) collective-permute-start(bf16[512,128]{1,0:T(8,128)(2,1)S(1)} %collective-permute-done.6.refs_1_), channel_id=1, source_target_pairs={{0,128},{8,136},{16,144},{24,152},{32,160},{40,168},{48,176},{56,1... | collective-permute-start | bytes 393224 | tf_op jit(solution)/shard_map/ppermute | solution.py:25
  18.2 1.2 collective-permute-start
  19.4 4.8 %collective-permute-start.3 = (bf16[256,128]{1,0:T(8,128)(2,1)}, bf16[256,128]{1,0:T(8,128)(2,1)S(1)}, u32[]{:S(2)}, u32[]{:S(2)}) collective-permute-start(bf16[256,128]{1,0:T(8,128)(2,1)} %param.7), channel_id=1, source_target_pairs={{0,128},{8,136},{16,144},{24,152},{32,160},{40,168},{48,176},{56,1... | collective-permute-start | bytes 196616 | tf_op jit(solution)/shard_map/ppermute | solution.py:25
  22.5 9.3 %collective-permute-start.5 = (bf16[768,128]{1,0:T(8,128)(2,1)S(1)}, bf16[768,128]{1,0:T(8,128)(2,1)S(1)}, u32[]{:S(2)}, u32[]{:S(2)}) collective-permute-start(bf16[768,128]{1,0:T(8,128)(2,1)S(1)} %append.3), channel_id=1, source_target_pairs={{0,112},{8,24},{16,0},{24,40},{32,16},{40,56},{48,32},{56,72},{64,... | collective-permute-start | bytes 589832 | tf_op jit(solution)/shard_map/ppermute | solution.py:41
  24.2 0.9 copy-start.2
  25.1 12.9 %collective-permute-start.12 = (bf16[1568,128]{1,0:T(8,128)(2,1)S(1)}, bf16[1568,128]{1,0:T(8,128)(2,1)S(1)}, u32[]{:S(2)}, u32[]{:S(2)}) collective-permute-start(bf16[1568,128]{1,0:T(8,128)(2,1)S(1)} %append.4.refs_0_), channel_id=1, source_target_pairs={{0,3},{1,0},{2,1},{3,2},{4,7},{5,4},{6,5},{7,6},{8,11},{9,8},{10,9... | collective-permute-start | bytes 1204232 | tf_op jit(solution)/shard_map/ppermute | solution.py:29
  28.0 10.1 %collective-permute-start.11 = (bf16[1568,128]{1,0:T(8,128)(2,1)S(1)}, bf16[1568,128]{1,0:T(8,128)(2,1)S(1)}, u32[]{:S(2)}, u32[]{:S(2)}) collective-permute-start(bf16[1568,128]{1,0:T(8,128)(2,1)S(1)} %append.4.refs_0_), channel_id=1, source_target_pairs={{0,1},{1,2},{2,3},{3,0},{4,5},{5,6},{6,7},{7,4},{8,9},{9,10},{10,1... | collective-permute-start | bytes 1204232 | tf_op jit(solution)/shard_map/ppermute | solution.py:29
  28.0 3.8 %collective-permute-start.7 = (bf16[512,128]{1,0:T(8,128)(2,1)S(1)}, bf16[512,128]{1,0:T(8,128)(2,1)S(1)}, u32[]{:S(2)}, u32[]{:S(2)}) collective-permute-start(bf16[512,128]{1,0:T(8,128)(2,1)S(1)} %collective-permute-done.4.b.refs_0_), channel_id=1, source_target_pairs={{0,128},{8,136},{16,144},{24,152},{32,160},{40,168},{48,176},{56,1... | collective-permute-start | bytes 393224 | tf_op jit(solution)/shard_map/ppermute | solution.py:25
  31.8 6.2 %collective-permute-start.9 = (bf16[768,128]{1,0:T(8,128)(2,1)S(1)}, bf16[768,128]{1,0:T(8,128)(2,1)S(1)}, u32[]{:S(2)}, u32[]{:S(2)}) collective-permute-start(bf16[768,128]{1,0:T(8,128)(2,1)S(1)} %hold.1), channel_id=1, source_target_pairs={{0,128},{8,136},{16,144},{24,152},{32,160},{40,168},{48,176},{56,1... | collective-permute-start | bytes 589832 | tf_op jit(solution)/shard_map/ppermute | solution.py:25
  32.9 0.7 copy-start.3
  33.6 0.7 copy-start.5
  34.2 0.7 copy-start.6
  38.0 15.8 %collective-permute-start.14 = (bf16[784,128]{1,0:T(8,128)(2,1)S(1)}, bf16[784,128]{1,0:T(8,128)(2,1)S(1)}, u32[]{:S(2)}, u32[]{:S(2)}) collective-permute-start(bf16[784,128]{1,0:T(8,128)(2,1)S(1)} %get-tuple-element.27.refs_8_), channel_id=1, source_target_pairs={{0,1},{1,2},{2,3},{3,0},{4,5},{5,6},{6,7},{7,4},{8,9},{9,10},{10,1... | collective-permute-start | bytes 602120 | tf_op jit(solution)/shard_map/ppermute | solution.py:29
  38.1 15.7 %collective-permute-start.15 = (bf16[784,128]{1,0:T(8,128)(2,1)S(1)}, bf16[784,128]{1,0:T(8,128)(2,1)S(1)}, u32[]{:S(2)}, u32[]{:S(2)}) collective-permute-start(bf16[784,128]{1,0:T(8,128)(2,1)S(1)} %get-tuple-element.28.refs_9_), channel_id=1, source_target_pairs={{0,3},{1,0},{2,1},{3,2},{4,7},{5,4},{6,5},{7,6},{8,11},{9,8},{10,9... | collective-permute-start | bytes 602120 | tf_op jit(solution)/shard_map/ppermute | solution.py:29
  40.8 18.9 %copy-start.4 = (s32[2]{0:T(128)S(1)}, s32[2]{0:T(128)}, u32[]{:S(2)}) copy-start(s32[2]{0:T(128)} %pad_add_fusion.1.ids) | copy-start | bytes 28
  47.0 25.5 %copy-start.1 = (bf16[128,1024]{1,0:T(8,128)(2,1)S(1)}, bf16[128,1024]{1,0:T(8,128)(2,1)}, u32[]{:S(2)}) copy-start(bf16[128,1024]{1,0:T(8,128)(2,1)} %w_own.1) | copy-start | bytes 786436
  47.1 7.7 %collective-permute-start.13 = (f32[2,128,128]{2,1,0:T(8,128)S(1)}, f32[2,128,128]{2,1,0:T(8,128)S(1)}, u32[]{:S(2)}, u32[]{:S(2)}) collective-permute-start(f32[2,128,128]{2,1,0:T(8,128)S(1)} %get-tuple-element.30), channel_id=1, source_target_pairs={{0,8},{8,0},{16,24},{24,16},{32,40},{40,32},{48,56},{56,48},{64,72... | collective-permute-start | bytes 393224 | tf_op jit(solution)/shard_map/ppermute | solution.py:25
  54.8 4.9 %collective-permute-start.16 = (bf16[256,128]{1,0:T(8,128)(2,1)S(1)}, bf16[256,128]{1,0:T(8,128)(2,1)S(1)}, u32[]{:S(2)}, u32[]{:S(2)}) collective-permute-start(bf16[256,128]{1,0:T(8,128)(2,1)S(1)} %bitcast.30), channel_id=1, source_target_pairs={{0,4},{1,5},{2,6},{3,7},{4,0},{5,1},{6,2},{7,3},{8,12},{9,13},{10,... | collective-permute-start | bytes 196616 | tf_op jit(solution)/shard_map/ppermute | solution.py:29
  61.2 11.4 %collective-permute-start.20 = (bf16[1024,512]{1,0:T(8,128)(2,1)S(1)}, bf16[1024,512]{1,0:T(8,128)(2,1)S(1)}, u32[]{:S(2)}, u32[]{:S(2)}) collective-permute-start(bf16[1024,512]{1,0:T(8,128)(2,1)S(1)} %get-tuple-element.31.w0), channel_id=1, source_target_pairs={{0,8},{8,0},{16,24},{24,16},{32,40},{40,32},{48,56},{56,48},{64,72... | collective-permute-start | bytes 3145736 | tf_op jit(solution)/shard_map/ppermute | solution.py:25
  62.8 6.6 %collective-permute-start.19 = (bf16[512,128]{1,0:T(8,128)(2,1)S(1)}, bf16[512,128]{1,0:T(8,128)(2,1)S(1)}, u32[]{:S(2)}, u32[]{:S(2)}) collective-permute-start(bf16[512,128]{1,0:T(8,128)(2,1)S(1)} %pad_maximum_fusion.2.refs_5_.p0), channel_id=1, source_target_pairs={{0,2},{1,3},{2,0},{3,1},{4,6},{5,7},{6,4},{7,5},{8,10},{9,11},{10,... | collective-permute-start | bytes 393224 | tf_op jit(solution)/shard_map/ppermute | solution.py:29
  63.7 7.6 %collective-permute-start.18 = (bf16[512,128]{1,0:T(8,128)(2,1)S(1)}, bf16[512,128]{1,0:T(8,128)(2,1)S(1)}, u32[]{:S(2)}, u32[]{:S(2)}) collective-permute-start(bf16[512,128]{1,0:T(8,128)(2,1)S(1)} %pad_maximum_fusion.2.refs_5_.p0), channel_id=1, source_target_pairs={{0,3},{1,0},{2,1},{3,2},{4,7},{5,4},{6,5},{7,6},{8,11},{9,8},{10,9... | collective-permute-start | bytes 393224 | tf_op jit(solution)/shard_map/ppermute | solution.py:29
  64.3 8.3 %collective-permute-start.17 = (bf16[512,128]{1,0:T(8,128)(2,1)S(1)}, bf16[512,128]{1,0:T(8,128)(2,1)S(1)}, u32[]{:S(2)}, u32[]{:S(2)}) collective-permute-start(bf16[512,128]{1,0:T(8,128)(2,1)S(1)} %pad_maximum_fusion.2.refs_5_.p0), channel_id=1, source_target_pairs={{0,1},{1,2},{2,3},{3,0},{4,5},{5,6},{6,7},{7,4},{8,9},{9,10},{10,1... | collective-permute-start | bytes 393224 | tf_op jit(solution)/shard_map/ppermute | solution.py:29
  74.7 1.7 %collective-permute-start.22 = (f32[64,1152]{1,0:T(8,128)S(1)}, f32[64,1152]{1,0:T(8,128)S(1)}, u32[]{:S(2)}, u32[]{:S(2)}) collective-permute-start(f32[64,1152]{1,0:T(8,128)S(1)} %get-tuple-element.37), channel_id=1, source_target_pairs={{0,8},{8,0},{16,24},{24,16},{32,40},{40,32},{48,56},{56,48},{64,72... | collective-permute-start | bytes 884744 | tf_op jit(solution)/shard_map/ppermute | solution.py:25
  75.2 2.3 %collective-permute-start.21 = (bf16[2,128,128]{2,1,0:T(8,128)(2,1)S(1)}, bf16[2,128,128]{2,1,0:T(8,128)(2,1)S(1)}, u32[]{:S(2)}, u32[]{:S(2)}) collective-permute-start(bf16[2,128,128]{2,1,0:T(8,128)(2,1)S(1)} %bitcast.32), channel_id=1, source_target_pairs={{0,8},{8,0},{16,24},{24,16},{32,40},{40,32},{48,56},{56,48},{64,72... | collective-permute-start | bytes 196616 | tf_op jit(solution)/shard_map/ppermute | solution.py:25
  76.4 6.8 %collective-permute-start.24 = (bf16[32,1152]{1,0:T(8,128)(2,1)S(1)}, bf16[32,1152]{1,0:T(8,128)(2,1)S(1)}, u32[]{:S(2)}, u32[]{:S(2)}) collective-permute-start(bf16[32,1152]{1,0:T(8,128)(2,1)S(1)} %fusion.send), channel_id=1, source_target_pairs={{0,128},{8,136},{16,144},{24,152},{32,160},{40,168},{48,176},{56,1... | collective-permute-start | bytes 221192 | tf_op jit(solution)/shard_map/ppermute | solution.py:25
  83.2 1.4 %collective-permute-start.25 = (bf16[32,1152]{1,0:T(8,128)(2,1)S(1)}, bf16[32,1152]{1,0:T(8,128)(2,1)S(1)}, u32[]{:S(2)}, u32[]{:S(2)}) collective-permute-start(bf16[32,1152]{1,0:T(8,128)(2,1)S(1)} %quarter_up.1.own), channel_id=1, source_target_pairs={{0,8},{8,0},{16,24},{24,16},{32,40},{40,32},{48,56},{56,48},{64,72... | collective-permute-start | bytes 221192 | tf_op jit(solution)/shard_map/ppermute | solution.py:25
  83.7 14.7 %collective-permute-start.23 = (bf16[16,128,128]{2,1,0:T(8,128)(2,1)S(1)}, bf16[16,128,128]{2,1,0:T(8,128)(2,1)S(1)}, u32[]{:S(2)}, u32[]{:S(2)}) collective-permute-start(bf16[16,128,128]{2,1,0:T(8,128)(2,1)S(1)} %get-tuple-element.39.far), channel_id=1, source_target_pairs={{0,128},{8,136},{16,144},{24,152},{32,160},{40,168},{48,176},{56,1... | collective-permute-start | bytes 1572872 | tf_op jit(solution)/shard_map/ppermute | solution.py:25
  84.7 10.9 %collective-permute-start.31 = (bf16[64,1152]{1,0:T(8,128)(2,1)S(1)}, bf16[64,1152]{1,0:T(8,128)(2,1)S(1)}, u32[]{:S(2)}, u32[]{:S(2)}) collective-permute-start(bf16[64,1152]{1,0:T(8,128)(2,1)S(1)} %pad_maximum_fusion.ready.a), channel_id=1, source_target_pairs={{0,96},{8,40},{16,112},{24,56},{32,0},{40,72},{48,16},{56,88},{64,... | collective-permute-start | bytes 442376 | tf_op jit(solution)/shard_map/ppermute | solution.py:41
  84.7 10.8 %collective-permute-start.30 = (bf16[64,1152]{1,0:T(8,128)(2,1)S(1)}, bf16[64,1152]{1,0:T(8,128)(2,1)S(1)}, u32[]{:S(2)}, u32[]{:S(2)}) collective-permute-start(bf16[64,1152]{1,0:T(8,128)(2,1)S(1)} %pad_maximum_fusion.ready.a), channel_id=1, source_target_pairs={{0,80},{8,56},{16,96},{24,72},{32,112},{40,88},{48,0},{56,104},{64... | collective-permute-start | bytes 442376 | tf_op jit(solution)/shard_map/ppermute | solution.py:41
  95.6 6.1 %collective-permute-start.32 = (bf16[96,1152]{1,0:T(8,128)(2,1)S(1)}, bf16[96,1152]{1,0:T(8,128)(2,1)S(1)}, u32[]{:S(2)}, u32[]{:S(2)}) collective-permute-start(bf16[96,1152]{1,0:T(8,128)(2,1)S(1)} %append.5), channel_id=1, source_target_pairs={{0,112},{8,24},{16,0},{24,40},{32,16},{40,56},{48,32},{56,72},{64,... | collective-permute-start | bytes 663560 | tf_op jit(solution)/shard_map/ppermute | solution.py:41
  98.5 7.9 %collective-permute-start.27 = (bf16[4,128,128]{2,1,0:T(8,128)(2,1)S(1)}, bf16[4,128,128]{2,1,0:T(8,128)(2,1)S(1)}, u32[]{:S(2)}, u32[]{:S(2)}) collective-permute-start(bf16[4,128,128]{2,1,0:T(8,128)(2,1)S(1)} %get-tuple-element.42), channel_id=1, source_target_pairs={{0,32},{8,104},{16,48},{24,120},{32,64},{40,8},{48,80},{56,24},{64... | collective-permute-start | bytes 393224 | tf_op jit(solution)/shard_map/ppermute | solution.py:41
  98.6 8.4 %collective-permute-start.26 = (bf16[6,128,128]{2,1,0:T(8,128)(2,1)S(1)}, bf16[6,128,128]{2,1,0:T(8,128)(2,1)S(1)}, u32[]{:S(2)}, u32[]{:S(2)}) collective-permute-start(bf16[6,128,128]{2,1,0:T(8,128)(2,1)S(1)} %get-tuple-element.41), channel_id=1, source_target_pairs={{0,16},{8,120},{16,32},{24,8},{32,48},{40,24},{48,64},{56,40},{64,... | collective-permute-start | bytes 589832 | tf_op jit(solution)/shard_map/ppermute | solution.py:41
  106.4 2.5 %collective-permute-start.33 = (bf16[96,1152]{1,0:T(8,128)(2,1)S(1)}, bf16[96,1152]{1,0:T(8,128)(2,1)S(1)}, u32[]{:S(2)}, u32[]{:S(2)}) collective-permute-start(bf16[96,1152]{1,0:T(8,128)(2,1)S(1)} %peer_rows.1), channel_id=1, source_target_pairs={{0,8},{8,0},{16,24},{24,16},{32,40},{40,32},{48,56},{56,48},{64,72... | collective-permute-start | bytes 663560 | tf_op jit(solution)/shard_map/ppermute | solution.py:25
  107.0 5.8 %collective-permute-start.28 = (bf16[4,128,128]{2,1,0:T(8,128)(2,1)S(1)}, bf16[4,128,128]{2,1,0:T(8,128)(2,1)S(1)}, u32[]{:S(2)}, u32[]{:S(2)}) collective-permute-start(bf16[4,128,128]{2,1,0:T(8,128)(2,1)S(1)} %ride.1.t), channel_id=1, source_target_pairs={{0,48},{8,88},{16,64},{24,104},{32,80},{40,120},{48,96},{56,8},{64... | collective-permute-start | bytes 393224 | tf_op jit(solution)/shard_map/ppermute | solution.py:41
  109.5 8.7 %collective-permute-start.34 = (bf16[32,1152]{1,0:T(8,128)(2,1)S(1)}, bf16[32,1152]{1,0:T(8,128)(2,1)S(1)}, u32[]{:S(2)}, u32[]{:S(2)}) collective-permute-start(bf16[32,1152]{1,0:T(8,128)(2,1)S(1)} %sum_z.1), channel_id=1, source_target_pairs={{0,128},{8,136},{16,144},{24,152},{32,160},{40,168},{48,176},{56,1... | collective-permute-start | bytes 221192 | tf_op jit(solution)/shard_map/ppermute | solution.py:25
  112.9 6.3 %collective-permute-start.29 = (f32[2,128,128]{2,1,0:T(8,128)S(1)}, f32[2,128,128]{2,1,0:T(8,128)S(1)}, u32[]{:S(2)}, u32[]{:S(2)}) collective-permute-start(f32[2,128,128]{2,1,0:T(8,128)S(1)} %slice.35), channel_id=1, source_target_pairs={{0,8},{8,0},{16,24},{24,16},{32,40},{40,32},{48,56},{56,48},{64,72... | collective-permute-start | bytes 393224 | tf_op jit(solution)/shard_map/ppermute | solution.py:25
  118.3 1.7 %collective-permute-start.35 = (bf16[64,1152]{1,0:T(8,128)(2,1)S(1)}, bf16[64,1152]{1,0:T(8,128)(2,1)S(1)}, u32[]{:S(2)}, u32[]{:S(2)}) collective-permute-start(bf16[64,1152]{1,0:T(8,128)(2,1)S(1)} %pad_maximum_fusion.1.mine), channel_id=1, source_target_pairs={{0,8},{8,0},{16,24},{24,16},{32,40},{40,32},{48,56},{56,48},{64,72... | collective-permute-start | bytes 442376 | tf_op jit(solution)/shard_map/ppermute | solution.py:25

commit v8 on v7

--- a/solution.py
+++ b/solution.py
@@ -117,7 +117,7 @@
     )(u, d, *ready)
 
 
-def hold_body(v, r0, r1, out):
+def hold_body(v, r0, r1, r2, out):
     out[...] = v[...]
 
 
@@ -125,7 +125,7 @@
     return pl.pallas_call(
         hold_body,
         out_shape=jax.ShapeDtypeStruct(v.shape, v.dtype),
-        in_specs=[VM, ANY, ANY],
+        in_specs=[VM, ANY, ANY, ANY],
         out_specs=VM,
         compiler_params=params(4),
         cost_estimate=cost(0, 1 << 18),
@@ -149,14 +149,14 @@
     )(mine, came, a, b)
 
 
-def plan_body(ids, c0, d0, c1, d1, out):
+def plan_body(ids, mine, theirs, out):
     me = ids[0]
     mx, mz, mc = me >> 4, (me >> 1) & 7, me & 1
-    for side, (cols, dest) in enumerate(((c0, d0), (c1, d1))):
+    for side, ref in enumerate((mine, theirs)):
         base = 8 + 72 * side
 
-        def step(i, n, cols=cols, dest=dest, base=base, side=side):
-            b = cols[i]
+        def step(i, n, ref=ref, base=base, side=side):
+            b = ref[0, i]
             o = b >> 1
             dx, dz, dc = (o >> 4) ^ mx, ((o >> 1) - mz) & 7, (o & 1) ^ mc
             k = jnp.where(mc == 0, dz, NZ - dz)
@@ -164,7 +164,7 @@
             held = jnp.where(edge, 1 - dc, jnp.where(k <= 3, 1, 0))
             j = jnp.where(edge, jnp.where(dz == 0, 7, 6), (3 - k) * 2 + dc)
             slot = dx * 16 + j * 2 + (b & 1)
-            out[base + n] = i | (slot << 8) | ((dest[i] + 2 * side) << 16)
+            out[base + n] = i | (slot << 8) | ((ref[1, i] + 2 * side) << 16)
             return n + held
 
         n = lax.fori_loop(0, 64, step, 0, unroll=8)
@@ -173,16 +173,16 @@
         out[side] = (n + 3) >> 2
 
 
-def plan_tiles(ids, c0, d0, c1, d1):
+def plan_tiles(ids, mine, theirs):
     return pl.pallas_call(
         plan_body,
         out_shape=jax.ShapeDtypeStruct((160,), jnp.int32),
-        in_specs=[SM] * 5,
+        in_specs=[SM] * 3,
         out_specs=SM,
         compiler_params=params(4),
         cost_estimate=cost(10000, 4096),
         name="plan_tiles",
-    )(ids, c0, d0, c1, d1)
+    )(ids, mine, theirs)
 
 
 def each_tile(plan, tiles, more, use):
@@ -476,13 +476,13 @@
             at = pl.multiple_of(c * 64 + (x ^ i) * 32, 32)
             buf[pl.ds(at, 32), :] = ref[i * 32 : (i + 1) * 32, :].astype(f32)
     w_out[...] = buf[:, 0:1024]
-    b_out[...] = buf[0:8, 1024:1152]
+    b_out[...] = buf[0, 1024:1152]
 
 
 def weight_out(ids, mine, theirs):
     return pl.pallas_call(
         wout_body,
-        out_shape=(jax.ShapeDtypeStruct((B, 1024), f32), jax.ShapeDtypeStruct((8, B), f32)),
+        out_shape=(jax.ShapeDtypeStruct((B, 1024), f32), jax.ShapeDtypeStruct((B,), f32)),
         in_specs=[SM, VM, VM],
         out_specs=(VM, VM),
         scratch_shapes=[pltpu.VMEM((B, 1152), f32)],
@@ -497,22 +497,24 @@
 
     both = jnp.concatenate([features, row_send(features, dc=1)], axis=0)
     x0 = row_send(features, dx=1)
-    lists = row_send(jnp.stack([col_blocks, dest_blocks]), dc=1)
+    listed = jnp.stack([col_blocks, dest_blocks])
+    lists = row_send(listed, dc=1)
     swap, both_a = tie(adj_tiles, both)
     more = row_send(swap, dc=1)
     o3, o2 = spin_send(both, 3, -1), spin_send(both, 2, -1)
-    plan = plan_tiles(ids, col_blocks, dest_blocks, lists[0], lists[1])
+    plan = plan_tiles(ids, listed, lists)
 
     pack = pack_up(ids, weight, out_grad, bias_vector[None, :])
     pack_x = feat_send(pack, dx=1)
 
-    pair = append(1568, pack, pack_x, o3, o2, x0)
-    o14 = spin_send(append(768, both, o3, lists), 1, -1)
+    ext = append(768, both, o3, lists)
+    o14 = spin_send(ext, 1, -1)
+    pair = append(1568, pack, pack_x, ext, o2, x0)
     p3, p2 = row_send(o3, dx=1), row_send(o2, dx=1)
-    p14 = row_send(hold(o14, p3, p2), dx=1)
+    p14 = row_send(hold(o14, p3, p2, plan), dx=1)
     wu, wd = feat_send(pair, dy=1), feat_send(pair, dy=-1)
 
-    wa, wb = turn(wu, wd, p14, plan)
+    wa, wb = turn(wu, wd, plan)
     mine, theirs = aggregate(plan, adj_tiles, more, (both_a, x0, o14, o2, o3, p14, p2, p3), wa, wb)
     wa, wb = feat_send(wa, dy=1), feat_send(wb, dy=-1)
     aggregated = settle(mine, row_send(theirs, dc=1), wa, wb).reshape(256, B)
@@ -532,8 +534,7 @@
     quarter = quarter_up(keep, got, got_x, far)
     halves = jnp.concatenate([quarter, row_send(quarter, dc=1)], axis=0)
     d3, d2 = spin_send(halves, 3, -1), spin_send(halves, 2, -1)
-    last = append(96, halves, d3, d2)
-    d1 = spin_send(last, 1, -1)
+    d1 = spin_send(append(96, halves, d3, d2), 1, -1)
 
     t14, t2, t3, t0 = join(near, came, halves)
     r14, r2 = spin_send(t14, 1), spin_send(t2, 2)
@@ -548,7 +549,7 @@
 
     r = r14[:4].astype(f32) + r2.astype(f32) + r3.astype(f32)
     out = t0 + r[:2] + row_send(r[2:], dc=1)
-    return hidden, out.reshape(256, B), weight_grad, bias_grad[0]
+    return hidden, out.reshape(256, B), weight_grad, bias_grad
 
 
 def solution(mesh):

time: 122 us -> 120 us (0.984)
  waiting for transfers between devices: 41.2 us -> 38.2 us
  starting transfers between devices: 50.6 us -> 52.7 us
  local copies, waits for them, and re-layouts: 4.29 us -> 2.46 us
    ppermute x9, starting transfers between devices: 13.6 us -> 22.2 us  [spin_send(): return lax.ppermute(v, 'row', perm)]
    ppermute x9, waiting for transfers between devices: 11 us -> 16.2 us  [feat_send(): lax.ppermute(v, 'feat', [(i, (i >> 2 ^ dx) << 2 | i + dy & 3) for i in ra...]
    ppermute x9, waiting for transfers between devices: 21.9 us -> 17.3 us  [spin_send(): return lax.ppermute(v, 'row', perm)]
    ppermute x18, waiting for transfers between devices: 8.31 us -> 4.71 us  [row_send(): return lax.ppermute(v, 'row', perm)]
    ppermute x9, starting transfers between devices: 12 us -> 8.61 us  [feat_send(): lax.ppermute(v, 'feat', [(i, (i >> 2 ^ dx) << 2 | i + dy & 3) for i in ra...]
    ppermute x18, starting transfers between devices: 25 us -> 21.9 us  [row_send(): return lax.ppermute(v, 'row', perm)]
    unnamed x15 -> x11, local copies, waits for them, and re-layouts: 3.75 us -> 2.44 us
where the time goes in v8:
time: 120 us
  starting transfers between devices  52.7 us (44%)
  waiting for transfers between devices  38.2 us (32%)
  Pallas kernels  23.4 us (20%)
  local copies, waits for them, and re-layouts  2.46 us (2%)
  other arithmetic  2.04 us (2%)
    ppermute x9, starting transfers between devices, spin_send(): return lax.ppermute(v, 'row', perm)  22.2 us
    ppermute x18, starting transfers between devices, row_send(): return lax.ppermute(v, 'row', perm)  21.9 us
    ppermute x9, waiting for transfers between devices, spin_send(): return lax.ppermute(v, 'row', perm)  17.3 us
    ppermute x9, waiting for transfers between devices, feat_send(): lax.ppermute(v, 'feat', [(i, (i >> 2 ^ dx) << 2 | i + dy & 3) for i in ra...  16.2 us
    ppermute x9, starting transfers between devices, feat_send(): lax.ppermute(v, 'feat', [(i, (i >> 2 ^ dx) << 2 | i + dy & 3) for i in ra...  8.61 us
    pallas_call x1, Pallas kernels, aggregate(): pl.pallas_call(agg_body, out_shape=(jax.ShapeDtypeStruct((2, B, B), f32),...  6.41 us
    pallas_call x1, Pallas kernels, spread(): pl.pallas_call(spread_body, out_shape=(jax.ShapeDtypeStruct((16, B, B), f...  5.9 us
    ppermute x18, waiting for transfers between devices, row_send(): return lax.ppermute(v, 'row', perm)  4.71 us
  transfers between devices with their start and end apart: 36, of which 19 were waited for; matrix products, arithmetic and copies ran while one was open for 2% of the time, Pallas kernels for 15%

profile of v8, /device:TPU:1, one launch (start us, length us, event | category | flops | bytes accessed | tf_op | source)
XLA Modules:
  0.0 119.6 jit_solution(810619739902142018)
XLA Ops:
  0.6 3.3 %collective-permute-start.1 = (bf16[256,128]{1,0:T(8,128)(2,1)}, bf16[256,128]{1,0:T(8,128)(2,1)S(1)}, u32[]{:S(2)}, u32[]{:S(2)}) collective-permute-start(bf16[256,128]{1,0:T(8,128)(2,1)} %param.7), channel_id=1, source_target_pairs={{0,8},{8,0},{16,24},{24,16},{32,40},{40,32},{48,56},{56,48},{64,72... | collective-permute-start | bytes 196616 | tf_op jit(solution)/shard_map/ppermute | solution.py:25
  4.0 0.8 constant_dynamic-update-slice_fusion.1
  5.5 0.6 pad_add_fusion.1.ids
  6.1 2.3 %pack_up.1.a = bf16[784,128]{1,0:T(8,128)(2,1)} custom-call(s32[2]{0:T(128)} %pad_add_fusion.1.ids, bf16[128,1024]{1,0:T(8,128)(2,1)} %w_own.1, bf16[256,128]{1,0:T(8,128)(2,1)} %og.1, bf16[1,128]{1,0:T(2,128)(2,1)} %bitcast.31), custom_call_target="tpu_custom_call" | custom-call | bytes 524288 | tf_op jit(solution)/shard_map/pack_up/pallas_call | solution.py:70
  8.4 1.1 collective-permute-start.10
  9.5 3.0 %collective-permute-start.6 = (bf16[512,128]{1,0:T(8,128)(2,1)S(1)}, bf16[512,128]{1,0:T(8,128)(2,1)S(1)}, u32[]{:S(2)}, u32[]{:S(2)}) collective-permute-start(bf16[512,128]{1,0:T(8,128)(2,1)S(1)} %constant_dynamic-update-slice_fusion.a), channel_id=1, source_target_pairs={{0,96},{8,40},{16,112},{24,56},{32,0},{40,72},{48,16},{56,88},{64,... | collective-permute-start | bytes 393224 | tf_op jit(solution)/shard_map/ppermute | solution.py:41
  12.5 4.7 %collective-permute-start.4 = (bf16[512,128]{1,0:T(8,128)(2,1)S(1)}, bf16[512,128]{1,0:T(8,128)(2,1)S(1)}, u32[]{:S(2)}, u32[]{:S(2)}) collective-permute-start(bf16[512,128]{1,0:T(8,128)(2,1)S(1)} %constant_dynamic-update-slice_fusion.a), channel_id=1, source_target_pairs={{0,80},{8,56},{16,96},{24,72},{32,112},{40,88},{48,0},{56,104},{64... | collective-permute-start | bytes 393224 | tf_op jit(solution)/shard_map/ppermute | solution.py:41
  17.2 0.7 pad_add_fusion.mine
  17.9 1.1 collective-permute-done.theirs.refs_0_
  19.3 1.2 collective-permute-start.8
  20.5 3.3 %collective-permute-done.4.b = bf16[512,128]{1,0:T(8,128)(2,1)S(1)} collective-permute-done((bf16[512,128]{1,0:T(8,128)(2,1)S(1)}, bf16[512,128]{1,0:T(8,128)(2,1)S(1)}, u32[]{:S(2)}, u32[]{:S(2)}) %collective-permute-start.4) | collective-permute-done | bytes 131104 | tf_op jit(solution)/shard_map/ppermute | solution.py:41
  23.8 0.9 copy-done.2
  24.8 2.8 %collective-permute-start.12 = (bf16[1568,128]{1,0:T(8,128)(2,1)S(1)}, bf16[1568,128]{1,0:T(8,128)(2,1)S(1)}, u32[]{:S(2)}, u32[]{:S(2)}) collective-permute-start(bf16[1568,128]{1,0:T(8,128)(2,1)S(1)} %append.4.refs_0_), channel_id=1, source_target_pairs={{0,3},{1,0},{2,1},{3,2},{4,7},{5,4},{6,5},{7,6},{8,11},{9,8},{10,9... | collective-permute-start | bytes 1204232 | tf_op jit(solution)/shard_map/ppermute | solution.py:29
  28.1 0.7 copy-done.3
  28.8 2.8 %plan_tiles.1.r2.refs_0_.plan = s32[160]{0:T(256)S(1)} custom-call(s32[2]{0:T(128)S(1)} %copy-done.3, s32[2,64]{1,0:T(2,128)S(1)} %pad_add_fusion.mine, s32[2,64]{1,0:T(2,128)S(1)} %collective-permute-done.theirs.refs_0_), custom_call_target="tpu_custom_call" | custom-call | flops 10000 | bytes 4096 | tf_op jit(solution)/shard_map/plan_tiles/pallas_call | solution.py:177
  31.9 1.4 %collective-permute-done.5.v = bf16[768,128]{1,0:T(8,128)(2,1)S(1)} collective-permute-done((bf16[768,128]{1,0:T(8,128)(2,1)S(1)}, bf16[768,128]{1,0:T(8,128)(2,1)S(1)}, u32[]{:S(2)}, u32[]{:S(2)}) %collective-permute-start.5) | collective-permute-done | bytes 196640 | tf_op jit(solution)/shard_map/ppermute | solution.py:41
  34.1 3.1 %collective-permute-done.11.u.refs_1_ = bf16[1568,128]{1,0:T(8,128)(2,1)S(1)} collective-permute-done((bf16[1568,128]{1,0:T(8,128)(2,1)S(1)}, bf16[1568,128]{1,0:T(8,128)(2,1)S(1)}, u32[]{:S(2)}, u32[]{:S(2)}) %collective-permute-start.11) | collective-permute-done | bytes 401440 | tf_op jit(solution)/shard_map/ppermute | solution.py:29
  37.3 2.7 %collective-permute-start.15 = (bf16[784,128]{1,0:T(8,128)(2,1)S(1)}, bf16[784,128]{1,0:T(8,128)(2,1)S(1)}, u32[]{:S(2)}, u32[]{:S(2)}) collective-permute-start(bf16[784,128]{1,0:T(8,128)(2,1)S(1)} %get-tuple-element.28.refs_9_), channel_id=1, source_target_pairs={{0,3},{1,0},{2,1},{3,2},{4,7},{5,4},{6,5},{7,6},{8,11},{9,8},{10,9... | collective-permute-start | bytes 602120 | tf_op jit(solution)/shard_map/ppermute | solution.py:29
  40.0 6.4 %aggregate.1 = (f32[2,128,128]{2,1,0:T(8,128)S(1)}, f32[2,128,128]{2,1,0:T(8,128)S(1)}) custom-call(s32[160]{0:T(256)S(1)} %plan_tiles.1.r2.refs_0_.plan, bf16[64,128,128]{2,1,0:T(8,128)(2,1)S(1)} %copy-done, bf16[64,128,128]{2,1,0:T(8,128)(2,1)} %collective-permute-done.2.more, bf16[4,128,128]{2,1,0:T(8,128)(2,1)S(1)} %bitcast.16, ...), custom_call_target="tpu_custom_call" | custom-call | flops 268435456 | bytes 4194304 | tf_op jit(solution)/shard_map/aggregate/pallas_call | solution.py:228
  46.4 3.6 %collective-permute-start.13 = (f32[2,128,128]{2,1,0:T(8,128)S(1)}, f32[2,128,128]{2,1,0:T(8,128)S(1)}, u32[]{:S(2)}, u32[]{:S(2)}) collective-permute-start(f32[2,128,128]{2,1,0:T(8,128)S(1)} %get-tuple-element.30), channel_id=1, source_target_pairs={{0,8},{8,0},{16,24},{24,16},{32,40},{40,32},{48,56},{56,48},{64,72... | collective-permute-start | bytes 393224 | tf_op jit(solution)/shard_map/ppermute | solution.py:25
  50.0 1.0 collective-permute-done.13.came
  51.5 4.4 %collective-permute-done.16 = bf16[256,128]{1,0:T(8,128)(2,1)S(1)} collective-permute-done((bf16[256,128]{1,0:T(8,128)(2,1)S(1)}, bf16[256,128]{1,0:T(8,128)(2,1)S(1)}, u32[]{:S(2)}, u32[]{:S(2)}) %collective-permute-start.16) | collective-permute-done | bytes 65568 | tf_op jit(solution)/shard_map/ppermute | solution.py:29
  55.9 1.4 %lay_out.1 = (bf16[1024,512]{1,0:T(8,128)(2,1)S(1)}, bf16[256,1024]{1,0:T(8,128)(2,1)S(1)}, f32[8,1024]{1,0:T(8,128)S(1)}) custom-call(s32[2]{0:T(128)S(1)} %copy-done.4, bf16[1568,128]{1,0:T(8,128)(2,1)S(1)} %append.4.refs_0_, bf16[1568,128]{1,0:T(8,128)(2,1)S(1)} %collective-permute-done.11.u.refs_1_, ...), custom_call_target="tpu_custom_call" | custom-call | bytes 3145728 | tf_op jit(solution)/shard_map/lay_out/pallas_call | solution.py:271
  57.4 1.6 %collective-permute-start.20 = (bf16[1024,512]{1,0:T(8,128)(2,1)S(1)}, bf16[1024,512]{1,0:T(8,128)(2,1)S(1)}, u32[]{:S(2)}, u32[]{:S(2)}) collective-permute-start(bf16[1024,512]{1,0:T(8,128)(2,1)S(1)} %get-tuple-element.31.w0), channel_id=1, source_target_pairs={{0,8},{8,0},{16,24},{24,16},{32,40},{40,32},{48,56},{56,48},{64,72... | collective-permute-start | bytes 3145736 | tf_op jit(solution)/shard_map/ppermute | solution.py:25
  59.0 1.0 collective-permute-start.18
  60.4 5.1 %collective-permute-done.19.p3 = bf16[512,128]{1,0:T(8,128)(2,1)S(1)} collective-permute-done((bf16[512,128]{1,0:T(8,128)(2,1)S(1)}, bf16[512,128]{1,0:T(8,128)(2,1)S(1)}, u32[]{:S(2)}, u32[]{:S(2)}) %collective-permute-start.19) | collective-permute-done | bytes 131104 | tf_op jit(solution)/shard_map/ppermute | solution.py:29
  65.5 0.9 collective-permute-done.18.p2
  66.5 2.2 %collective-permute-done.17.p1 = bf16[512,128]{1,0:T(8,128)(2,1)S(1)} collective-permute-done((bf16[512,128]{1,0:T(8,128)(2,1)S(1)}, bf16[512,128]{1,0:T(8,128)(2,1)S(1)}, u32[]{:S(2)}, u32[]{:S(2)}) %collective-permute-start.17) | collective-permute-done | bytes 131104 | tf_op jit(solution)/shard_map/ppermute | solution.py:29
  68.7 2.1 %middle.1 = (f32[256,128]{1,0:T(8,128)}, bf16[256,128]{1,0:T(8,128)(2,1)S(1)}, f32[64,1152]{1,0:T(8,128)S(1)}, f32[64,1152]{1,0:T(8,128)S(1)}) custom-call(s32[2]{0:T(128)S(1)} %copy-done.4, bf16[512,128]{1,0:T(8,128)(2,1)S(1)} %pad_maximum_fusion.2.refs_5_.p0, bf16[512,128]{1,0:T(8,128)(2,1)S(1)} %collective-permute-done.17.p1, ...), custom_call_target="tpu_custom_call" | custom-call | flops 671088640 | bytes 5242880 | tf_op jit(solution)/shard_map/middle/pallas_call | solution.py:317
  71.4 1.2 collective-permute-done.22.got
  72.6 0.8 collective-permute-start.24
  73.3 5.9 %spread.1 = (f32[16,128,128]{2,1,0:T(8,128)S(1)}, bf16[16,128,128]{2,1,0:T(8,128)(2,1)S(1)}) custom-call(s32[160]{0:T(256)S(1)} %plan_tiles.1.r2.refs_0_.plan, bf16[64,128,128]{2,1,0:T(8,128)(2,1)S(1)} %copy-done, bf16[64,128,128]{2,1,0:T(8,128)(2,1)} %collective-permute-done.2.more, bf16[2,128,128]{2,1,0:T(8,128)(2,1)S(1)} %bitcast.27, ...), custom_call_target="tpu_custom_call" | custom-call | flops 268435456 | bytes 6291456 | tf_op jit(solution)/shard_map/spread/pallas_call | solution.py:356
  79.6 1.2 %collective-permute-start.23 = (bf16[16,128,128]{2,1,0:T(8,128)(2,1)S(1)}, bf16[16,128,128]{2,1,0:T(8,128)(2,1)S(1)}, u32[]{:S(2)}, u32[]{:S(2)}) collective-permute-start(bf16[16,128,128]{2,1,0:T(8,128)(2,1)S(1)} %get-tuple-element.39.far), channel_id=1, source_target_pairs={{0,128},{8,136},{16,144},{24,152},{32,160},{40,168},{48,176},{56,1... | collective-permute-start | bytes 1572872 | tf_op jit(solution)/shard_map/ppermute | solution.py:25
  81.2 4.0 %collective-permute-start.30 = (bf16[64,1152]{1,0:T(8,128)(2,1)S(1)}, bf16[64,1152]{1,0:T(8,128)(2,1)S(1)}, u32[]{:S(2)}, u32[]{:S(2)}) collective-permute-start(bf16[64,1152]{1,0:T(8,128)(2,1)S(1)} %pad_maximum_fusion.ready.a), channel_id=1, source_target_pairs={{0,80},{8,56},{16,96},{24,72},{32,112},{40,88},{48,0},{56,104},{64... | collective-permute-start | bytes 442376 | tf_op jit(solution)/shard_map/ppermute | solution.py:41
  85.2 4.6 %collective-permute-done.31.refs_0_.d2 = bf16[64,1152]{1,0:T(8,128)(2,1)S(1)} collective-permute-done((bf16[64,1152]{1,0:T(8,128)(2,1)S(1)}, bf16[64,1152]{1,0:T(8,128)(2,1)S(1)}, u32[]{:S(2)}, u32[]{:S(2)}) %collective-permute-start.31) | collective-permute-done | bytes 147488 | tf_op jit(solution)/shard_map/ppermute | solution.py:41
  89.8 3.0 %collective-permute-start.32 = (bf16[96,1152]{1,0:T(8,128)(2,1)S(1)}, bf16[96,1152]{1,0:T(8,128)(2,1)S(1)}, u32[]{:S(2)}, u32[]{:S(2)}) collective-permute-start(bf16[96,1152]{1,0:T(8,128)(2,1)S(1)} %append.5), channel_id=1, source_target_pairs={{0,112},{8,24},{16,0},{24,40},{32,16},{40,56},{48,32},{56,72},{64,... | collective-permute-start | bytes 663560 | tf_op jit(solution)/shard_map/ppermute | solution.py:41
  92.9 4.4 %collective-permute-start.27 = (bf16[4,128,128]{2,1,0:T(8,128)(2,1)S(1)}, bf16[4,128,128]{2,1,0:T(8,128)(2,1)S(1)}, u32[]{:S(2)}, u32[]{:S(2)}) collective-permute-start(bf16[4,128,128]{2,1,0:T(8,128)(2,1)S(1)} %get-tuple-element.42), channel_id=1, source_target_pairs={{0,32},{8,104},{16,48},{24,120},{32,64},{40,8},{48,80},{56,24},{64... | collective-permute-start | bytes 393224 | tf_op jit(solution)/shard_map/ppermute | solution.py:41
  97.4 1.9 %collective-permute-done.32.d1 = bf16[96,1152]{1,0:T(8,128)(2,1)S(1)} collective-permute-done((bf16[96,1152]{1,0:T(8,128)(2,1)S(1)}, bf16[96,1152]{1,0:T(8,128)(2,1)S(1)}, u32[]{:S(2)}, u32[]{:S(2)}) %collective-permute-start.32) | collective-permute-done | bytes 221216 | tf_op jit(solution)/shard_map/ppermute | solution.py:41
  99.3 2.6 %collective-permute-done.27.t = bf16[4,128,128]{2,1,0:T(8,128)(2,1)S(1)} collective-permute-done((bf16[4,128,128]{2,1,0:T(8,128)(2,1)S(1)}, bf16[4,128,128]{2,1,0:T(8,128)(2,1)S(1)}, u32[]{:S(2)}, u32[]{:S(2)}) %collective-permute-start.27) | collective-permute-done | bytes 131104 | tf_op jit(solution)/shard_map/ppermute | solution.py:41
  101.9 2.3 %collective-permute-start.33 = (bf16[96,1152]{1,0:T(8,128)(2,1)S(1)}, bf16[96,1152]{1,0:T(8,128)(2,1)S(1)}, u32[]{:S(2)}, u32[]{:S(2)}) collective-permute-start(bf16[96,1152]{1,0:T(8,128)(2,1)S(1)} %peer_rows.1), channel_id=1, source_target_pairs={{0,8},{8,0},{16,24},{24,16},{32,40},{40,32},{48,56},{56,48},{64,72... | collective-permute-start | bytes 663560 | tf_op jit(solution)/shard_map/ppermute | solution.py:25
  104.6 2.7 %collective-permute-start.28 = (bf16[4,128,128]{2,1,0:T(8,128)(2,1)S(1)}, bf16[4,128,128]{2,1,0:T(8,128)(2,1)S(1)}, u32[]{:S(2)}, u32[]{:S(2)}) collective-permute-start(bf16[4,128,128]{2,1,0:T(8,128)(2,1)S(1)} %ride.1.t), channel_id=1, source_target_pairs={{0,48},{8,88},{16,64},{24,104},{32,80},{40,120},{48,96},{56,8},{64... | collective-permute-start | bytes 393224 | tf_op jit(solution)/shard_map/ppermute | solution.py:41
  107.3 0.7 sum_z.1
  108.0 1.0 collective-permute-start.34
  109.0 3.0 %collective-permute-done.28 = bf16[4,128,128]{2,1,0:T(8,128)(2,1)S(1)} collective-permute-done((bf16[4,128,128]{2,1,0:T(8,128)(2,1)S(1)}, bf16[4,128,128]{2,1,0:T(8,128)(2,1)S(1)}, u32[]{:S(2)}, u32[]{:S(2)}) %collective-permute-start.28) | collective-permute-done | bytes 131104 | tf_op jit(solution)/shard_map/ppermute | solution.py:41
  112.1 4.5 %collective-permute-start.29 = (f32[2,128,128]{2,1,0:T(8,128)S(1)}, f32[2,128,128]{2,1,0:T(8,128)S(1)}, u32[]{:S(2)}, u32[]{:S(2)}) collective-permute-start(f32[2,128,128]{2,1,0:T(8,128)S(1)} %slice.23), channel_id=1, source_target_pairs={{0,8},{8,0},{16,24},{24,16},{32,40},{40,32},{48,56},{56,48},{64,72... | collective-permute-start | bytes 393224 | tf_op jit(solution)/shard_map/ppermute | solution.py:25
  116.7 0.9 collective-permute-done.29
  117.5 0.7 fusion.1
  118.2 1.4 %weight_out.1 = (f32[128,1024]{1,0:T(8,128)}, f32[128]{0:T(128)}) custom-call(s32[2]{0:T(128)S(1)} %copy-done.4, bf16[64,1152]{1,0:T(8,128)(2,1)S(1)} %pad_maximum_fusion.1.mine, bf16[64,1152]{1,0:T(8,128)(2,1)S(1)} %collective-permute-done.35.theirs), custom_call_target="tpu_custom_call" | custom-call | bytes 1048576 | tf_op jit(solution)/shard_map/weight_out/pallas_call | solution.py:483
  (63 shorter events, 5.9 us)
Async XLA Ops:
  0.6 39.4 %copy-start = (bf16[64,128,128]{2,1,0:T(8,128)(2,1)S(1)}, bf16[64,128,128]{2,1,0:T(8,128)(2,1)}, u32[]{:S(2)}) copy-start(bf16[64,128,128]{2,1,0:T(8,128)(2,1)} %tiles.3) | copy-start | bytes 6291460
  0.6 4.4 %collective-permute-start.1 = (bf16[256,128]{1,0:T(8,128)(2,1)}, bf16[256,128]{1,0:T(8,128)(2,1)S(1)}, u32[]{:S(2)}, u32[]{:S(2)}) collective-permute-start(bf16[256,128]{1,0:T(8,128)(2,1)} %param.7), channel_id=1, source_target_pairs={{0,8},{8,0},{16,24},{24,16},{32,40},{40,32},{48,56},{56,48},{64,72... | collective-permute-start | bytes 196616 | tf_op jit(solution)/shard_map/ppermute | solution.py:25
  5.1 34.9 %collective-permute-start.2 = (bf16[64,128,128]{2,1,0:T(8,128)(2,1)}, bf16[64,128,128]{2,1,0:T(8,128)(2,1)}, u32[]{:S(2)}, u32[]{:S(2)}) collective-permute-start(bf16[64,128,128]{2,1,0:T(8,128)(2,1)} %tiles.3), channel_id=1, source_target_pairs={{0,8},{8,0},{16,24},{24,16},{32,40},{40,32},{48,56},{56,48},{64,72... | collective-permute-start | bytes 6291464 | tf_op jit(solution)/shard_map/ppermute | solution.py:25
  8.4 15.3 %collective-permute-start.10 = (bf16[784,128]{1,0:T(8,128)(2,1)}, bf16[784,128]{1,0:T(8,128)(2,1)S(1)}, u32[]{:S(2)}, u32[]{:S(2)}) collective-permute-start(bf16[784,128]{1,0:T(8,128)(2,1)} %pack_up.1.a), channel_id=1, source_target_pairs={{0,4},{1,5},{2,6},{3,7},{4,0},{5,1},{6,2},{7,3},{8,12},{9,13},{10,... | collective-permute-start | bytes 602120 | tf_op jit(solution)/shard_map/ppermute | solution.py:29
  9.5 9.8 %collective-permute-start.6 = (bf16[512,128]{1,0:T(8,128)(2,1)S(1)}, bf16[512,128]{1,0:T(8,128)(2,1)S(1)}, u32[]{:S(2)}, u32[]{:S(2)}) collective-permute-start(bf16[512,128]{1,0:T(8,128)(2,1)S(1)} %constant_dynamic-update-slice_fusion.a), channel_id=1, source_target_pairs={{0,96},{8,40},{16,112},{24,56},{32,0},{40,72},{48,16},{56,88},{64,... | collective-permute-start | bytes 393224 | tf_op jit(solution)/shard_map/ppermute | solution.py:41
  12.5 11.2 %collective-permute-start.4 = (bf16[512,128]{1,0:T(8,128)(2,1)S(1)}, bf16[512,128]{1,0:T(8,128)(2,1)S(1)}, u32[]{:S(2)}, u32[]{:S(2)}) collective-permute-start(bf16[512,128]{1,0:T(8,128)(2,1)S(1)} %constant_dynamic-update-slice_fusion.a), channel_id=1, source_target_pairs={{0,80},{8,56},{16,96},{24,72},{32,112},{40,88},{48,0},{56,104},{64... | collective-permute-start | bytes 393224 | tf_op jit(solution)/shard_map/ppermute | solution.py:41
  17.9 1.1 collective-permute-start
  19.0 4.8 %collective-permute-start.3 = (bf16[256,128]{1,0:T(8,128)(2,1)}, bf16[256,128]{1,0:T(8,128)(2,1)S(1)}, u32[]{:S(2)}, u32[]{:S(2)}) collective-permute-start(bf16[256,128]{1,0:T(8,128)(2,1)} %param.7), channel_id=1, source_target_pairs={{0,128},{8,136},{16,144},{24,152},{32,160},{40,168},{48,176},{56,1... | collective-permute-start | bytes 196616 | tf_op jit(solution)/shard_map/ppermute | solution.py:25
  19.3 8.5 %collective-permute-start.8 = (bf16[512,128]{1,0:T(8,128)(2,1)S(1)}, bf16[512,128]{1,0:T(8,128)(2,1)S(1)}, u32[]{:S(2)}, u32[]{:S(2)}) collective-permute-start(bf16[512,128]{1,0:T(8,128)(2,1)S(1)} %collective-permute-done.6.refs_1_), channel_id=1, source_target_pairs={{0,128},{8,136},{16,144},{24,152},{32,160},{40,168},{48,176},{56,1... | collective-permute-start | bytes 393224 | tf_op jit(solution)/shard_map/ppermute | solution.py:25
  23.8 0.9 copy-start.2
  24.8 9.3 %collective-permute-start.12 = (bf16[1568,128]{1,0:T(8,128)(2,1)S(1)}, bf16[1568,128]{1,0:T(8,128)(2,1)S(1)}, u32[]{:S(2)}, u32[]{:S(2)}) collective-permute-start(bf16[1568,128]{1,0:T(8,128)(2,1)S(1)} %append.4.refs_0_), channel_id=1, source_target_pairs={{0,3},{1,0},{2,1},{3,2},{4,7},{5,4},{6,5},{7,6},{8,11},{9,8},{10,9... | collective-permute-start | bytes 1204232 | tf_op jit(solution)/shard_map/ppermute | solution.py:29
  27.6 9.6 %collective-permute-start.11 = (bf16[1568,128]{1,0:T(8,128)(2,1)S(1)}, bf16[1568,128]{1,0:T(8,128)(2,1)S(1)}, u32[]{:S(2)}, u32[]{:S(2)}) collective-permute-start(bf16[1568,128]{1,0:T(8,128)(2,1)S(1)} %append.4.refs_0_), channel_id=1, source_target_pairs={{0,1},{1,2},{2,3},{3,0},{4,5},{5,6},{6,7},{7,4},{8,9},{9,10},{10,1... | collective-permute-start | bytes 1204232 | tf_op jit(solution)/shard_map/ppermute | solution.py:29
  27.6 5.7 %collective-permute-start.5 = (bf16[768,128]{1,0:T(8,128)(2,1)S(1)}, bf16[768,128]{1,0:T(8,128)(2,1)S(1)}, u32[]{:S(2)}, u32[]{:S(2)}) collective-permute-start(bf16[768,128]{1,0:T(8,128)(2,1)S(1)} %append.3.refs_0_), channel_id=1, source_target_pairs={{0,112},{8,24},{16,0},{24,40},{32,16},{40,56},{48,32},{56,72},{64,... | collective-permute-start | bytes 589832 | tf_op jit(solution)/shard_map/ppermute | solution.py:41
  27.8 4.1 %collective-permute-start.7 = (bf16[512,128]{1,0:T(8,128)(2,1)S(1)}, bf16[512,128]{1,0:T(8,128)(2,1)S(1)}, u32[]{:S(2)}, u32[]{:S(2)}) collective-permute-start(bf16[512,128]{1,0:T(8,128)(2,1)S(1)} %collective-permute-done.4.b), channel_id=1, source_target_pairs={{0,128},{8,136},{16,144},{24,152},{32,160},{40,168},{48,176},{56,1... | collective-permute-start | bytes 393224 | tf_op jit(solution)/shard_map/ppermute | solution.py:25
  28.1 0.7 copy-start.3
  33.3 6.7 %collective-permute-start.9 = (bf16[768,128]{1,0:T(8,128)(2,1)S(1)}, bf16[768,128]{1,0:T(8,128)(2,1)S(1)}, u32[]{:S(2)}, u32[]{:S(2)}) collective-permute-start(bf16[768,128]{1,0:T(8,128)(2,1)S(1)} %hold.1), channel_id=1, source_target_pairs={{0,128},{8,136},{16,144},{24,152},{32,160},{40,168},{48,176},{56,1... | collective-permute-start | bytes 589832 | tf_op jit(solution)/shard_map/ppermute | solution.py:25
  37.2 12.8 %collective-permute-start.14 = (bf16[784,128]{1,0:T(8,128)(2,1)S(1)}, bf16[784,128]{1,0:T(8,128)(2,1)S(1)}, u32[]{:S(2)}, u32[]{:S(2)}) collective-permute-start(bf16[784,128]{1,0:T(8,128)(2,1)S(1)} %get-tuple-element.27.refs_8_), channel_id=1, source_target_pairs={{0,1},{1,2},{2,3},{3,0},{4,5},{5,6},{6,7},{7,4},{8,9},{9,10},{10,1... | collective-permute-start | bytes 602120 | tf_op jit(solution)/shard_map/ppermute | solution.py:29
  37.3 12.7 %collective-permute-start.15 = (bf16[784,128]{1,0:T(8,128)(2,1)S(1)}, bf16[784,128]{1,0:T(8,128)(2,1)S(1)}, u32[]{:S(2)}, u32[]{:S(2)}) collective-permute-start(bf16[784,128]{1,0:T(8,128)(2,1)S(1)} %get-tuple-element.28.refs_9_), channel_id=1, source_target_pairs={{0,3},{1,0},{2,1},{3,2},{4,7},{5,4},{6,5},{7,6},{8,11},{9,8},{10,9... | collective-permute-start | bytes 602120 | tf_op jit(solution)/shard_map/ppermute | solution.py:29
  40.0 15.9 %copy-start.4 = (s32[2]{0:T(128)S(1)}, s32[2]{0:T(128)}, u32[]{:S(2)}) copy-start(s32[2]{0:T(128)} %pad_add_fusion.1.ids) | copy-start | bytes 28
  46.4 22.3 %copy-start.1 = (bf16[128,1024]{1,0:T(8,128)(2,1)S(1)}, bf16[128,1024]{1,0:T(8,128)(2,1)}, u32[]{:S(2)}) copy-start(bf16[128,1024]{1,0:T(8,128)(2,1)} %w_own.1) | copy-start | bytes 786436
  46.4 4.5 %collective-permute-start.13 = (f32[2,128,128]{2,1,0:T(8,128)S(1)}, f32[2,128,128]{2,1,0:T(8,128)S(1)}, u32[]{:S(2)}, u32[]{:S(2)}) collective-permute-start(f32[2,128,128]{2,1,0:T(8,128)S(1)} %get-tuple-element.30), channel_id=1, source_target_pairs={{0,8},{8,0},{16,24},{24,16},{32,40},{40,32},{48,56},{56,48},{64,72... | collective-permute-start | bytes 393224 | tf_op jit(solution)/shard_map/ppermute | solution.py:25
  51.0 4.9 %collective-permute-start.16 = (bf16[256,128]{1,0:T(8,128)(2,1)S(1)}, bf16[256,128]{1,0:T(8,128)(2,1)S(1)}, u32[]{:S(2)}, u32[]{:S(2)}) collective-permute-start(bf16[256,128]{1,0:T(8,128)(2,1)S(1)} %bitcast.23), channel_id=1, source_target_pairs={{0,4},{1,5},{2,6},{3,7},{4,0},{5,1},{6,2},{7,3},{8,12},{9,13},{10,... | collective-permute-start | bytes 196616 | tf_op jit(solution)/shard_map/ppermute | solution.py:29
  57.4 11.4 %collective-permute-start.20 = (bf16[1024,512]{1,0:T(8,128)(2,1)S(1)}, bf16[1024,512]{1,0:T(8,128)(2,1)S(1)}, u32[]{:S(2)}, u32[]{:S(2)}) collective-permute-start(bf16[1024,512]{1,0:T(8,128)(2,1)S(1)} %get-tuple-element.31.w0), channel_id=1, source_target_pairs={{0,8},{8,0},{16,24},{24,16},{32,40},{40,32},{48,56},{56,48},{64,72... | collective-permute-start | bytes 3145736 | tf_op jit(solution)/shard_map/ppermute | solution.py:25
  59.0 6.6 %collective-permute-start.19 = (bf16[512,128]{1,0:T(8,128)(2,1)S(1)}, bf16[512,128]{1,0:T(8,128)(2,1)S(1)}, u32[]{:S(2)}, u32[]{:S(2)}) collective-permute-start(bf16[512,128]{1,0:T(8,128)(2,1)S(1)} %pad_maximum_fusion.2.refs_5_.p0), channel_id=1, source_target_pairs={{0,2},{1,3},{2,0},{3,1},{4,6},{5,7},{6,4},{7,5},{8,10},{9,11},{10,... | collective-permute-start | bytes 393224 | tf_op jit(solution)/shard_map/ppermute | solution.py:29
  59.0 7.5 %collective-permute-start.18 = (bf16[512,128]{1,0:T(8,128)(2,1)S(1)}, bf16[512,128]{1,0:T(8,128)(2,1)S(1)}, u32[]{:S(2)}, u32[]{:S(2)}) collective-permute-start(bf16[512,128]{1,0:T(8,128)(2,1)S(1)} %pad_maximum_fusion.2.refs_5_.p0), channel_id=1, source_target_pairs={{0,3},{1,0},{2,1},{3,2},{4,7},{5,4},{6,5},{7,6},{8,11},{9,8},{10,9... | collective-permute-start | bytes 393224 | tf_op jit(solution)/shard_map/ppermute | solution.py:29
  60.0 8.7 %collective-permute-start.17 = (bf16[512,128]{1,0:T(8,128)(2,1)S(1)}, bf16[512,128]{1,0:T(8,128)(2,1)S(1)}, u32[]{:S(2)}, u32[]{:S(2)}) collective-permute-start(bf16[512,128]{1,0:T(8,128)(2,1)S(1)} %pad_maximum_fusion.2.refs_5_.p0), channel_id=1, source_target_pairs={{0,1},{1,2},{2,3},{3,0},{4,5},{5,6},{6,7},{7,4},{8,9},{9,10},{10,1... | collective-permute-start | bytes 393224 | tf_op jit(solution)/shard_map/ppermute | solution.py:29
  70.9 1.7 %collective-permute-start.22 = (f32[64,1152]{1,0:T(8,128)S(1)}, f32[64,1152]{1,0:T(8,128)S(1)}, u32[]{:S(2)}, u32[]{:S(2)}) collective-permute-start(f32[64,1152]{1,0:T(8,128)S(1)} %get-tuple-element.37), channel_id=1, source_target_pairs={{0,8},{8,0},{16,24},{24,16},{32,40},{40,32},{48,56},{56,48},{64,72... | collective-permute-start | bytes 884744 | tf_op jit(solution)/shard_map/ppermute | solution.py:25
  71.3 2.0 %collective-permute-start.21 = (bf16[2,128,128]{2,1,0:T(8,128)(2,1)S(1)}, bf16[2,128,128]{2,1,0:T(8,128)(2,1)S(1)}, u32[]{:S(2)}, u32[]{:S(2)}) collective-permute-start(bf16[2,128,128]{2,1,0:T(8,128)(2,1)S(1)} %bitcast.26), channel_id=1, source_target_pairs={{0,8},{8,0},{16,24},{24,16},{32,40},{40,32},{48,56},{56,48},{64,72... | collective-permute-start | bytes 196616 | tf_op jit(solution)/shard_map/ppermute | solution.py:25
  72.6 6.7 %collective-permute-start.24 = (bf16[32,1152]{1,0:T(8,128)(2,1)S(1)}, bf16[32,1152]{1,0:T(8,128)(2,1)S(1)}, u32[]{:S(2)}, u32[]{:S(2)}) collective-permute-start(bf16[32,1152]{1,0:T(8,128)(2,1)S(1)} %fusion.send), channel_id=1, source_target_pairs={{0,128},{8,136},{16,144},{24,152},{32,160},{40,168},{48,176},{56,1... | collective-permute-start | bytes 221192 | tf_op jit(solution)/shard_map/ppermute | solution.py:25
  79.3 1.5 %collective-permute-start.25 = (bf16[32,1152]{1,0:T(8,128)(2,1)S(1)}, bf16[32,1152]{1,0:T(8,128)(2,1)S(1)}, u32[]{:S(2)}, u32[]{:S(2)}) collective-permute-start(bf16[32,1152]{1,0:T(8,128)(2,1)S(1)} %quarter_up.1.own), channel_id=1, source_target_pairs={{0,8},{8,0},{16,24},{24,16},{32,40},{40,32},{48,56},{56,48},{64,72... | collective-permute-start | bytes 221192 | tf_op jit(solution)/shard_map/ppermute | solution.py:25
  79.6 13.2 %collective-permute-start.23 = (bf16[16,128,128]{2,1,0:T(8,128)(2,1)S(1)}, bf16[16,128,128]{2,1,0:T(8,128)(2,1)S(1)}, u32[]{:S(2)}, u32[]{:S(2)}) collective-permute-start(bf16[16,128,128]{2,1,0:T(8,128)(2,1)S(1)} %get-tuple-element.39.far), channel_id=1, source_target_pairs={{0,128},{8,136},{16,144},{24,152},{32,160},{40,168},{48,176},{56,1... | collective-permute-start | bytes 1572872 | tf_op jit(solution)/shard_map/ppermute | solution.py:25
  80.9 8.9 %collective-permute-start.31 = (bf16[64,1152]{1,0:T(8,128)(2,1)S(1)}, bf16[64,1152]{1,0:T(8,128)(2,1)S(1)}, u32[]{:S(2)}, u32[]{:S(2)}) collective-permute-start(bf16[64,1152]{1,0:T(8,128)(2,1)S(1)} %pad_maximum_fusion.ready.a), channel_id=1, source_target_pairs={{0,96},{8,40},{16,112},{24,56},{32,0},{40,72},{48,16},{56,88},{64,... | collective-permute-start | bytes 442376 | tf_op jit(solution)/shard_map/ppermute | solution.py:41
  81.2 8.6 %collective-permute-start.30 = (bf16[64,1152]{1,0:T(8,128)(2,1)S(1)}, bf16[64,1152]{1,0:T(8,128)(2,1)S(1)}, u32[]{:S(2)}, u32[]{:S(2)}) collective-permute-start(bf16[64,1152]{1,0:T(8,128)(2,1)S(1)} %pad_maximum_fusion.ready.a), channel_id=1, source_target_pairs={{0,80},{8,56},{16,96},{24,72},{32,112},{40,88},{48,0},{56,104},{64... | collective-permute-start | bytes 442376 | tf_op jit(solution)/shard_map/ppermute | solution.py:41
  89.8 9.5 %collective-permute-start.32 = (bf16[96,1152]{1,0:T(8,128)(2,1)S(1)}, bf16[96,1152]{1,0:T(8,128)(2,1)S(1)}, u32[]{:S(2)}, u32[]{:S(2)}) collective-permute-start(bf16[96,1152]{1,0:T(8,128)(2,1)S(1)} %append.5), channel_id=1, source_target_pairs={{0,112},{8,24},{16,0},{24,40},{32,16},{40,56},{48,32},{56,72},{64,... | collective-permute-start | bytes 663560 | tf_op jit(solution)/shard_map/ppermute | solution.py:41
  92.9 9.0 %collective-permute-start.27 = (bf16[4,128,128]{2,1,0:T(8,128)(2,1)S(1)}, bf16[4,128,128]{2,1,0:T(8,128)(2,1)S(1)}, u32[]{:S(2)}, u32[]{:S(2)}) collective-permute-start(bf16[4,128,128]{2,1,0:T(8,128)(2,1)S(1)} %get-tuple-element.42), channel_id=1, source_target_pairs={{0,32},{8,104},{16,48},{24,120},{32,64},{40,8},{48,80},{56,24},{64... | collective-permute-start | bytes 393224 | tf_op jit(solution)/shard_map/ppermute | solution.py:41
  97.3 7.3 %collective-permute-start.26 = (bf16[6,128,128]{2,1,0:T(8,128)(2,1)S(1)}, bf16[6,128,128]{2,1,0:T(8,128)(2,1)S(1)}, u32[]{:S(2)}, u32[]{:S(2)}) collective-permute-start(bf16[6,128,128]{2,1,0:T(8,128)(2,1)S(1)} %get-tuple-element.41), channel_id=1, source_target_pairs={{0,16},{8,120},{16,32},{24,8},{32,48},{40,24},{48,64},{56,40},{64,... | collective-permute-start | bytes 589832 | tf_op jit(solution)/shard_map/ppermute | solution.py:41
  101.9 5.4 %collective-permute-start.33 = (bf16[96,1152]{1,0:T(8,128)(2,1)S(1)}, bf16[96,1152]{1,0:T(8,128)(2,1)S(1)}, u32[]{:S(2)}, u32[]{:S(2)}) collective-permute-start(bf16[96,1152]{1,0:T(8,128)(2,1)S(1)} %peer_rows.1), channel_id=1, source_target_pairs={{0,8},{8,0},{16,24},{24,16},{32,40},{40,32},{48,56},{56,48},{64,72... | collective-permute-start | bytes 663560 | tf_op jit(solution)/shard_map/ppermute | solution.py:25
  104.6 7.4 %collective-permute-start.28 = (bf16[4,128,128]{2,1,0:T(8,128)(2,1)S(1)}, bf16[4,128,128]{2,1,0:T(8,128)(2,1)S(1)}, u32[]{:S(2)}, u32[]{:S(2)}) collective-permute-start(bf16[4,128,128]{2,1,0:T(8,128)(2,1)S(1)} %ride.1.t), channel_id=1, source_target_pairs={{0,48},{8,88},{16,64},{24,104},{32,80},{40,120},{48,96},{56,8},{64... | collective-permute-start | bytes 393224 | tf_op jit(solution)/shard_map/ppermute | solution.py:41
  108.0 8.6 %collective-permute-start.34 = (bf16[32,1152]{1,0:T(8,128)(2,1)S(1)}, bf16[32,1152]{1,0:T(8,128)(2,1)S(1)}, u32[]{:S(2)}, u32[]{:S(2)}) collective-permute-start(bf16[32,1152]{1,0:T(8,128)(2,1)S(1)} %sum_z.1), channel_id=1, source_target_pairs={{0,128},{8,136},{16,144},{24,152},{32,160},{40,168},{48,176},{56,1... | collective-permute-start | bytes 221192 | tf_op jit(solution)/shard_map/ppermute | solution.py:25
  112.1 5.5 %collective-permute-start.29 = (f32[2,128,128]{2,1,0:T(8,128)S(1)}, f32[2,128,128]{2,1,0:T(8,128)S(1)}, u32[]{:S(2)}, u32[]{:S(2)}) collective-permute-start(f32[2,128,128]{2,1,0:T(8,128)S(1)} %slice.23), channel_id=1, source_target_pairs={{0,8},{8,0},{16,24},{24,16},{32,40},{40,32},{48,56},{56,48},{64,72... | collective-permute-start | bytes 393224 | tf_op jit(solution)/shard_map/ppermute | solution.py:25
  116.6 1.6 %collective-permute-start.35 = (bf16[64,1152]{1,0:T(8,128)(2,1)S(1)}, bf16[64,1152]{1,0:T(8,128)(2,1)S(1)}, u32[]{:S(2)}, u32[]{:S(2)}) collective-permute-start(bf16[64,1152]{1,0:T(8,128)(2,1)S(1)} %pad_maximum_fusion.1.mine), channel_id=1, source_target_pairs={{0,8},{8,0},{16,24},{24,16},{32,40},{40,32},{48,56},{56,48},{64,72... | collective-permute-start | bytes 442376 | tf_op jit(solution)/shard_map/ppermute | solution.py:25

commit v9 on v8

--- a/solution.py
+++ b/solution.py
@@ -190,14 +190,15 @@
         def step(g, carry, side=side, ref=ref):
             for u in range(4):
                 e = plan[8 + 72 * side + g * 4 + u]
-                use(ref[e & 255], (e >> 8) & 255, e >> 16)
+                use(u, ref[e & 255], (e >> 8) & 255, e >> 16)
             return carry
 
         lax.fori_loop(0, plan[side], step, 0)
 
 
 def agg_body(plan, tiles, more, *refs):
-    mine, theirs, src, acc, sem = refs[10:]
+    mine, theirs, src, acc0, acc1, acc2, acc3, sem = refs[10:]
+    accs = (acc0, acc1, acc2, acc3)
     both, x0, o14, o2, o3, p14, p2, p3 = refs[0:8]
     copies = []
 
@@ -210,17 +211,18 @@
     for dx, (v3, v2, v14, v0) in enumerate(((o3, o2, o14, both.at[0:2]), (p3, p2, p14, x0))):
         for j, v in ((0, v3), (2, v2), (4, v14), (7, v0)):
             put(dx, j, v)
-    acc[...] = jnp.zeros_like(acc)
+    for acc in accs:
+        acc[...] = jnp.zeros_like(acc)
     src[32] = jnp.zeros((B, B), bf16)
     for c in copies:
         c.wait()
 
-    def use(tile, slot, dest):
-        acc[dest] += jnp.dot(tile, src[slot], preferred_element_type=f32)
+    def use(u, tile, slot, dest):
+        accs[u][dest] += jnp.dot(tile, src[slot], preferred_element_type=f32)
 
     each_tile(plan, tiles, more, use)
-    mine[...] = acc[0:2]
-    theirs[...] = acc[2:4]
+    mine[...] = (acc0[0:2] + acc1[0:2]) + (acc2[0:2] + acc3[0:2])
+    theirs[...] = (acc0[2:4] + acc1[2:4]) + (acc2[2:4] + acc3[2:4])
 
 
 def aggregate(plan, tiles, more, pieces, *ready):
@@ -232,7 +234,7 @@
         out_specs=(VM, VM),
         scratch_shapes=[
             pltpu.VMEM((33, B, B), bf16),
-            pltpu.VMEM((5, B, B), f32),
+            *[pltpu.VMEM((5, B, B), f32)] * 4,
             pltpu.SemaphoreType.DMA((8,)),
         ],
         compiler_params=params(12),
@@ -336,20 +338,22 @@
     )(ids, *pieces, w0, w1, og, bias, w_own)
 
 
-def spread_body(plan, tiles, more, prop, peer, send, near, far, acc, both):
-    acc[...] = jnp.zeros_like(acc)
+def spread_body(plan, tiles, more, prop, peer, send, near, far, acc0, acc1, both):
+    accs = (acc0, acc1)
+    for acc in accs:
+        acc[...] = jnp.zeros_like(acc)
     both[0:2] = prop[...]
     both[2:4] = peer[...]
     both[4] = jnp.zeros((B, B), bf16)
 
-    def use(tile, slot, dest):
-        acc[slot] += lax.dot_general(
+    def use(u, tile, slot, dest):
+        accs[u & 1][slot] += lax.dot_general(
             tile, both[dest], (((0,), (0,)), ((), ())), preferred_element_type=f32
         )
 
     each_tile(plan, tiles, more, use)
-    near[...] = acc[0:16]
-    far[...] = acc[16:32].astype(bf16)
+    near[...] = acc0[0:16] + acc1[0:16]
+    far[...] = (acc0[16:32] + acc1[16:32]).astype(bf16)
 
 
 def spread(plan, tiles, more, prop, peer, send):
@@ -361,8 +365,8 @@
         ),
         in_specs=[SM] + [VM] * 4 + [ANY],
         out_specs=(VM, VM),
-        scratch_shapes=[pltpu.VMEM((33, B, B), f32), pltpu.VMEM((5, B, B), bf16)],
-        compiler_params=params(12),
+        scratch_shapes=[pltpu.VMEM((33, B, B), f32), pltpu.VMEM((33, B, B), f32), pltpu.VMEM((5, B, B), bf16)],
+        compiler_params=params(14),
         cost_estimate=cost(2 * 64 * B**3, 6 << 20),
         name="spread",
     )(plan, tiles, more, prop, peer, send)

time: 120 us -> 120 us (level)
  transfers between devices with their start and end apart: 36 -> 36, of which waited for: 19 -> 20; matrix products, arithmetic and copies ran while one was open for 2% -> 2% of each run, Pallas kernels for 15% -> 15%
where the time goes in v9:
time: 120 us
  starting transfers between devices  53.3 us (44%)
  waiting for transfers between devices  38.6 us (32%)
  Pallas kernels  22.7 us (19%)
  local copies, waits for them, and re-layouts  2.46 us (2%)
  other arithmetic  2.04 us (2%)
    ppermute x18, starting transfers between devices, row_send(): return lax.ppermute(v, 'row', perm)  22.9 us
    ppermute x9, starting transfers between devices, spin_send(): return lax.ppermute(v, 'row', perm)  21.8 us
    ppermute x9, waiting for transfers between devices, spin_send(): return lax.ppermute(v, 'row', perm)  17.2 us
    ppermute x9, waiting for transfers between devices, feat_send(): lax.ppermute(v, 'feat', [(i, (i >> 2 ^ dx) << 2 | i + dy & 3) for i in ra...  16.2 us
    ppermute x9, starting transfers between devices, feat_send(): lax.ppermute(v, 'feat', [(i, (i >> 2 ^ dx) << 2 | i + dy & 3) for i in ra...  8.61 us
    pallas_call x1, Pallas kernels, aggregate(): pl.pallas_call(agg_body, out_shape=(jax.ShapeDtypeStruct((2, B, B), f32),...  6.04 us
    pallas_call x1, Pallas kernels, spread(): pl.pallas_call(spread_body, out_shape=(jax.ShapeDtypeStruct((16, B, B), f...  5.55 us
    ppermute x18, waiting for transfers between devices, row_send(): return lax.ppermute(v, 'row', perm)  5.23 us
  transfers between devices with their start and end apart: 36, of which 20 were waited for; matrix products, arithmetic and copies ran while one was open for 2% of the time, Pallas kernels for 15%

profile of v9, /device:TPU:1, one launch (start us, length us, event | category | flops | bytes accessed | tf_op | source)
XLA Modules:
  0.0 120.0 jit_solution(11935665433246580251)
XLA Ops:
  0.6 3.3 %collective-permute-start.1 = (bf16[256,128]{1,0:T(8,128)(2,1)}, bf16[256,128]{1,0:T(8,128)(2,1)S(1)}, u32[]{:S(2)}, u32[]{:S(2)}) collective-permute-start(bf16[256,128]{1,0:T(8,128)(2,1)} %param.7), channel_id=1, source_target_pairs={{0,8},{8,0},{16,24},{24,16},{32,40},{40,32},{48,56},{56,48},{64,72... | collective-permute-start | bytes 196616 | tf_op jit(solution)/shard_map/ppermute | solution.py:25
  4.0 0.8 constant_dynamic-update-slice_fusion.1
  5.5 0.6 pad_add_fusion.1.ids
  6.1 2.3 %pack_up.1.a = bf16[784,128]{1,0:T(8,128)(2,1)} custom-call(s32[2]{0:T(128)} %pad_add_fusion.1.ids, bf16[128,1024]{1,0:T(8,128)(2,1)} %w_own.1, bf16[256,128]{1,0:T(8,128)(2,1)} %og.1, bf16[1,128]{1,0:T(2,128)(2,1)} %bitcast.31), custom_call_target="tpu_custom_call" | custom-call | bytes 524288 | tf_op jit(solution)/shard_map/pack_up/pallas_call | solution.py:70
  8.4 1.1 collective-permute-start.10
  9.5 3.0 %collective-permute-start.6 = (bf16[512,128]{1,0:T(8,128)(2,1)S(1)}, bf16[512,128]{1,0:T(8,128)(2,1)S(1)}, u32[]{:S(2)}, u32[]{:S(2)}) collective-permute-start(bf16[512,128]{1,0:T(8,128)(2,1)S(1)} %constant_dynamic-update-slice_fusion.a), channel_id=1, source_target_pairs={{0,96},{8,40},{16,112},{24,56},{32,0},{40,72},{48,16},{56,88},{64,... | collective-permute-start | bytes 393224 | tf_op jit(solution)/shard_map/ppermute | solution.py:41
  12.5 4.7 %collective-permute-start.4 = (bf16[512,128]{1,0:T(8,128)(2,1)S(1)}, bf16[512,128]{1,0:T(8,128)(2,1)S(1)}, u32[]{:S(2)}, u32[]{:S(2)}) collective-permute-start(bf16[512,128]{1,0:T(8,128)(2,1)S(1)} %constant_dynamic-update-slice_fusion.a), channel_id=1, source_target_pairs={{0,80},{8,56},{16,96},{24,72},{32,112},{40,88},{48,0},{56,104},{64... | collective-permute-start | bytes 393224 | tf_op jit(solution)/shard_map/ppermute | solution.py:41
  17.2 0.7 pad_add_fusion.mine
  17.9 1.1 collective-permute-done.theirs.refs_0_
  19.3 1.2 collective-permute-start.8
  20.5 3.3 %collective-permute-done.4.b = bf16[512,128]{1,0:T(8,128)(2,1)S(1)} collective-permute-done((bf16[512,128]{1,0:T(8,128)(2,1)S(1)}, bf16[512,128]{1,0:T(8,128)(2,1)S(1)}, u32[]{:S(2)}, u32[]{:S(2)}) %collective-permute-start.4) | collective-permute-done | bytes 131104 | tf_op jit(solution)/shard_map/ppermute | solution.py:41
  23.8 0.9 copy-done.2
  24.8 2.8 %collective-permute-start.12 = (bf16[1568,128]{1,0:T(8,128)(2,1)S(1)}, bf16[1568,128]{1,0:T(8,128)(2,1)S(1)}, u32[]{:S(2)}, u32[]{:S(2)}) collective-permute-start(bf16[1568,128]{1,0:T(8,128)(2,1)S(1)} %append.4.refs_0_), channel_id=1, source_target_pairs={{0,3},{1,0},{2,1},{3,2},{4,7},{5,4},{6,5},{7,6},{8,11},{9,8},{10,9... | collective-permute-start | bytes 1204232 | tf_op jit(solution)/shard_map/ppermute | solution.py:29
  28.1 0.7 copy-done.3
  28.8 2.8 %plan_tiles.1.r2.refs_0_.plan = s32[160]{0:T(256)S(1)} custom-call(s32[2]{0:T(128)S(1)} %copy-done.3, s32[2,64]{1,0:T(2,128)S(1)} %pad_add_fusion.mine, s32[2,64]{1,0:T(2,128)S(1)} %collective-permute-done.theirs.refs_0_), custom_call_target="tpu_custom_call" | custom-call | flops 10000 | bytes 4096 | tf_op jit(solution)/shard_map/plan_tiles/pallas_call | solution.py:177
  31.9 1.4 %collective-permute-done.5.v = bf16[768,128]{1,0:T(8,128)(2,1)S(1)} collective-permute-done((bf16[768,128]{1,0:T(8,128)(2,1)S(1)}, bf16[768,128]{1,0:T(8,128)(2,1)S(1)}, u32[]{:S(2)}, u32[]{:S(2)}) %collective-permute-start.5) | collective-permute-done | bytes 196640 | tf_op jit(solution)/shard_map/ppermute | solution.py:41
  34.1 3.1 %collective-permute-done.11.u.refs_1_ = bf16[1568,128]{1,0:T(8,128)(2,1)S(1)} collective-permute-done((bf16[1568,128]{1,0:T(8,128)(2,1)S(1)}, bf16[1568,128]{1,0:T(8,128)(2,1)S(1)}, u32[]{:S(2)}, u32[]{:S(2)}) %collective-permute-start.11) | collective-permute-done | bytes 401440 | tf_op jit(solution)/shard_map/ppermute | solution.py:29
  37.3 2.7 %collective-permute-start.15 = (bf16[784,128]{1,0:T(8,128)(2,1)S(1)}, bf16[784,128]{1,0:T(8,128)(2,1)S(1)}, u32[]{:S(2)}, u32[]{:S(2)}) collective-permute-start(bf16[784,128]{1,0:T(8,128)(2,1)S(1)} %get-tuple-element.28.refs_9_), channel_id=1, source_target_pairs={{0,3},{1,0},{2,1},{3,2},{4,7},{5,4},{6,5},{7,6},{8,11},{9,8},{10,9... | collective-permute-start | bytes 602120 | tf_op jit(solution)/shard_map/ppermute | solution.py:29
  40.0 6.0 %aggregate.1 = (f32[2,128,128]{2,1,0:T(8,128)S(1)}, f32[2,128,128]{2,1,0:T(8,128)S(1)}) custom-call(s32[160]{0:T(256)S(1)} %plan_tiles.1.r2.refs_0_.plan, bf16[64,128,128]{2,1,0:T(8,128)(2,1)S(1)} %copy-done, bf16[64,128,128]{2,1,0:T(8,128)(2,1)} %collective-permute-done.2.more, bf16[4,128,128]{2,1,0:T(8,128)(2,1)S(1)} %bitcast.16, ...), custom_call_target="tpu_custom_call" | custom-call | flops 268435456 | bytes 4194304 | tf_op jit(solution)/shard_map/aggregate/pallas_call | solution.py:230
  46.1 4.3 %collective-permute-start.13 = (f32[2,128,128]{2,1,0:T(8,128)S(1)}, f32[2,128,128]{2,1,0:T(8,128)S(1)}, u32[]{:S(2)}, u32[]{:S(2)}) collective-permute-start(f32[2,128,128]{2,1,0:T(8,128)S(1)} %get-tuple-element.30), channel_id=1, source_target_pairs={{0,8},{8,0},{16,24},{24,16},{32,40},{40,32},{48,56},{56,48},{64,72... | collective-permute-start | bytes 393224 | tf_op jit(solution)/shard_map/ppermute | solution.py:25
  50.4 1.0 collective-permute-done.13.came
  51.9 4.4 %collective-permute-done.16 = bf16[256,128]{1,0:T(8,128)(2,1)S(1)} collective-permute-done((bf16[256,128]{1,0:T(8,128)(2,1)S(1)}, bf16[256,128]{1,0:T(8,128)(2,1)S(1)}, u32[]{:S(2)}, u32[]{:S(2)}) %collective-permute-start.16) | collective-permute-done | bytes 65568 | tf_op jit(solution)/shard_map/ppermute | solution.py:29
  56.3 1.4 %lay_out.1 = (bf16[1024,512]{1,0:T(8,128)(2,1)S(1)}, bf16[256,1024]{1,0:T(8,128)(2,1)S(1)}, f32[8,1024]{1,0:T(8,128)S(1)}) custom-call(s32[2]{0:T(128)S(1)} %copy-done.4, bf16[1568,128]{1,0:T(8,128)(2,1)S(1)} %append.4.refs_0_, bf16[1568,128]{1,0:T(8,128)(2,1)S(1)} %collective-permute-done.11.u.refs_1_, ...), custom_call_target="tpu_custom_call" | custom-call | bytes 3145728 | tf_op jit(solution)/shard_map/lay_out/pallas_call | solution.py:273
  57.7 1.6 %collective-permute-start.20 = (bf16[1024,512]{1,0:T(8,128)(2,1)S(1)}, bf16[1024,512]{1,0:T(8,128)(2,1)S(1)}, u32[]{:S(2)}, u32[]{:S(2)}) collective-permute-start(bf16[1024,512]{1,0:T(8,128)(2,1)S(1)} %get-tuple-element.31.w0), channel_id=1, source_target_pairs={{0,8},{8,0},{16,24},{24,16},{32,40},{40,32},{48,56},{56,48},{64,72... | collective-permute-start | bytes 3145736 | tf_op jit(solution)/shard_map/ppermute | solution.py:25
  59.3 1.0 collective-permute-start.18
  60.8 5.1 %collective-permute-done.19.p3 = bf16[512,128]{1,0:T(8,128)(2,1)S(1)} collective-permute-done((bf16[512,128]{1,0:T(8,128)(2,1)S(1)}, bf16[512,128]{1,0:T(8,128)(2,1)S(1)}, u32[]{:S(2)}, u32[]{:S(2)}) %collective-permute-start.19) | collective-permute-done | bytes 131104 | tf_op jit(solution)/shard_map/ppermute | solution.py:29
  65.9 0.9 collective-permute-done.18.p2
  66.8 2.2 %collective-permute-done.17.p1 = bf16[512,128]{1,0:T(8,128)(2,1)S(1)} collective-permute-done((bf16[512,128]{1,0:T(8,128)(2,1)S(1)}, bf16[512,128]{1,0:T(8,128)(2,1)S(1)}, u32[]{:S(2)}, u32[]{:S(2)}) %collective-permute-start.17) | collective-permute-done | bytes 131104 | tf_op jit(solution)/shard_map/ppermute | solution.py:29
  69.1 2.1 %middle.1 = (f32[256,128]{1,0:T(8,128)}, bf16[256,128]{1,0:T(8,128)(2,1)S(1)}, f32[64,1152]{1,0:T(8,128)S(1)}, f32[64,1152]{1,0:T(8,128)S(1)}) custom-call(s32[2]{0:T(128)S(1)} %copy-done.4, bf16[512,128]{1,0:T(8,128)(2,1)S(1)} %pad_maximum_fusion.2.refs_5_.p0, bf16[512,128]{1,0:T(8,128)(2,1)S(1)} %collective-permute-done.17.p1, ...), custom_call_target="tpu_custom_call" | custom-call | flops 671088640 | bytes 5242880 | tf_op jit(solution)/shard_map/middle/pallas_call | solution.py:319
  71.7 1.2 collective-permute-done.22.got
  73.3 5.6 %spread.1 = (f32[16,128,128]{2,1,0:T(8,128)S(1)}, bf16[16,128,128]{2,1,0:T(8,128)(2,1)S(1)}) custom-call(s32[160]{0:T(256)S(1)} %plan_tiles.1.r2.refs_0_.plan, bf16[64,128,128]{2,1,0:T(8,128)(2,1)S(1)} %copy-done, bf16[64,128,128]{2,1,0:T(8,128)(2,1)} %collective-permute-done.2.more, bf16[2,128,128]{2,1,0:T(8,128)(2,1)S(1)} %bitcast.27, ...), custom_call_target="tpu_custom_call" | custom-call | flops 268435456 | bytes 6291456 | tf_op jit(solution)/shard_map/spread/pallas_call | solution.py:360
  78.9 1.2 collective-permute-start.25
  80.1 1.2 collective-permute-start.23
  81.4 4.1 %collective-permute-start.30 = (bf16[64,1152]{1,0:T(8,128)(2,1)S(1)}, bf16[64,1152]{1,0:T(8,128)(2,1)S(1)}, u32[]{:S(2)}, u32[]{:S(2)}) collective-permute-start(bf16[64,1152]{1,0:T(8,128)(2,1)S(1)} %pad_maximum_fusion.ready.a), channel_id=1, source_target_pairs={{0,80},{8,56},{16,96},{24,72},{32,112},{40,88},{48,0},{56,104},{64... | collective-permute-start | bytes 442376 | tf_op jit(solution)/shard_map/ppermute | solution.py:41
  85.4 4.6 %collective-permute-done.31.refs_0_.d2 = bf16[64,1152]{1,0:T(8,128)(2,1)S(1)} collective-permute-done((bf16[64,1152]{1,0:T(8,128)(2,1)S(1)}, bf16[64,1152]{1,0:T(8,128)(2,1)S(1)}, u32[]{:S(2)}, u32[]{:S(2)}) %collective-permute-start.31) | collective-permute-done | bytes 147488 | tf_op jit(solution)/shard_map/ppermute | solution.py:41
  90.1 3.0 %collective-permute-start.32 = (bf16[96,1152]{1,0:T(8,128)(2,1)S(1)}, bf16[96,1152]{1,0:T(8,128)(2,1)S(1)}, u32[]{:S(2)}, u32[]{:S(2)}) collective-permute-start(bf16[96,1152]{1,0:T(8,128)(2,1)S(1)} %append.5), channel_id=1, source_target_pairs={{0,112},{8,24},{16,0},{24,40},{32,16},{40,56},{48,32},{56,72},{64,... | collective-permute-start | bytes 663560 | tf_op jit(solution)/shard_map/ppermute | solution.py:41
  93.7 3.9 %collective-permute-start.27 = (bf16[4,128,128]{2,1,0:T(8,128)(2,1)S(1)}, bf16[4,128,128]{2,1,0:T(8,128)(2,1)S(1)}, u32[]{:S(2)}, u32[]{:S(2)}) collective-permute-start(bf16[4,128,128]{2,1,0:T(8,128)(2,1)S(1)} %get-tuple-element.42), channel_id=1, source_target_pairs={{0,32},{8,104},{16,48},{24,120},{32,64},{40,8},{48,80},{56,24},{64... | collective-permute-start | bytes 393224 | tf_op jit(solution)/shard_map/ppermute | solution.py:41
  97.6 2.0 %collective-permute-done.32.d1 = bf16[96,1152]{1,0:T(8,128)(2,1)S(1)} collective-permute-done((bf16[96,1152]{1,0:T(8,128)(2,1)S(1)}, bf16[96,1152]{1,0:T(8,128)(2,1)S(1)}, u32[]{:S(2)}, u32[]{:S(2)}) %collective-permute-start.32) | collective-permute-done | bytes 221216 | tf_op jit(solution)/shard_map/ppermute | solution.py:41
  99.6 2.5 %collective-permute-done.27.t = bf16[4,128,128]{2,1,0:T(8,128)(2,1)S(1)} collective-permute-done((bf16[4,128,128]{2,1,0:T(8,128)(2,1)S(1)}, bf16[4,128,128]{2,1,0:T(8,128)(2,1)S(1)}, u32[]{:S(2)}, u32[]{:S(2)}) %collective-permute-start.27) | collective-permute-done | bytes 131104 | tf_op jit(solution)/shard_map/ppermute | solution.py:41
  102.1 2.6 %collective-permute-start.33 = (bf16[96,1152]{1,0:T(8,128)(2,1)S(1)}, bf16[96,1152]{1,0:T(8,128)(2,1)S(1)}, u32[]{:S(2)}, u32[]{:S(2)}) collective-permute-start(bf16[96,1152]{1,0:T(8,128)(2,1)S(1)} %peer_rows.1), channel_id=1, source_target_pairs={{0,8},{8,0},{16,24},{24,16},{32,40},{40,32},{48,56},{56,48},{64,72... | collective-permute-start | bytes 663560 | tf_op jit(solution)/shard_map/ppermute | solution.py:25
  105.0 2.9 %collective-permute-start.28 = (bf16[4,128,128]{2,1,0:T(8,128)(2,1)S(1)}, bf16[4,128,128]{2,1,0:T(8,128)(2,1)S(1)}, u32[]{:S(2)}, u32[]{:S(2)}) collective-permute-start(bf16[4,128,128]{2,1,0:T(8,128)(2,1)S(1)} %ride.1.t), channel_id=1, source_target_pairs={{0,48},{8,88},{16,64},{24,104},{32,80},{40,120},{48,96},{56,8},{64... | collective-permute-start | bytes 393224 | tf_op jit(solution)/shard_map/ppermute | solution.py:41
  107.8 0.7 sum_z.1
  108.5 0.6 collective-permute-start.34
  109.1 3.3 %collective-permute-done.28 = bf16[4,128,128]{2,1,0:T(8,128)(2,1)S(1)} collective-permute-done((bf16[4,128,128]{2,1,0:T(8,128)(2,1)S(1)}, bf16[4,128,128]{2,1,0:T(8,128)(2,1)S(1)}, u32[]{:S(2)}, u32[]{:S(2)}) %collective-permute-start.28) | collective-permute-done | bytes 131104 | tf_op jit(solution)/shard_map/ppermute | solution.py:41
  112.4 4.5 %collective-permute-start.29 = (f32[2,128,128]{2,1,0:T(8,128)S(1)}, f32[2,128,128]{2,1,0:T(8,128)S(1)}, u32[]{:S(2)}, u32[]{:S(2)}) collective-permute-start(f32[2,128,128]{2,1,0:T(8,128)S(1)} %slice.23), channel_id=1, source_target_pairs={{0,8},{8,0},{16,24},{24,16},{32,40},{40,32},{48,56},{56,48},{64,72... | collective-permute-start | bytes 393224 | tf_op jit(solution)/shard_map/ppermute | solution.py:25
  117.0 0.9 collective-permute-done.29
  117.9 0.7 fusion.1
  118.6 1.4 %weight_out.1 = (f32[128,1024]{1,0:T(8,128)}, f32[128]{0:T(128)}) custom-call(s32[2]{0:T(128)S(1)} %copy-done.4, bf16[64,1152]{1,0:T(8,128)(2,1)S(1)} %pad_maximum_fusion.1.mine, bf16[64,1152]{1,0:T(8,128)(2,1)S(1)} %collective-permute-done.35.theirs), custom_call_target="tpu_custom_call" | custom-call | bytes 1048576 | tf_op jit(solution)/shard_map/weight_out/pallas_call | solution.py:487
  (63 shorter events, 6.1 us)
Async XLA Ops:
  0.6 39.4 %copy-start = (bf16[64,128,128]{2,1,0:T(8,128)(2,1)S(1)}, bf16[64,128,128]{2,1,0:T(8,128)(2,1)}, u32[]{:S(2)}) copy-start(bf16[64,128,128]{2,1,0:T(8,128)(2,1)} %tiles.3) | copy-start | bytes 6291460
  0.6 4.4 %collective-permute-start.1 = (bf16[256,128]{1,0:T(8,128)(2,1)}, bf16[256,128]{1,0:T(8,128)(2,1)S(1)}, u32[]{:S(2)}, u32[]{:S(2)}) collective-permute-start(bf16[256,128]{1,0:T(8,128)(2,1)} %param.7), channel_id=1, source_target_pairs={{0,8},{8,0},{16,24},{24,16},{32,40},{40,32},{48,56},{56,48},{64,72... | collective-permute-start | bytes 196616 | tf_op jit(solution)/shard_map/ppermute | solution.py:25
  5.1 34.9 %collective-permute-start.2 = (bf16[64,128,128]{2,1,0:T(8,128)(2,1)}, bf16[64,128,128]{2,1,0:T(8,128)(2,1)}, u32[]{:S(2)}, u32[]{:S(2)}) collective-permute-start(bf16[64,128,128]{2,1,0:T(8,128)(2,1)} %tiles.3), channel_id=1, source_target_pairs={{0,8},{8,0},{16,24},{24,16},{32,40},{40,32},{48,56},{56,48},{64,72... | collective-permute-start | bytes 6291464 | tf_op jit(solution)/shard_map/ppermute | solution.py:25
  8.4 15.3 %collective-permute-start.10 = (bf16[784,128]{1,0:T(8,128)(2,1)}, bf16[784,128]{1,0:T(8,128)(2,1)S(1)}, u32[]{:S(2)}, u32[]{:S(2)}) collective-permute-start(bf16[784,128]{1,0:T(8,128)(2,1)} %pack_up.1.a), channel_id=1, source_target_pairs={{0,4},{1,5},{2,6},{3,7},{4,0},{5,1},{6,2},{7,3},{8,12},{9,13},{10,... | collective-permute-start | bytes 602120 | tf_op jit(solution)/shard_map/ppermute | solution.py:29
  9.5 9.8 %collective-permute-start.6 = (bf16[512,128]{1,0:T(8,128)(2,1)S(1)}, bf16[512,128]{1,0:T(8,128)(2,1)S(1)}, u32[]{:S(2)}, u32[]{:S(2)}) collective-permute-start(bf16[512,128]{1,0:T(8,128)(2,1)S(1)} %constant_dynamic-update-slice_fusion.a), channel_id=1, source_target_pairs={{0,96},{8,40},{16,112},{24,56},{32,0},{40,72},{48,16},{56,88},{64,... | collective-permute-start | bytes 393224 | tf_op jit(solution)/shard_map/ppermute | solution.py:41
  12.5 11.2 %collective-permute-start.4 = (bf16[512,128]{1,0:T(8,128)(2,1)S(1)}, bf16[512,128]{1,0:T(8,128)(2,1)S(1)}, u32[]{:S(2)}, u32[]{:S(2)}) collective-permute-start(bf16[512,128]{1,0:T(8,128)(2,1)S(1)} %constant_dynamic-update-slice_fusion.a), channel_id=1, source_target_pairs={{0,80},{8,56},{16,96},{24,72},{32,112},{40,88},{48,0},{56,104},{64... | collective-permute-start | bytes 393224 | tf_op jit(solution)/shard_map/ppermute | solution.py:41
  17.9 1.1 collective-permute-start
  19.0 4.8 %collective-permute-start.3 = (bf16[256,128]{1,0:T(8,128)(2,1)}, bf16[256,128]{1,0:T(8,128)(2,1)S(1)}, u32[]{:S(2)}, u32[]{:S(2)}) collective-permute-start(bf16[256,128]{1,0:T(8,128)(2,1)} %param.7), channel_id=1, source_target_pairs={{0,128},{8,136},{16,144},{24,152},{32,160},{40,168},{48,176},{56,1... | collective-permute-start | bytes 196616 | tf_op jit(solution)/shard_map/ppermute | solution.py:25
  19.3 8.5 %collective-permute-start.8 = (bf16[512,128]{1,0:T(8,128)(2,1)S(1)}, bf16[512,128]{1,0:T(8,128)(2,1)S(1)}, u32[]{:S(2)}, u32[]{:S(2)}) collective-permute-start(bf16[512,128]{1,0:T(8,128)(2,1)S(1)} %collective-permute-done.6.refs_1_), channel_id=1, source_target_pairs={{0,128},{8,136},{16,144},{24,152},{32,160},{40,168},{48,176},{56,1... | collective-permute-start | bytes 393224 | tf_op jit(solution)/shard_map/ppermute | solution.py:25
  23.8 0.9 copy-start.2
  24.8 9.3 %collective-permute-start.12 = (bf16[1568,128]{1,0:T(8,128)(2,1)S(1)}, bf16[1568,128]{1,0:T(8,128)(2,1)S(1)}, u32[]{:S(2)}, u32[]{:S(2)}) collective-permute-start(bf16[1568,128]{1,0:T(8,128)(2,1)S(1)} %append.4.refs_0_), channel_id=1, source_target_pairs={{0,3},{1,0},{2,1},{3,2},{4,7},{5,4},{6,5},{7,6},{8,11},{9,8},{10,9... | collective-permute-start | bytes 1204232 | tf_op jit(solution)/shard_map/ppermute | solution.py:29
  27.6 9.6 %collective-permute-start.11 = (bf16[1568,128]{1,0:T(8,128)(2,1)S(1)}, bf16[1568,128]{1,0:T(8,128)(2,1)S(1)}, u32[]{:S(2)}, u32[]{:S(2)}) collective-permute-start(bf16[1568,128]{1,0:T(8,128)(2,1)S(1)} %append.4.refs_0_), channel_id=1, source_target_pairs={{0,1},{1,2},{2,3},{3,0},{4,5},{5,6},{6,7},{7,4},{8,9},{9,10},{10,1... | collective-permute-start | bytes 1204232 | tf_op jit(solution)/shard_map/ppermute | solution.py:29
  27.6 5.7 %collective-permute-start.5 = (bf16[768,128]{1,0:T(8,128)(2,1)S(1)}, bf16[768,128]{1,0:T(8,128)(2,1)S(1)}, u32[]{:S(2)}, u32[]{:S(2)}) collective-permute-start(bf16[768,128]{1,0:T(8,128)(2,1)S(1)} %append.3.refs_0_), channel_id=1, source_target_pairs={{0,112},{8,24},{16,0},{24,40},{32,16},{40,56},{48,32},{56,72},{64,... | collective-permute-start | bytes 589832 | tf_op jit(solution)/shard_map/ppermute | solution.py:41
  27.8 4.1 %collective-permute-start.7 = (bf16[512,128]{1,0:T(8,128)(2,1)S(1)}, bf16[512,128]{1,0:T(8,128)(2,1)S(1)}, u32[]{:S(2)}, u32[]{:S(2)}) collective-permute-start(bf16[512,128]{1,0:T(8,128)(2,1)S(1)} %collective-permute-done.4.b), channel_id=1, source_target_pairs={{0,128},{8,136},{16,144},{24,152},{32,160},{40,168},{48,176},{56,1... | collective-permute-start | bytes 393224 | tf_op jit(solution)/shard_map/ppermute | solution.py:25
  28.1 0.7 copy-start.3
  33.3 6.7 %collective-permute-start.9 = (bf16[768,128]{1,0:T(8,128)(2,1)S(1)}, bf16[768,128]{1,0:T(8,128)(2,1)S(1)}, u32[]{:S(2)}, u32[]{:S(2)}) collective-permute-start(bf16[768,128]{1,0:T(8,128)(2,1)S(1)} %hold.1), channel_id=1, source_target_pairs={{0,128},{8,136},{16,144},{24,152},{32,160},{40,168},{48,176},{56,1... | collective-permute-start | bytes 589832 | tf_op jit(solution)/shard_map/ppermute | solution.py:25
  37.2 13.1 %collective-permute-start.14 = (bf16[784,128]{1,0:T(8,128)(2,1)S(1)}, bf16[784,128]{1,0:T(8,128)(2,1)S(1)}, u32[]{:S(2)}, u32[]{:S(2)}) collective-permute-start(bf16[784,128]{1,0:T(8,128)(2,1)S(1)} %get-tuple-element.27.refs_8_), channel_id=1, source_target_pairs={{0,1},{1,2},{2,3},{3,0},{4,5},{5,6},{6,7},{7,4},{8,9},{9,10},{10,1... | collective-permute-start | bytes 602120 | tf_op jit(solution)/shard_map/ppermute | solution.py:29
  37.3 13.0 %collective-permute-start.15 = (bf16[784,128]{1,0:T(8,128)(2,1)S(1)}, bf16[784,128]{1,0:T(8,128)(2,1)S(1)}, u32[]{:S(2)}, u32[]{:S(2)}) collective-permute-start(bf16[784,128]{1,0:T(8,128)(2,1)S(1)} %get-tuple-element.28.refs_9_), channel_id=1, source_target_pairs={{0,3},{1,0},{2,1},{3,2},{4,7},{5,4},{6,5},{7,6},{8,11},{9,8},{10,9... | collective-permute-start | bytes 602120 | tf_op jit(solution)/shard_map/ppermute | solution.py:29
  40.0 16.3 %copy-start.4 = (s32[2]{0:T(128)S(1)}, s32[2]{0:T(128)}, u32[]{:S(2)}) copy-start(s32[2]{0:T(128)} %pad_add_fusion.1.ids) | copy-start | bytes 28
  46.1 23.0 %copy-start.1 = (bf16[128,1024]{1,0:T(8,128)(2,1)S(1)}, bf16[128,1024]{1,0:T(8,128)(2,1)}, u32[]{:S(2)}) copy-start(bf16[128,1024]{1,0:T(8,128)(2,1)} %w_own.1) | copy-start | bytes 786436
  46.1 5.3 %collective-permute-start.13 = (f32[2,128,128]{2,1,0:T(8,128)S(1)}, f32[2,128,128]{2,1,0:T(8,128)S(1)}, u32[]{:S(2)}, u32[]{:S(2)}) collective-permute-start(f32[2,128,128]{2,1,0:T(8,128)S(1)} %get-tuple-element.30), channel_id=1, source_target_pairs={{0,8},{8,0},{16,24},{24,16},{32,40},{40,32},{48,56},{56,48},{64,72... | collective-permute-start | bytes 393224 | tf_op jit(solution)/shard_map/ppermute | solution.py:25
  51.4 4.9 %collective-permute-start.16 = (bf16[256,128]{1,0:T(8,128)(2,1)S(1)}, bf16[256,128]{1,0:T(8,128)(2,1)S(1)}, u32[]{:S(2)}, u32[]{:S(2)}) collective-permute-start(bf16[256,128]{1,0:T(8,128)(2,1)S(1)} %bitcast.23), channel_id=1, source_target_pairs={{0,4},{1,5},{2,6},{3,7},{4,0},{5,1},{6,2},{7,3},{8,12},{9,13},{10,... | collective-permute-start | bytes 196616 | tf_op jit(solution)/shard_map/ppermute | solution.py:29
  57.7 11.4 %collective-permute-start.20 = (bf16[1024,512]{1,0:T(8,128)(2,1)S(1)}, bf16[1024,512]{1,0:T(8,128)(2,1)S(1)}, u32[]{:S(2)}, u32[]{:S(2)}) collective-permute-start(bf16[1024,512]{1,0:T(8,128)(2,1)S(1)} %get-tuple-element.31.w0), channel_id=1, source_target_pairs={{0,8},{8,0},{16,24},{24,16},{32,40},{40,32},{48,56},{56,48},{64,72... | collective-permute-start | bytes 3145736 | tf_op jit(solution)/shard_map/ppermute | solution.py:25
  59.3 6.6 %collective-permute-start.19 = (bf16[512,128]{1,0:T(8,128)(2,1)S(1)}, bf16[512,128]{1,0:T(8,128)(2,1)S(1)}, u32[]{:S(2)}, u32[]{:S(2)}) collective-permute-start(bf16[512,128]{1,0:T(8,128)(2,1)S(1)} %pad_maximum_fusion.2.refs_5_.p0), channel_id=1, source_target_pairs={{0,2},{1,3},{2,0},{3,1},{4,6},{5,7},{6,4},{7,5},{8,10},{9,11},{10,... | collective-permute-start | bytes 393224 | tf_op jit(solution)/shard_map/ppermute | solution.py:29
  59.3 7.5 %collective-permute-start.18 = (bf16[512,128]{1,0:T(8,128)(2,1)S(1)}, bf16[512,128]{1,0:T(8,128)(2,1)S(1)}, u32[]{:S(2)}, u32[]{:S(2)}) collective-permute-start(bf16[512,128]{1,0:T(8,128)(2,1)S(1)} %pad_maximum_fusion.2.refs_5_.p0), channel_id=1, source_target_pairs={{0,3},{1,0},{2,1},{3,2},{4,7},{5,4},{6,5},{7,6},{8,11},{9,8},{10,9... | collective-permute-start | bytes 393224 | tf_op jit(solution)/shard_map/ppermute | solution.py:29
  60.3 8.7 %collective-permute-start.17 = (bf16[512,128]{1,0:T(8,128)(2,1)S(1)}, bf16[512,128]{1,0:T(8,128)(2,1)S(1)}, u32[]{:S(2)}, u32[]{:S(2)}) collective-permute-start(bf16[512,128]{1,0:T(8,128)(2,1)S(1)} %pad_maximum_fusion.2.refs_5_.p0), channel_id=1, source_target_pairs={{0,1},{1,2},{2,3},{3,0},{4,5},{5,6},{6,7},{7,4},{8,9},{9,10},{10,1... | collective-permute-start | bytes 393224 | tf_op jit(solution)/shard_map/ppermute | solution.py:29
  71.2 1.7 %collective-permute-start.22 = (f32[64,1152]{1,0:T(8,128)S(1)}, f32[64,1152]{1,0:T(8,128)S(1)}, u32[]{:S(2)}, u32[]{:S(2)}) collective-permute-start(f32[64,1152]{1,0:T(8,128)S(1)} %get-tuple-element.37), channel_id=1, source_target_pairs={{0,8},{8,0},{16,24},{24,16},{32,40},{40,32},{48,56},{56,48},{64,72... | collective-permute-start | bytes 884744 | tf_op jit(solution)/shard_map/ppermute | solution.py:25
  71.7 1.6 %collective-permute-start.21 = (bf16[2,128,128]{2,1,0:T(8,128)(2,1)S(1)}, bf16[2,128,128]{2,1,0:T(8,128)(2,1)S(1)}, u32[]{:S(2)}, u32[]{:S(2)}) collective-permute-start(bf16[2,128,128]{2,1,0:T(8,128)(2,1)S(1)} %bitcast.26), channel_id=1, source_target_pairs={{0,8},{8,0},{16,24},{24,16},{32,40},{40,32},{48,56},{56,48},{64,72... | collective-permute-start | bytes 196616 | tf_op jit(solution)/shard_map/ppermute | solution.py:25
  72.9 6.0 %collective-permute-start.24 = (bf16[32,1152]{1,0:T(8,128)(2,1)S(1)}, bf16[32,1152]{1,0:T(8,128)(2,1)S(1)}, u32[]{:S(2)}, u32[]{:S(2)}) collective-permute-start(bf16[32,1152]{1,0:T(8,128)(2,1)S(1)} %fusion.send), channel_id=1, source_target_pairs={{0,128},{8,136},{16,144},{24,152},{32,160},{40,168},{48,176},{56,1... | collective-permute-start | bytes 221192 | tf_op jit(solution)/shard_map/ppermute | solution.py:25
  78.9 2.3 %collective-permute-start.25 = (bf16[32,1152]{1,0:T(8,128)(2,1)S(1)}, bf16[32,1152]{1,0:T(8,128)(2,1)S(1)}, u32[]{:S(2)}, u32[]{:S(2)}) collective-permute-start(bf16[32,1152]{1,0:T(8,128)(2,1)S(1)} %quarter_up.1.own), channel_id=1, source_target_pairs={{0,8},{8,0},{16,24},{24,16},{32,40},{40,32},{48,56},{56,48},{64,72... | collective-permute-start | bytes 221192 | tf_op jit(solution)/shard_map/ppermute | solution.py:25
  80.1 13.5 %collective-permute-start.23 = (bf16[16,128,128]{2,1,0:T(8,128)(2,1)S(1)}, bf16[16,128,128]{2,1,0:T(8,128)(2,1)S(1)}, u32[]{:S(2)}, u32[]{:S(2)}) collective-permute-start(bf16[16,128,128]{2,1,0:T(8,128)(2,1)S(1)} %get-tuple-element.39.far), channel_id=1, source_target_pairs={{0,128},{8,136},{16,144},{24,152},{32,160},{40,168},{48,176},{56,1... | collective-permute-start | bytes 1572872 | tf_op jit(solution)/shard_map/ppermute | solution.py:25
  81.3 8.8 %collective-permute-start.31 = (bf16[64,1152]{1,0:T(8,128)(2,1)S(1)}, bf16[64,1152]{1,0:T(8,128)(2,1)S(1)}, u32[]{:S(2)}, u32[]{:S(2)}) collective-permute-start(bf16[64,1152]{1,0:T(8,128)(2,1)S(1)} %pad_maximum_fusion.ready.a), channel_id=1, source_target_pairs={{0,96},{8,40},{16,112},{24,56},{32,0},{40,72},{48,16},{56,88},{64,... | collective-permute-start | bytes 442376 | tf_op jit(solution)/shard_map/ppermute | solution.py:41
  81.4 8.7 %collective-permute-start.30 = (bf16[64,1152]{1,0:T(8,128)(2,1)S(1)}, bf16[64,1152]{1,0:T(8,128)(2,1)S(1)}, u32[]{:S(2)}, u32[]{:S(2)}) collective-permute-start(bf16[64,1152]{1,0:T(8,128)(2,1)S(1)} %pad_maximum_fusion.ready.a), channel_id=1, source_target_pairs={{0,80},{8,56},{16,96},{24,72},{32,112},{40,88},{48,0},{56,104},{64... | collective-permute-start | bytes 442376 | tf_op jit(solution)/shard_map/ppermute | solution.py:41
  90.1 9.5 %collective-permute-start.32 = (bf16[96,1152]{1,0:T(8,128)(2,1)S(1)}, bf16[96,1152]{1,0:T(8,128)(2,1)S(1)}, u32[]{:S(2)}, u32[]{:S(2)}) collective-permute-start(bf16[96,1152]{1,0:T(8,128)(2,1)S(1)} %append.5), channel_id=1, source_target_pairs={{0,112},{8,24},{16,0},{24,40},{32,16},{40,56},{48,32},{56,72},{64,... | collective-permute-start | bytes 663560 | tf_op jit(solution)/shard_map/ppermute | solution.py:41
  93.7 8.4 %collective-permute-start.27 = (bf16[4,128,128]{2,1,0:T(8,128)(2,1)S(1)}, bf16[4,128,128]{2,1,0:T(8,128)(2,1)S(1)}, u32[]{:S(2)}, u32[]{:S(2)}) collective-permute-start(bf16[4,128,128]{2,1,0:T(8,128)(2,1)S(1)} %get-tuple-element.42), channel_id=1, source_target_pairs={{0,32},{8,104},{16,48},{24,120},{32,64},{40,8},{48,80},{56,24},{64... | collective-permute-start | bytes 393224 | tf_op jit(solution)/shard_map/ppermute | solution.py:41
  97.6 7.3 %collective-permute-start.26 = (bf16[6,128,128]{2,1,0:T(8,128)(2,1)S(1)}, bf16[6,128,128]{2,1,0:T(8,128)(2,1)S(1)}, u32[]{:S(2)}, u32[]{:S(2)}) collective-permute-start(bf16[6,128,128]{2,1,0:T(8,128)(2,1)S(1)} %get-tuple-element.41), channel_id=1, source_target_pairs={{0,16},{8,120},{16,32},{24,8},{32,48},{40,24},{48,64},{56,40},{64,... | collective-permute-start | bytes 589832 | tf_op jit(solution)/shard_map/ppermute | solution.py:41
  102.1 5.7 %collective-permute-start.33 = (bf16[96,1152]{1,0:T(8,128)(2,1)S(1)}, bf16[96,1152]{1,0:T(8,128)(2,1)S(1)}, u32[]{:S(2)}, u32[]{:S(2)}) collective-permute-start(bf16[96,1152]{1,0:T(8,128)(2,1)S(1)} %peer_rows.1), channel_id=1, source_target_pairs={{0,8},{8,0},{16,24},{24,16},{32,40},{40,32},{48,56},{56,48},{64,72... | collective-permute-start | bytes 663560 | tf_op jit(solution)/shard_map/ppermute | solution.py:25
  105.0 7.4 %collective-permute-start.28 = (bf16[4,128,128]{2,1,0:T(8,128)(2,1)S(1)}, bf16[4,128,128]{2,1,0:T(8,128)(2,1)S(1)}, u32[]{:S(2)}, u32[]{:S(2)}) collective-permute-start(bf16[4,128,128]{2,1,0:T(8,128)(2,1)S(1)} %ride.1.t), channel_id=1, source_target_pairs={{0,48},{8,88},{16,64},{24,104},{32,80},{40,120},{48,96},{56,8},{64... | collective-permute-start | bytes 393224 | tf_op jit(solution)/shard_map/ppermute | solution.py:41
  108.5 8.4 %collective-permute-start.34 = (bf16[32,1152]{1,0:T(8,128)(2,1)S(1)}, bf16[32,1152]{1,0:T(8,128)(2,1)S(1)}, u32[]{:S(2)}, u32[]{:S(2)}) collective-permute-start(bf16[32,1152]{1,0:T(8,128)(2,1)S(1)} %sum_z.1), channel_id=1, source_target_pairs={{0,128},{8,136},{16,144},{24,152},{32,160},{40,168},{48,176},{56,1... | collective-permute-start | bytes 221192 | tf_op jit(solution)/shard_map/ppermute | solution.py:25
  112.4 5.5 %collective-permute-start.29 = (f32[2,128,128]{2,1,0:T(8,128)S(1)}, f32[2,128,128]{2,1,0:T(8,128)S(1)}, u32[]{:S(2)}, u32[]{:S(2)}) collective-permute-start(f32[2,128,128]{2,1,0:T(8,128)S(1)} %slice.23), channel_id=1, source_target_pairs={{0,8},{8,0},{16,24},{24,16},{32,40},{40,32},{48,56},{56,48},{64,72... | collective-permute-start | bytes 393224 | tf_op jit(solution)/shard_map/ppermute | solution.py:25
  116.9 1.6 %collective-permute-start.35 = (bf16[64,1152]{1,0:T(8,128)(2,1)S(1)}, bf16[64,1152]{1,0:T(8,128)(2,1)S(1)}, u32[]{:S(2)}, u32[]{:S(2)}) collective-permute-start(bf16[64,1152]{1,0:T(8,128)(2,1)S(1)} %pad_maximum_fusion.1.mine), channel_id=1, source_target_pairs={{0,8},{8,0},{16,24},{24,16},{32,40},{40,32},{48,56},{56,48},{64,72... | collective-permute-start | bytes 442376 | tf_op jit(solution)/shard_map/ppermute | solution.py:25

commit v10 on v9

--- a/solution.py
+++ b/solution.py
@@ -412,21 +412,22 @@
     )(near, came, ready)
 
 
-def ride_body(t3, r14, out):
+def ride_body(t3, r14, t2, out, on):
     out[0:2] = (t3[0:2] + r14[4:6].astype(f32)).astype(bf16)
     out[2:4] = t3[2:4].astype(bf16)
-
-
-def ride(t3, r14):
+    on[...] = t2[...]
+
+
+def ride(t3, r14, t2):
     return pl.pallas_call(
         ride_body,
-        out_shape=jax.ShapeDtypeStruct((4, B, B), bf16),
-        in_specs=[VM, VM],
-        out_specs=VM,
+        out_shape=(jax.ShapeDtypeStruct((4, B, B), bf16),) * 2,
+        in_specs=[VM, VM, VM],
+        out_specs=(VM, VM),
         compiler_params=params(4),
         cost_estimate=cost(0, 1 << 18),
         name="ride",
-    )(t3, r14)
+    )(t3, r14, t2)
 
 
 def rows_body(d1, d2, d3, t, out):
@@ -541,11 +542,11 @@
     d1 = spin_send(append(96, halves, d3, d2), 1, -1)
 
     t14, t2, t3, t0 = join(near, came, halves)
-    r14, r2 = spin_send(t14, 1), spin_send(t2, 2)
-    t3 = ride(t3, r14)
-    r3 = spin_send(t3, 3)
-
-    e = row_send(peer_rows(d1, d2, d3, r2), dc=1)
+    r14 = spin_send(t14, 1)
+    t3, t2 = ride(t3, r14, t2)
+    r2, r3 = spin_send(t2, 2), spin_send(t3, 3)
+
+    e = row_send(peer_rows(d1, d2, d3, r14), dc=1)
     scale = float(256 * lax.axis_size("row")) ** (-0.5)
     total = sum_z(scale, ids, quarter, d1, d2, d3, e, t3)
     two = jnp.concatenate([total, row_send(total, dx=1)], axis=0)

time: 120 us -> 119 us (level)
  starting transfers between devices: 53.3 us -> 49 us
  waiting for transfers between devices: 38.6 us -> 41.3 us
    ppermute x18, starting transfers between devices: 22.9 us -> 20.4 us  [row_send(): return lax.ppermute(v, 'row', perm)]
    ppermute x9, waiting for transfers between devices: 17.2 us -> 19.6 us  [spin_send(): return lax.ppermute(v, 'row', perm)]
    ppermute x9, starting transfers between devices: 21.8 us -> 20 us  [spin_send(): return lax.ppermute(v, 'row', perm)]
  transfers between devices with their start and end apart: 36 -> 36, of which waited for: 20 -> 21; matrix products, arithmetic and copies ran while one was open for 2% -> 2% of each run, Pallas kernels for 15% -> 15%
where the time goes in v10:
time: 119 us
  starting transfers between devices  49 us (41%)
  waiting for transfers between devices  41.3 us (35%)
  Pallas kernels  23.1 us (19%)
  local copies, waits for them, and re-layouts  2.46 us (2%)
  other arithmetic  2.04 us (2%)
    ppermute x18, starting transfers between devices, row_send(): return lax.ppermute(v, 'row', perm)  20.4 us
    ppermute x9, starting transfers between devices, spin_send(): return lax.ppermute(v, 'row', perm)  20 us
    ppermute x9, waiting for transfers between devices, spin_send(): return lax.ppermute(v, 'row', perm)  19.6 us
    ppermute x9, waiting for transfers between devices, feat_send(): lax.ppermute(v, 'feat', [(i, (i >> 2 ^ dx) << 2 | i + dy & 3) for i in ra...  16.2 us
    ppermute x9, starting transfers between devices, feat_send(): lax.ppermute(v, 'feat', [(i, (i >> 2 ^ dx) << 2 | i + dy & 3) for i in ra...  8.61 us
    pallas_call x1, Pallas kernels, aggregate(): pl.pallas_call(agg_body, out_shape=(jax.ShapeDtypeStruct((2, B, B), f32),...  6.22 us
    pallas_call x1, Pallas kernels, spread(): pl.pallas_call(spread_body, out_shape=(jax.ShapeDtypeStruct((16, B, B), f...  5.77 us
    ppermute x18, waiting for transfers between devices, row_send(): return lax.ppermute(v, 'row', perm)  5.6 us
  transfers between devices with their start and end apart: 36, of which 21 were waited for; matrix products, arithmetic and copies ran while one was open for 2% of the time, Pallas kernels for 15%

profile of v10, /device:TPU:1, one launch (start us, length us, event | category | flops | bytes accessed | tf_op | source)
XLA Modules:
  0.0 118.8 jit_solution(8893270804380401400)
XLA Ops:
  0.6 3.3 %collective-permute-start.1 = (bf16[256,128]{1,0:T(8,128)(2,1)}, bf16[256,128]{1,0:T(8,128)(2,1)S(1)}, u32[]{:S(2)}, u32[]{:S(2)}) collective-permute-start(bf16[256,128]{1,0:T(8,128)(2,1)} %param.7), channel_id=1, source_target_pairs={{0,8},{8,0},{16,24},{24,16},{32,40},{40,32},{48,56},{56,48},{64,72... | collective-permute-start | bytes 196616 | tf_op jit(solution)/shard_map/ppermute | solution.py:25
  4.0 0.8 constant_dynamic-update-slice_fusion.1
  6.1 2.3 %pack_up.1.a = bf16[784,128]{1,0:T(8,128)(2,1)} custom-call(s32[2]{0:T(128)} %pad_add_fusion.1.ids, bf16[128,1024]{1,0:T(8,128)(2,1)} %w_own.1, bf16[256,128]{1,0:T(8,128)(2,1)} %og.1, bf16[1,128]{1,0:T(2,128)(2,1)} %bitcast.31), custom_call_target="tpu_custom_call" | custom-call | bytes 524288 | tf_op jit(solution)/shard_map/pack_up/pallas_call | solution.py:70
  8.4 1.1 collective-permute-start.10
  9.5 3.0 %collective-permute-start.6 = (bf16[512,128]{1,0:T(8,128)(2,1)S(1)}, bf16[512,128]{1,0:T(8,128)(2,1)S(1)}, u32[]{:S(2)}, u32[]{:S(2)}) collective-permute-start(bf16[512,128]{1,0:T(8,128)(2,1)S(1)} %constant_dynamic-update-slice_fusion.a), channel_id=1, source_target_pairs={{0,96},{8,40},{16,112},{24,56},{32,0},{40,72},{48,16},{56,88},{64,... | collective-permute-start | bytes 393224 | tf_op jit(solution)/shard_map/ppermute | solution.py:41
  12.5 4.7 %collective-permute-start.4 = (bf16[512,128]{1,0:T(8,128)(2,1)S(1)}, bf16[512,128]{1,0:T(8,128)(2,1)S(1)}, u32[]{:S(2)}, u32[]{:S(2)}) collective-permute-start(bf16[512,128]{1,0:T(8,128)(2,1)S(1)} %constant_dynamic-update-slice_fusion.a), channel_id=1, source_target_pairs={{0,80},{8,56},{16,96},{24,72},{32,112},{40,88},{48,0},{56,104},{64... | collective-permute-start | bytes 393224 | tf_op jit(solution)/shard_map/ppermute | solution.py:41
  17.2 0.7 pad_add_fusion.mine
  17.9 1.1 collective-permute-done.theirs.refs_0_
  19.3 1.2 collective-permute-start.8
  20.5 3.3 %collective-permute-done.4.b = bf16[512,128]{1,0:T(8,128)(2,1)S(1)} collective-permute-done((bf16[512,128]{1,0:T(8,128)(2,1)S(1)}, bf16[512,128]{1,0:T(8,128)(2,1)S(1)}, u32[]{:S(2)}, u32[]{:S(2)}) %collective-permute-start.4) | collective-permute-done | bytes 131104 | tf_op jit(solution)/shard_map/ppermute | solution.py:41
  23.8 0.9 copy-done.2
  24.8 2.8 %collective-permute-start.12 = (bf16[1568,128]{1,0:T(8,128)(2,1)S(1)}, bf16[1568,128]{1,0:T(8,128)(2,1)S(1)}, u32[]{:S(2)}, u32[]{:S(2)}) collective-permute-start(bf16[1568,128]{1,0:T(8,128)(2,1)S(1)} %append.4.refs_0_), channel_id=1, source_target_pairs={{0,3},{1,0},{2,1},{3,2},{4,7},{5,4},{6,5},{7,6},{8,11},{9,8},{10,9... | collective-permute-start | bytes 1204232 | tf_op jit(solution)/shard_map/ppermute | solution.py:29
  28.8 2.8 %plan_tiles.1.r2.refs_0_.plan = s32[160]{0:T(256)S(1)} custom-call(s32[2]{0:T(128)S(1)} %copy-done.3, s32[2,64]{1,0:T(2,128)S(1)} %pad_add_fusion.mine, s32[2,64]{1,0:T(2,128)S(1)} %collective-permute-done.theirs.refs_0_), custom_call_target="tpu_custom_call" | custom-call | flops 10000 | bytes 4096 | tf_op jit(solution)/shard_map/plan_tiles/pallas_call | solution.py:177
  31.9 1.4 %collective-permute-done.5.v = bf16[768,128]{1,0:T(8,128)(2,1)S(1)} collective-permute-done((bf16[768,128]{1,0:T(8,128)(2,1)S(1)}, bf16[768,128]{1,0:T(8,128)(2,1)S(1)}, u32[]{:S(2)}, u32[]{:S(2)}) %collective-permute-start.5) | collective-permute-done | bytes 196640 | tf_op jit(solution)/shard_map/ppermute | solution.py:41
  34.1 3.1 %collective-permute-done.11.u.refs_1_ = bf16[1568,128]{1,0:T(8,128)(2,1)S(1)} collective-permute-done((bf16[1568,128]{1,0:T(8,128)(2,1)S(1)}, bf16[1568,128]{1,0:T(8,128)(2,1)S(1)}, u32[]{:S(2)}, u32[]{:S(2)}) %collective-permute-start.11) | collective-permute-done | bytes 401440 | tf_op jit(solution)/shard_map/ppermute | solution.py:29
  37.3 2.7 %collective-permute-start.15 = (bf16[784,128]{1,0:T(8,128)(2,1)S(1)}, bf16[784,128]{1,0:T(8,128)(2,1)S(1)}, u32[]{:S(2)}, u32[]{:S(2)}) collective-permute-start(bf16[784,128]{1,0:T(8,128)(2,1)S(1)} %get-tuple-element.30.refs_9_), channel_id=1, source_target_pairs={{0,3},{1,0},{2,1},{3,2},{4,7},{5,4},{6,5},{7,6},{8,11},{9,8},{10,9... | collective-permute-start | bytes 602120 | tf_op jit(solution)/shard_map/ppermute | solution.py:29
  40.0 6.2 %aggregate.1 = (f32[2,128,128]{2,1,0:T(8,128)S(1)}, f32[2,128,128]{2,1,0:T(8,128)S(1)}) custom-call(s32[160]{0:T(256)S(1)} %plan_tiles.1.r2.refs_0_.plan, bf16[64,128,128]{2,1,0:T(8,128)(2,1)S(1)} %copy-done, bf16[64,128,128]{2,1,0:T(8,128)(2,1)} %collective-permute-done.2.more, bf16[4,128,128]{2,1,0:T(8,128)(2,1)S(1)} %bitcast.16, ...), custom_call_target="tpu_custom_call" | custom-call | flops 268435456 | bytes 4194304 | tf_op jit(solution)/shard_map/aggregate/pallas_call | solution.py:230
  46.2 3.9 %collective-permute-start.13 = (f32[2,128,128]{2,1,0:T(8,128)S(1)}, f32[2,128,128]{2,1,0:T(8,128)S(1)}, u32[]{:S(2)}, u32[]{:S(2)}) collective-permute-start(f32[2,128,128]{2,1,0:T(8,128)S(1)} %get-tuple-element.32), channel_id=1, source_target_pairs={{0,8},{8,0},{16,24},{24,16},{32,40},{40,32},{48,56},{56,48},{64,72... | collective-permute-start | bytes 393224 | tf_op jit(solution)/shard_map/ppermute | solution.py:25
  50.2 1.0 collective-permute-done.13.came
  51.7 4.4 %collective-permute-done.16 = bf16[256,128]{1,0:T(8,128)(2,1)S(1)} collective-permute-done((bf16[256,128]{1,0:T(8,128)(2,1)S(1)}, bf16[256,128]{1,0:T(8,128)(2,1)S(1)}, u32[]{:S(2)}, u32[]{:S(2)}) %collective-permute-start.16) | collective-permute-done | bytes 65568 | tf_op jit(solution)/shard_map/ppermute | solution.py:29
  56.1 1.4 %lay_out.1 = (bf16[1024,512]{1,0:T(8,128)(2,1)S(1)}, bf16[256,1024]{1,0:T(8,128)(2,1)S(1)}, f32[8,1024]{1,0:T(8,128)S(1)}) custom-call(s32[2]{0:T(128)S(1)} %copy-done.4, bf16[1568,128]{1,0:T(8,128)(2,1)S(1)} %append.4.refs_0_, bf16[1568,128]{1,0:T(8,128)(2,1)S(1)} %collective-permute-done.11.u.refs_1_, ...), custom_call_target="tpu_custom_call" | custom-call | bytes 3145728 | tf_op jit(solution)/shard_map/lay_out/pallas_call | solution.py:273
  57.5 1.6 %collective-permute-start.20 = (bf16[1024,512]{1,0:T(8,128)(2,1)S(1)}, bf16[1024,512]{1,0:T(8,128)(2,1)S(1)}, u32[]{:S(2)}, u32[]{:S(2)}) collective-permute-start(bf16[1024,512]{1,0:T(8,128)(2,1)S(1)} %get-tuple-element.33.w0), channel_id=1, source_target_pairs={{0,8},{8,0},{16,24},{24,16},{32,40},{40,32},{48,56},{56,48},{64,72... | collective-permute-start | bytes 3145736 | tf_op jit(solution)/shard_map/ppermute | solution.py:25
  59.1 1.0 collective-permute-start.18
  60.6 5.1 %collective-permute-done.19.p3 = bf16[512,128]{1,0:T(8,128)(2,1)S(1)} collective-permute-done((bf16[512,128]{1,0:T(8,128)(2,1)S(1)}, bf16[512,128]{1,0:T(8,128)(2,1)S(1)}, u32[]{:S(2)}, u32[]{:S(2)}) %collective-permute-start.19) | collective-permute-done | bytes 131104 | tf_op jit(solution)/shard_map/ppermute | solution.py:29
  65.7 0.9 collective-permute-done.18.p2
  66.7 2.2 %collective-permute-done.17.p1 = bf16[512,128]{1,0:T(8,128)(2,1)S(1)} collective-permute-done((bf16[512,128]{1,0:T(8,128)(2,1)S(1)}, bf16[512,128]{1,0:T(8,128)(2,1)S(1)}, u32[]{:S(2)}, u32[]{:S(2)}) %collective-permute-start.17) | collective-permute-done | bytes 131104 | tf_op jit(solution)/shard_map/ppermute | solution.py:29
  68.9 2.1 %middle.1 = (f32[256,128]{1,0:T(8,128)}, bf16[256,128]{1,0:T(8,128)(2,1)S(1)}, f32[64,1152]{1,0:T(8,128)S(1)}, f32[64,1152]{1,0:T(8,128)S(1)}) custom-call(s32[2]{0:T(128)S(1)} %copy-done.4, bf16[512,128]{1,0:T(8,128)(2,1)S(1)} %pad_maximum_fusion.2.refs_5_.p0, bf16[512,128]{1,0:T(8,128)(2,1)S(1)} %collective-permute-done.17.p1, ...), custom_call_target="tpu_custom_call" | custom-call | flops 671088640 | bytes 5242880 | tf_op jit(solution)/shard_map/middle/pallas_call | solution.py:319
  71.5 1.2 collective-permute-done.22.got
  73.3 5.8 %spread.1 = (f32[16,128,128]{2,1,0:T(8,128)S(1)}, bf16[16,128,128]{2,1,0:T(8,128)(2,1)S(1)}) custom-call(s32[160]{0:T(256)S(1)} %plan_tiles.1.r2.refs_0_.plan, bf16[64,128,128]{2,1,0:T(8,128)(2,1)S(1)} %copy-done, bf16[64,128,128]{2,1,0:T(8,128)(2,1)} %collective-permute-done.2.more, bf16[2,128,128]{2,1,0:T(8,128)(2,1)S(1)} %bitcast.27, ...), custom_call_target="tpu_custom_call" | custom-call | flops 268435456 | bytes 6291456 | tf_op jit(solution)/shard_map/spread/pallas_call | solution.py:360
  79.1 0.8 collective-permute-start.23
  80.0 1.5 %collective-permute-start.25 = (bf16[32,1152]{1,0:T(8,128)(2,1)S(1)}, bf16[32,1152]{1,0:T(8,128)(2,1)S(1)}, u32[]{:S(2)}, u32[]{:S(2)}) collective-permute-start(bf16[32,1152]{1,0:T(8,128)(2,1)S(1)} %quarter_up.1.own), channel_id=1, source_target_pairs={{0,8},{8,0},{16,24},{24,16},{32,40},{40,32},{48,56},{56,48},{64,72... | collective-permute-start | bytes 221192 | tf_op jit(solution)/shard_map/ppermute | solution.py:25
  81.4 0.9 collective-permute-done.25
  82.7 3.0 %collective-permute-start.30 = (bf16[64,1152]{1,0:T(8,128)(2,1)S(1)}, bf16[64,1152]{1,0:T(8,128)(2,1)S(1)}, u32[]{:S(2)}, u32[]{:S(2)}) collective-permute-start(bf16[64,1152]{1,0:T(8,128)(2,1)S(1)} %pad_maximum_fusion.ready.a), channel_id=1, source_target_pairs={{0,80},{8,56},{16,96},{24,72},{32,112},{40,88},{48,0},{56,104},{64... | collective-permute-start | bytes 442376 | tf_op jit(solution)/shard_map/ppermute | solution.py:41
  85.7 4.5 %collective-permute-done.31.refs_0_.d2 = bf16[64,1152]{1,0:T(8,128)(2,1)S(1)} collective-permute-done((bf16[64,1152]{1,0:T(8,128)(2,1)S(1)}, bf16[64,1152]{1,0:T(8,128)(2,1)S(1)}, u32[]{:S(2)}, u32[]{:S(2)}) %collective-permute-start.31) | collective-permute-done | bytes 147488 | tf_op jit(solution)/shard_map/ppermute | solution.py:41
  90.2 0.8 collective-permute-done.30.b.d3
  91.0 2.5 %collective-permute-start.32 = (bf16[96,1152]{1,0:T(8,128)(2,1)S(1)}, bf16[96,1152]{1,0:T(8,128)(2,1)S(1)}, u32[]{:S(2)}, u32[]{:S(2)}) collective-permute-start(bf16[96,1152]{1,0:T(8,128)(2,1)S(1)} %append.5), channel_id=1, source_target_pairs={{0,112},{8,24},{16,0},{24,40},{32,16},{40,56},{48,32},{56,72},{64,... | collective-permute-start | bytes 663560 | tf_op jit(solution)/shard_map/ppermute | solution.py:41
  93.6 2.4 %collective-permute-start.26 = (bf16[6,128,128]{2,1,0:T(8,128)(2,1)S(1)}, bf16[6,128,128]{2,1,0:T(8,128)(2,1)S(1)}, u32[]{:S(2)}, u32[]{:S(2)}) collective-permute-start(bf16[6,128,128]{2,1,0:T(8,128)(2,1)S(1)} %get-tuple-element.43), channel_id=1, source_target_pairs={{0,16},{8,120},{16,32},{24,8},{32,48},{40,24},{48,64},{56,40},{64,... | collective-permute-start | bytes 589832 | tf_op jit(solution)/shard_map/ppermute | solution.py:41
  96.0 3.1 %collective-permute-done.32.d1 = bf16[96,1152]{1,0:T(8,128)(2,1)S(1)} collective-permute-done((bf16[96,1152]{1,0:T(8,128)(2,1)S(1)}, bf16[96,1152]{1,0:T(8,128)(2,1)S(1)}, u32[]{:S(2)}, u32[]{:S(2)}) %collective-permute-start.32) | collective-permute-done | bytes 221216 | tf_op jit(solution)/shard_map/ppermute | solution.py:41
  99.1 2.2 %collective-permute-done.26.r14.t = bf16[6,128,128]{2,1,0:T(8,128)(2,1)S(1)} collective-permute-done((bf16[6,128,128]{2,1,0:T(8,128)(2,1)S(1)}, bf16[6,128,128]{2,1,0:T(8,128)(2,1)S(1)}, u32[]{:S(2)}, u32[]{:S(2)}) %collective-permute-start.26) | collective-permute-done | bytes 196640 | tf_op jit(solution)/shard_map/ppermute | solution.py:41
  101.3 3.7 %collective-permute-start.33 = (bf16[96,1152]{1,0:T(8,128)(2,1)S(1)}, bf16[96,1152]{1,0:T(8,128)(2,1)S(1)}, u32[]{:S(2)}, u32[]{:S(2)}) collective-permute-start(bf16[96,1152]{1,0:T(8,128)(2,1)S(1)} %peer_rows.1), channel_id=1, source_target_pairs={{0,8},{8,0},{16,24},{24,16},{32,40},{40,32},{48,56},{56,48},{64,72... | collective-permute-start | bytes 663560 | tf_op jit(solution)/shard_map/ppermute | solution.py:25
  105.0 1.2 %collective-permute-start.27 = (bf16[4,128,128]{2,1,0:T(8,128)(2,1)S(1)}, bf16[4,128,128]{2,1,0:T(8,128)(2,1)S(1)}, u32[]{:S(2)}, u32[]{:S(2)}) collective-permute-start(bf16[4,128,128]{2,1,0:T(8,128)(2,1)S(1)} %get-tuple-element.46), channel_id=1, source_target_pairs={{0,32},{8,104},{16,48},{24,120},{32,64},{40,8},{48,80},{56,24},{64... | collective-permute-start | bytes 393224 | tf_op jit(solution)/shard_map/ppermute | solution.py:41
  106.2 2.8 %collective-permute-start.28 = (bf16[4,128,128]{2,1,0:T(8,128)(2,1)S(1)}, bf16[4,128,128]{2,1,0:T(8,128)(2,1)S(1)}, u32[]{:S(2)}, u32[]{:S(2)}) collective-permute-start(bf16[4,128,128]{2,1,0:T(8,128)(2,1)S(1)} %get-tuple-element.47.t), channel_id=1, source_target_pairs={{0,48},{8,88},{16,64},{24,104},{32,80},{40,120},{48,96},{56,8},{64... | collective-permute-start | bytes 393224 | tf_op jit(solution)/shard_map/ppermute | solution.py:41
  109.0 0.7 sum_z.1
  109.8 0.9 collective-permute-done.27
  110.6 3.4 %collective-permute-done.28 = bf16[4,128,128]{2,1,0:T(8,128)(2,1)S(1)} collective-permute-done((bf16[4,128,128]{2,1,0:T(8,128)(2,1)S(1)}, bf16[4,128,128]{2,1,0:T(8,128)(2,1)S(1)}, u32[]{:S(2)}, u32[]{:S(2)}) %collective-permute-start.28) | collective-permute-done | bytes 131104 | tf_op jit(solution)/shard_map/ppermute | solution.py:41
  114.1 1.6 %collective-permute-start.29 = (f32[2,128,128]{2,1,0:T(8,128)S(1)}, f32[2,128,128]{2,1,0:T(8,128)S(1)}, u32[]{:S(2)}, u32[]{:S(2)}) collective-permute-start(f32[2,128,128]{2,1,0:T(8,128)S(1)} %slice.23), channel_id=1, source_target_pairs={{0,8},{8,0},{16,24},{24,16},{32,40},{40,32},{48,56},{56,48},{64,72... | collective-permute-start | bytes 393224 | tf_op jit(solution)/shard_map/ppermute | solution.py:25
  115.8 0.9 collective-permute-done.29
  117.3 1.4 %weight_out.1 = (f32[128,1024]{1,0:T(8,128)}, f32[128]{0:T(128)}) custom-call(s32[2]{0:T(128)S(1)} %copy-done.4, bf16[64,1152]{1,0:T(8,128)(2,1)S(1)} %pad_maximum_fusion.1.mine, bf16[64,1152]{1,0:T(8,128)(2,1)S(1)} %collective-permute-done.35.theirs), custom_call_target="tpu_custom_call" | custom-call | bytes 1048576 | tf_op jit(solution)/shard_map/weight_out/pallas_call | solution.py:488
  (63 shorter events, 7.8 us)
Async XLA Ops:
  0.6 39.4 %copy-start = (bf16[64,128,128]{2,1,0:T(8,128)(2,1)S(1)}, bf16[64,128,128]{2,1,0:T(8,128)(2,1)}, u32[]{:S(2)}) copy-start(bf16[64,128,128]{2,1,0:T(8,128)(2,1)} %tiles.3) | copy-start | bytes 6291460
  0.6 4.4 %collective-permute-start.1 = (bf16[256,128]{1,0:T(8,128)(2,1)}, bf16[256,128]{1,0:T(8,128)(2,1)S(1)}, u32[]{:S(2)}, u32[]{:S(2)}) collective-permute-start(bf16[256,128]{1,0:T(8,128)(2,1)} %param.7), channel_id=1, source_target_pairs={{0,8},{8,0},{16,24},{24,16},{32,40},{40,32},{48,56},{56,48},{64,72... | collective-permute-start | bytes 196616 | tf_op jit(solution)/shard_map/ppermute | solution.py:25
  5.1 34.9 %collective-permute-start.2 = (bf16[64,128,128]{2,1,0:T(8,128)(2,1)}, bf16[64,128,128]{2,1,0:T(8,128)(2,1)}, u32[]{:S(2)}, u32[]{:S(2)}) collective-permute-start(bf16[64,128,128]{2,1,0:T(8,128)(2,1)} %tiles.3), channel_id=1, source_target_pairs={{0,8},{8,0},{16,24},{24,16},{32,40},{40,32},{48,56},{56,48},{64,72... | collective-permute-start | bytes 6291464 | tf_op jit(solution)/shard_map/ppermute | solution.py:25
  8.4 15.3 %collective-permute-start.10 = (bf16[784,128]{1,0:T(8,128)(2,1)}, bf16[784,128]{1,0:T(8,128)(2,1)S(1)}, u32[]{:S(2)}, u32[]{:S(2)}) collective-permute-start(bf16[784,128]{1,0:T(8,128)(2,1)} %pack_up.1.a), channel_id=1, source_target_pairs={{0,4},{1,5},{2,6},{3,7},{4,0},{5,1},{6,2},{7,3},{8,12},{9,13},{10,... | collective-permute-start | bytes 602120 | tf_op jit(solution)/shard_map/ppermute | solution.py:29
  9.5 9.8 %collective-permute-start.6 = (bf16[512,128]{1,0:T(8,128)(2,1)S(1)}, bf16[512,128]{1,0:T(8,128)(2,1)S(1)}, u32[]{:S(2)}, u32[]{:S(2)}) collective-permute-start(bf16[512,128]{1,0:T(8,128)(2,1)S(1)} %constant_dynamic-update-slice_fusion.a), channel_id=1, source_target_pairs={{0,96},{8,40},{16,112},{24,56},{32,0},{40,72},{48,16},{56,88},{64,... | collective-permute-start | bytes 393224 | tf_op jit(solution)/shard_map/ppermute | solution.py:41
  12.5 11.2 %collective-permute-start.4 = (bf16[512,128]{1,0:T(8,128)(2,1)S(1)}, bf16[512,128]{1,0:T(8,128)(2,1)S(1)}, u32[]{:S(2)}, u32[]{:S(2)}) collective-permute-start(bf16[512,128]{1,0:T(8,128)(2,1)S(1)} %constant_dynamic-update-slice_fusion.a), channel_id=1, source_target_pairs={{0,80},{8,56},{16,96},{24,72},{32,112},{40,88},{48,0},{56,104},{64... | collective-permute-start | bytes 393224 | tf_op jit(solution)/shard_map/ppermute | solution.py:41
  17.9 1.1 collective-permute-start
  19.0 4.8 %collective-permute-start.3 = (bf16[256,128]{1,0:T(8,128)(2,1)}, bf16[256,128]{1,0:T(8,128)(2,1)S(1)}, u32[]{:S(2)}, u32[]{:S(2)}) collective-permute-start(bf16[256,128]{1,0:T(8,128)(2,1)} %param.7), channel_id=1, source_target_pairs={{0,128},{8,136},{16,144},{24,152},{32,160},{40,168},{48,176},{56,1... | collective-permute-start | bytes 196616 | tf_op jit(solution)/shard_map/ppermute | solution.py:25
  19.3 8.5 %collective-permute-start.8 = (bf16[512,128]{1,0:T(8,128)(2,1)S(1)}, bf16[512,128]{1,0:T(8,128)(2,1)S(1)}, u32[]{:S(2)}, u32[]{:S(2)}) collective-permute-start(bf16[512,128]{1,0:T(8,128)(2,1)S(1)} %collective-permute-done.6.refs_1_), channel_id=1, source_target_pairs={{0,128},{8,136},{16,144},{24,152},{32,160},{40,168},{48,176},{56,1... | collective-permute-start | bytes 393224 | tf_op jit(solution)/shard_map/ppermute | solution.py:25
  23.8 0.9 copy-start.2
  24.8 9.3 %collective-permute-start.12 = (bf16[1568,128]{1,0:T(8,128)(2,1)S(1)}, bf16[1568,128]{1,0:T(8,128)(2,1)S(1)}, u32[]{:S(2)}, u32[]{:S(2)}) collective-permute-start(bf16[1568,128]{1,0:T(8,128)(2,1)S(1)} %append.4.refs_0_), channel_id=1, source_target_pairs={{0,3},{1,0},{2,1},{3,2},{4,7},{5,4},{6,5},{7,6},{8,11},{9,8},{10,9... | collective-permute-start | bytes 1204232 | tf_op jit(solution)/shard_map/ppermute | solution.py:29
  27.6 9.6 %collective-permute-start.11 = (bf16[1568,128]{1,0:T(8,128)(2,1)S(1)}, bf16[1568,128]{1,0:T(8,128)(2,1)S(1)}, u32[]{:S(2)}, u32[]{:S(2)}) collective-permute-start(bf16[1568,128]{1,0:T(8,128)(2,1)S(1)} %append.4.refs_0_), channel_id=1, source_target_pairs={{0,1},{1,2},{2,3},{3,0},{4,5},{5,6},{6,7},{7,4},{8,9},{9,10},{10,1... | collective-permute-start | bytes 1204232 | tf_op jit(solution)/shard_map/ppermute | solution.py:29
  27.6 5.7 %collective-permute-start.5 = (bf16[768,128]{1,0:T(8,128)(2,1)S(1)}, bf16[768,128]{1,0:T(8,128)(2,1)S(1)}, u32[]{:S(2)}, u32[]{:S(2)}) collective-permute-start(bf16[768,128]{1,0:T(8,128)(2,1)S(1)} %append.3.refs_0_), channel_id=1, source_target_pairs={{0,112},{8,24},{16,0},{24,40},{32,16},{40,56},{48,32},{56,72},{64,... | collective-permute-start | bytes 589832 | tf_op jit(solution)/shard_map/ppermute | solution.py:41
  27.8 4.1 %collective-permute-start.7 = (bf16[512,128]{1,0:T(8,128)(2,1)S(1)}, bf16[512,128]{1,0:T(8,128)(2,1)S(1)}, u32[]{:S(2)}, u32[]{:S(2)}) collective-permute-start(bf16[512,128]{1,0:T(8,128)(2,1)S(1)} %collective-permute-done.4.b), channel_id=1, source_target_pairs={{0,128},{8,136},{16,144},{24,152},{32,160},{40,168},{48,176},{56,1... | collective-permute-start | bytes 393224 | tf_op jit(solution)/shard_map/ppermute | solution.py:25
  28.1 0.7 copy-start.3
  33.3 6.7 %collective-permute-start.9 = (bf16[768,128]{1,0:T(8,128)(2,1)S(1)}, bf16[768,128]{1,0:T(8,128)(2,1)S(1)}, u32[]{:S(2)}, u32[]{:S(2)}) collective-permute-start(bf16[768,128]{1,0:T(8,128)(2,1)S(1)} %hold.1), channel_id=1, source_target_pairs={{0,128},{8,136},{16,144},{24,152},{32,160},{40,168},{48,176},{56,1... | collective-permute-start | bytes 589832 | tf_op jit(solution)/shard_map/ppermute | solution.py:25
  37.2 12.9 %collective-permute-start.14 = (bf16[784,128]{1,0:T(8,128)(2,1)S(1)}, bf16[784,128]{1,0:T(8,128)(2,1)S(1)}, u32[]{:S(2)}, u32[]{:S(2)}) collective-permute-start(bf16[784,128]{1,0:T(8,128)(2,1)S(1)} %get-tuple-element.29.refs_8_), channel_id=1, source_target_pairs={{0,1},{1,2},{2,3},{3,0},{4,5},{5,6},{6,7},{7,4},{8,9},{9,10},{10,1... | collective-permute-start | bytes 602120 | tf_op jit(solution)/shard_map/ppermute | solution.py:29
  37.3 12.9 %collective-permute-start.15 = (bf16[784,128]{1,0:T(8,128)(2,1)S(1)}, bf16[784,128]{1,0:T(8,128)(2,1)S(1)}, u32[]{:S(2)}, u32[]{:S(2)}) collective-permute-start(bf16[784,128]{1,0:T(8,128)(2,1)S(1)} %get-tuple-element.30.refs_9_), channel_id=1, source_target_pairs={{0,3},{1,0},{2,1},{3,2},{4,7},{5,4},{6,5},{7,6},{8,11},{9,8},{10,9... | collective-permute-start | bytes 602120 | tf_op jit(solution)/shard_map/ppermute | solution.py:29
  40.0 16.1 %copy-start.4 = (s32[2]{0:T(128)S(1)}, s32[2]{0:T(128)}, u32[]{:S(2)}) copy-start(s32[2]{0:T(128)} %pad_add_fusion.1.ids) | copy-start | bytes 28
  46.2 22.7 %copy-start.1 = (bf16[128,1024]{1,0:T(8,128)(2,1)S(1)}, bf16[128,1024]{1,0:T(8,128)(2,1)}, u32[]{:S(2)}) copy-start(bf16[128,1024]{1,0:T(8,128)(2,1)} %w_own.1) | copy-start | bytes 786436
  46.2 4.9 %collective-permute-start.13 = (f32[2,128,128]{2,1,0:T(8,128)S(1)}, f32[2,128,128]{2,1,0:T(8,128)S(1)}, u32[]{:S(2)}, u32[]{:S(2)}) collective-permute-start(f32[2,128,128]{2,1,0:T(8,128)S(1)} %get-tuple-element.32), channel_id=1, source_target_pairs={{0,8},{8,0},{16,24},{24,16},{32,40},{40,32},{48,56},{56,48},{64,72... | collective-permute-start | bytes 393224 | tf_op jit(solution)/shard_map/ppermute | solution.py:25
  51.2 4.9 %collective-permute-start.16 = (bf16[256,128]{1,0:T(8,128)(2,1)S(1)}, bf16[256,128]{1,0:T(8,128)(2,1)S(1)}, u32[]{:S(2)}, u32[]{:S(2)}) collective-permute-start(bf16[256,128]{1,0:T(8,128)(2,1)S(1)} %bitcast.23), channel_id=1, source_target_pairs={{0,4},{1,5},{2,6},{3,7},{4,0},{5,1},{6,2},{7,3},{8,12},{9,13},{10,... | collective-permute-start | bytes 196616 | tf_op jit(solution)/shard_map/ppermute | solution.py:29
  57.5 11.4 %collective-permute-start.20 = (bf16[1024,512]{1,0:T(8,128)(2,1)S(1)}, bf16[1024,512]{1,0:T(8,128)(2,1)S(1)}, u32[]{:S(2)}, u32[]{:S(2)}) collective-permute-start(bf16[1024,512]{1,0:T(8,128)(2,1)S(1)} %get-tuple-element.33.w0), channel_id=1, source_target_pairs={{0,8},{8,0},{16,24},{24,16},{32,40},{40,32},{48,56},{56,48},{64,72... | collective-permute-start | bytes 3145736 | tf_op jit(solution)/shard_map/ppermute | solution.py:25
  59.1 6.6 %collective-permute-start.19 = (bf16[512,128]{1,0:T(8,128)(2,1)S(1)}, bf16[512,128]{1,0:T(8,128)(2,1)S(1)}, u32[]{:S(2)}, u32[]{:S(2)}) collective-permute-start(bf16[512,128]{1,0:T(8,128)(2,1)S(1)} %pad_maximum_fusion.2.refs_5_.p0), channel_id=1, source_target_pairs={{0,2},{1,3},{2,0},{3,1},{4,6},{5,7},{6,4},{7,5},{8,10},{9,11},{10,... | collective-permute-start | bytes 393224 | tf_op jit(solution)/shard_map/ppermute | solution.py:29
  59.1 7.5 %collective-permute-start.18 = (bf16[512,128]{1,0:T(8,128)(2,1)S(1)}, bf16[512,128]{1,0:T(8,128)(2,1)S(1)}, u32[]{:S(2)}, u32[]{:S(2)}) collective-permute-start(bf16[512,128]{1,0:T(8,128)(2,1)S(1)} %pad_maximum_fusion.2.refs_5_.p0), channel_id=1, source_target_pairs={{0,3},{1,0},{2,1},{3,2},{4,7},{5,4},{6,5},{7,6},{8,11},{9,8},{10,9... | collective-permute-start | bytes 393224 | tf_op jit(solution)/shard_map/ppermute | solution.py:29
  60.1 8.7 %collective-permute-start.17 = (bf16[512,128]{1,0:T(8,128)(2,1)S(1)}, bf16[512,128]{1,0:T(8,128)(2,1)S(1)}, u32[]{:S(2)}, u32[]{:S(2)}) collective-permute-start(bf16[512,128]{1,0:T(8,128)(2,1)S(1)} %pad_maximum_fusion.2.refs_5_.p0), channel_id=1, source_target_pairs={{0,1},{1,2},{2,3},{3,0},{4,5},{5,6},{6,7},{7,4},{8,9},{9,10},{10,1... | collective-permute-start | bytes 393224 | tf_op jit(solution)/shard_map/ppermute | solution.py:29
  71.0 1.7 %collective-permute-start.22 = (f32[64,1152]{1,0:T(8,128)S(1)}, f32[64,1152]{1,0:T(8,128)S(1)}, u32[]{:S(2)}, u32[]{:S(2)}) collective-permute-start(f32[64,1152]{1,0:T(8,128)S(1)} %get-tuple-element.39), channel_id=1, source_target_pairs={{0,8},{8,0},{16,24},{24,16},{32,40},{40,32},{48,56},{56,48},{64,72... | collective-permute-start | bytes 884744 | tf_op jit(solution)/shard_map/ppermute | solution.py:25
  71.5 1.8 %collective-permute-start.21 = (bf16[2,128,128]{2,1,0:T(8,128)(2,1)S(1)}, bf16[2,128,128]{2,1,0:T(8,128)(2,1)S(1)}, u32[]{:S(2)}, u32[]{:S(2)}) collective-permute-start(bf16[2,128,128]{2,1,0:T(8,128)(2,1)S(1)} %bitcast.26), channel_id=1, source_target_pairs={{0,8},{8,0},{16,24},{24,16},{32,40},{40,32},{48,56},{56,48},{64,72... | collective-permute-start | bytes 196616 | tf_op jit(solution)/shard_map/ppermute | solution.py:25
  72.7 7.2 %collective-permute-start.24 = (bf16[32,1152]{1,0:T(8,128)(2,1)S(1)}, bf16[32,1152]{1,0:T(8,128)(2,1)S(1)}, u32[]{:S(2)}, u32[]{:S(2)}) collective-permute-start(bf16[32,1152]{1,0:T(8,128)(2,1)S(1)} %fusion.send), channel_id=1, source_target_pairs={{0,128},{8,136},{16,144},{24,152},{32,160},{40,168},{48,176},{56,1... | collective-permute-start | bytes 221192 | tf_op jit(solution)/shard_map/ppermute | solution.py:25
  79.1 14.4 %collective-permute-start.23 = (bf16[16,128,128]{2,1,0:T(8,128)(2,1)S(1)}, bf16[16,128,128]{2,1,0:T(8,128)(2,1)S(1)}, u32[]{:S(2)}, u32[]{:S(2)}) collective-permute-start(bf16[16,128,128]{2,1,0:T(8,128)(2,1)S(1)} %get-tuple-element.41.far), channel_id=1, source_target_pairs={{0,128},{8,136},{16,144},{24,152},{32,160},{40,168},{48,176},{56,1... | collective-permute-start | bytes 1572872 | tf_op jit(solution)/shard_map/ppermute | solution.py:25
  80.0 2.4 %collective-permute-start.25 = (bf16[32,1152]{1,0:T(8,128)(2,1)S(1)}, bf16[32,1152]{1,0:T(8,128)(2,1)S(1)}, u32[]{:S(2)}, u32[]{:S(2)}) collective-permute-start(bf16[32,1152]{1,0:T(8,128)(2,1)S(1)} %quarter_up.1.own), channel_id=1, source_target_pairs={{0,8},{8,0},{16,24},{24,16},{32,40},{40,32},{48,56},{56,48},{64,72... | collective-permute-start | bytes 221192 | tf_op jit(solution)/shard_map/ppermute | solution.py:25
  82.4 7.8 %collective-permute-start.31 = (bf16[64,1152]{1,0:T(8,128)(2,1)S(1)}, bf16[64,1152]{1,0:T(8,128)(2,1)S(1)}, u32[]{:S(2)}, u32[]{:S(2)}) collective-permute-start(bf16[64,1152]{1,0:T(8,128)(2,1)S(1)} %pad_maximum_fusion.ready.a), channel_id=1, source_target_pairs={{0,96},{8,40},{16,112},{24,56},{32,0},{40,72},{48,16},{56,88},{64,... | collective-permute-start | bytes 442376 | tf_op jit(solution)/shard_map/ppermute | solution.py:41
  82.7 8.3 %collective-permute-start.30 = (bf16[64,1152]{1,0:T(8,128)(2,1)S(1)}, bf16[64,1152]{1,0:T(8,128)(2,1)S(1)}, u32[]{:S(2)}, u32[]{:S(2)}) collective-permute-start(bf16[64,1152]{1,0:T(8,128)(2,1)S(1)} %pad_maximum_fusion.ready.a), channel_id=1, source_target_pairs={{0,80},{8,56},{16,96},{24,72},{32,112},{40,88},{48,0},{56,104},{64... | collective-permute-start | bytes 442376 | tf_op jit(solution)/shard_map/ppermute | solution.py:41
  91.0 8.1 %collective-permute-start.32 = (bf16[96,1152]{1,0:T(8,128)(2,1)S(1)}, bf16[96,1152]{1,0:T(8,128)(2,1)S(1)}, u32[]{:S(2)}, u32[]{:S(2)}) collective-permute-start(bf16[96,1152]{1,0:T(8,128)(2,1)S(1)} %append.5), channel_id=1, source_target_pairs={{0,112},{8,24},{16,0},{24,40},{32,16},{40,56},{48,32},{56,72},{64,... | collective-permute-start | bytes 663560 | tf_op jit(solution)/shard_map/ppermute | solution.py:41
  93.6 7.7 %collective-permute-start.26 = (bf16[6,128,128]{2,1,0:T(8,128)(2,1)S(1)}, bf16[6,128,128]{2,1,0:T(8,128)(2,1)S(1)}, u32[]{:S(2)}, u32[]{:S(2)}) collective-permute-start(bf16[6,128,128]{2,1,0:T(8,128)(2,1)S(1)} %get-tuple-element.43), channel_id=1, source_target_pairs={{0,16},{8,120},{16,32},{24,8},{32,48},{40,24},{48,64},{56,40},{64,... | collective-permute-start | bytes 589832 | tf_op jit(solution)/shard_map/ppermute | solution.py:41
  101.3 7.6 %collective-permute-start.33 = (bf16[96,1152]{1,0:T(8,128)(2,1)S(1)}, bf16[96,1152]{1,0:T(8,128)(2,1)S(1)}, u32[]{:S(2)}, u32[]{:S(2)}) collective-permute-start(bf16[96,1152]{1,0:T(8,128)(2,1)S(1)} %peer_rows.1), channel_id=1, source_target_pairs={{0,8},{8,0},{16,24},{24,16},{32,40},{40,32},{48,56},{56,48},{64,72... | collective-permute-start | bytes 663560 | tf_op jit(solution)/shard_map/ppermute | solution.py:25
  105.0 5.6 %collective-permute-start.27 = (bf16[4,128,128]{2,1,0:T(8,128)(2,1)S(1)}, bf16[4,128,128]{2,1,0:T(8,128)(2,1)S(1)}, u32[]{:S(2)}, u32[]{:S(2)}) collective-permute-start(bf16[4,128,128]{2,1,0:T(8,128)(2,1)S(1)} %get-tuple-element.46), channel_id=1, source_target_pairs={{0,32},{8,104},{16,48},{24,120},{32,64},{40,8},{48,80},{56,24},{64... | collective-permute-start | bytes 393224 | tf_op jit(solution)/shard_map/ppermute | solution.py:41
  106.2 7.8 %collective-permute-start.28 = (bf16[4,128,128]{2,1,0:T(8,128)(2,1)S(1)}, bf16[4,128,128]{2,1,0:T(8,128)(2,1)S(1)}, u32[]{:S(2)}, u32[]{:S(2)}) collective-permute-start(bf16[4,128,128]{2,1,0:T(8,128)(2,1)S(1)} %get-tuple-element.47.t), channel_id=1, source_target_pairs={{0,48},{8,88},{16,64},{24,104},{32,80},{40,120},{48,96},{56,8},{64... | collective-permute-start | bytes 393224 | tf_op jit(solution)/shard_map/ppermute | solution.py:41
  109.7 6.0 %collective-permute-start.34 = (bf16[32,1152]{1,0:T(8,128)(2,1)S(1)}, bf16[32,1152]{1,0:T(8,128)(2,1)S(1)}, u32[]{:S(2)}, u32[]{:S(2)}) collective-permute-start(bf16[32,1152]{1,0:T(8,128)(2,1)S(1)} %sum_z.1), channel_id=1, source_target_pairs={{0,128},{8,136},{16,144},{24,152},{32,160},{40,168},{48,176},{56,1... | collective-permute-start | bytes 221192 | tf_op jit(solution)/shard_map/ppermute | solution.py:25
  114.1 2.5 %collective-permute-start.29 = (f32[2,128,128]{2,1,0:T(8,128)S(1)}, f32[2,128,128]{2,1,0:T(8,128)S(1)}, u32[]{:S(2)}, u32[]{:S(2)}) collective-permute-start(f32[2,128,128]{2,1,0:T(8,128)S(1)} %slice.23), channel_id=1, source_target_pairs={{0,8},{8,0},{16,24},{24,16},{32,40},{40,32},{48,56},{56,48},{64,72... | collective-permute-start | bytes 393224 | tf_op jit(solution)/shard_map/ppermute | solution.py:25
  115.7 1.6 %collective-permute-start.35 = (bf16[64,1152]{1,0:T(8,128)(2,1)S(1)}, bf16[64,1152]{1,0:T(8,128)(2,1)S(1)}, u32[]{:S(2)}, u32[]{:S(2)}) collective-permute-start(bf16[64,1152]{1,0:T(8,128)(2,1)S(1)} %pad_maximum_fusion.1.mine), channel_id=1, source_target_pairs={{0,8},{8,0},{16,24},{24,16},{32,40},{40,32},{48,56},{56,48},{64,72... | collective-permute-start | bytes 442376 | tf_op jit(solution)/shard_map/ppermute | solution.py:25
